TPU v7x, 32 devices: a whole 2x2x4 slice. The times are simulated.
32 devices in a mesh: ctx: 8 (over z, y), mem: 4 (over x, core).
Axes of the slice: x: 2, y: 2, z: 4, core: 2. Of those that a mesh axis runs over, the one named last changes fastest.
Arguments:
- hidden_states: bfloat16 [1024, 4096], P('ctx', 'mem'), may hold values from -6 to 6
- w_query: bfloat16 [4096, 4096], P(None, 'mem'), may hold values from -0.09375 to 0.09375
- local_keys: bfloat16 [1024, 4096], P('ctx', 'mem')
- local_values: bfloat16 [1024, 4096], P('ctx', 'mem'), may hold values from -6 to 6
- memory_keys: bfloat16 [16384, 4096], P(('ctx', 'mem'))
- memory_values: bfloat16 [16384, 4096], P(('ctx', 'mem')), may hold values from -6 to 6
- tile_ids: int32 [1024, 16], P('ctx'), may hold values from 0 to 127, as said below
- tile_counts: int32 [1024], P('ctx'), may hold values from 12 to 16
- gate_bias: float32 [64], P('mem'), may hold values from -2 to 2
- w_output: bfloat16 [4096, 4096], P('mem'), may hold values from -0.09375 to 0.09375
Outputs:
- attended: bfloat16 [1024, 4096], P('ctx', 'mem')
Inputs may be any that keep to these rules, and one draw needn't show every extreme that they name: `tile_ids`: the 16 tiles named in one row are distinct; only the first tile_counts of them are live. Among the live picks of the 128 rows of one ctx shard (aligned blocks), no tile is named by more than 32 rows, and in every such block some tile is named by exactly 32 rows.
All inputs are finite; a program needn't handle non-finite values.
Results may differ from a plain program's by a relative error of at most 0.02.
Values may be sent and summed in bfloat16 or wider, within the bound.
No kernel may reach another device: no remote copies, remote signals or barrier semaphores. Data moves between devices by JAX's collectives and lax.ppermute only.
A program may use at most 192 MiB of HBM per device.

v0:
```python
import jax
import jax.numpy as jnp
from jax import lax
from jax.sharding import PartitionSpec as P

DH = 64
TILE_ROWS = 128


score_scale = 0.125


def from_behind(block, axis, distance):
    devices = range(lax.axis_size(axis))
    route = [(i - distance, i) for i in devices if i - distance in devices]
    return lax.ppermute(block, axis, route)


def serve_tiles(asked, memory_keys, memory_values, ctx_size, mem_size, heads_here):
    tiles_here = memory_keys.shape[0] // TILE_ROWS
    features = asked.shape[1]
    grouped = asked.reshape(ctx_size, mem_size, tiles_here, -1, heads_here, DH)
    key_tiles = memory_keys.reshape(tiles_here, TILE_ROWS, mem_size, heads_here, DH)
    value_tiles = memory_values.reshape(tiles_here, TILE_ROWS, mem_size, heads_here, DH)
    outputs = []
    maxima = []
    totals = []
    for tile_index in range(tiles_here):
        scores = (
            jnp.einsum(
                "cmshd,rmhd->cmhsr",
                grouped[:, :, tile_index],
                key_tiles[tile_index],
                preferred_element_type=jnp.float32,
            )
            * score_scale
        )
        highest = jnp.max(scores, axis=-1)
        weights_f = jnp.exp(scores - highest[..., None])
        summed = jnp.sum(weights_f, axis=-1)
        mixed = jnp.einsum(
            "cmhsr,rmhd->cmshd",
            weights_f.astype(jnp.bfloat16),
            value_tiles[tile_index],
            preferred_element_type=jnp.float32,
        )
        summed_turned = jnp.transpose(summed, (0, 1, 3, 2))
        outputs.append((mixed / summed_turned[..., None]).astype(jnp.bfloat16))
        maxima.append(jnp.transpose(highest, (0, 1, 3, 2)))
        totals.append(summed_turned)
    out_rows = jnp.stack(outputs, axis=2).reshape(-1, features)
    max_rows = jnp.stack(maxima, axis=2).reshape(-1, heads_here)
    total_rows = jnp.stack(totals, axis=2).reshape(-1, heads_here)
    return (out_rows, max_rows, total_rows)


def on_device(
    hidden_states,
    w_query,
    local_keys,
    local_values,
    memory_keys,
    memory_values,
    tile_ids,
    tile_counts,
    gate_bias,
    w_output,
):
    row_count = hidden_states.shape[0]
    features = w_query.shape[1]
    heads_here = features // DH
    ctx_size = lax.axis_size("ctx")
    mem_size = lax.axis_size("mem")
    pick_count = tile_ids.shape[1]
    queries = jnp.dot(
        lax.all_gather(hidden_states, "mem", axis=1, tiled=True),
        w_query,
        preferred_element_type=jnp.float32,
    ).astype(jnp.bfloat16)
    earlier = from_behind((local_keys, local_values), "ctx", 1)
    window_keys = jnp.concatenate([earlier[0], local_keys], 0).reshape(
        2 * row_count, heads_here, DH
    )
    window_values = jnp.concatenate([earlier[1], local_values], 0).reshape(
        2 * row_count, heads_here, DH
    )
    query_heads = queries.reshape(row_count, heads_here, DH)
    scores = (
        jnp.einsum("ihd,jhd->hij", query_heads, window_keys, preferred_element_type=jnp.float32)
        * score_scale
    )
    query_pos = jnp.arange(row_count, dtype=jnp.int32)[:, None]
    key_pos = jnp.arange(2 * row_count, dtype=jnp.int32)[None, :]
    allowed = (
        (key_pos > query_pos)
        & (key_pos <= query_pos + row_count)
        & ((key_pos >= row_count) | (lax.axis_index("ctx") > 0))
    )
    scores = jnp.where(allowed[None], scores, -jnp.inf)
    highest = jnp.max(scores, axis=-1, keepdims=True)
    weights_f = jnp.exp(scores - highest)
    summed = jnp.sum(weights_f, axis=-1)
    mixed = jnp.einsum(
        "hij,jhd->ihd",
        weights_f.astype(jnp.bfloat16),
        window_values,
        preferred_element_type=jnp.float32,
    )
    local_out = mixed / jnp.transpose(summed)[..., None]
    total_tiles = memory_keys.shape[0] // TILE_ROWS * ctx_size * mem_size
    most_rows = 2 * ((row_count * pick_count + total_tiles - 1) // total_tiles)
    slot_count = total_tiles * most_rows
    live = jnp.arange(pick_count, dtype=jnp.int32)[None, :] < tile_counts[:, None]
    hits = jnp.sum(
        (
            (tile_ids[:, :, None] == jnp.arange(total_tiles, dtype=jnp.int32)[None, None, :])
            & live[:, :, None]
        ).astype(jnp.int32),
        axis=1,
    )
    before = jnp.cumsum(hits, axis=0) - hits
    ranks = jnp.take_along_axis(before, tile_ids, axis=1)
    target = jnp.where(live, tile_ids * most_rows + ranks, slot_count).reshape(-1)
    sources = jnp.broadcast_to(queries[:, None, :], (row_count, pick_count, features)).reshape(
        -1, features
    )
    outgoing = jnp.zeros((slot_count, features), jnp.bfloat16).at[target].set(sources, mode="drop")
    asked = lax.all_to_all(outgoing, ("ctx", "mem"), split_axis=0, concat_axis=0, tiled=True)
    served = serve_tiles(asked, memory_keys, memory_values, ctx_size, mem_size, heads_here)
    answer = (
        lax.all_to_all(served[0], ("ctx", "mem"), split_axis=0, concat_axis=0, tiled=True),
        lax.all_to_all(
            served[1].astype(jnp.bfloat16), ("ctx", "mem"), split_axis=0, concat_axis=0, tiled=True
        ).astype(jnp.float32),
        lax.all_to_all(
            served[2].astype(jnp.bfloat16), ("ctx", "mem"), split_axis=0, concat_axis=0, tiled=True
        ).astype(jnp.float32),
    )
    safe_target = jnp.minimum(target, slot_count - 1)
    picked = (
        jnp.take(answer[0], safe_target, axis=0)
        .reshape(row_count, pick_count, heads_here, DH)
        .astype(jnp.float32)
    )
    picked_max = jnp.take(answer[1], safe_target, axis=0).reshape(row_count, pick_count, heads_here)
    picked_total = jnp.take(answer[2], safe_target, axis=0).reshape(
        row_count, pick_count, heads_here
    )
    live_heads = live[:, :, None]
    top_max = jnp.max(jnp.where(live_heads, picked_max, -jnp.inf), axis=1, keepdims=True)
    factor = jnp.where(
        live_heads, picked_total * jnp.exp(jnp.where(live_heads, picked_max - top_max, 0.0)), 0.0
    )
    memory_out = jnp.sum(factor[..., None] * picked, axis=1) / jnp.sum(factor, axis=1)[..., None]
    gate = jax.nn.sigmoid(gate_bias)[None, :, None]
    combined = (
        (gate * memory_out + (1.0 - gate) * local_out)
        .astype(jnp.bfloat16)
        .reshape(row_count, features)
    )
    partial_out = jnp.dot(combined, w_output, preferred_element_type=jnp.float32)
    return lax.psum_scatter(
        partial_out.astype(jnp.bfloat16), "mem", scatter_dimension=1, tiled=True
    )


def solution(mesh):
    in_specs = (
        P("ctx", "mem"),
        P(None, "mem"),
        P("ctx", "mem"),
        P("ctx", "mem"),
        P(("ctx", "mem"), None),
        P(("ctx", "mem"), None),
        P("ctx", None),
        P("ctx"),
        P("mem"),
        P("mem", None),
    )
    out_specs = P("ctx", "mem")
    return jax.shard_map(
        on_device, mesh=mesh, in_specs=in_specs, out_specs=out_specs, check_vma=False
    )
```

profile of v0, /device:TPU:0, one launch (start us, length us, event | category | flops | bytes accessed | tf_op | source)
XLA Modules:
  0.0 704.2 jit_solution(6302673889866297548)
XLA Ops:
  6.5 0.7 all-gather.2.cloned.1.call-update
  7.3 0.8 copy.173
  9.5 0.9 convert_reduce_fusion
  11.5 13.1 %gather_fusion.1 = s32[2048]{0:T(1024)S(1)} fusion(s32[128,128]{1,0:T(8,128)S(1)} %sub.59, s32[2048]{0:T(1024)S(1)} %reshape.287), kind=kCustom, calls=%fused_computation.3 | custom fusion | bytes 32768 | tf_op jit(solution)/shard_map/jit(take_along_axis)/gather | solution.py:122
  26.2 2.2 all-gather.2.cloned.1.call-done
  28.4 5.0 convolution_convert_fusion.1
  33.4 2.6 broadcast_in_dim.98
  35.9 15.3 %scatter_custom_fusion = bf16[4096,1024]{1,0:T(8,128)(2,1)} fusion(s32[2048]{0:T(1024)S(1)} %bitcast.252, bf16[2048,1024]{1,0:T(8,128)(2,1)} %bitcast.231, bf16[]{:T(256)} %constant.24.clone.1), kind=kCustom, calls=%fused_computation.57 | custom fusion | bytes 8389120 | tf_op jit(solution)/shard_map/scatter | solution.py:127
  51.2 5.4 all-to-all-start
  56.6 3.5 fusion.92
  60.1 1.4 copy.189
  61.5 4.0 fusion.91
  65.5 2.3 copy.203
  67.7 2.3 copy.186
  70.0 2.3 copy.202
  72.3 1.3 copy.183
  73.6 2.3 copy.201
  75.9 1.3 copy.180
  77.2 1.3 copy.200
  78.5 164.2 %all-to-all-done = bf16[32,128,1024]{2,1,0:T(8,128)(2,1)} async-done(((bf16[32,128,1024]{2,1,0:T(8,128)(2,1)}), bf16[32,128,1024]{2,1,0:T(8,128)(2,1)}, u32[]{:S(2)}, u32[]{:S(2)}) %all-to-all-start) | async-done | bytes 8388640 | tf_op jit(solution)/shard_map/all_to_all | solution.py:128
  242.7 22.1 %reshape.254 = bf16[8,4,4,32,16,64]{5,4,3,2,1,0:T(8,128)(2,1)} reshape(bf16[32,128,1024]{2,1,0:T(8,128)(2,1)} %all-to-all-done) | data formatting | bytes 16777216 | tf_op jit(solution)/shard_map/reshape | solution.py:22
  264.7 9.2 %fusion.90 = (bf16[8,4,1,32,16,64]{5,4,3,2,1,0:T(8,128)(2,1)S(1)}, bf16[8,4,1,32,16,64]{5,4,3,2,1,0:T(8,128)(2,1)}, bf16[8,4,1,32,16,64]{5,4,3,2,1,0:T(8,128)(2,1)S(1)}, bf16[8,4,1,32,16,64]{5,4,3,2,1,0:T(8,128)(2,1)S(1)}) fusion(bf16[8,4,4,32,16,64]{5,4,3,2,1,0:T(8,128)(2,1)} %reshape.254), kind=kLoop, calls=%fused_computation.140 | loop fusion | bytes 16777216 | tf_op jit(solution)/shard_map/slice | solution.py:32
  273.9 2.4 bitcast_reduce_fusion
  276.4 5.5 fusion.16
  281.8 5.6 bitcast_reduce_fusion.1
  287.4 1.1 convert_bitcast_fusion.1
  288.6 6.8 fusion.14
  295.4 4.4 bitcast_reduce_fusion.2
  299.7 1.3 convert_bitcast_fusion.2
  301.0 5.7 fusion.12
  306.7 2.4 bitcast_reduce_fusion.3
  309.2 3.1 copy-done.3
  312.4 4.7 fusion.10
  317.6 0.9 convert_element_type.69
  318.6 2.6 all-to-all-start.2
  321.4 9.4 %fusion.42 = bf16[8,4,1,32,16,64]{5,3,0,4,1,2:T(8,128)(2,1)} fusion(f32[8,4,32,16]{2,0,3,1:T(8,128)S(1)} %bitcast.237, bf16[128,4,16,64,1]{0,3,4,2,1:T(8,128)(2,1)} %bitcast.245, f32[4,16,8,32,128]{4,3,2,1,0:T(8,128)} %copy-done, f32[8,4,16,32]{3,0,2,1:T(8,128)S(1)} %copy-done.9), kind=kOutput, calls=%fused_computation.62 | convolution fusion | flops 276824064 | bytes 11665408 | tf_op jit(solution)/shard_map/cmhsr,rmhd->cmshd/dot_general | solution.py:41
  330.8 6.4 fusion.41
  337.3 6.4 fusion.40
  343.7 6.5 fusion.39
  350.7 0.9 convert_element_type.66
  351.6 5.8 all-to-all-start.1
  357.4 9.4 %pad_maximum_fusion = bf16[8,4,4,32,16,64]{5,3,0,4,1,2:T(8,128)(2,1)S(1)} fusion(bf16[8,4,1,32,16,64]{5,3,0,4,1,2:T(8,128)(2,1)} %fusion.42, bf16[8,4,1,32,16,64]{5,3,0,4,1,2:T(8,128)(2,1)} %fusion.41, bf16[8,4,1,32,16,64]{5,3,0,4,1,2:T(8,128)(2,1)} %fusion.40, bf16[8,4,1,32,16,64]{5,3,0,4,1,2:T(8,128)(2,1)} %fusion.39), kind=kLoop, calls=%fused_computation.6 | loop fusion | flops 12582912 | bytes 16777216 | tf_op jit(solution)/shard_map/stack | solution.py:51
  366.9 15.8 %copy.204 = bf16[8,4,4,32,16,64]{5,4,3,2,1,0:T(8,128)(2,1)} copy(bf16[8,4,4,32,16,64]{5,3,0,4,1,2:T(8,128)(2,1)S(1)} %pad_maximum_fusion) | data formatting | bytes 16777216 | tf_op jit(solution)/shard_map/stack | solution.py:51
  382.7 22.5 %all_to_all.26 = bf16[32,128,1024]{2,1,0:T(8,128)(2,1)} reshape(bf16[8,4,4,32,16,64]{5,4,3,2,1,0:T(8,128)(2,1)} %copy.204) | data formatting | bytes 16777216 | tf_op jit(solution)/shard_map/all_to_all | solution.py:131
  405.3 6.0 all-to-all-start.3
  411.3 3.6 collective-permute-start
  414.9 3.4 collective-permute-start.1
  420.6 40.6 %collective-permute-done = bf16[128,1024]{1,0:T(8,128)(2,1)S(1)} collective-permute-done((bf16[128,1024]{1,0:T(8,128)(2,1)S(1)}, bf16[128,1024]{1,0:T(8,128)(2,1)S(1)}, u32[]{:S(2)}, u32[]{:S(2)}) %collective-permute-start) | collective-permute-done | bytes 262176 | tf_op jit(solution)/shard_map/ppermute | solution.py:16
  461.3 1.0 copy.207
  462.3 19.4 %collective-permute-done.1 = bf16[128,1024]{1,0:T(8,128)(2,1)S(1)} collective-permute-done((bf16[128,1024]{1,0:T(8,128)(2,1)S(1)}, bf16[128,1024]{1,0:T(8,128)(2,1)S(1)}, u32[]{:S(2)}, u32[]{:S(2)}) %collective-permute-start.1) | collective-permute-done | bytes 262176 | tf_op jit(solution)/shard_map/ppermute | solution.py:16
  482.7 1.3 copy-done.4
  484.0 0.9 fusion.52
  485.3 5.5 gather_fusion.3
  491.1 7.6 %gather_fusion.2 = f32[2048,16]{1,0:T(8,128)} fusion(f32[4096,16]{1,0:T(8,128)S(1)} %bitcast.222, s32[2048]{0:T(1024)S(1)} %fusion.82), kind=kCustom, calls=%fused_computation.clone | custom fusion | bytes 270336 | tf_op jit(solution)/shard_map/jit(_take)/gather | solution.py:146
  498.7 1.6 broadcast_select_fusion
  500.3 2.2 fusion.93
  502.5 94.8 %all-to-all-done.3 = bf16[32,128,1024]{2,1,0:T(8,128)(2,1)} async-done(((bf16[32,128,1024]{2,1,0:T(8,128)(2,1)}), bf16[32,128,1024]{2,1,0:T(8,128)(2,1)}, u32[]{:S(2)}, u32[]{:S(2)}) %all-to-all-start.3) | async-done | bytes 8388640 | tf_op jit(solution)/shard_map/all_to_all | solution.py:131
  597.4 15.4 %gather_fusion = bf16[2048,1024]{1,0:T(8,128)(2,1)} fusion(bf16[4096,1024]{1,0:T(8,128)(2,1)} %bitcast.64, s32[2048]{0:T(1024)S(1)} %broadcast_clamp_fusion), kind=kCustom, calls=%fused_computation.2 | custom fusion | bytes 8396800 | tf_op jit(solution)/shard_map/jit(_take)/gather | solution.py:141
  612.8 11.6 %gather.15 = bf16[128,16,16,64]{3,2,1,0:T(8,128)(2,1)} reshape(bf16[2048,1024]{1,0:T(8,128)(2,1)} %gather_fusion) | data formatting | bytes 8388608 | tf_op jit(solution)/shard_map/jit(_take)/gather | solution.py:141
  624.4 9.3 %multiply_reduce_fusion = f32[128,16,64]{2,1,0:T(8,128)S(1)} fusion(bf16[128,16,16,64]{3,2,1,0:T(8,128)(2,1)} %gather.15, f32[128,16,16]{2,1,0:T(8,128)} %get-tuple-element.37, pred[128,16]{1,0:T(8,128)(4,1)S(1)} %copy-done.22), kind=kLoop, calls=%fused_computation.7 | loop fusion | flops 8257536 | bytes 4851712 | tf_op jit(solution)/shard_map/reduce_sum | solution.py:154
  633.8 1.2 copy.206
  635.0 1.9 fusion.71
  636.9 5.7 convolution_convert_fusion
  642.6 54.6 %reduce-scatter.2.cloned.1.call-done = bf16[128,1024]{1,0:T(8,128)(2,1)} async-done(((bf16[128,4096]{1,0:T(8,128)(2,1)}), bf16[128,1024]{1,0:T(8,128)(2,1)}) %reduce-scatter.2.cloned.1.call-update) | async-done | bytes 262160 | tf_op jit(solution)/shard_map/reduce_scatter | solution.py:162
  (128 shorter events, 9.3 us)
Async XLA Ops:
  6.5 21.8 %all-gather.2.cloned.1.call-start = ((), (), s32[]{:S(2)}) async-start(), calls=%async_computation.5 | async-start | bytes 1310720 | tf_op jit(solution)/shard_map/all_gather | solution.py:76
  8.8 0.6 copy-start.23
  11.5 13.2 %copy-start.21 = (s32[128,16]{0,1:T(8,128)S(1)}, s32[128,16]{0,1:T(8,128)}, u32[]{:S(2)}) copy-start(s32[128,16]{0,1:T(8,128)} %param.18) | copy-start | bytes 24580
  11.5 13.2 %copy-start.28 = (s32[128]{0:T(128)S(1)}, s32[128]{0:T(128)}, u32[]{:S(2)}) copy-start(s32[128]{0:T(128)} %param.19) | copy-start | bytes 1540
  51.2 191.4 %all-to-all-start = ((bf16[32,128,1024]{2,1,0:T(8,128)(2,1)}), bf16[32,128,1024]{2,1,0:T(8,128)(2,1)}, u32[]{:S(2)}, u32[]{:S(2)}) async-start(bf16[32,128,1024]{2,1,0:T(8,128)(2,1)} %bitcast.230), calls=%async_computation | async-start | bytes 16777216 | tf_op jit(solution)/shard_map/all_to_all | solution.py:128
  264.7 9.2 %copy-start.7 = (bf16[128,4096]{0,1:T(8,128)(2,1)S(1)}, bf16[128,4096]{0,1:T(8,128)(2,1)}, u32[]{:S(2)}) copy-start(bf16[128,4096]{0,1:T(8,128)(2,1)} %copy.189) | copy-start | bytes 3145732
  276.3 5.5 copy-start.8
  276.3 11.1 %copy-start = (f32[4,16,8,32,128]{4,3,2,1,0:T(8,128)}, f32[4,16,8,32,128]{4,3,2,1,0:T(8,128)S(1)}, u32[]{:S(2)}) copy-start(f32[4,16,8,32,128]{4,3,2,1,0:T(8,128)S(1)} %get-tuple-element.29) | copy-start | bytes 25165828
  287.4 12.3 %copy-start.1 = (f32[4,16,8,32,128]{4,3,2,1,0:T(8,128)}, f32[4,16,8,32,128]{4,3,2,1,0:T(8,128)S(1)}, u32[]{:S(2)}) copy-start(f32[4,16,8,32,128]{4,3,2,1,0:T(8,128)S(1)} %get-tuple-element.31) | copy-start | bytes 25165828
  299.7 9.4 %copy-start.2 = (f32[4,16,8,32,128]{4,3,2,1,0:T(8,128)}, f32[4,16,8,32,128]{4,3,2,1,0:T(8,128)S(1)}, u32[]{:S(2)}) copy-start(f32[4,16,8,32,128]{4,3,2,1,0:T(8,128)S(1)} %get-tuple-element.33) | copy-start | bytes 25165828
  299.7 7.0 copy-start.6
  309.2 3.2 copy-start.3
  309.2 12.0 %copy-start.12 = (f32[8,4,16,32]{3,0,2,1:T(8,128)S(1)}, f32[8,4,16,32]{3,0,2,1:T(8,128)}, u32[]{:S(2)}) copy-start(f32[8,4,16,32]{3,0,2,1:T(8,128)} %fusion.16) | copy-start | bytes 196612
  309.2 12.0 %copy-start.13 = (f32[8,4,16,32]{3,0,2,1:T(8,128)S(1)}, f32[8,4,16,32]{3,0,2,1:T(8,128)}, u32[]{:S(2)}) copy-start(f32[8,4,16,32]{3,0,2,1:T(8,128)} %fusion.14) | copy-start | bytes 196612
  309.2 12.1 %copy-start.9 = (f32[8,4,16,32]{3,0,2,1:T(8,128)S(1)}, f32[8,4,16,32]{3,0,2,1:T(8,128)}, u32[]{:S(2)}) copy-start(f32[8,4,16,32]{3,0,2,1:T(8,128)} %copy-done.8) | copy-start | bytes 196612
  318.6 33.0 %all-to-all-start.2 = ((bf16[32,128,16]{1,2,0:T(8,128)(2,1)}), bf16[32,128,16]{1,2,0:T(8,128)(2,1)S(1)}, u32[]{:S(2)}, u32[]{:S(2)}) async-start(bf16[32,128,16]{1,2,0:T(8,128)(2,1)} %convert_element_type.69), calls=%async_computation.2 | async-start | bytes 262144 | tf_op jit(solution)/shard_map/all_to_all | solution.py:132
  321.2 9.5 %slice-start = ((s8[8388608]{0:T(1024)(128)(4,1)}), s8[4194304]{0:T(1024)(128)(4,1)S(1)}, s32[]{:S(2)}) async-start(s8[8388608]{0:T(1024)(128)(4,1)} %bitcast.224), calls=%async_computation.7 | async-start | bytes 8388608
  321.3 9.5 %slice-start.1 = ((s8[8388608]{0:T(1024)(128)(4,1)}), s8[4194304]{0:T(1024)(128)(4,1)S(1)}, s32[]{:S(2)}) async-start(s8[8388608]{0:T(1024)(128)(4,1)} %bitcast.224), calls=%async_computation.8 | async-start | bytes 8388608
  321.3 9.5 %copy-start.10 = (f32[8,4,16,32]{3,0,2,1:T(8,128)S(1)}, f32[8,4,16,32]{3,0,2,1:T(8,128)}, u32[]{:S(2)}) copy-start(f32[8,4,16,32]{3,0,2,1:T(8,128)} %get-tuple-element.30) | copy-start | bytes 196612
  321.3 9.5 %copy-start.15 = (bf16[128,4096]{0,1:T(8,128)(2,1)S(1)}, bf16[128,4096]{0,1:T(8,128)(2,1)}, u32[]{:S(2)}) copy-start(bf16[128,4096]{0,1:T(8,128)(2,1)} %copy.202) | copy-start | bytes 3145732
  321.3 15.9 %slice-start.2 = ((s8[8388608]{0:T(1024)(128)(4,1)}), s8[4194304]{0:T(1024)(128)(4,1)S(1)}, s32[]{:S(2)}) async-start(s8[8388608]{0:T(1024)(128)(4,1)} %bitcast.226), calls=%async_computation.9 | async-start | bytes 8388608
  330.8 6.4 slice-start.3
  330.8 6.4 copy-start.11
  330.8 6.4 copy-start.14
  330.8 12.8 %slice-start.4 = ((s8[8388608]{0:T(1024)(128)(4,1)}), s8[4194304]{0:T(1024)(128)(4,1)S(1)}, s32[]{:S(2)}) async-start(s8[8388608]{0:T(1024)(128)(4,1)} %bitcast.228), calls=%async_computation.11 | async-start | bytes 8388608
  337.2 6.4 slice-start.5
  337.2 6.4 copy-start.16
  351.6 53.6 %all-to-all-start.1 = ((bf16[32,128,16]{1,2,0:T(8,128)(2,1)}), bf16[32,128,16]{1,2,0:T(8,128)(2,1)S(1)}, u32[]{:S(2)}, u32[]{:S(2)}) async-start(bf16[32,128,16]{1,2,0:T(8,128)(2,1)} %convert_element_type.66), calls=%async_computation.1 | async-start | bytes 262144 | tf_op jit(solution)/shard_map/all_to_all | solution.py:135
  405.2 6.1 copy-start.19
  405.2 9.7 %copy-start.20 = (bf16[128,1024]{1,0:T(8,128)(2,1)S(1)}, bf16[128,1024]{1,0:T(8,128)(2,1)}, u32[]{:S(2)}) copy-start(bf16[128,1024]{1,0:T(8,128)(2,1)} %param.14) | copy-start | bytes 786436
  405.2 13.3 %copy-start.25 = (s32[2048,1]{0,1:T(1,128)S(1)}, s32[2048,1]{0,1:T(1,128)}, u32[]{:S(2)}) copy-start(s32[2048,1]{0,1:T(1,128)} %get-tuple-element.22) | copy-start | bytes 24580
  405.2 14.1 %copy-start.27 = (pred[128,16]{0,1:T(8,128)(4,1)S(1)}, pred[128,16]{0,1:T(8,128)(4,1)}, u32[]{:S(2)}) copy-start(pred[128,16]{0,1:T(8,128)(4,1)} %get-tuple-element.8) | copy-start | bytes 6148
  405.2 14.8 %copy-start.29 = (f32[16]{0:T(128)S(1)}, f32[16]{0:T(128)}, u32[]{:S(2)}) copy-start(f32[16]{0:T(128)} %param.20) | copy-start | bytes 196
  405.3 192.1 %all-to-all-start.3 = ((bf16[32,128,1024]{2,1,0:T(8,128)(2,1)}), bf16[32,128,1024]{2,1,0:T(8,128)(2,1)}, u32[]{:S(2)}, u32[]{:S(2)}) async-start(bf16[32,128,1024]{2,1,0:T(8,128)(2,1)} %all_to_all.26), calls=%async_computation.3 | async-start | bytes 16777216 | tf_op jit(solution)/shard_map/all_to_all | solution.py:131
  411.2 285.9 %reduce-scatter.2.cloned.1.call-start = ((), (), s32[]{:S(2)}) async-start(), calls=%async_computation.6 | async-start | bytes 1310720 | tf_op jit(solution)/shard_map/reduce_scatter | solution.py:162
  411.3 49.9 %collective-permute-start = (bf16[128,1024]{1,0:T(8,128)(2,1)S(1)}, bf16[128,1024]{1,0:T(8,128)(2,1)S(1)}, u32[]{:S(2)}, u32[]{:S(2)}) collective-permute-start(bf16[128,1024]{1,0:T(8,128)(2,1)S(1)} %copy-done.19), channel_id=1, source_target_pairs={{0,4},{4,8},{8,12},{12,16},{16,20},{20,24},{24,28},{1,5},{5,9},{9,... | collective-permute-start | bytes 786440 | tf_op jit(solution)/shard_map/ppermute | solution.py:16
  414.9 66.8 %collective-permute-start.1 = (bf16[128,1024]{1,0:T(8,128)(2,1)S(1)}, bf16[128,1024]{1,0:T(8,128)(2,1)S(1)}, u32[]{:S(2)}, u32[]{:S(2)}) collective-permute-start(bf16[128,1024]{1,0:T(8,128)(2,1)S(1)} %copy-done.20), channel_id=1, source_target_pairs={{0,4},{4,8},{8,12},{12,16},{16,20},{20,24},{24,28},{1,5},{5,9},{9,... | collective-permute-start | bytes 786440 | tf_op jit(solution)/shard_map/ppermute | solution.py:16
  418.7 66.6 %copy-start.17 = (pred[128,256]{1,0:T(8,128)(4,1)}, pred[128,256]{1,0:T(8,128)(4,1)S(1)}, u32[]{:S(2)}) copy-start(pred[128,256]{1,0:T(8,128)(4,1)S(1)} %fusion.81) | copy-start | bytes 98308
  482.7 1.3 copy-start.4
  485.3 13.4 %copy-start.26 = (pred[2048]{0:T(1024)(128)(4,1)S(1)}, pred[2048]{0:T(1024)(128)(4,1)}, u32[]{:S(2)}) copy-start(pred[2048]{0:T(1024)(128)(4,1)} %compare_and_fusion) | copy-start | bytes 6148
  490.8 9.5 %copy-start.24 = (pred[128,16]{1,0:T(8,128)(4,1)S(1)}, pred[128,16]{1,0:T(8,128)(4,1)}, u32[]{:S(2)}) copy-start(pred[128,16]{1,0:T(8,128)(4,1)} %copy-done.23) | copy-start | bytes 6148
  612.8 11.6 %copy-start.22 = (pred[128,16]{1,0:T(8,128)(4,1)S(1)}, pred[128,16]{1,0:T(8,128)(4,1)}, u32[]{:S(2)}) copy-start(pred[128,16]{1,0:T(8,128)(4,1)} %copy.199) | copy-start | bytes 6148
  624.4 10.6 %copy-start.5 = (f32[16,128,256]{2,1,0:T(8,128)S(1)}, f32[16,128,256]{2,1,0:T(8,128)}, u32[]{:S(2)}) copy-start(f32[16,128,256]{2,1,0:T(8,128)} %copy-done.4) | copy-start | bytes 6291460
  624.4 10.6 %copy-start.18 = (pred[128,256]{1,0:T(8,128)(4,1)S(1)}, pred[128,256]{1,0:T(8,128)(4,1)}, u32[]{:S(2)}) copy-start(pred[128,256]{1,0:T(8,128)(4,1)} %copy-done.17) | copy-start | bytes 98308
  624.4 10.6 %copy-start.30 = (f32[16]{0:T(128)S(1)}, f32[16]{0:T(128)}, u32[]{:S(2)}) copy-start(f32[16]{0:T(128)} %get-tuple-element.6) | copy-start | bytes 196
  624.4 10.6 %copy-start.31 = (f32[16]{0:T(128)S(1)}, f32[16]{0:T(128)}, u32[]{:S(2)}) copy-start(f32[16]{0:T(128)} %get-tuple-element.7) | copy-start | bytes 196
Sparse Core Ops, SparseCore 0:
  8.9 19.4 all-gather.1
  642.7 54.3 reduce-scatter.1
where the time goes:
time: 714 us; the launch traced here: 704 us
  waiting for transfers between devices  377 us (53%)
  local copies, waits for them, and re-layouts  176 us (25%)
  matrix products  56.6 us (8%)
  other arithmetic  54 us (8%)
  starting transfers between devices  26.8 us (4%)
  between operations  14.3 us (2%)
    all_to_all x1, waiting for transfers between devices, on_device(): lax.all_to_all(outgoing, ('ctx', 'mem'), split_axis=0, concat_axis=0, til...  164 us
    all_to_all x1, waiting for transfers between devices, on_device(): lax.all_to_all(served[0], ('ctx', 'mem'), split_axis=0, concat_axis=0, ti...  94.8 us
    ppermute x2, waiting for transfers between devices, from_behind(): return lax.ppermute(block, axis, route)  60.1 us
    reduce_scatter x1, waiting for transfers between devices, on_device(): lax.psum_scatter(partial_out.astype(jnp.bfloat16), 'mem', scatter_dimensi...  54.6 us
    dot_general x4, matrix products, serve_tiles(): jnp.einsum('cmhsr,rmhd->cmshd', weights_f.astype(jnp.bfloat16), value_til...  28.7 us
    gather x2, local copies, waits for them, and re-layouts, on_device(): jnp.take(answer[0], safe_target, axis=0)  27.1 us
    reduce_sum x4, other arithmetic, serve_tiles(): summed = jnp.sum(weights_f, axis=-1)  22.7 us
    all_to_all x1, local copies, waits for them, and re-layouts, on_device(): lax.all_to_all(served[0], ('ctx', 'mem'), split_axis=0, concat_axis=0, ti...  22.5 us
  transfers between devices with their start and end apart: 8, of which 6 were waited for; matrix products, arithmetic and copies ran while one was open for 17% of the time, Pallas kernels for 0%

commit v1 on v0

v1 whole, which is shorter than its diff:
```python
import functools

import jax
import jax.numpy as jnp
from jax import lax
from jax.experimental import pallas as pl
from jax.experimental.pallas import tpu as pltpu
from jax.sharding import PartitionSpec as P

DH = 64
PAIR = 2 * DH
TILE_ROWS = 128
QB = 256
CHUNK_HEADS = 4
STAT_ROWS = 16
EMPTY = -1e38


def swap(block, axis, distance):
    return lax.ppermute(block, axis, [(i, i ^ distance) for i in range(lax.axis_size(axis))])


def turn(block, axis, distance):
    size = lax.axis_size(axis)
    return lax.ppermute(block, axis, [(i, (i + distance) % size) for i in range(size)])


def from_behind(block, axis, distance):
    devices = range(lax.axis_size(axis))
    route = [(i - distance, i) for i in devices if i - distance in devices]
    return lax.ppermute(block, axis, route)


def both_heads(q):
    lane = lax.broadcasted_iota(jnp.int32, q.shape, 1)
    scaled = q * jnp.asarray(0.125, q.dtype)
    zero = jnp.zeros_like(scaled)
    return jnp.concatenate(
        [jnp.where(lane < DH, scaled, zero), jnp.where(lane >= DH, scaled, zero)], axis=0
    )


def attend(qm, keys, vts, bits, first_bit):
    scores = []
    masks = []
    top = None
    bit = first_bit
    for key in keys:
        s = lax.dot_general(key, qm, (((1,), (1,)), ((), ())), preferred_element_type=jnp.float32)
        scores.append(s)
        for tile in range(key.shape[0] // TILE_ROWS):
            mask = ((bits >> bit) & 1) == 1
            mask = jnp.concatenate([mask, mask], axis=1)
            masks.append(mask)
            high = jnp.max(s[tile * TILE_ROWS : (tile + 1) * TILE_ROWS], axis=0, keepdims=True)
            high = jnp.where(mask, high, EMPTY)
            top = high if top is None else jnp.maximum(top, high)
            bit += 1
    total = None
    sums = [None, None]
    index = 0
    for s, vt in zip(scores, vts):
        parts = []
        for tile in range(s.shape[0] // TILE_ROWS):
            minus = jnp.where(masks[index], top, jnp.inf)
            p = jnp.exp(s[tile * TILE_ROWS : (tile + 1) * TILE_ROWS] - minus)
            added = jnp.sum(p, axis=0, keepdims=True)
            total = added if total is None else total + added
            parts.append(p.astype(jnp.bfloat16))
            index += 1
        p = jnp.concatenate(parts, axis=0)
        for head in range(2):
            o = jnp.dot(
                vt[head * DH : (head + 1) * DH],
                p[:, head * QB : (head + 1) * QB],
                preferred_element_type=jnp.float32,
            )
            sums[head] = o if sums[head] is None else sums[head] + o
    return top, total, sums


def near_kernel(m_ref, q_ref, k0_ref, v0_ref, k1_ref, v1_ref, bits_ref, acc_ref, stat_ref, vt_ref):
    @pl.when(pl.program_id(1) == 0)
    def _():
        vt_ref[0] = jnp.transpose(v0_ref[...])
        vt_ref[1] = jnp.transpose(v1_ref[0])

    top, total, sums = attend(
        both_heads(q_ref[...]),
        [k0_ref[...], k1_ref[0]],
        [vt_ref[0], vt_ref[1]],
        bits_ref[...],
        0,
    )
    acc_ref[0:DH] = sums[0]
    acc_ref[DH:PAIR] = sums[1]
    stat_ref[0, 0:1] = top[:, :QB]
    stat_ref[0, 1:2] = top[:, QB:]
    stat_ref[0, 2:3] = total[:, :QB]
    stat_ref[0, 3:4] = total[:, QB:]


def three(x):
    hi = x.astype(jnp.bfloat16)
    rest = x - hi.astype(jnp.float32)
    mid = rest.astype(jnp.bfloat16)
    low = (rest - mid.astype(jnp.float32)).astype(jnp.bfloat16)
    return [hi, mid, low]


def far_kernel(q_ref, k2_ref, v2_ref, k3_ref, v3_ref, bits_ref, acc_ref, stat_ref, out_ref, vt_ref):
    pairs = CHUNK_HEADS // 2

    @pl.when(pl.program_id(0) == 0)
    def _():
        for pair in range(pairs):
            cols = slice(pair * PAIR, (pair + 1) * PAIR)
            vt_ref[0, cols] = jnp.transpose(v2_ref[0, :, cols])
            vt_ref[1, cols] = jnp.transpose(v3_ref[0, :, cols])

    tiles = k2_ref.shape[1] // TILE_ROWS
    stats = []
    for pair in range(pairs):
        cols = slice(pair * PAIR, (pair + 1) * PAIR)
        top, total, sums = attend(
            both_heads(q_ref[:, cols]),
            [k2_ref[0, :, cols], k3_ref[0, :, cols]],
            [vt_ref[0, cols], vt_ref[1, cols]],
            bits_ref[...],
            2 * tiles,
        )
        for head in range(2):
            lanes = slice(head * QB, (head + 1) * QB)
            near_top = stat_ref[pair, head : head + 1]
            near_total = stat_ref[pair, 2 + head : 3 + head]
            new = jnp.maximum(top[:, lanes], near_top)
            near_w = jnp.exp(near_top - new)
            far_w = jnp.exp(top[:, lanes] - new)
            all_total = near_w * near_total + far_w * total[:, lanes]
            some = all_total > 0.0
            safe = jnp.where(some, all_total, 1.0)
            inv = 1.0 / safe
            row = pair * PAIR + head * DH
            o = (near_w * inv) * acc_ref[row : row + DH] + (far_w * inv) * sums[head]
            o = o.astype(jnp.bfloat16)
            lse = jnp.where(some, new + jnp.log(safe), EMPTY)
            stats += three(lse)
            for part in range(QB // TILE_ROWS):
                out_ref[part, row : row + DH] = o[:, part * TILE_ROWS : (part + 1) * TILE_ROWS]
    stats.append(jnp.zeros((STAT_ROWS - len(stats), QB), jnp.bfloat16))
    stats = jnp.concatenate([s.astype(jnp.float32) for s in stats], axis=0).astype(jnp.bfloat16)
    base = CHUNK_HEADS * DH
    for part in range(QB // TILE_ROWS):
        out_ref[part, base : base + STAT_ROWS] = stats[:, part * TILE_ROWS : (part + 1) * TILE_ROWS]


def lse_of(stats, head):
    return stats[3 * head : 3 * head + 1] + stats[3 * head + 1 : 3 * head + 2] + stats[3 * head + 2 : 3 * head + 3]


def merge_kernel(a_ref, b_ref, out_ref):
    base = CHUNK_HEADS * DH
    stats_a = a_ref[0, base:].astype(jnp.float32)
    stats_b = b_ref[0, base:].astype(jnp.float32)
    stats = []
    for head in range(CHUNK_HEADS):
        lse_a = lse_of(stats_a, head)
        lse_b = lse_of(stats_b, head)
        top = jnp.maximum(lse_a, lse_b)
        w_a = jnp.exp(lse_a - top)
        w_b = jnp.exp(lse_b - top)
        total = w_a + w_b
        inv = 1.0 / total
        rows = slice(head * DH, (head + 1) * DH)
        out_ref[0, rows] = (
            (w_a * inv) * a_ref[0, rows].astype(jnp.float32)
            + (w_b * inv) * b_ref[0, rows].astype(jnp.float32)
        ).astype(jnp.bfloat16)
        stats += three(top + jnp.log(total))
    stats.append(jnp.zeros((STAT_ROWS - len(stats), TILE_ROWS), jnp.bfloat16))
    stats = jnp.concatenate([s.astype(jnp.float32) for s in stats], axis=0)
    out_ref[0, base:] = stats.astype(jnp.bfloat16)


def final_kernel(*refs):
    *msg_refs, local_ref, gate_ref, out_ref = refs
    base = CHUNK_HEADS * DH
    stats = [r[base:].astype(jnp.float32) for r in msg_refs]
    for head in range(CHUNK_HEADS):
        lses = [lse_of(s, head) for s in stats]
        top = functools.reduce(jnp.maximum, lses)
        ws = [jnp.exp(x - top) for x in lses]
        inv = 1.0 / functools.reduce(jnp.add, ws)
        rows = slice(head * DH, (head + 1) * DH)
        mem = None
        for r, w in zip(msg_refs, ws):
            term = w * r[rows].astype(jnp.float32)
            mem = term if mem is None else mem + term
        gate = gate_ref[head : head + 1]
        out_ref[rows] = (
            (gate * inv) * mem + (1.0 - gate) * local_ref[rows].astype(jnp.float32)
        ).astype(jnp.bfloat16)


def on_device(
    hidden_states,
    w_query,
    local_keys,
    local_values,
    memory_keys,
    memory_values,
    tile_ids,
    tile_counts,
    gate_bias,
    w_output,
):
    row_count = hidden_states.shape[0]
    features = w_query.shape[1]
    heads_here = features // DH
    ctx_size = lax.axis_size("ctx")
    mem_size = lax.axis_size("mem")
    turns = ctx_size // 2
    pick_count = tile_ids.shape[1]
    mem_rows = memory_keys.shape[0]
    tiles_here = mem_rows // TILE_ROWS
    group_tiles = tiles_here * mem_size
    all_rows = ctx_size * row_count
    me = lax.axis_index("mem")
    my_ctx = lax.axis_index("ctx")
    chunks = heads_here // CHUNK_HEADS
    width = CHUNK_HEADS * DH
    pairs = heads_here // 2

    h1 = swap(hidden_states, "mem", 1)
    h2 = swap(hidden_states, "mem", 2)
    h3 = swap(h2, "mem", 1)
    have = [hidden_states, h1, h2, h3]
    hidden = jnp.zeros((row_count, mem_size * hidden_states.shape[1]), jnp.bfloat16)
    for k in range(mem_size):
        hidden = lax.dynamic_update_slice(hidden, have[k], (0, (me ^ k) * hidden_states.shape[1]))

    def share(k, first, cols):
        at = (me ^ k) * features + first
        return jnp.stack(
            [
                lax.dynamic_slice(memory_keys, (0, at), (mem_rows, cols)),
                lax.dynamic_slice(memory_values, (0, at), (mem_rows, cols)),
            ]
        )

    near = swap(share(1, 0, features), "mem", 1)
    to_send = [[share(k, j * width, width) for k in (2, 3)] for j in range(chunks)]
    to_send, _ = lax.optimization_barrier((to_send, h2))
    far = [[swap(to_send[j][k - 2], "mem", k) for k in (2, 3)] for j in range(chunks)]

    live = jnp.arange(pick_count, dtype=jnp.int32)[None, :] < tile_counts[:, None]
    ids = jnp.transpose(jnp.where(live, tile_ids, -1))
    ids = lax.all_gather(ids, "ctx", axis=1, tiled=True)
    here = (ids >= my_ctx * group_tiles) & (ids < (my_ctx + 1) * group_tiles)
    place = (((ids // tiles_here) % mem_size) ^ me) * tiles_here + ids % tiles_here
    bits = jnp.sum(jnp.where(here, 1 << jnp.where(here, place, 0), 0), axis=0)
    bits = bits.reshape(ctx_size, row_count)
    block = jnp.arange(ctx_size, dtype=jnp.int32)
    origin = ((my_ctx - 2 * (block % turns)) % ctx_size) ^ (block // turns)
    bits = jnp.sum(
        jnp.where((origin[:, None] == block[None, :])[:, :, None], bits[None], 0), axis=1
    ).reshape(1, all_rows)

    queries = jnp.dot(hidden, w_query, preferred_element_type=jnp.float32).astype(jnp.bfloat16)
    q_blocks = [queries] + [turn(queries, "ctx", 2 * k) for k in range(1, turns)]
    q_blocks += [swap(q, "ctx", 1) for q in q_blocks]
    all_q = jnp.concatenate(q_blocks, axis=0)

    earlier_k = from_behind(local_keys, "ctx", 1)
    earlier_v = from_behind(local_values, "ctx", 1)
    window_keys = jnp.concatenate([earlier_k, local_keys], 0).reshape(2 * row_count, heads_here, DH)
    window_values = jnp.concatenate([earlier_v, local_values], 0).reshape(
        2 * row_count, heads_here, DH
    )
    query_heads = queries.reshape(row_count, heads_here, DH)
    scores = (
        jnp.einsum("ihd,jhd->hij", query_heads, window_keys, preferred_element_type=jnp.float32)
        * 0.125
    )
    query_pos = jnp.arange(row_count, dtype=jnp.int32)[:, None]
    key_pos = jnp.arange(2 * row_count, dtype=jnp.int32)[None, :]
    allowed = (
        (key_pos > query_pos)
        & (key_pos <= query_pos + row_count)
        & ((key_pos >= row_count) | (my_ctx > 0))
    )
    scores = jnp.where(allowed[None], scores, -jnp.inf)
    highest = jnp.max(scores, axis=-1, keepdims=True)
    weights_f = jnp.exp(scores - highest)
    summed = jnp.sum(weights_f, axis=-1)
    mixed = jnp.einsum(
        "hij,jhd->hdi",
        weights_f.astype(jnp.bfloat16),
        window_values,
        preferred_element_type=jnp.float32,
    )
    local_out = (mixed / summed[:, None, :]).reshape(features, row_count)

    f32 = jnp.float32
    near_flops = 2 * 2 * all_rows * 2 * mem_rows * features
    acc, stat = pl.pallas_call(
        near_kernel,
        grid_spec=pltpu.PrefetchScalarGridSpec(
            num_scalar_prefetch=1,
            grid=(pairs, all_rows // QB),
            in_specs=[
                pl.BlockSpec((QB, PAIR), lambda p, i, m: (i, p)),
                pl.BlockSpec((mem_rows, PAIR), lambda p, i, m: (0, m[0] * pairs + p)),
                pl.BlockSpec((mem_rows, PAIR), lambda p, i, m: (0, m[0] * pairs + p)),
                pl.BlockSpec((1, mem_rows, PAIR), lambda p, i, m: (0, 0, p)),
                pl.BlockSpec((1, mem_rows, PAIR), lambda p, i, m: (1, 0, p)),
                pl.BlockSpec((1, QB), lambda p, i, m: (0, i)),
            ],
            out_specs=[
                pl.BlockSpec((PAIR, QB), lambda p, i, m: (p, i)),
                pl.BlockSpec((1, 8, QB), lambda p, i, m: (p, 0, i)),
            ],
            scratch_shapes=[pltpu.VMEM((2, PAIR, mem_rows), jnp.bfloat16)],
        ),
        out_shape=[
            jax.ShapeDtypeStruct((features, all_rows), f32),
            jax.ShapeDtypeStruct((pairs, 8, all_rows), f32),
        ],
        compiler_params=pltpu.CompilerParams(vmem_limit_bytes=48 << 20),
        cost_estimate=pl.CostEstimate(
            flops=near_flops, transcendentals=all_rows * 2 * mem_rows * heads_here, bytes_accessed=12 << 20
        ),
        name="near_tiles",
    )(me.reshape(1), all_q, memory_keys, memory_values, near, near, bits)

    gate = jax.nn.sigmoid(gate_bias)
    combined = []
    chunk_pairs = CHUNK_HEADS // 2
    msg_rows = width + STAT_ROWS
    for j in range(chunks):
        far2, far3 = far[j]
        message = pl.pallas_call(
            far_kernel,
            grid=(all_rows // QB,),
            in_specs=[
                pl.BlockSpec((QB, width), lambda i, j=j: (i, j)),
                pl.BlockSpec((1, mem_rows, width), lambda i: (0, 0, 0)),
                pl.BlockSpec((1, mem_rows, width), lambda i: (1, 0, 0)),
                pl.BlockSpec((1, mem_rows, width), lambda i: (0, 0, 0)),
                pl.BlockSpec((1, mem_rows, width), lambda i: (1, 0, 0)),
                pl.BlockSpec((1, QB), lambda i: (0, i)),
                pl.BlockSpec((width, QB), lambda i, j=j: (j, i)),
                pl.BlockSpec((chunk_pairs, 8, QB), lambda i, j=j: (j, 0, i)),
            ],
            out_specs=pl.BlockSpec((QB // TILE_ROWS, msg_rows, TILE_ROWS), lambda i: (i, 0, 0)),
            out_shape=jax.ShapeDtypeStruct((ctx_size, msg_rows, row_count), jnp.bfloat16),
            scratch_shapes=[pltpu.VMEM((2, width, mem_rows), jnp.bfloat16)],
            compiler_params=pltpu.CompilerParams(vmem_limit_bytes=48 << 20),
            cost_estimate=pl.CostEstimate(
                flops=near_flops // chunks,
                transcendentals=all_rows * 2 * mem_rows * CHUNK_HEADS,
                bytes_accessed=4 << 20,
            ),
            name="far_tiles",
        )(all_q, far2, far2, far3, far3, bits, acc, stat)
        other = swap(message[turns:], "ctx", 1)
        merged = pl.pallas_call(
            merge_kernel,
            grid=(turns,),
            in_specs=[pl.BlockSpec((1, msg_rows, row_count), lambda i: (i, 0, 0))] * 2,
            out_specs=pl.BlockSpec((1, msg_rows, row_count), lambda i: (i, 0, 0)),
            out_shape=jax.ShapeDtypeStruct((turns, msg_rows, row_count), jnp.bfloat16),
            name="merge_pair",
        )(message, other)
        answers = [merged[0]] + [turn(merged[k], "ctx", -2 * k) for k in range(1, turns)]
        gate_rows = jnp.broadcast_to(
            lax.slice(gate, (j * CHUNK_HEADS,), ((j + 1) * CHUNK_HEADS,))[:, None],
            (CHUNK_HEADS, row_count),
        )
        combined.append(
            pl.pallas_call(
                final_kernel,
                out_shape=jax.ShapeDtypeStruct((width, row_count), jnp.bfloat16),
                name="merge_all",
            )(*answers, local_out[j * width : (j + 1) * width], gate_rows)
        )
    combined = jnp.concatenate(combined, axis=0)
    partial_out = lax.dot_general(
        combined, w_output, (((0,), (0,)), ((), ())), preferred_element_type=jnp.float32
    ).astype(jnp.bfloat16)
    cols = partial_out.shape[1] // mem_size

    def piece(k):
        return lax.dynamic_slice(partial_out, (0, (me ^ k) * cols), (row_count, cols))

    result = piece(0).astype(f32)
    for k in range(1, mem_size):
        result = result + swap(piece(k), "mem", k).astype(f32)
    return result.astype(jnp.bfloat16)


def solution(mesh):
    in_specs = (
        P("ctx", "mem"),
        P(None, "mem"),
        P("ctx", "mem"),
        P("ctx", "mem"),
        P(("ctx", "mem"), None),
        P(("ctx", "mem"), None),
        P("ctx", None),
        P("ctx"),
        P("mem"),
        P("mem", None),
    )
    out_specs = P("ctx", "mem")
    return jax.shard_map(
        on_device, mesh=mesh, in_specs=in_specs, out_specs=out_specs, check_vma=False
    )
```

time: 714 us -> 278 us (0.39); the launches traced: 704 us -> 276 us
  waiting for transfers between devices: 377 us -> 63 us
  local copies, waits for them, and re-layouts: 176 us -> 19.9 us
  Pallas kernels: 0 us -> 93.7 us
  matrix products: 56.6 us -> 12.7 us
  other arithmetic: 54 us -> 10.6 us
  blocking collectives: 0 us -> 31 us
  starting transfers between devices: 26.8 us -> 44.6 us
  between operations: 14.3 us -> 0.61 us
    all_to_all x4 -> x0, waiting for transfers between devices: 259 us -> none  [the longest x1 164 us: on_device(): lax.all_to_all(outgoing, ('ctx', 'mem'), split_axis=0, concat_axis=0, til...]
    pallas_call x0 -> x13, Pallas kernels: none -> 93.7 us  [the longest x4 37.3 us: on_device(): pl.pallas_call(far_kernel, grid=(all_rows // QB,), in_specs=[pl.BlockSpec...]
    ppermute x0 -> x38, waiting for transfers between devices: none -> 63 us  [the longest x23 45.2 us: swap(): lax.ppermute(block, axis, [(i, i ^ distance) for i in range(lax.axis_size...]
    ppermute x2, waiting for transfers between devices: 60.1 us -> 0.01 us  [from_behind(): return lax.ppermute(block, axis, route)]
    reduce_scatter x1 -> x0, waiting for transfers between devices: 54.6 us -> none  [on_device(): lax.psum_scatter(partial_out.astype(jnp.bfloat16), 'mem', scatter_dimensi...]
    gather x9 -> x0, local copies, waits for them, and re-layouts: 53.5 us -> none  [the longest x2 27.1 us: on_device(): jnp.take(answer[0], safe_target, axis=0)]
    dot_general x11 -> x3, matrix products: 56 us -> 11 us  [the longest x1 4.82 us: on_device(): lax.dot_general(combined, w_output, (((0,), (0,)), ((), ())), preferred_e...]
    ppermute x0 -> x38, starting transfers between devices: none -> 37.8 us  [the longest x15 20.9 us: turn(): lax.ppermute(block, axis, [(i, (i + distance) % size) for i in range(size)])]
  transfers between devices with their start and end apart: 8 -> 40, of which waited for: 6 -> 8; matrix products, arithmetic and copies ran while one was open for 17% -> 13% of each run, Pallas kernels for 0% -> 33%
where the time goes in v1:
time: 278 us; the launch traced here: 276 us
  Pallas kernels  93.7 us (34%)
  waiting for transfers between devices  63 us (23%)
  starting transfers between devices  44.6 us (16%)
  blocking collectives  31 us (11%)
  local copies, waits for them, and re-layouts  19.9 us (7%)
  matrix products  12.7 us (5%)
  other arithmetic  10.6 us (4%)
    ppermute x23, waiting for transfers between devices, swap(): lax.ppermute(block, axis, [(i, i ^ distance) for i in range(lax.axis_size...  45.2 us
    pallas_call x4, Pallas kernels, on_device(): pl.pallas_call(far_kernel, grid=(all_rows // QB,), in_specs=[pl.BlockSpec...  37.3 us
    pallas_call x1, Pallas kernels, on_device(): pl.pallas_call(near_kernel, grid_spec=pltpu.PrefetchScalarGridSpec(num_sc...  36.6 us
    all_gather x1, blocking collectives, on_device(): ids = lax.all_gather(ids, 'ctx', axis=1, tiled=True)  31 us
    ppermute x15, starting transfers between devices, turn(): lax.ppermute(block, axis, [(i, (i + distance) % size) for i in range(size)])  20.9 us
    ppermute x15, waiting for transfers between devices, turn(): lax.ppermute(block, axis, [(i, (i + distance) % size) for i in range(size)])  17.8 us
    ppermute x23, starting transfers between devices, swap(): lax.ppermute(block, axis, [(i, i ^ distance) for i in range(lax.axis_size...  16.8 us
    pallas_call x4, Pallas kernels, on_device(): pl.pallas_call(merge_kernel, grid=(turns,), in_specs=[pl.BlockSpec((1, ms...  12.9 us
  transfers between devices with their start and end apart: 40, of which 8 were waited for; matrix products, arithmetic and copies ran while one was open for 13% of the time, Pallas kernels for 33%

profile of v1, /device:TPU:0, one launch (start us, length us, event | category | flops | bytes accessed | tf_op | source)
XLA Modules:
  0.0 276.2 jit_solution(7138458263067484713)
XLA Ops:
  0.0 2.9 %collective-permute-start.1 = (bf16[128,1024]{1,0:T(8,128)(2,1)}, bf16[128,1024]{1,0:T(8,128)(2,1)S(1)}, u32[]{:S(2)}, u32[]{:S(2)}) collective-permute-start(bf16[128,1024]{1,0:T(8,128)(2,1)} %param.10), channel_id=1, source_target_pairs={{0,2},{1,3},{2,0},{3,1},{4,6},{5,7},{6,4},{7,5},{8,10},{9,11},{10,... | collective-permute-start | bytes 786440 | tf_op jit(solution)/shard_map/ppermute | solution.py:20
  2.9 3.4 %collective-permute-start.18 = (bf16[128,1024]{1,0:T(8,128)(2,1)}, bf16[128,1024]{1,0:T(8,128)(2,1)S(1)}, u32[]{:S(2)}, u32[]{:S(2)}) collective-permute-start(bf16[128,1024]{1,0:T(8,128)(2,1)} %param.12), channel_id=1, source_target_pairs={{0,4},{4,8},{8,12},{12,16},{16,20},{20,24},{24,28},{1,5},{5,9},{9,... | collective-permute-start | bytes 786440 | tf_op jit(solution)/shard_map/ppermute | solution.py:31
  6.4 3.4 %collective-permute-start.17 = (bf16[128,1024]{1,0:T(8,128)(2,1)}, bf16[128,1024]{1,0:T(8,128)(2,1)S(1)}, u32[]{:S(2)}, u32[]{:S(2)}) collective-permute-start(bf16[128,1024]{1,0:T(8,128)(2,1)} %param.13), channel_id=1, source_target_pairs={{0,4},{4,8},{8,12},{12,16},{16,20},{20,24},{24,28},{1,5},{5,9},{9,... | collective-permute-start | bytes 786440 | tf_op jit(solution)/shard_map/ppermute | solution.py:31
  9.8 1.7 dynamic-slice_bitcast_fusion
  11.6 1.5 pad_maximum_fusion
  13.3 31.0 %all_gather.3 = s32[16,1024]{1,0:T(8,128)S(1)} all-gather(s32[16,128]{1,0:T(8,128)S(1)} %select_bitcast_fusion), channel_id=1, replica_groups=mesh['ctx'=8,'mem'=4] {'ctx'}, dimensions={1}, use_global_device_ids=true | all-gather | bytes 73728 | tf_op jit(solution)/shard_map/all_gather | solution.py:258
  44.5 2.5 dynamic-slice_bitcast_fusion.2
  47.0 0.9 pad_maximum_fusion.8
  47.8 0.8 pad_maximum_fusion.7
  48.7 0.9 pad_maximum_fusion.6
  49.5 0.8 pad_maximum_fusion.5
  50.4 0.9 pad_maximum_fusion.4
  51.3 0.9 pad_maximum_fusion.3
  52.2 0.9 pad_maximum_fusion.2
  53.2 0.8 pad_maximum_fusion.1
  54.5 1.0 copy.19
  55.5 1.0 copy.17
  56.6 4.7 %constant_dynamic-update-slice_fusion.7 = (bf16[1024,1024]{1,0:T(8,128)(2,1)S(1)}, bf16[128,1024]{1,0:T(8,128)(2,1)S(1)}) fusion(bf16[128,4096]{1,0:T(8,128)(2,1)S(1)} %constant_dynamic-update-slice_fusion.8, bf16[4096,1024]{1,0:T(8,128)(2,1)} %param.11), kind=kOutput, calls=%fused_computation.95 | convolution fusion | flops 1073872896 | bytes 9961472 | tf_op jit(solution)/shard_map/dot_general | solution.py:269
  62.2 3.3 %collective-permute-start.5 = (bf16[128,1024]{1,0:T(8,128)(2,1)S(1)}, bf16[128,1024]{1,0:T(8,128)(2,1)S(1)}, u32[]{:S(2)}, u32[]{:S(2)}) collective-permute-start(bf16[128,1024]{1,0:T(8,128)(2,1)S(1)} %get-tuple-element.71), channel_id=1, source_target_pairs={{0,24},{4,28},{8,0},{12,4},{16,8},{20,12},{24,16},{28,20},{1,25},{... | collective-permute-start | bytes 786440 | tf_op jit(solution)/shard_map/ppermute | solution.py:25
  66.0 1.7 fusion
  67.7 0.9 fusion.1
  68.6 17.7 %collective-permute-done.4 = bf16[128,1024]{1,0:T(8,128)(2,1)S(1)} collective-permute-done((bf16[128,1024]{1,0:T(8,128)(2,1)S(1)}, bf16[128,1024]{1,0:T(8,128)(2,1)S(1)}, u32[]{:S(2)}, u32[]{:S(2)}) %collective-permute-start.4) | collective-permute-done | bytes 262176 | tf_op jit(solution)/shard_map/ppermute | solution.py:25
  87.1 1.5 convolution_divide_fusion
  88.6 1.3 collective-permute-start.7
  90.6 4.9 %collective-permute-done.8 = bf16[128,1024]{1,0:T(8,128)(2,1)S(1)} collective-permute-done((bf16[128,1024]{1,0:T(8,128)(2,1)S(1)}, bf16[128,1024]{1,0:T(8,128)(2,1)S(1)}, u32[]{:S(2)}, u32[]{:S(2)}) %collective-permute-start.8) | collective-permute-done | bytes 262176 | tf_op jit(solution)/shard_map/ppermute | solution.py:20
  96.1 3.6 %collective-permute-done.7 = bf16[128,1024]{1,0:T(8,128)(2,1)S(1)} collective-permute-done((bf16[128,1024]{1,0:T(8,128)(2,1)S(1)}, bf16[128,1024]{1,0:T(8,128)(2,1)S(1)}, u32[]{:S(2)}, u32[]{:S(2)}) %collective-permute-start.7) | collective-permute-done | bytes 262176 | tf_op jit(solution)/shard_map/ppermute | solution.py:20
  100.4 6.2 %collective-permute-done.9 = bf16[128,1024]{1,0:T(8,128)(2,1)S(1)} collective-permute-done((bf16[128,1024]{1,0:T(8,128)(2,1)S(1)}, bf16[128,1024]{1,0:T(8,128)(2,1)S(1)}, u32[]{:S(2)}, u32[]{:S(2)}) %collective-permute-start.9) | collective-permute-done | bytes 262176 | tf_op jit(solution)/shard_map/ppermute | solution.py:20
  107.2 7.1 %collective-permute-done.11.k3_ref.v3_ref = bf16[2,512,256]{2,1,0:T(8,128)(2,1)S(1)} collective-permute-done((bf16[2,512,256]{2,1,0:T(8,128)(2,1)S(1)}, bf16[2,512,256]{2,1,0:T(8,128)(2,1)S(1)}, u32[]{:S(2)}, u32[]{:S(2)}) %collective-permute-start.11) | collective-permute-done | bytes 524320 | tf_op jit(solution)/shard_map/ppermute | solution.py:20
  114.2 1.9 collective-permute-start.26
  116.1 11.3 %collective-permute-done.19.k2_ref.v2_ref = bf16[2,512,256]{2,1,0:T(8,128)(2,1)S(1)} collective-permute-done((bf16[2,512,256]{2,1,0:T(8,128)(2,1)S(1)}, bf16[2,512,256]{2,1,0:T(8,128)(2,1)S(1)}, u32[]{:S(2)}, u32[]{:S(2)}) %collective-permute-start.19) | collective-permute-done | bytes 524320 | tf_op jit(solution)/shard_map/ppermute | solution.py:20
  128.0 36.6 %near_tiles.1 = (f32[1024,1024]{1,0:T(8,128)}, f32[8,8,1024]{2,1,0:T(8,128)S(1)}) custom-call(s32[1]{0:T(128)} %bitcast.19.m_ref, bf16[1024,1024]{1,0:T(8,128)(2,1)S(1)} %constant_dynamic-update-slice_fusion.q_ref, bf16[512,4096]{1,0:T(8,128)(2,1)} %k0_ref.1, bf16[512,4096]{1,0:T(8,128)(2,1)} %v0_ref.1, ...), custom_call_target="tpu_custom_call" | custom-call | flops 4294967296 | bytes 12582912 | tf_op jit(solution)/shard_map/near_tiles/pallas_call | solution.py:306
  164.5 9.3 %far_tiles.4.a_ref = bf16[8,272,128]{2,1,0:T(8,128)(2,1)S(1)} custom-call(bf16[1024,1024]{1,0:T(8,128)(2,1)S(1)} %constant_dynamic-update-slice_fusion.q_ref, bf16[2,512,256]{2,1,0:T(8,128)(2,1)S(1)} %collective-permute-done.10.k2_ref.v2_ref, bf16[2,512,256]{2,1,0:T(8,128)(2,1)S(1)} %collective-permute-done.10.k2_ref.v2_ref, ...), custom_call_target="tpu_custom_call" | custom-call | flops 1073741824 | bytes 4194304 | tf_op jit(solution)/shard_map/far_tiles/pallas_call | solution.py:342
  175.5 9.3 %far_tiles.5.a_ref = bf16[8,272,128]{2,1,0:T(8,128)(2,1)S(1)} custom-call(bf16[1024,1024]{1,0:T(8,128)(2,1)S(1)} %constant_dynamic-update-slice_fusion.q_ref, bf16[2,512,256]{2,1,0:T(8,128)(2,1)S(1)} %collective-permute-done.19.k2_ref.v2_ref, bf16[2,512,256]{2,1,0:T(8,128)(2,1)S(1)} %collective-permute-done.19.k2_ref.v2_ref, ...), custom_call_target="tpu_custom_call" | custom-call | flops 1073741824 | bytes 4194304 | tf_op jit(solution)/shard_map/far_tiles/pallas_call | solution.py:342
  184.8 0.8 slice.134
  185.6 1.2 collective-permute-start.21
  186.8 9.3 %far_tiles.6.a_ref = bf16[8,272,128]{2,1,0:T(8,128)(2,1)S(1)} custom-call(bf16[1024,1024]{1,0:T(8,128)(2,1)S(1)} %constant_dynamic-update-slice_fusion.q_ref, bf16[2,512,256]{2,1,0:T(8,128)(2,1)S(1)} %collective-permute-done.25.k2_ref.v2_ref, bf16[2,512,256]{2,1,0:T(8,128)(2,1)S(1)} %collective-permute-done.25.k2_ref.v2_ref, ...), custom_call_target="tpu_custom_call" | custom-call | flops 1073741824 | bytes 4194304 | tf_op jit(solution)/shard_map/far_tiles/pallas_call | solution.py:342
  197.0 0.8 collective-permute-start.27
  197.8 9.3 %far_tiles.7.a_ref = bf16[8,272,128]{2,1,0:T(8,128)(2,1)S(1)} custom-call(bf16[1024,1024]{1,0:T(8,128)(2,1)S(1)} %constant_dynamic-update-slice_fusion.q_ref, bf16[2,512,256]{2,1,0:T(8,128)(2,1)S(1)} %collective-permute-done.31.k2_ref.v2_ref, bf16[2,512,256]{2,1,0:T(8,128)(2,1)S(1)} %collective-permute-done.31.k2_ref.v2_ref, ...), custom_call_target="tpu_custom_call" | custom-call | flops 1073741824 | bytes 4194304 | tf_op jit(solution)/shard_map/far_tiles/pallas_call | solution.py:342
  207.2 1.3 collective-permute-start.33
  208.5 3.2 %merge_pair.4 = bf16[4,272,128]{2,1,0:T(8,128)(2,1)} custom-call(bf16[8,272,128]{2,1,0:T(8,128)(2,1)} %copy-done.3, bf16[4,272,128]{2,1,0:T(8,128)(2,1)} %collective-permute-done.13.b_ref), custom_call_target="tpu_custom_call" | custom-call | tf_op jit(solution)/shard_map/merge_pair/pallas_call | solution.py:367
  211.7 1.6 slice_bitcast_fusion.12
  213.3 1.2 collective-permute-start.15
  214.5 2.9 %collective-permute-start.14 = (bf16[272,128]{1,0:T(8,128)(2,1)S(1)}, bf16[272,128]{1,0:T(8,128)(2,1)S(1)}, u32[]{:S(2)}, u32[]{:S(2)}) collective-permute-start(bf16[272,128]{1,0:T(8,128)(2,1)S(1)} %get-tuple-element.50), channel_id=1, source_target_pairs={{0,24},{4,28},{8,0},{12,4},{16,8},{20,12},{24,16},{28,20},{1,25},{... | collective-permute-start | bytes 208904 | tf_op jit(solution)/shard_map/ppermute | solution.py:25
  217.5 3.2 %merge_pair.5 = bf16[4,272,128]{2,1,0:T(8,128)(2,1)} custom-call(bf16[8,272,128]{2,1,0:T(8,128)(2,1)} %copy-done.2, bf16[4,272,128]{2,1,0:T(8,128)(2,1)} %collective-permute-done.21.b_ref), custom_call_target="tpu_custom_call" | custom-call | tf_op jit(solution)/shard_map/merge_pair/pallas_call | solution.py:367
  220.7 1.7 slice_bitcast_fusion.8
  223.1 3.2 %merge_pair.6 = bf16[4,272,128]{2,1,0:T(8,128)(2,1)} custom-call(bf16[8,272,128]{2,1,0:T(8,128)(2,1)} %copy-done.1, bf16[4,272,128]{2,1,0:T(8,128)(2,1)} %copy-done.14), custom_call_target="tpu_custom_call" | custom-call | tf_op jit(solution)/shard_map/merge_pair/pallas_call | solution.py:367
  226.3 1.6 slice_bitcast_fusion.4
  227.9 1.7 collective-permute-start.23
  229.6 3.2 %merge_pair.7 = bf16[4,272,128]{2,1,0:T(8,128)(2,1)} custom-call(bf16[8,272,128]{2,1,0:T(8,128)(2,1)} %copy-done, bf16[4,272,128]{2,1,0:T(8,128)(2,1)} %copy-done.15), custom_call_target="tpu_custom_call" | custom-call | tf_op jit(solution)/shard_map/merge_pair/pallas_call | solution.py:367
  232.9 2.3 collective-permute-start.22
  235.1 1.7 slice_bitcast_fusion
  236.8 1.2 collective-permute-start.29
  238.0 2.9 %collective-permute-start.28 = (bf16[272,128]{1,0:T(8,128)(2,1)S(1)}, bf16[272,128]{1,0:T(8,128)(2,1)S(1)}, u32[]{:S(2)}, u32[]{:S(2)}) collective-permute-start(bf16[272,128]{1,0:T(8,128)(2,1)S(1)} %get-tuple-element.58), channel_id=1, source_target_pairs={{0,24},{4,28},{8,0},{12,4},{16,8},{20,12},{24,16},{28,20},{1,25},{... | collective-permute-start | bytes 208904 | tf_op jit(solution)/shard_map/ppermute | solution.py:25
  241.2 1.5 collective-permute-start.35
  242.7 2.8 %collective-permute-start.34 = (bf16[272,128]{1,0:T(8,128)(2,1)S(1)}, bf16[272,128]{1,0:T(8,128)(2,1)S(1)}, u32[]{:S(2)}, u32[]{:S(2)}) collective-permute-start(bf16[272,128]{1,0:T(8,128)(2,1)S(1)} %get-tuple-element.62), channel_id=1, source_target_pairs={{0,24},{4,28},{8,0},{12,4},{16,8},{20,12},{24,16},{28,20},{1,25},{... | collective-permute-start | bytes 208904 | tf_op jit(solution)/shard_map/ppermute | solution.py:25
  247.0 1.8 merge_all.4
  249.4 1.8 merge_all.5
  251.9 1.8 merge_all.6
  254.3 1.8 merge_all.7
  256.1 4.8 %convolution_convert_fusion = bf16[128,4096]{1,0:T(8,128)(2,1)S(1)} fusion(bf16[1024,4096]{1,0:T(8,128)(2,1)} %param.19, bf16[256,128]{1,0:T(8,128)(2,1)} %merge_all.7, bf16[256,128]{1,0:T(8,128)(2,1)} %merge_all.6, bf16[256,128]{1,0:T(8,128)(2,1)} %merge_all.5, bf16[256,128]{1,0:T(8,128)(2,1)} %merge_all.4), kind=kOutput, calls=%fused_computation | convolution fusion | flops 1075314688 | bytes 9699328 | tf_op jit(solution)/shard_map/dot_general | solution.py:388
  261.1 1.6 collective-permute-start.39
  263.2 6.1 %collective-permute-done.39 = bf16[128,1024]{1,0:T(8,128)(2,1)S(1)} collective-permute-done((bf16[128,1024]{1,0:T(8,128)(2,1)S(1)}, bf16[128,1024]{1,0:T(8,128)(2,1)S(1)}, u32[]{:S(2)}, u32[]{:S(2)}) %collective-permute-start.39) | collective-permute-done | bytes 262176 | tf_op jit(solution)/shard_map/ppermute | solution.py:20
  269.3 6.0 %collective-permute-done.38 = bf16[128,1024]{1,0:T(8,128)(2,1)S(1)} collective-permute-done((bf16[128,1024]{1,0:T(8,128)(2,1)S(1)}, bf16[128,1024]{1,0:T(8,128)(2,1)S(1)}, u32[]{:S(2)}, u32[]{:S(2)}) %collective-permute-start.38) | collective-permute-done | bytes 262176 | tf_op jit(solution)/shard_map/ppermute | solution.py:20
  275.3 0.9 add_convert_fusion
  (156 shorter events, 13.7 us)
Async XLA Ops:
  0.0 54.3 %collective-permute-start.1 = (bf16[128,1024]{1,0:T(8,128)(2,1)}, bf16[128,1024]{1,0:T(8,128)(2,1)S(1)}, u32[]{:S(2)}, u32[]{:S(2)}) collective-permute-start(bf16[128,1024]{1,0:T(8,128)(2,1)} %param.10), channel_id=1, source_target_pairs={{0,2},{1,3},{2,0},{3,1},{4,6},{5,7},{6,4},{7,5},{8,10},{9,11},{10,... | collective-permute-start | bytes 786440 | tf_op jit(solution)/shard_map/ppermute | solution.py:20
  2.9 53.6 %collective-permute-start = (bf16[128,1024]{1,0:T(8,128)(2,1)}, bf16[128,1024]{1,0:T(8,128)(2,1)S(1)}, u32[]{:S(2)}, u32[]{:S(2)}) collective-permute-start(bf16[128,1024]{1,0:T(8,128)(2,1)} %param.10), channel_id=1, source_target_pairs={{0,1},{1,0},{2,3},{3,2},{4,5},{5,4},{6,7},{7,6},{8,9},{9,8},{10,11... | collective-permute-start | bytes 786440 | tf_op jit(solution)/shard_map/ppermute | solution.py:20
  2.9 51.4 %collective-permute-start.18 = (bf16[128,1024]{1,0:T(8,128)(2,1)}, bf16[128,1024]{1,0:T(8,128)(2,1)S(1)}, u32[]{:S(2)}, u32[]{:S(2)}) collective-permute-start(bf16[128,1024]{1,0:T(8,128)(2,1)} %param.12), channel_id=1, source_target_pairs={{0,4},{4,8},{8,12},{12,16},{16,20},{20,24},{24,28},{1,5},{5,9},{9,... | collective-permute-start | bytes 786440 | tf_op jit(solution)/shard_map/ppermute | solution.py:31
  6.4 48.0 %collective-permute-start.17 = (bf16[128,1024]{1,0:T(8,128)(2,1)}, bf16[128,1024]{1,0:T(8,128)(2,1)S(1)}, u32[]{:S(2)}, u32[]{:S(2)}) collective-permute-start(bf16[128,1024]{1,0:T(8,128)(2,1)} %param.13), channel_id=1, source_target_pairs={{0,4},{4,8},{8,12},{12,16},{16,20},{20,24},{24,28},{1,5},{5,9},{9,... | collective-permute-start | bytes 786440 | tf_op jit(solution)/shard_map/ppermute | solution.py:31
  11.6 1.8 copy-start.31
  11.6 1.8 copy-start.32
  13.1 114.8 %collective-permute-start.12 = (bf16[2,512,1024]{2,1,0:T(8,128)(2,1)}, bf16[2,512,1024]{2,1,0:T(8,128)(2,1)}, u32[]{:S(2)}, u32[]{:S(2)}) collective-permute-start(bf16[2,512,1024]{2,1,0:T(8,128)(2,1)} %pad_maximum_fusion), channel_id=1, source_target_pairs={{0,1},{1,0},{2,3},{3,2},{4,5},{5,4},{6,7},{7,6},{8,9},{9,8},{10,11... | collective-permute-start | bytes 6291464 | tf_op jit(solution)/shard_map/ppermute | solution.py:20
  51.3 2.9 %copy-start.16 = (bf16[128,1024]{1,0:T(8,128)(2,1)S(1)}, bf16[128,1024]{1,0:T(8,128)(2,1)}, u32[]{:S(2)}) copy-start(bf16[128,1024]{1,0:T(8,128)(2,1)} %param.10) | copy-start | bytes 786436
  52.2 2.2 copy-start.17
  54.3 2.3 collective-permute-start.2
  61.5 28.5 %collective-permute-start.6 = (bf16[128,1024]{1,0:T(8,128)(2,1)S(1)}, bf16[128,1024]{1,0:T(8,128)(2,1)S(1)}, u32[]{:S(2)}, u32[]{:S(2)}) collective-permute-start(bf16[128,1024]{1,0:T(8,128)(2,1)S(1)} %get-tuple-element.71), channel_id=1, source_target_pairs={{0,4},{4,0},{8,12},{12,8},{16,20},{20,16},{24,28},{28,24},{1,5},{5... | collective-permute-start | bytes 786440 | tf_op jit(solution)/shard_map/ppermute | solution.py:20
  62.2 28.4 %collective-permute-start.5 = (bf16[128,1024]{1,0:T(8,128)(2,1)S(1)}, bf16[128,1024]{1,0:T(8,128)(2,1)S(1)}, u32[]{:S(2)}, u32[]{:S(2)}) collective-permute-start(bf16[128,1024]{1,0:T(8,128)(2,1)S(1)} %get-tuple-element.71), channel_id=1, source_target_pairs={{0,24},{4,28},{8,0},{12,4},{16,8},{20,12},{24,16},{28,20},{1,25},{... | collective-permute-start | bytes 786440 | tf_op jit(solution)/shard_map/ppermute | solution.py:25
  65.4 20.9 %collective-permute-start.4 = (bf16[128,1024]{1,0:T(8,128)(2,1)S(1)}, bf16[128,1024]{1,0:T(8,128)(2,1)S(1)}, u32[]{:S(2)}, u32[]{:S(2)}) collective-permute-start(bf16[128,1024]{1,0:T(8,128)(2,1)S(1)} %get-tuple-element.71), channel_id=1, source_target_pairs={{0,16},{4,20},{8,24},{12,28},{16,0},{20,4},{24,8},{28,12},{1,17},{... | collective-permute-start | bytes 786440 | tf_op jit(solution)/shard_map/ppermute | solution.py:25
  65.4 23.2 %collective-permute-start.3 = (bf16[128,1024]{1,0:T(8,128)(2,1)S(1)}, bf16[128,1024]{1,0:T(8,128)(2,1)S(1)}, u32[]{:S(2)}, u32[]{:S(2)}) collective-permute-start(bf16[128,1024]{1,0:T(8,128)(2,1)S(1)} %get-tuple-element.71), channel_id=1, source_target_pairs={{0,8},{4,12},{8,16},{12,20},{16,24},{20,28},{24,0},{28,4},{1,9},{5... | collective-permute-start | bytes 786440 | tf_op jit(solution)/shard_map/ppermute | solution.py:25
  66.0 21.1 %copy-start.13 = (bf16[256,1024]{0,1:T(8,128)(2,1)S(1)}, bf16[256,1024]{0,1:T(8,128)(2,1)}, u32[]{:S(2)}) copy-start(bf16[256,1024]{0,1:T(8,128)(2,1)} %copy.17) | copy-start | bytes 1572868
  86.3 9.2 %collective-permute-start.8 = (bf16[128,1024]{1,0:T(8,128)(2,1)S(1)}, bf16[128,1024]{1,0:T(8,128)(2,1)S(1)}, u32[]{:S(2)}, u32[]{:S(2)}) collective-permute-start(bf16[128,1024]{1,0:T(8,128)(2,1)S(1)} %collective-permute-done.4), channel_id=1, source_target_pairs={{0,4},{4,0},{8,12},{12,8},{16,20},{20,16},{24,28},{28,24},{1,5},{5... | collective-permute-start | bytes 786440 | tf_op jit(solution)/shard_map/ppermute | solution.py:20
  87.1 2.9 %copy-start.12 = (bf16[2,512,256]{2,1,0:T(8,128)(2,1)S(1)}, bf16[2,512,256]{2,1,0:T(8,128)(2,1)}, u32[]{:S(2)}) copy-start(bf16[2,512,256]{2,1,0:T(8,128)(2,1)} %pad_maximum_fusion.1) | copy-start | bytes 1572868
  87.1 3.5 %copy-start.11 = (bf16[2,512,256]{2,1,0:T(8,128)(2,1)S(1)}, bf16[2,512,256]{2,1,0:T(8,128)(2,1)}, u32[]{:S(2)}) copy-start(bf16[2,512,256]{2,1,0:T(8,128)(2,1)} %pad_maximum_fusion.2) | copy-start | bytes 1572868
  87.1 8.4 %copy-start.10 = (bf16[2,512,256]{2,1,0:T(8,128)(2,1)S(1)}, bf16[2,512,256]{2,1,0:T(8,128)(2,1)}, u32[]{:S(2)}) copy-start(bf16[2,512,256]{2,1,0:T(8,128)(2,1)} %pad_maximum_fusion.3) | copy-start | bytes 1572868
  88.6 17.9 %copy-start.9 = (bf16[2,512,256]{2,1,0:T(8,128)(2,1)S(1)}, bf16[2,512,256]{2,1,0:T(8,128)(2,1)}, u32[]{:S(2)}) copy-start(bf16[2,512,256]{2,1,0:T(8,128)(2,1)} %pad_maximum_fusion.4) | copy-start | bytes 1572868
  88.6 18.0 %copy-start.8 = (bf16[2,512,256]{2,1,0:T(8,128)(2,1)S(1)}, bf16[2,512,256]{2,1,0:T(8,128)(2,1)}, u32[]{:S(2)}) copy-start(bf16[2,512,256]{2,1,0:T(8,128)(2,1)} %pad_maximum_fusion.5) | copy-start | bytes 1572868
  88.6 25.6 %copy-start.7 = (bf16[2,512,256]{2,1,0:T(8,128)(2,1)S(1)}, bf16[2,512,256]{2,1,0:T(8,128)(2,1)}, u32[]{:S(2)}) copy-start(bf16[2,512,256]{2,1,0:T(8,128)(2,1)} %pad_maximum_fusion.6) | copy-start | bytes 1572868
  88.6 38.8 %copy-start.6 = (bf16[2,512,256]{2,1,0:T(8,128)(2,1)S(1)}, bf16[2,512,256]{2,1,0:T(8,128)(2,1)}, u32[]{:S(2)}) copy-start(bf16[2,512,256]{2,1,0:T(8,128)(2,1)} %pad_maximum_fusion.7) | copy-start | bytes 1572868
  88.6 39.3 %copy-start.5 = (bf16[2,512,256]{2,1,0:T(8,128)(2,1)S(1)}, bf16[2,512,256]{2,1,0:T(8,128)(2,1)}, u32[]{:S(2)}) copy-start(bf16[2,512,256]{2,1,0:T(8,128)(2,1)} %pad_maximum_fusion.8) | copy-start | bytes 1572868
  88.6 11.1 %collective-permute-start.7 = (bf16[128,1024]{1,0:T(8,128)(2,1)S(1)}, bf16[128,1024]{1,0:T(8,128)(2,1)S(1)}, u32[]{:S(2)}, u32[]{:S(2)}) collective-permute-start(bf16[128,1024]{1,0:T(8,128)(2,1)S(1)} %collective-permute-done.3), channel_id=1, source_target_pairs={{0,4},{4,0},{8,12},{12,8},{16,20},{20,16},{24,28},{28,24},{1,5},{5... | collective-permute-start | bytes 786440 | tf_op jit(solution)/shard_map/ppermute | solution.py:20
  90.0 16.6 %collective-permute-start.10 = (bf16[2,512,256]{2,1,0:T(8,128)(2,1)S(1)}, bf16[2,512,256]{2,1,0:T(8,128)(2,1)S(1)}, u32[]{:S(2)}, u32[]{:S(2)}) collective-permute-start(bf16[2,512,256]{2,1,0:T(8,128)(2,1)S(1)} %copy-done.12), channel_id=1, source_target_pairs={{0,2},{1,3},{2,0},{3,1},{4,6},{5,7},{6,4},{7,5},{8,10},{9,11},{10,... | collective-permute-start | bytes 1572872 | tf_op jit(solution)/shard_map/ppermute | solution.py:20
  90.6 23.6 %collective-permute-start.11 = (bf16[2,512,256]{2,1,0:T(8,128)(2,1)S(1)}, bf16[2,512,256]{2,1,0:T(8,128)(2,1)S(1)}, u32[]{:S(2)}, u32[]{:S(2)}) collective-permute-start(bf16[2,512,256]{2,1,0:T(8,128)(2,1)S(1)} %copy-done.11), channel_id=1, source_target_pairs={{0,3},{1,2},{2,1},{3,0},{4,7},{5,6},{6,5},{7,4},{8,11},{9,10},{10,... | collective-permute-start | bytes 1572872 | tf_op jit(solution)/shard_map/ppermute | solution.py:20
  95.6 31.9 %collective-permute-start.19 = (bf16[2,512,256]{2,1,0:T(8,128)(2,1)S(1)}, bf16[2,512,256]{2,1,0:T(8,128)(2,1)S(1)}, u32[]{:S(2)}, u32[]{:S(2)}) collective-permute-start(bf16[2,512,256]{2,1,0:T(8,128)(2,1)S(1)} %copy-done.10), channel_id=1, source_target_pairs={{0,2},{1,3},{2,0},{3,1},{4,6},{5,7},{6,4},{7,5},{8,10},{9,11},{10,... | collective-permute-start | bytes 1572872 | tf_op jit(solution)/shard_map/ppermute | solution.py:20
  99.7 6.9 %collective-permute-start.9 = (bf16[128,1024]{1,0:T(8,128)(2,1)S(1)}, bf16[128,1024]{1,0:T(8,128)(2,1)S(1)}, u32[]{:S(2)}, u32[]{:S(2)}) collective-permute-start(bf16[128,1024]{1,0:T(8,128)(2,1)S(1)} %collective-permute-done.5), channel_id=1, source_target_pairs={{0,4},{4,0},{8,12},{12,8},{16,20},{20,16},{24,28},{28,24},{1,5},{5... | collective-permute-start | bytes 786440 | tf_op jit(solution)/shard_map/ppermute | solution.py:20
  106.6 67.3 %collective-permute-start.20 = (bf16[2,512,256]{2,1,0:T(8,128)(2,1)S(1)}, bf16[2,512,256]{2,1,0:T(8,128)(2,1)S(1)}, u32[]{:S(2)}, u32[]{:S(2)}) collective-permute-start(bf16[2,512,256]{2,1,0:T(8,128)(2,1)S(1)} %copy-done.9), channel_id=1, source_target_pairs={{0,3},{1,2},{2,1},{3,0},{4,7},{5,6},{6,5},{7,4},{8,11},{9,10},{10,... | collective-permute-start | bytes 1572872 | tf_op jit(solution)/shard_map/ppermute | solution.py:20
  106.6 79.0 %collective-permute-start.25 = (bf16[2,512,256]{2,1,0:T(8,128)(2,1)S(1)}, bf16[2,512,256]{2,1,0:T(8,128)(2,1)S(1)}, u32[]{:S(2)}, u32[]{:S(2)}) collective-permute-start(bf16[2,512,256]{2,1,0:T(8,128)(2,1)S(1)} %copy-done.8), channel_id=1, source_target_pairs={{0,2},{1,3},{2,0},{3,1},{4,6},{5,7},{6,4},{7,5},{8,10},{9,11},{10,... | collective-permute-start | bytes 1572872 | tf_op jit(solution)/shard_map/ppermute | solution.py:20
  114.2 72.6 %collective-permute-start.26 = (bf16[2,512,256]{2,1,0:T(8,128)(2,1)S(1)}, bf16[2,512,256]{2,1,0:T(8,128)(2,1)S(1)}, u32[]{:S(2)}, u32[]{:S(2)}) collective-permute-start(bf16[2,512,256]{2,1,0:T(8,128)(2,1)S(1)} %copy-done.7), channel_id=1, source_target_pairs={{0,3},{1,2},{2,1},{3,0},{4,7},{5,6},{6,5},{7,4},{8,11},{9,10},{10,... | collective-permute-start | bytes 1572872 | tf_op jit(solution)/shard_map/ppermute | solution.py:20
  127.4 70.4 %collective-permute-start.31 = (bf16[2,512,256]{2,1,0:T(8,128)(2,1)S(1)}, bf16[2,512,256]{2,1,0:T(8,128)(2,1)S(1)}, u32[]{:S(2)}, u32[]{:S(2)}) collective-permute-start(bf16[2,512,256]{2,1,0:T(8,128)(2,1)S(1)} %copy-done.6), channel_id=1, source_target_pairs={{0,2},{1,3},{2,0},{3,1},{4,6},{5,7},{6,4},{7,5},{8,10},{9,11},{10,... | collective-permute-start | bytes 1572872 | tf_op jit(solution)/shard_map/ppermute | solution.py:20
  127.9 69.8 %collective-permute-start.32 = (bf16[2,512,256]{2,1,0:T(8,128)(2,1)S(1)}, bf16[2,512,256]{2,1,0:T(8,128)(2,1)S(1)}, u32[]{:S(2)}, u32[]{:S(2)}) collective-permute-start(bf16[2,512,256]{2,1,0:T(8,128)(2,1)S(1)} %copy-done.5), channel_id=1, source_target_pairs={{0,3},{1,2},{2,1},{3,0},{4,7},{5,6},{6,5},{7,4},{8,11},{9,10},{10,... | collective-permute-start | bytes 1572872 | tf_op jit(solution)/shard_map/ppermute | solution.py:20
  174.7 33.8 %collective-permute-start.13 = (bf16[4,272,128]{2,1,0:T(8,128)(2,1)S(1)}, bf16[4,272,128]{2,1,0:T(8,128)(2,1)}, u32[]{:S(2)}, u32[]{:S(2)}) collective-permute-start(bf16[4,272,128]{2,1,0:T(8,128)(2,1)S(1)} %slice.128), channel_id=1, source_target_pairs={{0,4},{4,0},{8,12},{12,8},{16,20},{20,16},{24,28},{28,24},{1,5},{5... | collective-permute-start | bytes 835592 | tf_op jit(solution)/shard_map/ppermute | solution.py:20
  184.8 11.4 %copy-start.2 = (bf16[8,272,128]{2,1,0:T(8,128)(2,1)}, bf16[8,272,128]{2,1,0:T(8,128)(2,1)S(1)}, u32[]{:S(2)}) copy-start(bf16[8,272,128]{2,1,0:T(8,128)(2,1)S(1)} %far_tiles.5.a_ref) | copy-start | bytes 1671172
  185.6 28.9 %collective-permute-start.21 = (bf16[4,272,128]{2,1,0:T(8,128)(2,1)}, bf16[4,272,128]{2,1,0:T(8,128)(2,1)}, u32[]{:S(2)}, u32[]{:S(2)}) collective-permute-start(bf16[4,272,128]{2,1,0:T(8,128)(2,1)} %slice.134), channel_id=1, source_target_pairs={{0,4},{4,0},{8,12},{12,8},{16,20},{20,16},{24,28},{28,24},{1,5},{5... | collective-permute-start | bytes 835592 | tf_op jit(solution)/shard_map/ppermute | solution.py:20
  196.2 10.9 %copy-start.1 = (bf16[8,272,128]{2,1,0:T(8,128)(2,1)}, bf16[8,272,128]{2,1,0:T(8,128)(2,1)S(1)}, u32[]{:S(2)}) copy-start(bf16[8,272,128]{2,1,0:T(8,128)(2,1)S(1)} %far_tiles.6.a_ref) | copy-start | bytes 1671172
  197.0 25.4 %collective-permute-start.27 = (bf16[4,272,128]{2,1,0:T(8,128)(2,1)}, bf16[4,272,128]{2,1,0:T(8,128)(2,1)S(1)}, u32[]{:S(2)}, u32[]{:S(2)}) collective-permute-start(bf16[4,272,128]{2,1,0:T(8,128)(2,1)} %slice.140), channel_id=1, source_target_pairs={{0,4},{4,0},{8,12},{12,8},{16,20},{20,16},{24,28},{28,24},{1,5},{5... | collective-permute-start | bytes 835592 | tf_op jit(solution)/shard_map/ppermute | solution.py:20
  207.1 19.2 %copy-start = (bf16[8,272,128]{2,1,0:T(8,128)(2,1)}, bf16[8,272,128]{2,1,0:T(8,128)(2,1)S(1)}, u32[]{:S(2)}) copy-start(bf16[8,272,128]{2,1,0:T(8,128)(2,1)S(1)} %far_tiles.7.a_ref) | copy-start | bytes 1671172
  207.2 20.8 %collective-permute-start.33 = (bf16[4,272,128]{2,1,0:T(8,128)(2,1)S(1)}, bf16[4,272,128]{2,1,0:T(8,128)(2,1)S(1)}, u32[]{:S(2)}, u32[]{:S(2)}) collective-permute-start(bf16[4,272,128]{2,1,0:T(8,128)(2,1)S(1)} %slice.146), channel_id=1, source_target_pairs={{0,4},{4,0},{8,12},{12,8},{16,20},{20,16},{24,28},{28,24},{1,5},{5... | collective-permute-start | bytes 835592 | tf_op jit(solution)/shard_map/ppermute | solution.py:20
  213.3 19.6 %collective-permute-start.16 = (bf16[272,128]{1,0:T(8,128)(2,1)S(1)}, bf16[272,128]{1,0:T(8,128)(2,1)S(1)}, u32[]{:S(2)}, u32[]{:S(2)}) collective-permute-start(bf16[272,128]{1,0:T(8,128)(2,1)S(1)} %get-tuple-element.48), channel_id=1, source_target_pairs={{0,8},{4,12},{8,16},{12,20},{16,24},{20,28},{24,0},{28,4},{1,9},{5... | collective-permute-start | bytes 208904 | tf_op jit(solution)/shard_map/ppermute | solution.py:25
  213.3 21.8 %collective-permute-start.15 = (bf16[272,128]{1,0:T(8,128)(2,1)S(1)}, bf16[272,128]{1,0:T(8,128)(2,1)S(1)}, u32[]{:S(2)}, u32[]{:S(2)}) collective-permute-start(bf16[272,128]{1,0:T(8,128)(2,1)S(1)} %get-tuple-element.49), channel_id=1, source_target_pairs={{0,16},{4,20},{8,24},{12,28},{16,0},{20,4},{24,8},{28,12},{1,17},{... | collective-permute-start | bytes 208904 | tf_op jit(solution)/shard_map/ppermute | solution.py:25
  214.5 22.2 %collective-permute-start.14 = (bf16[272,128]{1,0:T(8,128)(2,1)S(1)}, bf16[272,128]{1,0:T(8,128)(2,1)S(1)}, u32[]{:S(2)}, u32[]{:S(2)}) collective-permute-start(bf16[272,128]{1,0:T(8,128)(2,1)S(1)} %get-tuple-element.50), channel_id=1, source_target_pairs={{0,24},{4,28},{8,0},{12,4},{16,8},{20,12},{24,16},{28,20},{1,25},{... | collective-permute-start | bytes 208904 | tf_op jit(solution)/shard_map/ppermute | solution.py:25
  220.7 24.9 %copy-start.4 = (f32[16,64,128]{2,1,0:T(8,128)S(1)}, f32[16,64,128]{2,1,0:T(8,128)}, u32[]{:S(2)}) copy-start(f32[16,64,128]{2,1,0:T(8,128)} %convolution_divide_fusion) | copy-start | bytes 1572868
  222.4 15.7 %collective-permute-start.24 = (bf16[272,128]{1,0:T(8,128)(2,1)S(1)}, bf16[272,128]{1,0:T(8,128)(2,1)S(1)}, u32[]{:S(2)}, u32[]{:S(2)}) collective-permute-start(bf16[272,128]{1,0:T(8,128)(2,1)S(1)} %get-tuple-element.52), channel_id=1, source_target_pairs={{0,8},{4,12},{8,16},{12,20},{16,24},{20,28},{24,0},{28,4},{1,9},{5... | collective-permute-start | bytes 208904 | tf_op jit(solution)/shard_map/ppermute | solution.py:25
  227.9 13.0 %collective-permute-start.23 = (bf16[272,128]{1,0:T(8,128)(2,1)S(1)}, bf16[272,128]{1,0:T(8,128)(2,1)S(1)}, u32[]{:S(2)}, u32[]{:S(2)}) collective-permute-start(bf16[272,128]{1,0:T(8,128)(2,1)S(1)} %get-tuple-element.53), channel_id=1, source_target_pairs={{0,16},{4,20},{8,24},{12,28},{16,0},{20,4},{24,8},{28,12},{1,17},{... | collective-permute-start | bytes 208904 | tf_op jit(solution)/shard_map/ppermute | solution.py:25
  232.9 14.1 %copy-start.19 = (bf16[272,128]{1,0:T(8,128)(2,1)}, bf16[272,128]{1,0:T(8,128)(2,1)S(1)}, u32[]{:S(2)}) copy-start(bf16[272,128]{1,0:T(8,128)(2,1)S(1)} %collective-permute-done.16.refs_3_) | copy-start | bytes 208900
  232.9 8.4 %collective-permute-start.22 = (bf16[272,128]{1,0:T(8,128)(2,1)S(1)}, bf16[272,128]{1,0:T(8,128)(2,1)S(1)}, u32[]{:S(2)}, u32[]{:S(2)}) collective-permute-start(bf16[272,128]{1,0:T(8,128)(2,1)S(1)} %get-tuple-element.54), channel_id=1, source_target_pairs={{0,24},{4,28},{8,0},{12,4},{16,8},{20,12},{24,16},{28,20},{1,25},{... | collective-permute-start | bytes 208904 | tf_op jit(solution)/shard_map/ppermute | solution.py:25
  235.1 11.9 %copy-start.20 = (bf16[272,128]{1,0:T(8,128)(2,1)}, bf16[272,128]{1,0:T(8,128)(2,1)S(1)}, u32[]{:S(2)}) copy-start(bf16[272,128]{1,0:T(8,128)(2,1)S(1)} %collective-permute-done.15.refs_2_) | copy-start | bytes 208900
  235.1 7.6 %collective-permute-start.30 = (bf16[272,128]{1,0:T(8,128)(2,1)S(1)}, bf16[272,128]{1,0:T(8,128)(2,1)S(1)}, u32[]{:S(2)}, u32[]{:S(2)}) collective-permute-start(bf16[272,128]{1,0:T(8,128)(2,1)S(1)} %get-tuple-element.56), channel_id=1, source_target_pairs={{0,8},{4,12},{8,16},{12,20},{16,24},{20,28},{24,0},{28,4},{1,9},{5... | collective-permute-start | bytes 208904 | tf_op jit(solution)/shard_map/ppermute | solution.py:25
  236.8 10.2 %copy-start.21 = (bf16[272,128]{1,0:T(8,128)(2,1)}, bf16[272,128]{1,0:T(8,128)(2,1)S(1)}, u32[]{:S(2)}) copy-start(bf16[272,128]{1,0:T(8,128)(2,1)S(1)} %collective-permute-done.14.refs_1_) | copy-start | bytes 208900
  236.8 14.4 %collective-permute-start.29 = (bf16[272,128]{1,0:T(8,128)(2,1)S(1)}, bf16[272,128]{1,0:T(8,128)(2,1)S(1)}, u32[]{:S(2)}, u32[]{:S(2)}) collective-permute-start(bf16[272,128]{1,0:T(8,128)(2,1)S(1)} %get-tuple-element.57), channel_id=1, source_target_pairs={{0,16},{4,20},{8,24},{12,28},{16,0},{20,4},{24,8},{28,12},{1,17},{... | collective-permute-start | bytes 208904 | tf_op jit(solution)/shard_map/ppermute | solution.py:25
  238.0 11.4 %copy-start.22 = (bf16[272,128]{1,0:T(8,128)(2,1)}, bf16[272,128]{1,0:T(8,128)(2,1)S(1)}, u32[]{:S(2)}) copy-start(bf16[272,128]{1,0:T(8,128)(2,1)S(1)} %collective-permute-done.24.refs_3_) | copy-start | bytes 208900
  238.0 13.1 %collective-permute-start.28 = (bf16[272,128]{1,0:T(8,128)(2,1)S(1)}, bf16[272,128]{1,0:T(8,128)(2,1)S(1)}, u32[]{:S(2)}, u32[]{:S(2)}) collective-permute-start(bf16[272,128]{1,0:T(8,128)(2,1)S(1)} %get-tuple-element.58), channel_id=1, source_target_pairs={{0,24},{4,28},{8,0},{12,4},{16,8},{20,12},{24,16},{28,20},{1,25},{... | collective-permute-start | bytes 208904 | tf_op jit(solution)/shard_map/ppermute | solution.py:25
  240.9 8.5 %copy-start.23 = (bf16[272,128]{1,0:T(8,128)(2,1)}, bf16[272,128]{1,0:T(8,128)(2,1)S(1)}, u32[]{:S(2)}) copy-start(bf16[272,128]{1,0:T(8,128)(2,1)S(1)} %collective-permute-done.23.refs_2_) | copy-start | bytes 208900
  240.9 12.7 %collective-permute-start.36 = (bf16[272,128]{1,0:T(8,128)(2,1)S(1)}, bf16[272,128]{1,0:T(8,128)(2,1)S(1)}, u32[]{:S(2)}, u32[]{:S(2)}) collective-permute-start(bf16[272,128]{1,0:T(8,128)(2,1)S(1)} %get-tuple-element.60), channel_id=1, source_target_pairs={{0,8},{4,12},{8,16},{12,20},{16,24},{20,28},{24,0},{28,4},{1,9},{5... | collective-permute-start | bytes 208904 | tf_op jit(solution)/shard_map/ppermute | solution.py:25
  241.2 8.2 %copy-start.26 = (bf16[272,128]{1,0:T(8,128)(2,1)}, bf16[272,128]{1,0:T(8,128)(2,1)S(1)}, u32[]{:S(2)}) copy-start(bf16[272,128]{1,0:T(8,128)(2,1)S(1)} %collective-permute-done.22.refs_1_) | copy-start | bytes 208900
  241.2 12.4 %collective-permute-start.35 = (bf16[272,128]{1,0:T(8,128)(2,1)S(1)}, bf16[272,128]{1,0:T(8,128)(2,1)S(1)}, u32[]{:S(2)}, u32[]{:S(2)}) collective-permute-start(bf16[272,128]{1,0:T(8,128)(2,1)S(1)} %get-tuple-element.61), channel_id=1, source_target_pairs={{0,16},{4,20},{8,24},{12,28},{16,0},{20,4},{24,8},{28,12},{1,17},{... | collective-permute-start | bytes 208904 | tf_op jit(solution)/shard_map/ppermute | solution.py:25
  242.7 9.1 %copy-start.24 = (bf16[272,128]{1,0:T(8,128)(2,1)}, bf16[272,128]{1,0:T(8,128)(2,1)S(1)}, u32[]{:S(2)}) copy-start(bf16[272,128]{1,0:T(8,128)(2,1)S(1)} %collective-permute-done.30.refs_3_) | copy-start | bytes 208900
  242.7 10.9 %collective-permute-start.34 = (bf16[272,128]{1,0:T(8,128)(2,1)S(1)}, bf16[272,128]{1,0:T(8,128)(2,1)S(1)}, u32[]{:S(2)}, u32[]{:S(2)}) collective-permute-start(bf16[272,128]{1,0:T(8,128)(2,1)S(1)} %get-tuple-element.62), channel_id=1, source_target_pairs={{0,24},{4,28},{8,0},{12,4},{16,8},{20,12},{24,16},{28,20},{1,25},{... | collective-permute-start | bytes 208904 | tf_op jit(solution)/shard_map/ppermute | solution.py:25
  261.0 2.2 collective-permute-start.37
  261.1 8.3 %collective-permute-start.39 = (bf16[128,1024]{1,0:T(8,128)(2,1)S(1)}, bf16[128,1024]{1,0:T(8,128)(2,1)S(1)}, u32[]{:S(2)}, u32[]{:S(2)}) collective-permute-start(bf16[128,1024]{1,0:T(8,128)(2,1)S(1)} %get-tuple-element.42), channel_id=1, source_target_pairs={{0,3},{1,2},{2,1},{3,0},{4,7},{5,6},{6,5},{7,4},{8,11},{9,10},{10,... | collective-permute-start | bytes 786440 | tf_op jit(solution)/shard_map/ppermute | solution.py:20
  262.7 12.7 %collective-permute-start.38 = (bf16[128,1024]{1,0:T(8,128)(2,1)S(1)}, bf16[128,1024]{1,0:T(8,128)(2,1)S(1)}, u32[]{:S(2)}, u32[]{:S(2)}) collective-permute-start(bf16[128,1024]{1,0:T(8,128)(2,1)S(1)} %get-tuple-element.43), channel_id=1, source_target_pairs={{0,2},{1,3},{2,0},{3,1},{4,6},{5,7},{6,4},{7,5},{8,10},{9,11},{10,... | collective-permute-start | bytes 786440 | tf_op jit(solution)/shard_map/ppermute | solution.py:20
  (10 other events, 9.7 us)

commit v2 on v0

v2 whole, which is shorter than its diff:
```python
import functools

import jax
import jax.numpy as jnp
from jax import lax
from jax.experimental import pallas as pl
from jax.experimental.pallas import tpu as pltpu
from jax.sharding import PartitionSpec as P

DH = 64
PAIR = 2 * DH
TILE_ROWS = 128
QB = 256
CHUNK_HEADS = 4
STAT_ROWS = 16
EMPTY = -1e38


def swap(block, axis, distance):
    return lax.ppermute(block, axis, [(i, i ^ distance) for i in range(lax.axis_size(axis))])


def turn(block, axis, distance):
    size = lax.axis_size(axis)
    return lax.ppermute(block, axis, [(i, (i + distance) % size) for i in range(size)])


def from_behind(block, axis, distance):
    devices = range(lax.axis_size(axis))
    route = [(i - distance, i) for i in devices if i - distance in devices]
    return lax.ppermute(block, axis, route)


def pipelined(q_ref, key_refs, vt_ref, bits_ref, s_ref, first_bit, emit):
    rows = q_ref.shape[0]
    n = key_refs[0].shape[0]
    tiles = n // TILE_ROWS
    step = 2 if tiles % 2 == 0 else 1
    units = [
        (pair, block, head)
        for pair in range(CHUNK_HEADS // 2)
        for block in range(rows // QB)
        for head in range(2)
    ]
    places = [(src, t) for src in range(len(key_refs)) for t in range(0, tiles, step)]
    lane = lax.broadcasted_iota(jnp.int32, (QB, PAIR), 1)
    ones = jnp.ones((16, step * TILE_ROWS), jnp.bfloat16)

    def query(unit):
        pair, block, head = units[unit]
        q = q_ref[block * QB : (block + 1) * QB, pair * PAIR : (pair + 1) * PAIR]
        q = q * jnp.asarray(0.125, q.dtype)
        return jnp.where((lane < DH) if head == 0 else (lane >= DH), q, jnp.zeros_like(q))

    def mask(unit, src, t):
        block = units[unit][1]
        bit = first_bit + src * tiles + t
        return ((bits_ref[:, block * QB : (block + 1) * QB] >> bit) & 1) == 1

    def score(unit, q, place, top):
        src, t0 = place
        pair = units[unit][0]
        key = key_refs[src][t0 * TILE_ROWS : (t0 + step) * TILE_ROWS, pair * PAIR : (pair + 1) * PAIR]
        s = lax.dot_general(key, q, (((1,), (1,)), ((), ())), preferred_element_type=jnp.float32)
        s_ref[unit % 2, src, t0 * TILE_ROWS : (t0 + step) * TILE_ROWS] = s
        for i in range(step):
            high = jnp.max(s[i * TILE_ROWS : (i + 1) * TILE_ROWS], axis=0, keepdims=True)
            high = jnp.where(mask(unit, src, t0 + i), high, EMPTY)
            top = high if top is None else jnp.maximum(top, high)
        return top

    def weigh(unit, place, top, sums):
        src, t0 = place
        pair, _, head = units[unit]
        parts = []
        for i in range(step):
            minus = jnp.where(mask(unit, src, t0 + i), top, jnp.inf)
            s = s_ref[unit % 2, src, (t0 + i) * TILE_ROWS : (t0 + i + 1) * TILE_ROWS]
            parts.append(jnp.exp(s - minus).astype(jnp.bfloat16))
        first = pair * PAIR + head * DH
        left = vt_ref[src, first : first + DH, t0 * TILE_ROWS : (t0 + step) * TILE_ROWS]
        o = jnp.dot(
            jnp.concatenate([left, ones], axis=0),
            jnp.concatenate(parts, axis=0),
            preferred_element_type=jnp.float32,
        )
        return o if sums is None else sums + o

    top = None
    q = query(0)
    for place in places:
        top = score(0, q, place, top)
    for unit in range(len(units)):
        sums = None
        later = None
        if unit + 1 < len(units):
            q = query(unit + 1)
        for place in places:
            if unit + 1 < len(units):
                later = score(unit + 1, q, place, later)
            sums = weigh(unit, place, top, sums)
        emit(*units[unit], top, sums[DH : DH + 1], sums[:DH])
        top = later


def near_kernel(m_ref, q_ref, k0_ref, v0_ref, k1_ref, v1_ref, bits_ref, acc_ref, stat_ref, vt_ref, s_ref):
    vt_ref[0] = jnp.transpose(v0_ref[...])
    vt_ref[1] = jnp.transpose(v1_ref[0])

    def emit(pair, block, head, top, total, sums):
        lanes = slice(block * QB, (block + 1) * QB)
        row = pair * PAIR + head * DH
        acc_ref[row : row + DH, lanes] = sums
        stat_ref[pair, head : head + 1, lanes] = top
        stat_ref[pair, 2 + head : 3 + head, lanes] = total

    pipelined(q_ref, [k0_ref, k1_ref.at[0]], vt_ref, bits_ref, s_ref, 0, emit)


def three(x):
    hi = x.astype(jnp.bfloat16)
    rest = x - hi.astype(jnp.float32)
    mid = rest.astype(jnp.bfloat16)
    low = (rest - mid.astype(jnp.float32)).astype(jnp.bfloat16)
    return [hi.astype(jnp.float32), mid.astype(jnp.float32), low.astype(jnp.float32)]


def packed(lses):
    rows = [part for x in lses for part in three(x)]
    rows.append(jnp.zeros((STAT_ROWS - len(rows), rows[0].shape[1]), jnp.float32))
    return jnp.concatenate(rows, axis=0).astype(jnp.bfloat16)


def far_kernel(
    q_ref, k2_ref, v2_ref, k3_ref, v3_ref, bits_ref, acc_ref, stat_ref, out_ref, vt_ref, s_ref
):
    vt_ref[0] = jnp.transpose(v2_ref[0])
    vt_ref[1] = jnp.transpose(v3_ref[0])
    base = CHUNK_HEADS * DH
    lses = {}

    def emit(pair, block, head, top, total, sums):
        lanes = slice(block * QB, (block + 1) * QB)
        near_top = stat_ref[pair, head : head + 1, lanes]
        near_total = stat_ref[pair, 2 + head : 3 + head, lanes]
        new = jnp.maximum(top, near_top)
        near_w = jnp.exp(near_top - new)
        far_w = jnp.exp(top - new)
        both = near_w * near_total + far_w * total
        some = both > 0.0
        safe = jnp.where(some, both, 1.0)
        inv = 1.0 / safe
        row = pair * PAIR + head * DH
        o = (near_w * inv) * acc_ref[row : row + DH, lanes] + (far_w * inv) * sums
        o = o.astype(jnp.bfloat16)
        lses[pair, block, head] = jnp.where(some, new + jnp.log(safe), EMPTY)
        for part in range(QB // TILE_ROWS):
            out_ref[block * (QB // TILE_ROWS) + part, row : row + DH] = o[
                :, part * TILE_ROWS : (part + 1) * TILE_ROWS
            ]

    pipelined(
        q_ref, [k2_ref.at[0], k3_ref.at[0]], vt_ref, bits_ref, s_ref, 2 * (k2_ref.shape[1] // TILE_ROWS), emit
    )
    for block in range(q_ref.shape[0] // QB):
        stats = packed(
            [lses[pair, block, head] for pair in range(CHUNK_HEADS // 2) for head in range(2)]
        )
        for part in range(QB // TILE_ROWS):
            out_ref[block * (QB // TILE_ROWS) + part, base : base + STAT_ROWS] = stats[
                :, part * TILE_ROWS : (part + 1) * TILE_ROWS
            ]


def lse_of(stats, head):
    return stats[3 * head : 3 * head + 1] + stats[3 * head + 1 : 3 * head + 2] + stats[3 * head + 2 : 3 * head + 3]


def merge_kernel(a_ref, b_ref, *out_refs):
    base = CHUNK_HEADS * DH
    for k, out_ref in enumerate(out_refs):
        stats_a = a_ref[k, base:].astype(jnp.float32)
        stats_b = b_ref[k, base:].astype(jnp.float32)
        lses = []
        for head in range(CHUNK_HEADS):
            lse_a = lse_of(stats_a, head)
            lse_b = lse_of(stats_b, head)
            top = jnp.maximum(lse_a, lse_b)
            w_a = jnp.exp(lse_a - top)
            w_b = jnp.exp(lse_b - top)
            total = w_a + w_b
            inv = 1.0 / total
            rows = slice(head * DH, (head + 1) * DH)
            out_ref[rows] = (
                (w_a * inv) * a_ref[k, rows].astype(jnp.float32)
                + (w_b * inv) * b_ref[k, rows].astype(jnp.float32)
            ).astype(jnp.bfloat16)
            lses.append(top + jnp.log(total))
        out_ref[base:] = packed(lses)


def final_kernel(*refs):
    *msg_refs, local_ref, gate_ref, out_ref = refs
    base = CHUNK_HEADS * DH
    stats = [r[base:].astype(jnp.float32) for r in msg_refs]
    for head in range(CHUNK_HEADS):
        lses = [lse_of(s, head) for s in stats]
        top = functools.reduce(jnp.maximum, lses)
        ws = [jnp.exp(x - top) for x in lses]
        inv = 1.0 / functools.reduce(jnp.add, ws)
        rows = slice(head * DH, (head + 1) * DH)
        mem = None
        for r, w in zip(msg_refs, ws):
            term = w * r[rows].astype(jnp.float32)
            mem = term if mem is None else mem + term
        gate = gate_ref[head : head + 1]
        out_ref[rows] = (
            (gate * inv) * mem + (1.0 - gate) * local_ref[rows].astype(jnp.float32)
        ).astype(jnp.bfloat16)


def on_device(
    hidden_states,
    w_query,
    local_keys,
    local_values,
    memory_keys,
    memory_values,
    tile_ids,
    tile_counts,
    gate_bias,
    w_output,
):
    row_count = hidden_states.shape[0]
    features = w_query.shape[1]
    heads_here = features // DH
    ctx_size = lax.axis_size("ctx")
    mem_size = lax.axis_size("mem")
    turns = ctx_size // 2
    pick_count = tile_ids.shape[1]
    mem_rows = memory_keys.shape[0]
    tiles_here = mem_rows // TILE_ROWS
    group_tiles = tiles_here * mem_size
    all_rows = ctx_size * row_count
    me = lax.axis_index("mem")
    my_ctx = lax.axis_index("ctx")
    chunks = heads_here // CHUNK_HEADS
    width = CHUNK_HEADS * DH
    pairs = heads_here // 2

    half = all_rows // 2
    f32 = jnp.float32

    live = jnp.arange(pick_count, dtype=jnp.int32)[None, :] < tile_counts[:, None]
    ids = jnp.transpose(jnp.where(live, tile_ids, -1))
    ids = jnp.stack([ids, swap(ids, "ctx", 1)])
    ids = [ids] + [turn(ids, "ctx", 2 * k) for k in range(1, turns)]
    ids = jnp.stack(ids, axis=1)
    here = (ids >= my_ctx * group_tiles) & (ids < (my_ctx + 1) * group_tiles)
    place = (((ids // tiles_here) % mem_size) ^ me) * tiles_here + ids % tiles_here
    bits = jnp.sum(jnp.where(here, 1 << jnp.where(here, place, 0), 0), axis=2)
    bits = [bits[part].reshape(1, half) for part in range(2)]

    h1 = swap(hidden_states, "mem", 1)
    h2 = swap(hidden_states, "mem", 2)
    h3 = swap(h2, "mem", 1)
    have = [hidden_states, h1, h2, h3]
    hidden = jnp.zeros((row_count, mem_size * hidden_states.shape[1]), jnp.bfloat16)
    for k in range(mem_size):
        hidden = lax.dynamic_update_slice(hidden, have[k], (0, (me ^ k) * hidden_states.shape[1]))
    queries = jnp.dot(hidden, w_query, preferred_element_type=f32).astype(jnp.bfloat16)

    def share(at, cols):
        return jnp.stack(
            [
                lax.dynamic_slice(memory_keys, (0, at), (mem_rows, cols)),
                lax.dynamic_slice(memory_values, (0, at), (mem_rows, cols)),
            ]
        )

    first_send = [share((me ^ k) * features, width) for k in (2, 3)]
    first_send, _ = lax.optimization_barrier((first_send, h2))
    later_me, _ = lax.optimization_barrier((me, queries))
    far = [[swap(x, "mem", k) for x, k in zip(first_send, (2, 3))]]
    near = swap(share((later_me ^ 1) * features, features), "mem", 1)
    far += [
        [swap(share((later_me ^ k) * features + j * width, width), "mem", k) for k in (2, 3)]
        for j in range(1, chunks)
    ]

    q_blocks = [queries] + [turn(queries, "ctx", 2 * k) for k in range(1, turns)]
    q_blocks += [swap(q, "ctx", 1) for q in q_blocks]
    q_halves = [jnp.concatenate(q_blocks[part * turns : (part + 1) * turns], 0) for part in range(2)]

    window, _ = lax.optimization_barrier(((local_keys, local_values), q_blocks[-1]))
    earlier_k = from_behind(window[0], "ctx", 1)
    earlier_v = from_behind(window[1], "ctx", 1)
    window_keys = jnp.concatenate([earlier_k, local_keys], 0).reshape(2 * row_count, heads_here, DH)
    window_values = jnp.concatenate([earlier_v, local_values], 0).reshape(
        2 * row_count, heads_here, DH
    )
    query_heads = queries.reshape(row_count, heads_here, DH)
    scores = (
        jnp.einsum("ihd,jhd->hij", query_heads, window_keys, preferred_element_type=f32) * 0.125
    )
    query_pos = jnp.arange(row_count, dtype=jnp.int32)[:, None]
    key_pos = jnp.arange(2 * row_count, dtype=jnp.int32)[None, :]
    allowed = (
        (key_pos > query_pos)
        & (key_pos <= query_pos + row_count)
        & ((key_pos >= row_count) | (my_ctx > 0))
    )
    scores = jnp.where(allowed[None], scores, -jnp.inf)
    highest = jnp.max(scores, axis=-1, keepdims=True)
    weights_f = jnp.exp(scores - highest)
    summed = jnp.sum(weights_f, axis=-1)
    mixed = jnp.einsum(
        "hij,jhd->hdi",
        weights_f.astype(jnp.bfloat16),
        window_values,
        preferred_element_type=f32,
    )
    local_out = (mixed / summed[:, None, :]).reshape(features, row_count)

    chunk_pairs = CHUNK_HEADS // 2
    near_flops = 2 * 2 * half * 2 * mem_rows * features
    scratch = [
        pltpu.VMEM((2, width, mem_rows), jnp.bfloat16),
        pltpu.VMEM((2, 2, mem_rows, QB), f32),
    ]
    near_state = []
    for part in range(2):
        near_state.append(
            pl.pallas_call(
                near_kernel,
                grid_spec=pltpu.PrefetchScalarGridSpec(
                    num_scalar_prefetch=1,
                    grid=(chunks,),
                    in_specs=[
                        pl.BlockSpec((half, width), lambda p, m: (0, p)),
                        pl.BlockSpec((mem_rows, width), lambda p, m: (0, m[0] * chunks + p)),
                        pl.BlockSpec((mem_rows, width), lambda p, m: (0, m[0] * chunks + p)),
                        pl.BlockSpec((1, mem_rows, width), lambda p, m: (0, 0, p)),
                        pl.BlockSpec((1, mem_rows, width), lambda p, m: (1, 0, p)),
                        pl.BlockSpec((1, half), lambda p, m: (0, 0)),
                    ],
                    out_specs=[
                        pl.BlockSpec((width, half), lambda p, m: (p, 0)),
                        pl.BlockSpec((chunk_pairs, 8, half), lambda p, m: (p, 0, 0)),
                    ],
                    scratch_shapes=scratch,
                ),
                out_shape=[
                    jax.ShapeDtypeStruct((features, half), f32),
                    jax.ShapeDtypeStruct((pairs, 8, half), f32),
                ],
                compiler_params=pltpu.CompilerParams(vmem_limit_bytes=48 << 20),
                cost_estimate=pl.CostEstimate(
                    flops=near_flops,
                    transcendentals=half * 2 * mem_rows * heads_here,
                    bytes_accessed=8 << 20,
                ),
                name="near_tiles",
            )(me.reshape(1), q_halves[part], memory_keys, memory_values, near, near, bits[part])
        )

    gate = jax.nn.sigmoid(gate_bias)
    gate_rows = jnp.broadcast_to(gate[:, None], (heads_here, row_count)).reshape(
        chunks, CHUNK_HEADS, row_count
    )
    combined = []
    msg_rows = width + STAT_ROWS
    for j in range(chunks):
        far2, far3 = far[j]
        message = [None, None]
        for part in (1, 0):
            acc, stat = near_state[part]
            message[part] = pl.pallas_call(
                far_kernel,
                grid=(1,),
                in_specs=[
                    pl.BlockSpec((half, width), lambda i, j=j: (0, j)),
                    pl.BlockSpec((1, mem_rows, width), lambda i: (0, 0, 0)),
                    pl.BlockSpec((1, mem_rows, width), lambda i: (1, 0, 0)),
                    pl.BlockSpec((1, mem_rows, width), lambda i: (0, 0, 0)),
                    pl.BlockSpec((1, mem_rows, width), lambda i: (1, 0, 0)),
                    pl.BlockSpec((1, half), lambda i: (0, 0)),
                    pl.BlockSpec((width, half), lambda i, j=j: (j, 0)),
                    pl.BlockSpec((chunk_pairs, 8, half), lambda i, j=j: (j, 0, 0)),
                ],
                out_specs=pl.BlockSpec((turns, msg_rows, row_count), lambda i: (0, 0, 0)),
                out_shape=jax.ShapeDtypeStruct((turns, msg_rows, row_count), jnp.bfloat16),
                scratch_shapes=scratch,
                compiler_params=pltpu.CompilerParams(vmem_limit_bytes=48 << 20),
                cost_estimate=pl.CostEstimate(
                    flops=near_flops // chunks,
                    transcendentals=half * 2 * mem_rows * CHUNK_HEADS,
                    bytes_accessed=3 << 20,
                ),
                name="far_tiles",
            )(q_halves[part], far2, far2, far3, far3, bits[part], acc, stat)
        other = swap(message[1], "ctx", 1)
        merged = pl.pallas_call(
            merge_kernel,
            out_shape=[jax.ShapeDtypeStruct((msg_rows, row_count), jnp.bfloat16)] * turns,
            name="merge_pair",
        )(message[0], other)
        answers = [merged[0]] + [turn(merged[k], "ctx", -2 * k) for k in range(1, turns)]
        combined.append(
            pl.pallas_call(
                final_kernel,
                out_shape=jax.ShapeDtypeStruct((width, row_count), jnp.bfloat16),
                name="merge_all",
            )(*answers, local_out[j * width : (j + 1) * width], gate_rows[j])
        )
    early = jnp.concatenate(combined[:-1], axis=0)
    cols = w_output.shape[1] // mem_size
    over_rows = (((0,), (0,)), ((), ()))

    def piece(k):
        w = lax.dynamic_slice(w_output, (0, (me ^ k) * cols), (features, cols))
        split = early.shape[0]
        return lax.dot_general(early, w[:split], over_rows, preferred_element_type=f32) + lax.dot_general(
            combined[-1], w[split:], over_rows, preferred_element_type=f32
        )

    away = piece(2) + swap(piece(3).astype(jnp.bfloat16), "mem", 1).astype(f32)
    away = swap(away.astype(jnp.bfloat16), "mem", 2)
    result = piece(0) + swap(piece(1).astype(jnp.bfloat16), "mem", 1).astype(f32)
    return (result + away.astype(f32)).astype(jnp.bfloat16)


def solution(mesh):
    in_specs = (
        P("ctx", "mem"),
        P(None, "mem"),
        P("ctx", "mem"),
        P("ctx", "mem"),
        P(("ctx", "mem"), None),
        P(("ctx", "mem"), None),
        P("ctx", None),
        P("ctx"),
        P("mem"),
        P("mem", None),
    )
    out_specs = P("ctx", "mem")
    return jax.shard_map(
        on_device, mesh=mesh, in_specs=in_specs, out_specs=out_specs, check_vma=False
    )
```

time: 714 us -> 229 us (0.32); the launches traced: 704 us -> 228 us
  waiting for transfers between devices: 377 us -> 47.6 us
  local copies, waits for them, and re-layouts: 176 us -> 23.7 us
  Pallas kernels: 0 us -> 59.2 us
  other arithmetic: 54 us -> 14.8 us
  matrix products: 56.6 us -> 20.4 us
  starting transfers between devices: 26.8 us -> 62 us
  between operations: 14.3 us -> 0.61 us
    all_to_all x4 -> x0, waiting for transfers between devices: 259 us -> none  [the longest x1 164 us: on_device(): lax.all_to_all(outgoing, ('ctx', 'mem'), split_axis=0, concat_axis=0, til...]
    ppermute x2, waiting for transfers between devices: 60.1 us -> 0.01 us  [from_behind(): return lax.ppermute(block, axis, route)]
    pallas_call x0 -> x18, Pallas kernels: none -> 59.2 us  [the longest x8 23.3 us: on_device(): pl.pallas_call(far_kernel, grid=(1,), in_specs=[pl.BlockSpec((half, width...]
    reduce_scatter x1 -> x0, waiting for transfers between devices: 54.6 us -> none  [on_device(): lax.psum_scatter(partial_out.astype(jnp.bfloat16), 'mem', scatter_dimensi...]
    gather x9 -> x0, local copies, waits for them, and re-layouts: 53.5 us -> none  [the longest x2 27.1 us: on_device(): jnp.take(answer[0], safe_target, axis=0)]
    ppermute x0 -> x42, starting transfers between devices: none -> 52.5 us  [the longest x18 31.6 us: turn(): lax.ppermute(block, axis, [(i, (i + distance) % size) for i in range(size)])]
    ppermute x0 -> x42, waiting for transfers between devices: none -> 47.6 us  [the longest x24 40.9 us: swap(): lax.ppermute(block, axis, [(i, i ^ distance) for i in range(lax.axis_size...]
    dot_general x11 -> x10, matrix products: 56 us -> 18.7 us  [the longest x4 8.14 us: piece(): lax.dot_general(early, w[:split], over_rows, preferred_element_type=f32)]
  transfers between devices with their start and end apart: 8 -> 44, of which waited for: 6 -> 14; matrix products, arithmetic and copies ran while one was open for 17% -> 19% of each run, Pallas kernels for 0% -> 25%
where the time goes in v2:
time: 229 us; the launch traced here: 228 us
  starting transfers between devices  62 us (27%)
  Pallas kernels  59.2 us (26%)
  waiting for transfers between devices  47.6 us (21%)
  local copies, waits for them, and re-layouts  23.7 us (10%)
  matrix products  20.4 us (9%)
  other arithmetic  14.8 us (6%)
    ppermute x24, waiting for transfers between devices, swap(): lax.ppermute(block, axis, [(i, i ^ distance) for i in range(lax.axis_size...  40.9 us
    ppermute x18, starting transfers between devices, turn(): lax.ppermute(block, axis, [(i, (i + distance) % size) for i in range(size)])  31.6 us
    pallas_call x8, Pallas kernels, on_device(): pl.pallas_call(far_kernel, grid=(1,), in_specs=[pl.BlockSpec((half, width...  23.3 us
    pallas_call x2, Pallas kernels, on_device(): pl.pallas_call(near_kernel, grid_spec=pltpu.PrefetchScalarGridSpec(num_sc...  21.4 us
    ppermute x24, starting transfers between devices, swap(): lax.ppermute(block, axis, [(i, i ^ distance) for i in range(lax.axis_size...  20.9 us
    ppermute x2, starting transfers between devices, from_behind(): return lax.ppermute(block, axis, route)  9.48 us
    another operation x9, other arithmetic, share(): jnp.stack([lax.dynamic_slice(memory_keys, (0, at), (mem_rows, cols)), lax...  8.45 us
    dot_general x4, matrix products, piece(): lax.dot_general(early, w[:split], over_rows, preferred_element_type=f32)  8.14 us
  transfers between devices with their start and end apart: 44, of which 14 were waited for; matrix products, arithmetic and copies ran while one was open for 19% of the time, Pallas kernels for 25%

profile of v2, /device:TPU:0, one launch (start us, length us, event | category | flops | bytes accessed | tf_op | source)
XLA Modules:
  0.0 228.3 jit_solution(7346398112497485181)
XLA Ops:
  0.0 2.9 %collective-permute-start.1 = (bf16[128,1024]{1,0:T(8,128)(2,1)}, bf16[128,1024]{1,0:T(8,128)(2,1)S(1)}, u32[]{:S(2)}, u32[]{:S(2)}) collective-permute-start(bf16[128,1024]{1,0:T(8,128)(2,1)} %param.10), channel_id=1, source_target_pairs={{0,2},{1,3},{2,0},{3,1},{4,6},{5,7},{6,4},{7,5},{8,10},{9,11},{10,... | collective-permute-start | bytes 786440 | tf_op jit(solution)/shard_map/ppermute | solution.py:20
  3.6 1.5 collective-permute-start.8
  7.3 2.6 %collective-permute-start.10 = (s32[2,16,128]{2,1,0:T(8,128)S(1)}, s32[2,16,128]{2,1,0:T(8,128)S(1)}, u32[]{:S(2)}, u32[]{:S(2)}) collective-permute-start(s32[2,16,128]{2,1,0:T(8,128)S(1)} %get-tuple-element.76), channel_id=1, source_target_pairs={{0,16},{4,20},{8,24},{12,28},{16,0},{20,4},{24,8},{28,12},{1,17},{... | collective-permute-start | bytes 49160 | tf_op jit(solution)/shard_map/ppermute | solution.py:25
  9.9 1.6 collective-permute-start.9
  11.5 2.2 collective-permute-start.11
  17.2 4.6 %convolution_convert_fusion = bf16[128,1024]{1,0:T(8,128)(2,1)S(1)} fusion(bf16[128,4096]{1,0:T(8,128)(2,1)S(1)} %constant_dynamic-update-slice_fusion.4, bf16[4096,1024]{1,0:T(8,128)(2,1)} %param.11), kind=kOutput, calls=%fused_computation.26 | convolution fusion | flops 1073872896 | bytes 9699328 | tf_op jit(solution)/shard_map/dot_general | solution.py:271
  21.8 1.6 collective-permute-start.13
  23.4 3.8 %collective-permute-start.5 = (bf16[128,1024]{1,0:T(8,128)(2,1)S(1)}, bf16[128,1024]{1,0:T(8,128)(2,1)}, u32[]{:S(2)}, u32[]{:S(2)}) collective-permute-start(bf16[128,1024]{1,0:T(8,128)(2,1)S(1)} %convolution_convert_fusion), channel_id=1, source_target_pairs={{0,24},{4,28},{8,0},{12,4},{16,8},{20,12},{24,16},{28,20},{1,25},{... | collective-permute-start | bytes 786440 | tf_op jit(solution)/shard_map/ppermute | solution.py:25
  27.8 1.7 dynamic-slice_bitcast_fusion
  29.5 1.6 pad_maximum_fusion
  31.1 2.5 %dynamic-slice_bitcast_fusion.14 = (bf16[1,512,256]{2,1,0:T(8,128)(2,1)S(1)}, bf16[1,512,256]{2,1,0:T(8,128)(2,1)S(1)}, bf16[1,512,256]{2,1,0:T(8,128)(2,1)S(1)}...) fusion(bf16[512,4096]{1,0:T(8,128)(2,1)} %v0_ref.3, ...), kind=kLoop, calls=%fused_computation.64 | loop fusion | bytes 8388640 | tf_op jit(solution)/shard_map/stack | solution.py:274
  40.1 4.9 %collective-permute-done.3 = bf16[128,1024]{1,0:T(8,128)(2,1)} collective-permute-done((bf16[128,1024]{1,0:T(8,128)(2,1)S(1)}, bf16[128,1024]{1,0:T(8,128)(2,1)}, u32[]{:S(2)}, u32[]{:S(2)}) %collective-permute-start.3) | collective-permute-done | bytes 262176 | tf_op jit(solution)/shard_map/ppermute | solution.py:25
  51.1 3.6 %collective-permute-done.14 = bf16[128,1024]{1,0:T(8,128)(2,1)} collective-permute-done((bf16[128,1024]{1,0:T(8,128)(2,1)}, bf16[128,1024]{1,0:T(8,128)(2,1)}, u32[]{:S(2)}, u32[]{:S(2)}) %collective-permute-start.14) | collective-permute-done | bytes 262176 | tf_op jit(solution)/shard_map/ppermute | solution.py:20
  54.6 2.4 %collective-permute-start.21 = (bf16[128,1024]{1,0:T(8,128)(2,1)}, bf16[128,1024]{1,0:T(8,128)(2,1)S(1)}, u32[]{:S(2)}, u32[]{:S(2)}) collective-permute-start(bf16[128,1024]{1,0:T(8,128)(2,1)} %param.13), channel_id=1, source_target_pairs={{0,4},{4,8},{8,12},{12,16},{16,20},{20,24},{24,28},{1,5},{5,9},{9,... | collective-permute-start | bytes 786440 | tf_op jit(solution)/shard_map/ppermute | solution.py:31
  58.0 1.7 collective-permute-done.15
  59.8 7.1 %collective-permute-start.22 = (bf16[128,1024]{1,0:T(8,128)(2,1)}, bf16[128,1024]{1,0:T(8,128)(2,1)}, u32[]{:S(2)}, u32[]{:S(2)}) collective-permute-start(bf16[128,1024]{1,0:T(8,128)(2,1)} %param.12), channel_id=1, source_target_pairs={{0,4},{4,8},{8,12},{12,16},{16,20},{20,24},{24,28},{1,5},{5,9},{9,... | collective-permute-start | bytes 786440 | tf_op jit(solution)/shard_map/ppermute | solution.py:31
  69.3 2.1 copy.17
  71.3 1.9 pad_maximum_fusion.5
  73.2 2.0 copy.19
  75.2 1.7 fusion
  78.9 1.5 collective-permute-start.23
  80.4 1.5 collective-permute-start.24
  81.9 2.4 %collective-permute-done.6.k2_ref.v2_ref = bf16[2,512,256]{2,1,0:T(8,128)(2,1)} collective-permute-done((bf16[2,512,256]{2,1,0:T(8,128)(2,1)}, bf16[2,512,256]{2,1,0:T(8,128)(2,1)}, u32[]{:S(2)}, u32[]{:S(2)}) %collective-permute-start.6) | collective-permute-done | bytes 524320 | tf_op jit(solution)/shard_map/ppermute | solution.py:20
  85.7 10.5 %near_tiles.3 = (f32[1024,512]{1,0:T(8,128)S(1)}, f32[8,8,512]{2,1,0:T(8,128)S(1)}) custom-call(s32[1]{0:T(128)} %bitcast.12.m_ref, bf16[512,1024]{1,0:T(8,128)(2,1)S(1)} %constant_dynamic-update-slice_fusion.q_ref, bf16[512,4096]{1,0:T(8,128)(2,1)} %k0_ref.3, bf16[512,4096]{1,0:T(8,128)(2,1)} %v0_ref.3, ...), custom_call_target="tpu_custom_call" | custom-call | flops 2147483648 | bytes 8388608 | tf_op jit(solution)/shard_map/near_tiles/pallas_call | solution.py:334
  96.2 2.4 %far_tiles.15 = bf16[4,272,128]{2,1,0:T(8,128)(2,1)S(1)} custom-call(bf16[512,1024]{1,0:T(8,128)(2,1)S(1)} %constant_dynamic-update-slice_fusion.q_ref, bf16[2,512,256]{2,1,0:T(8,128)(2,1)S(1)} %collective-permute-done.35.k2_ref.v2_ref, bf16[2,512,256]{2,1,0:T(8,128)(2,1)S(1)} %collective-permute-done.35.k2_ref.v2_ref, ...), custom_call_target="tpu_custom_call" | custom-call | flops 536870912 | bytes 3145728 | tf_op jit(solution)/shard_map/far_tiles/pallas_call | solution.py:378
  98.7 1.6 collective-permute-start.37
  100.3 4.3 %far_tiles.9 = bf16[4,272,128]{2,1,0:T(8,128)(2,1)} custom-call(bf16[512,1024]{1,0:T(8,128)(2,1)S(1)} %constant_dynamic-update-slice_fusion.q_ref, bf16[2,512,256]{2,1,0:T(8,128)(2,1)} %collective-permute-done.6.k2_ref.v2_ref, bf16[2,512,256]{2,1,0:T(8,128)(2,1)} %collective-permute-done.6.k2_ref.v2_ref, ...), custom_call_target="tpu_custom_call" | custom-call | flops 536870912 | bytes 3145728 | tf_op jit(solution)/shard_map/far_tiles/pallas_call | solution.py:378
  104.6 2.1 collective-permute-done.23.k2_ref.v2_ref
  106.7 1.5 collective-permute-start.17
  108.2 7.8 %collective-permute-done.24.k3_ref.v3_ref = bf16[2,512,256]{2,1,0:T(8,128)(2,1)S(1)} collective-permute-done((bf16[2,512,256]{2,1,0:T(8,128)(2,1)S(1)}, bf16[2,512,256]{2,1,0:T(8,128)(2,1)S(1)}, u32[]{:S(2)}, u32[]{:S(2)}) %collective-permute-start.24) | collective-permute-done | bytes 524320 | tf_op jit(solution)/shard_map/ppermute | solution.py:20
  116.0 3.2 %far_tiles.11 = bf16[4,272,128]{2,1,0:T(8,128)(2,1)} custom-call(bf16[512,1024]{1,0:T(8,128)(2,1)S(1)} %constant_dynamic-update-slice_fusion.q_ref, bf16[2,512,256]{2,1,0:T(8,128)(2,1)S(1)} %collective-permute-done.23.k2_ref.v2_ref, bf16[2,512,256]{2,1,0:T(8,128)(2,1)S(1)} %collective-permute-done.23.k2_ref.v2_ref, ...), custom_call_target="tpu_custom_call" | custom-call | flops 536870912 | bytes 3145728 | tf_op jit(solution)/shard_map/far_tiles/pallas_call | solution.py:378
  119.2 1.5 collective-permute-start.25
  120.7 8.5 %collective-permute-done.29.k2_ref.v2_ref = bf16[2,512,256]{2,1,0:T(8,128)(2,1)S(1)} collective-permute-done((bf16[2,512,256]{2,1,0:T(8,128)(2,1)S(1)}, bf16[2,512,256]{2,1,0:T(8,128)(2,1)S(1)}, u32[]{:S(2)}, u32[]{:S(2)}) %collective-permute-start.29) | collective-permute-done | bytes 524320 | tf_op jit(solution)/shard_map/ppermute | solution.py:20
  129.2 7.2 %collective-permute-done.30.k3_ref.v3_ref = bf16[2,512,256]{2,1,0:T(8,128)(2,1)S(1)} collective-permute-done((bf16[2,512,256]{2,1,0:T(8,128)(2,1)S(1)}, bf16[2,512,256]{2,1,0:T(8,128)(2,1)S(1)}, u32[]{:S(2)}, u32[]{:S(2)}) %collective-permute-start.30) | collective-permute-done | bytes 524320 | tf_op jit(solution)/shard_map/ppermute | solution.py:20
  136.4 2.5 %far_tiles.13 = bf16[4,272,128]{2,1,0:T(8,128)(2,1)S(1)} custom-call(bf16[512,1024]{1,0:T(8,128)(2,1)S(1)} %constant_dynamic-update-slice_fusion.q_ref, bf16[2,512,256]{2,1,0:T(8,128)(2,1)S(1)} %collective-permute-done.29.k2_ref.v2_ref, bf16[2,512,256]{2,1,0:T(8,128)(2,1)S(1)} %collective-permute-done.29.k2_ref.v2_ref, ...), custom_call_target="tpu_custom_call" | custom-call | flops 536870912 | bytes 3145728 | tf_op jit(solution)/shard_map/far_tiles/pallas_call | solution.py:378
  138.9 1.6 collective-permute-start.31
  140.5 10.8 %near_tiles.2 = (f32[1024,512]{1,0:T(8,128)S(1)}, f32[8,8,512]{2,1,0:T(8,128)S(1)}) custom-call(s32[1]{0:T(128)} %bitcast.12.m_ref, bf16[512,1024]{1,0:T(8,128)(2,1)S(1)} %pad_maximum_fusion.1.q_ref, bf16[512,4096]{1,0:T(8,128)(2,1)} %k0_ref.3, bf16[512,4096]{1,0:T(8,128)(2,1)} %v0_ref.3, bf16[2,512,1024]{2,1,0:T(8,128)(2,1)} %collective-permute-done.12.k1_ref.v1_ref, ...), custom_call_target="tpu_custom_call" | custom-call | flops 2147483648 | bytes 8388608 | tf_op jit(solution)/shard_map/near_tiles/pallas_call | solution.py:334
  151.4 2.5 %far_tiles.14.a_ref = bf16[4,272,128]{2,1,0:T(8,128)(2,1)S(1)} custom-call(bf16[512,1024]{1,0:T(8,128)(2,1)S(1)} %pad_maximum_fusion.1.q_ref, bf16[2,512,256]{2,1,0:T(8,128)(2,1)S(1)} %copy-done.1, bf16[2,512,256]{2,1,0:T(8,128)(2,1)S(1)} %copy-done.1, bf16[2,512,256]{2,1,0:T(8,128)(2,1)S(1)} %copy-done.3, bf16[2,512,256]{2,1,0:T(8,128)(2,1)S(1)} %copy-done.3, ...), custom_call_target="tpu_custom_call" | custom-call | flops 536870912 | bytes 3145728 | tf_op jit(solution)/shard_map/far_tiles/pallas_call | solution.py:378
  154.5 3.6 %far_tiles.8.a_ref = bf16[4,272,128]{2,1,0:T(8,128)(2,1)S(1)} custom-call(bf16[512,1024]{1,0:T(8,128)(2,1)S(1)} %pad_maximum_fusion.1.q_ref, bf16[2,512,256]{2,1,0:T(8,128)(2,1)} %collective-permute-done.6.k2_ref.v2_ref, bf16[2,512,256]{2,1,0:T(8,128)(2,1)} %collective-permute-done.6.k2_ref.v2_ref, ...), custom_call_target="tpu_custom_call" | custom-call | flops 536870912 | bytes 3145728 | tf_op jit(solution)/shard_map/far_tiles/pallas_call | solution.py:378
  158.8 1.9 merge_pair.7
  160.7 7.1 %collective-permute-start.39 = (bf16[272,128]{1,0:T(8,128)(2,1)}, bf16[272,128]{1,0:T(8,128)(2,1)}, u32[]{:S(2)}, u32[]{:S(2)}) collective-permute-start(bf16[272,128]{1,0:T(8,128)(2,1)} %get-tuple-element.53), channel_id=1, source_target_pairs={{0,16},{4,20},{8,24},{12,28},{16,0},{20,4},{24,8},{28,12},{1,17},{... | collective-permute-start | bytes 208904 | tf_op jit(solution)/shard_map/ppermute | solution.py:25
  167.8 2.0 collective-permute-start.40
  172.6 2.5 %far_tiles.10.a_ref = bf16[4,272,128]{2,1,0:T(8,128)(2,1)S(1)} custom-call(bf16[512,1024]{1,0:T(8,128)(2,1)S(1)} %pad_maximum_fusion.1.q_ref, bf16[2,512,256]{2,1,0:T(8,128)(2,1)S(1)} %copy-done.5, bf16[2,512,256]{2,1,0:T(8,128)(2,1)S(1)} %copy-done.5, bf16[2,512,256]{2,1,0:T(8,128)(2,1)S(1)} %copy-done.7, bf16[2,512,256]{2,1,0:T(8,128)(2,1)S(1)} %copy-done.7, ...), custom_call_target="tpu_custom_call" | custom-call | flops 536870912 | bytes 3145728 | tf_op jit(solution)/shard_map/far_tiles/pallas_call | solution.py:378
  175.7 2.4 %far_tiles.12.a_ref = bf16[4,272,128]{2,1,0:T(8,128)(2,1)S(1)} custom-call(bf16[512,1024]{1,0:T(8,128)(2,1)S(1)} %pad_maximum_fusion.1.q_ref, bf16[2,512,256]{2,1,0:T(8,128)(2,1)S(1)} %copy-done.9, bf16[2,512,256]{2,1,0:T(8,128)(2,1)S(1)} %copy-done.9, bf16[2,512,256]{2,1,0:T(8,128)(2,1)S(1)} %copy-done.11, bf16[2,512,256]{2,1,0:T(8,128)(2,1)S(1)} %copy-done.11, ...), custom_call_target="tpu_custom_call" | custom-call | flops 536870912 | bytes 3145728 | tf_op jit(solution)/shard_map/far_tiles/pallas_call | solution.py:378
  178.9 1.9 merge_pair.4
  180.7 2.1 collective-permute-start.18
  182.8 1.9 merge_pair.5
  184.8 1.8 merge_pair.6
  187.2 3.3 %collective-permute-start.26 = (bf16[272,128]{1,0:T(8,128)(2,1)}, bf16[272,128]{1,0:T(8,128)(2,1)S(1)}, u32[]{:S(2)}, u32[]{:S(2)}) collective-permute-start(bf16[272,128]{1,0:T(8,128)(2,1)} %get-tuple-element.44), channel_id=1, source_target_pairs={{0,24},{4,28},{8,0},{12,4},{16,8},{20,12},{24,16},{28,20},{1,25},{... | collective-permute-start | bytes 208904 | tf_op jit(solution)/shard_map/ppermute | solution.py:25
  191.6 1.3 broadcast_in_dim.48.refs_5_
  192.9 1.7 merge_all.7
  194.6 1.3 fusion.49
  196.3 3.6 %collective-permute-start.32 = (bf16[272,128]{1,0:T(8,128)(2,1)}, bf16[272,128]{1,0:T(8,128)(2,1)S(1)}, u32[]{:S(2)}, u32[]{:S(2)}) collective-permute-start(bf16[272,128]{1,0:T(8,128)(2,1)} %get-tuple-element.48), channel_id=1, source_target_pairs={{0,24},{4,28},{8,0},{12,4},{16,8},{20,12},{24,16},{28,20},{1,25},{... | collective-permute-start | bytes 208904 | tf_op jit(solution)/shard_map/ppermute | solution.py:25
  200.5 1.3 fusion.53
  202.5 1.8 merge_all.4
  205.0 1.8 merge_all.5
  208.1 1.8 merge_all.6
  209.8 2.0 fusion.38
  211.9 1.8 fusion.41
  214.3 1.3 fusion.51
  215.6 1.8 fusion.35
  218.4 1.3 fusion.55
  219.7 6.0 %collective-permute-done.43 = bf16[128,1024]{1,0:T(8,128)(2,1)S(1)} collective-permute-done((bf16[128,1024]{1,0:T(8,128)(2,1)S(1)}, bf16[128,1024]{1,0:T(8,128)(2,1)S(1)}, u32[]{:S(2)}, u32[]{:S(2)}) %collective-permute-start.43) | collective-permute-done | bytes 262176 | tf_op jit(solution)/shard_map/ppermute | solution.py:20
  225.7 2.5 %fusion.32 = bf16[128,1024]{1,0:T(8,128)(2,1)} fusion(f32[128,1024]{1,0:T(8,128)S(1)} %fusion.55, bf16[1024,4096]{1,0:T(8,128)(2,1)} %param.19, s32[]{:T(128)S(6)} %select_n.79, bf16[128,1024]{1,0:T(8,128)(2,1)S(1)} %collective-permute-done.43, bf16[128,1024]{1,0:T(8,128)(2,1)S(1)} %collective-permute-done.41, bf16[256,128]{1,0:T(8,128)(2,1)S(1)} %copy-done.21, ...), kind=kOutput, calls=%fused_computation.22 | convolution fusion | flops 202702848 | bytes 3080196 | tf_op jit(solution)/shard_map/dot_general | solution.py:423
  (178 shorter events, 38.5 us)
Async XLA Ops:
  0.0 15.6 %collective-permute-start.1 = (bf16[128,1024]{1,0:T(8,128)(2,1)}, bf16[128,1024]{1,0:T(8,128)(2,1)S(1)}, u32[]{:S(2)}, u32[]{:S(2)}) collective-permute-start(bf16[128,1024]{1,0:T(8,128)(2,1)} %param.10), channel_id=1, source_target_pairs={{0,2},{1,3},{2,0},{3,1},{4,6},{5,7},{6,4},{7,5},{8,10},{9,11},{10,... | collective-permute-start | bytes 786440 | tf_op jit(solution)/shard_map/ppermute | solution.py:20
  2.9 13.2 %collective-permute-start = (bf16[128,1024]{1,0:T(8,128)(2,1)}, bf16[128,1024]{1,0:T(8,128)(2,1)S(1)}, u32[]{:S(2)}, u32[]{:S(2)}) collective-permute-start(bf16[128,1024]{1,0:T(8,128)(2,1)} %param.10), channel_id=1, source_target_pairs={{0,1},{1,0},{2,3},{3,2},{4,5},{5,4},{6,7},{7,6},{8,9},{9,8},{10,11... | collective-permute-start | bytes 786440 | tf_op jit(solution)/shard_map/ppermute | solution.py:20
  3.6 3.7 %collective-permute-start.8 = (s32[16,128]{1,0:T(8,128)S(1)}, s32[16,128]{1,0:T(8,128)S(1)}, u32[]{:S(2)}, u32[]{:S(2)}) collective-permute-start(s32[16,128]{1,0:T(8,128)S(1)} %get-tuple-element.78), channel_id=1, source_target_pairs={{0,4},{4,0},{8,12},{12,8},{16,20},{20,16},{24,28},{28,24},{1,5},{5... | collective-permute-start | bytes 24584 | tf_op jit(solution)/shard_map/ppermute | solution.py:20
  7.3 7.5 %collective-permute-start.10 = (s32[2,16,128]{2,1,0:T(8,128)S(1)}, s32[2,16,128]{2,1,0:T(8,128)S(1)}, u32[]{:S(2)}, u32[]{:S(2)}) collective-permute-start(s32[2,16,128]{2,1,0:T(8,128)S(1)} %get-tuple-element.76), channel_id=1, source_target_pairs={{0,16},{4,20},{8,24},{12,28},{16,0},{20,4},{24,8},{28,12},{1,17},{... | collective-permute-start | bytes 49160 | tf_op jit(solution)/shard_map/ppermute | solution.py:25
  9.9 5.5 %collective-permute-start.9 = (s32[2,16,128]{2,1,0:T(8,128)S(1)}, s32[2,16,128]{2,1,0:T(8,128)S(1)}, u32[]{:S(2)}, u32[]{:S(2)}) collective-permute-start(s32[2,16,128]{2,1,0:T(8,128)S(1)} %get-tuple-element.76), channel_id=1, source_target_pairs={{0,8},{4,12},{8,16},{12,20},{16,24},{20,28},{24,0},{28,4},{1,9},{5... | collective-permute-start | bytes 49160 | tf_op jit(solution)/shard_map/ppermute | solution.py:25
  11.5 4.0 %collective-permute-start.11 = (s32[2,16,128]{2,1,0:T(8,128)S(1)}, s32[2,16,128]{2,1,0:T(8,128)S(1)}, u32[]{:S(2)}, u32[]{:S(2)}) collective-permute-start(s32[2,16,128]{2,1,0:T(8,128)S(1)} %get-tuple-element.76), channel_id=1, source_target_pairs={{0,24},{4,28},{8,0},{12,4},{16,8},{20,12},{24,16},{28,20},{1,25},{... | collective-permute-start | bytes 49160 | tf_op jit(solution)/shard_map/ppermute | solution.py:25
  15.6 1.6 collective-permute-start.2
  21.8 24.7 %collective-permute-start.13 = (bf16[128,1024]{1,0:T(8,128)(2,1)S(1)}, bf16[128,1024]{1,0:T(8,128)(2,1)S(1)}, u32[]{:S(2)}, u32[]{:S(2)}) collective-permute-start(bf16[128,1024]{1,0:T(8,128)(2,1)S(1)} %convolution_convert_fusion), channel_id=1, source_target_pairs={{0,4},{4,0},{8,12},{12,8},{16,20},{20,16},{24,28},{28,24},{1,5},{5... | collective-permute-start | bytes 786440 | tf_op jit(solution)/shard_map/ppermute | solution.py:20
  23.4 16.2 %collective-permute-start.5 = (bf16[128,1024]{1,0:T(8,128)(2,1)S(1)}, bf16[128,1024]{1,0:T(8,128)(2,1)}, u32[]{:S(2)}, u32[]{:S(2)}) collective-permute-start(bf16[128,1024]{1,0:T(8,128)(2,1)S(1)} %convolution_convert_fusion), channel_id=1, source_target_pairs={{0,24},{4,28},{8,0},{12,4},{16,8},{20,12},{24,16},{28,20},{1,25},{... | collective-permute-start | bytes 786440 | tf_op jit(solution)/shard_map/ppermute | solution.py:25
  27.3 20.5 %collective-permute-start.4 = (bf16[128,1024]{1,0:T(8,128)(2,1)S(1)}, bf16[128,1024]{1,0:T(8,128)(2,1)}, u32[]{:S(2)}, u32[]{:S(2)}) collective-permute-start(bf16[128,1024]{1,0:T(8,128)(2,1)S(1)} %convolution_convert_fusion), channel_id=1, source_target_pairs={{0,16},{4,20},{8,24},{12,28},{16,0},{20,4},{24,8},{28,12},{1,17},{... | collective-permute-start | bytes 786440 | tf_op jit(solution)/shard_map/ppermute | solution.py:25
  27.3 17.8 %collective-permute-start.3 = (bf16[128,1024]{1,0:T(8,128)(2,1)S(1)}, bf16[128,1024]{1,0:T(8,128)(2,1)}, u32[]{:S(2)}, u32[]{:S(2)}) collective-permute-start(bf16[128,1024]{1,0:T(8,128)(2,1)S(1)} %convolution_convert_fusion), channel_id=1, source_target_pairs={{0,8},{4,12},{8,16},{12,20},{16,24},{20,28},{24,0},{28,4},{1,9},{5... | collective-permute-start | bytes 786440 | tf_op jit(solution)/shard_map/ppermute | solution.py:25
  31.1 53.8 %collective-permute-start.12 = (bf16[2,512,1024]{2,1,0:T(8,128)(2,1)}, bf16[2,512,1024]{2,1,0:T(8,128)(2,1)}, u32[]{:S(2)}, u32[]{:S(2)}) collective-permute-start(bf16[2,512,1024]{2,1,0:T(8,128)(2,1)} %pad_maximum_fusion), channel_id=1, source_target_pairs={{0,1},{1,0},{2,3},{3,2},{4,5},{5,4},{6,7},{7,6},{8,9},{9,8},{10,11... | collective-permute-start | bytes 6291464 | tf_op jit(solution)/shard_map/ppermute | solution.py:20
  39.6 11.4 %collective-permute-start.16 = (bf16[128,1024]{1,0:T(8,128)(2,1)}, bf16[128,1024]{1,0:T(8,128)(2,1)}, u32[]{:S(2)}, u32[]{:S(2)}) collective-permute-start(bf16[128,1024]{1,0:T(8,128)(2,1)} %collective-permute-done.5), channel_id=1, source_target_pairs={{0,4},{4,0},{8,12},{12,8},{16,20},{20,16},{24,28},{28,24},{1,5},{5... | collective-permute-start | bytes 786440 | tf_op jit(solution)/shard_map/ppermute | solution.py:20
  45.0 9.6 %collective-permute-start.14 = (bf16[128,1024]{1,0:T(8,128)(2,1)}, bf16[128,1024]{1,0:T(8,128)(2,1)}, u32[]{:S(2)}, u32[]{:S(2)}) collective-permute-start(bf16[128,1024]{1,0:T(8,128)(2,1)} %collective-permute-done.3), channel_id=1, source_target_pairs={{0,4},{4,0},{8,12},{12,8},{16,20},{20,16},{24,28},{28,24},{1,5},{5... | collective-permute-start | bytes 786440 | tf_op jit(solution)/shard_map/ppermute | solution.py:20
  46.6 21.9 %copy-start.28 = (bf16[128,1024]{1,0:T(8,128)(2,1)S(1)}, bf16[128,1024]{1,0:T(8,128)(2,1)}, u32[]{:S(2)}) copy-start(bf16[128,1024]{1,0:T(8,128)(2,1)} %param.13) | copy-start | bytes 786436
  46.6 31.9 %collective-permute-start.35 = (bf16[2,512,256]{2,1,0:T(8,128)(2,1)}, bf16[2,512,256]{2,1,0:T(8,128)(2,1)S(1)}, u32[]{:S(2)}, u32[]{:S(2)}) collective-permute-start(bf16[2,512,256]{2,1,0:T(8,128)(2,1)} %pad_maximum_fusion.10), channel_id=1, source_target_pairs={{0,2},{1,3},{2,0},{3,1},{4,6},{5,7},{6,4},{7,5},{8,10},{9,11},{10,... | collective-permute-start | bytes 1572872 | tf_op jit(solution)/shard_map/ppermute | solution.py:20
  47.7 12.0 %collective-permute-start.15 = (bf16[128,1024]{1,0:T(8,128)(2,1)}, bf16[128,1024]{1,0:T(8,128)(2,1)S(1)}, u32[]{:S(2)}, u32[]{:S(2)}) collective-permute-start(bf16[128,1024]{1,0:T(8,128)(2,1)} %collective-permute-done.4), channel_id=1, source_target_pairs={{0,4},{4,0},{8,12},{12,8},{16,20},{20,16},{24,28},{28,24},{1,5},{5... | collective-permute-start | bytes 786440 | tf_op jit(solution)/shard_map/ppermute | solution.py:20
  51.0 29.4 %collective-permute-start.36 = (bf16[2,512,256]{2,1,0:T(8,128)(2,1)}, bf16[2,512,256]{2,1,0:T(8,128)(2,1)S(1)}, u32[]{:S(2)}, u32[]{:S(2)}) collective-permute-start(bf16[2,512,256]{2,1,0:T(8,128)(2,1)} %pad_maximum_fusion.11), channel_id=1, source_target_pairs={{0,3},{1,2},{2,1},{3,0},{4,7},{5,6},{6,5},{7,4},{8,11},{9,10},{10,... | collective-permute-start | bytes 1572872 | tf_op jit(solution)/shard_map/ppermute | solution.py:20
  54.6 13.2 %collective-permute-start.21 = (bf16[128,1024]{1,0:T(8,128)(2,1)}, bf16[128,1024]{1,0:T(8,128)(2,1)S(1)}, u32[]{:S(2)}, u32[]{:S(2)}) collective-permute-start(bf16[128,1024]{1,0:T(8,128)(2,1)} %param.13), channel_id=1, source_target_pairs={{0,4},{4,8},{8,12},{12,16},{16,20},{20,24},{24,28},{1,5},{5,9},{9,... | collective-permute-start | bytes 786440 | tf_op jit(solution)/shard_map/ppermute | solution.py:31
  59.8 11.6 %collective-permute-start.22 = (bf16[128,1024]{1,0:T(8,128)(2,1)}, bf16[128,1024]{1,0:T(8,128)(2,1)}, u32[]{:S(2)}, u32[]{:S(2)}) collective-permute-start(bf16[128,1024]{1,0:T(8,128)(2,1)} %param.12), channel_id=1, source_target_pairs={{0,4},{4,8},{8,12},{12,16},{16,20},{20,24},{24,28},{1,5},{5,9},{9,... | collective-permute-start | bytes 786440 | tf_op jit(solution)/shard_map/ppermute | solution.py:31
  67.8 16.5 %collective-permute-start.6 = (bf16[2,512,256]{2,1,0:T(8,128)(2,1)}, bf16[2,512,256]{2,1,0:T(8,128)(2,1)}, u32[]{:S(2)}, u32[]{:S(2)}) collective-permute-start(bf16[2,512,256]{2,1,0:T(8,128)(2,1)} %pad_maximum_fusion.2), channel_id=1, source_target_pairs={{0,2},{1,3},{2,0},{3,1},{4,6},{5,7},{6,4},{7,5},{8,10},{9,11},{10,... | collective-permute-start | bytes 1572872 | tf_op jit(solution)/shard_map/ppermute | solution.py:20
  71.3 27.3 %collective-permute-start.7 = (bf16[2,512,256]{2,1,0:T(8,128)(2,1)}, bf16[2,512,256]{2,1,0:T(8,128)(2,1)}, u32[]{:S(2)}, u32[]{:S(2)}) collective-permute-start(bf16[2,512,256]{2,1,0:T(8,128)(2,1)} %pad_maximum_fusion.3), channel_id=1, source_target_pairs={{0,3},{1,2},{2,1},{3,0},{4,7},{5,6},{6,5},{7,4},{8,11},{9,10},{10,... | collective-permute-start | bytes 1572872 | tf_op jit(solution)/shard_map/ppermute | solution.py:20
  77.8 6.5 %copy-start.23 = (bf16[2,512,256]{2,1,0:T(8,128)(2,1)S(1)}, bf16[2,512,256]{2,1,0:T(8,128)(2,1)}, u32[]{:S(2)}) copy-start(bf16[2,512,256]{2,1,0:T(8,128)(2,1)} %pad_maximum_fusion.8) | copy-start | bytes 1572868
  77.9 7.0 %copy-start.22 = (bf16[2,512,256]{2,1,0:T(8,128)(2,1)S(1)}, bf16[2,512,256]{2,1,0:T(8,128)(2,1)}, u32[]{:S(2)}) copy-start(bf16[2,512,256]{2,1,0:T(8,128)(2,1)} %pad_maximum_fusion.9) | copy-start | bytes 1572868
  78.9 17.3 %copy-start = (bf16[2,512,256]{2,1,0:T(8,128)(2,1)}, bf16[2,512,256]{2,1,0:T(8,128)(2,1)S(1)}, u32[]{:S(2)}) copy-start(bf16[2,512,256]{2,1,0:T(8,128)(2,1)S(1)} %collective-permute-done.35.k2_ref.v2_ref) | copy-start | bytes 1572868
  78.9 27.8 %collective-permute-start.23 = (bf16[2,512,256]{2,1,0:T(8,128)(2,1)S(1)}, bf16[2,512,256]{2,1,0:T(8,128)(2,1)S(1)}, u32[]{:S(2)}, u32[]{:S(2)}) collective-permute-start(bf16[2,512,256]{2,1,0:T(8,128)(2,1)S(1)} %copy-done.25), channel_id=1, source_target_pairs={{0,2},{1,3},{2,0},{3,1},{4,6},{5,7},{6,4},{7,5},{8,10},{9,11},{10,... | collective-permute-start | bytes 1572872 | tf_op jit(solution)/shard_map/ppermute | solution.py:20
  80.4 15.8 %copy-start.2 = (bf16[2,512,256]{2,1,0:T(8,128)(2,1)}, bf16[2,512,256]{2,1,0:T(8,128)(2,1)S(1)}, u32[]{:S(2)}) copy-start(bf16[2,512,256]{2,1,0:T(8,128)(2,1)S(1)} %collective-permute-done.36.k3_ref.v3_ref) | copy-start | bytes 1572868
  80.4 35.6 %collective-permute-start.24 = (bf16[2,512,256]{2,1,0:T(8,128)(2,1)S(1)}, bf16[2,512,256]{2,1,0:T(8,128)(2,1)S(1)}, u32[]{:S(2)}, u32[]{:S(2)}) collective-permute-start(bf16[2,512,256]{2,1,0:T(8,128)(2,1)S(1)} %copy-done.24), channel_id=1, source_target_pairs={{0,3},{1,2},{2,1},{3,0},{4,7},{5,6},{6,5},{7,4},{8,11},{9,10},{10,... | collective-permute-start | bytes 1572872 | tf_op jit(solution)/shard_map/ppermute | solution.py:20
  84.3 44.8 %collective-permute-start.29 = (bf16[2,512,256]{2,1,0:T(8,128)(2,1)S(1)}, bf16[2,512,256]{2,1,0:T(8,128)(2,1)S(1)}, u32[]{:S(2)}, u32[]{:S(2)}) collective-permute-start(bf16[2,512,256]{2,1,0:T(8,128)(2,1)S(1)} %copy-done.23), channel_id=1, source_target_pairs={{0,2},{1,3},{2,0},{3,1},{4,6},{5,7},{6,4},{7,5},{8,10},{9,11},{10,... | collective-permute-start | bytes 1572872 | tf_op jit(solution)/shard_map/ppermute | solution.py:20
  84.9 51.5 %collective-permute-start.30 = (bf16[2,512,256]{2,1,0:T(8,128)(2,1)S(1)}, bf16[2,512,256]{2,1,0:T(8,128)(2,1)S(1)}, u32[]{:S(2)}, u32[]{:S(2)}) collective-permute-start(bf16[2,512,256]{2,1,0:T(8,128)(2,1)S(1)} %copy-done.22), channel_id=1, source_target_pairs={{0,3},{1,2},{2,1},{3,0},{4,7},{5,6},{6,5},{7,4},{8,11},{9,10},{10,... | collective-permute-start | bytes 1572872 | tf_op jit(solution)/shard_map/ppermute | solution.py:20
  98.7 60.2 %collective-permute-start.37 = (bf16[4,272,128]{2,1,0:T(8,128)(2,1)S(1)}, bf16[4,272,128]{2,1,0:T(8,128)(2,1)}, u32[]{:S(2)}, u32[]{:S(2)}) collective-permute-start(bf16[4,272,128]{2,1,0:T(8,128)(2,1)S(1)} %far_tiles.15), channel_id=1, source_target_pairs={{0,4},{4,0},{8,12},{12,8},{16,20},{20,16},{24,28},{28,24},{1,5},{5... | collective-permute-start | bytes 835592 | tf_op jit(solution)/shard_map/ppermute | solution.py:20
  106.7 12.5 %copy-start.4 = (bf16[2,512,256]{2,1,0:T(8,128)(2,1)}, bf16[2,512,256]{2,1,0:T(8,128)(2,1)S(1)}, u32[]{:S(2)}) copy-start(bf16[2,512,256]{2,1,0:T(8,128)(2,1)S(1)} %collective-permute-done.23.k2_ref.v2_ref) | copy-start | bytes 1572868
  106.7 61.1 %collective-permute-start.17 = (bf16[4,272,128]{2,1,0:T(8,128)(2,1)}, bf16[4,272,128]{2,1,0:T(8,128)(2,1)}, u32[]{:S(2)}, u32[]{:S(2)}) collective-permute-start(bf16[4,272,128]{2,1,0:T(8,128)(2,1)} %far_tiles.9), channel_id=1, source_target_pairs={{0,4},{4,0},{8,12},{12,8},{16,20},{20,16},{24,28},{28,24},{1,5},{5... | collective-permute-start | bytes 835592 | tf_op jit(solution)/shard_map/ppermute | solution.py:20
  119.2 21.3 %copy-start.16 = (s32[1,512]{1,0:T(1,128)S(1)}, s32[1,512]{1,0:T(1,128)}, u32[]{:S(2)}) copy-start(s32[1,512]{1,0:T(1,128)} %get-tuple-element.80.bits_ref) | copy-start | bytes 6148
  119.2 61.6 %collective-permute-start.25 = (bf16[4,272,128]{2,1,0:T(8,128)(2,1)}, bf16[4,272,128]{2,1,0:T(8,128)(2,1)}, u32[]{:S(2)}, u32[]{:S(2)}) collective-permute-start(bf16[4,272,128]{2,1,0:T(8,128)(2,1)} %far_tiles.11), channel_id=1, source_target_pairs={{0,4},{4,0},{8,12},{12,8},{16,20},{20,16},{24,28},{28,24},{1,5},{5... | collective-permute-start | bytes 835592 | tf_op jit(solution)/shard_map/ppermute | solution.py:20
  129.2 9.7 %copy-start.8 = (bf16[2,512,256]{2,1,0:T(8,128)(2,1)}, bf16[2,512,256]{2,1,0:T(8,128)(2,1)S(1)}, u32[]{:S(2)}) copy-start(bf16[2,512,256]{2,1,0:T(8,128)(2,1)S(1)} %collective-permute-done.29.k2_ref.v2_ref) | copy-start | bytes 1572868
  138.9 45.8 %collective-permute-start.31 = (bf16[4,272,128]{2,1,0:T(8,128)(2,1)S(1)}, bf16[4,272,128]{2,1,0:T(8,128)(2,1)}, u32[]{:S(2)}, u32[]{:S(2)}) collective-permute-start(bf16[4,272,128]{2,1,0:T(8,128)(2,1)S(1)} %far_tiles.13), channel_id=1, source_target_pairs={{0,4},{4,0},{8,12},{12,8},{16,20},{20,16},{24,28},{28,24},{1,5},{5... | collective-permute-start | bytes 835592 | tf_op jit(solution)/shard_map/ppermute | solution.py:20
  140.5 10.9 %copy-start.1 = (bf16[2,512,256]{2,1,0:T(8,128)(2,1)S(1)}, bf16[2,512,256]{2,1,0:T(8,128)(2,1)}, u32[]{:S(2)}) copy-start(bf16[2,512,256]{2,1,0:T(8,128)(2,1)} %copy-done) | copy-start | bytes 1572868
  140.5 10.9 %copy-start.3 = (bf16[2,512,256]{2,1,0:T(8,128)(2,1)S(1)}, bf16[2,512,256]{2,1,0:T(8,128)(2,1)}, u32[]{:S(2)}) copy-start(bf16[2,512,256]{2,1,0:T(8,128)(2,1)} %copy-done.2) | copy-start | bytes 1572868
  160.7 25.9 %collective-permute-start.38 = (bf16[272,128]{1,0:T(8,128)(2,1)}, bf16[272,128]{1,0:T(8,128)(2,1)}, u32[]{:S(2)}, u32[]{:S(2)}) collective-permute-start(bf16[272,128]{1,0:T(8,128)(2,1)} %get-tuple-element.52), channel_id=1, source_target_pairs={{0,24},{4,28},{8,0},{12,4},{16,8},{20,12},{24,16},{28,20},{1,25},{... | collective-permute-start | bytes 208904 | tf_op jit(solution)/shard_map/ppermute | solution.py:25
  160.7 26.5 %collective-permute-start.39 = (bf16[272,128]{1,0:T(8,128)(2,1)}, bf16[272,128]{1,0:T(8,128)(2,1)}, u32[]{:S(2)}, u32[]{:S(2)}) collective-permute-start(bf16[272,128]{1,0:T(8,128)(2,1)} %get-tuple-element.53), channel_id=1, source_target_pairs={{0,16},{4,20},{8,24},{12,28},{16,0},{20,4},{24,8},{28,12},{1,17},{... | collective-permute-start | bytes 208904 | tf_op jit(solution)/shard_map/ppermute | solution.py:25
  167.8 22.7 %collective-permute-start.40 = (bf16[272,128]{1,0:T(8,128)(2,1)}, bf16[272,128]{1,0:T(8,128)(2,1)}, u32[]{:S(2)}, u32[]{:S(2)}) collective-permute-start(bf16[272,128]{1,0:T(8,128)(2,1)} %get-tuple-element.54), channel_id=1, source_target_pairs={{0,8},{4,12},{8,16},{12,20},{16,24},{20,28},{24,0},{28,4},{1,9},{5... | collective-permute-start | bytes 208904 | tf_op jit(solution)/shard_map/ppermute | solution.py:25
  178.9 23.0 %copy-start.40 = (f32[4]{0:T(128)S(1)}, f32[4]{0:T(128)}, u32[]{:S(2)}) copy-start(f32[4]{0:T(128)} %get-tuple-element.81) | copy-start | bytes 52
  180.7 23.6 %copy-start.39 = (f32[4]{0:T(128)S(1)}, f32[4]{0:T(128)}, u32[]{:S(2)}) copy-start(f32[4]{0:T(128)} %get-tuple-element.84) | copy-start | bytes 52
  180.7 15.2 %collective-permute-start.18 = (bf16[272,128]{1,0:T(8,128)(2,1)}, bf16[272,128]{1,0:T(8,128)(2,1)S(1)}, u32[]{:S(2)}, u32[]{:S(2)}) collective-permute-start(bf16[272,128]{1,0:T(8,128)(2,1)} %get-tuple-element.38), channel_id=1, source_target_pairs={{0,24},{4,28},{8,0},{12,4},{16,8},{20,12},{24,16},{28,20},{1,25},{... | collective-permute-start | bytes 208904 | tf_op jit(solution)/shard_map/ppermute | solution.py:25
  184.7 11.3 %copy-start.41 = (bf16[272,128]{1,0:T(8,128)(2,1)S(1)}, bf16[272,128]{1,0:T(8,128)(2,1)}, u32[]{:S(2)}) copy-start(bf16[272,128]{1,0:T(8,128)(2,1)} %get-tuple-element.46) | copy-start | bytes 208900
  184.7 22.7 %copy-start.38 = (f32[4]{0:T(128)S(1)}, f32[4]{0:T(128)}, u32[]{:S(2)}) copy-start(f32[4]{0:T(128)} %get-tuple-element.83) | copy-start | bytes 52
  184.7 11.6 %collective-permute-start.19 = (bf16[272,128]{1,0:T(8,128)(2,1)}, bf16[272,128]{1,0:T(8,128)(2,1)S(1)}, u32[]{:S(2)}, u32[]{:S(2)}) collective-permute-start(bf16[272,128]{1,0:T(8,128)(2,1)} %get-tuple-element.39), channel_id=1, source_target_pairs={{0,16},{4,20},{8,24},{12,28},{16,0},{20,4},{24,8},{28,12},{1,17},{... | collective-permute-start | bytes 208904 | tf_op jit(solution)/shard_map/ppermute | solution.py:25
  186.6 13.2 %collective-permute-start.20 = (bf16[272,128]{1,0:T(8,128)(2,1)}, bf16[272,128]{1,0:T(8,128)(2,1)S(1)}, u32[]{:S(2)}, u32[]{:S(2)}) collective-permute-start(bf16[272,128]{1,0:T(8,128)(2,1)} %get-tuple-element.40), channel_id=1, source_target_pairs={{0,8},{4,12},{8,16},{12,20},{16,24},{20,28},{24,0},{28,4},{1,9},{5... | collective-permute-start | bytes 208904 | tf_op jit(solution)/shard_map/ppermute | solution.py:25
  187.2 12.7 %collective-permute-start.26 = (bf16[272,128]{1,0:T(8,128)(2,1)}, bf16[272,128]{1,0:T(8,128)(2,1)S(1)}, u32[]{:S(2)}, u32[]{:S(2)}) collective-permute-start(bf16[272,128]{1,0:T(8,128)(2,1)} %get-tuple-element.44), channel_id=1, source_target_pairs={{0,24},{4,28},{8,0},{12,4},{16,8},{20,12},{24,16},{28,20},{1,25},{... | collective-permute-start | bytes 208904 | tf_op jit(solution)/shard_map/ppermute | solution.py:25
  190.5 13.8 %collective-permute-start.27 = (bf16[272,128]{1,0:T(8,128)(2,1)}, bf16[272,128]{1,0:T(8,128)(2,1)S(1)}, u32[]{:S(2)}, u32[]{:S(2)}) collective-permute-start(bf16[272,128]{1,0:T(8,128)(2,1)} %get-tuple-element.45), channel_id=1, source_target_pairs={{0,16},{4,20},{8,24},{12,28},{16,0},{20,4},{24,8},{28,12},{1,17},{... | collective-permute-start | bytes 208904 | tf_op jit(solution)/shard_map/ppermute | solution.py:25
  196.0 6.6 %copy-start.29 = (bf16[272,128]{1,0:T(8,128)(2,1)}, bf16[272,128]{1,0:T(8,128)(2,1)S(1)}, u32[]{:S(2)}) copy-start(bf16[272,128]{1,0:T(8,128)(2,1)S(1)} %collective-permute-done.18.refs_1_) | copy-start | bytes 208900
  196.0 8.3 %collective-permute-start.28 = (bf16[272,128]{1,0:T(8,128)(2,1)S(1)}, bf16[272,128]{1,0:T(8,128)(2,1)S(1)}, u32[]{:S(2)}, u32[]{:S(2)}) collective-permute-start(bf16[272,128]{1,0:T(8,128)(2,1)S(1)} %copy-done.41), channel_id=1, source_target_pairs={{0,8},{4,12},{8,16},{12,20},{16,24},{20,28},{24,0},{28,4},{1,9},{5... | collective-permute-start | bytes 208904 | tf_op jit(solution)/shard_map/ppermute | solution.py:25
  196.3 6.3 %copy-start.30 = (bf16[272,128]{1,0:T(8,128)(2,1)}, bf16[272,128]{1,0:T(8,128)(2,1)S(1)}, u32[]{:S(2)}) copy-start(bf16[272,128]{1,0:T(8,128)(2,1)S(1)} %collective-permute-done.19.refs_2_) | copy-start | bytes 208900
  196.3 10.5 %collective-permute-start.32 = (bf16[272,128]{1,0:T(8,128)(2,1)}, bf16[272,128]{1,0:T(8,128)(2,1)S(1)}, u32[]{:S(2)}, u32[]{:S(2)}) collective-permute-start(bf16[272,128]{1,0:T(8,128)(2,1)} %get-tuple-element.48), channel_id=1, source_target_pairs={{0,24},{4,28},{8,0},{12,4},{16,8},{20,12},{24,16},{28,20},{1,25},{... | collective-permute-start | bytes 208904 | tf_op jit(solution)/shard_map/ppermute | solution.py:25
  199.9 7.5 %collective-permute-start.33 = (bf16[272,128]{1,0:T(8,128)(2,1)}, bf16[272,128]{1,0:T(8,128)(2,1)S(1)}, u32[]{:S(2)}, u32[]{:S(2)}) collective-permute-start(bf16[272,128]{1,0:T(8,128)(2,1)} %get-tuple-element.49), channel_id=1, source_target_pairs={{0,16},{4,20},{8,24},{12,28},{16,0},{20,4},{24,8},{28,12},{1,17},{... | collective-permute-start | bytes 208904 | tf_op jit(solution)/shard_map/ppermute | solution.py:25
  199.9 5.1 %copy-start.31 = (bf16[272,128]{1,0:T(8,128)(2,1)}, bf16[272,128]{1,0:T(8,128)(2,1)S(1)}, u32[]{:S(2)}) copy-start(bf16[272,128]{1,0:T(8,128)(2,1)S(1)} %collective-permute-done.26.refs_1_) | copy-start | bytes 208900
  199.9 7.5 %collective-permute-start.34 = (bf16[272,128]{1,0:T(8,128)(2,1)}, bf16[272,128]{1,0:T(8,128)(2,1)S(1)}, u32[]{:S(2)}, u32[]{:S(2)}) collective-permute-start(bf16[272,128]{1,0:T(8,128)(2,1)} %get-tuple-element.50), channel_id=1, source_target_pairs={{0,8},{4,12},{8,16},{12,20},{16,24},{20,28},{24,0},{28,4},{1,9},{5... | collective-permute-start | bytes 208904 | tf_op jit(solution)/shard_map/ppermute | solution.py:25
  204.3 7.6 %copy-start.19 = (bf16[256,128]{1,0:T(8,128)(2,1)S(1)}, bf16[256,128]{1,0:T(8,128)(2,1)}, u32[]{:S(2)}) copy-start(bf16[256,128]{1,0:T(8,128)(2,1)} %merge_all.4) | copy-start | bytes 196612
  206.8 5.1 %copy-start.20 = (bf16[256,128]{1,0:T(8,128)(2,1)S(1)}, bf16[256,128]{1,0:T(8,128)(2,1)}, u32[]{:S(2)}) copy-start(bf16[256,128]{1,0:T(8,128)(2,1)} %merge_all.5) | copy-start | bytes 196612
  209.8 4.4 %copy-start.18 = (bf16[256,128]{1,0:T(8,128)(2,1)S(1)}, bf16[256,128]{1,0:T(8,128)(2,1)}, u32[]{:S(2)}) copy-start(bf16[256,128]{1,0:T(8,128)(2,1)} %merge_all.7) | copy-start | bytes 196612
  211.8 3.8 %collective-permute-start.42 = (bf16[128,1024]{1,0:T(8,128)(2,1)S(1)}, bf16[128,1024]{1,0:T(8,128)(2,1)S(1)}, u32[]{:S(2)}, u32[]{:S(2)}) collective-permute-start(bf16[128,1024]{1,0:T(8,128)(2,1)S(1)} %fusion.38), channel_id=1, source_target_pairs={{0,1},{1,0},{2,3},{3,2},{4,5},{5,4},{6,7},{7,6},{8,9},{9,8},{10,11... | collective-permute-start | bytes 786440 | tf_op jit(solution)/shard_map/ppermute | solution.py:20
  213.7 6.0 %collective-permute-start.41 = (bf16[128,1024]{1,0:T(8,128)(2,1)S(1)}, bf16[128,1024]{1,0:T(8,128)(2,1)S(1)}, u32[]{:S(2)}, u32[]{:S(2)}) collective-permute-start(bf16[128,1024]{1,0:T(8,128)(2,1)S(1)} %fusion.41), channel_id=1, source_target_pairs={{0,1},{1,0},{2,3},{3,2},{4,5},{5,4},{6,7},{7,6},{8,9},{9,8},{10,11... | collective-permute-start | bytes 786440 | tf_op jit(solution)/shard_map/ppermute | solution.py:20
  217.4 8.3 %collective-permute-start.43 = (bf16[128,1024]{1,0:T(8,128)(2,1)S(1)}, bf16[128,1024]{1,0:T(8,128)(2,1)S(1)}, u32[]{:S(2)}, u32[]{:S(2)}) collective-permute-start(bf16[128,1024]{1,0:T(8,128)(2,1)S(1)} %fusion.35), channel_id=1, source_target_pairs={{0,2},{1,3},{2,0},{3,1},{4,6},{5,7},{6,4},{7,5},{8,10},{9,11},{10,... | collective-permute-start | bytes 786440 | tf_op jit(solution)/shard_map/ppermute | solution.py:20
  (22 other events, 33.6 us)

commit v3 on v2

--- a/solution.py
+++ b/solution.py
@@ -199,6 +199,33 @@
         out_ref[base:] = packed(lses)
 
 
+def local_kernel(ctx_ref, q_ref, k0_ref, k1_ref, v0_ref, v1_ref, out_ref):
+    rows = q_ref.shape[0]
+    lane = lax.broadcasted_iota(jnp.int32, q_ref.shape, 1)
+    q = q_ref[...] * jnp.asarray(0.125, q_ref.dtype)
+    key_pos = lax.broadcasted_iota(jnp.int32, (2 * rows, rows), 0)
+    query_pos = lax.broadcasted_iota(jnp.int32, (2 * rows, rows), 1)
+    allowed = (
+        (key_pos > query_pos)
+        & (key_pos <= query_pos + rows)
+        & ((key_pos >= rows) | (ctx_ref[0] > 0))
+    )
+    ones = jnp.ones((16, 2 * rows), jnp.bfloat16)
+    vt = jnp.concatenate([jnp.transpose(v0_ref[...]), jnp.transpose(v1_ref[...])], axis=1)
+    keys = jnp.concatenate([k0_ref[...], k1_ref[...]], axis=0)
+    scores = []
+    for head in range(2):
+        mine = jnp.where((lane < DH) if head == 0 else (lane >= DH), q, jnp.zeros_like(q))
+        s = lax.dot_general(keys, mine, (((1,), (1,)), ((), ())), preferred_element_type=jnp.float32)
+        scores.append(jnp.where(allowed, s, -jnp.inf))
+    for head in range(2):
+        s = scores[head]
+        p = jnp.exp(s - jnp.max(s, axis=0, keepdims=True)).astype(jnp.bfloat16)
+        left = jnp.concatenate([vt[head * DH : (head + 1) * DH], ones], axis=0)
+        o = jnp.dot(left, p, preferred_element_type=jnp.float32)
+        out_ref[head * DH : (head + 1) * DH] = o[:DH] / o[DH : DH + 1]
+
+
 def final_kernel(*refs):
     *msg_refs, local_ref, gate_ref, out_ref = refs
     base = CHUNK_HEADS * DH
@@ -213,7 +240,7 @@
         for r, w in zip(msg_refs, ws):
             term = w * r[rows].astype(jnp.float32)
             mem = term if mem is None else mem + term
-        gate = gate_ref[head : head + 1]
+        gate = gate_ref[0, head : head + 1]
         out_ref[rows] = (
             (gate * inv) * mem + (1.0 - gate) * local_ref[rows].astype(jnp.float32)
         ).astype(jnp.bfloat16)
@@ -278,49 +305,20 @@
             ]
         )
 
-    first_send = [share((me ^ k) * features, width) for k in (2, 3)]
-    first_send, _ = lax.optimization_barrier((first_send, h2))
-    later_me, _ = lax.optimization_barrier((me, queries))
-    far = [[swap(x, "mem", k) for x, k in zip(first_send, (2, 3))]]
+    def across(at, j):
+        return jnp.stack([share((at ^ k) * features + j * width, width) for k in (2, 3)])
+
+    def after(value, *earlier):
+        return lax.optimization_barrier((value, earlier))[0]
+
+    later_me = after(me, queries)
+    crossed = [swap(across(after(me, h1), 0), "mem", 2)]
     near = swap(share((later_me ^ 1) * features, features), "mem", 1)
-    far += [
-        [swap(share((later_me ^ k) * features + j * width, width), "mem", k) for k in (2, 3)]
-        for j in range(1, chunks)
-    ]
 
     q_blocks = [queries] + [turn(queries, "ctx", 2 * k) for k in range(1, turns)]
     q_blocks += [swap(q, "ctx", 1) for q in q_blocks]
+    crossed.append(swap(after(across(later_me, 1), q_blocks[turns]), "mem", 2))
     q_halves = [jnp.concatenate(q_blocks[part * turns : (part + 1) * turns], 0) for part in range(2)]
-
-    window, _ = lax.optimization_barrier(((local_keys, local_values), q_blocks[-1]))
-    earlier_k = from_behind(window[0], "ctx", 1)
-    earlier_v = from_behind(window[1], "ctx", 1)
-    window_keys = jnp.concatenate([earlier_k, local_keys], 0).reshape(2 * row_count, heads_here, DH)
-    window_values = jnp.concatenate([earlier_v, local_values], 0).reshape(
-        2 * row_count, heads_here, DH
-    )
-    query_heads = queries.reshape(row_count, heads_here, DH)
-    scores = (
-        jnp.einsum("ihd,jhd->hij", query_heads, window_keys, preferred_element_type=f32) * 0.125
-    )
-    query_pos = jnp.arange(row_count, dtype=jnp.int32)[:, None]
-    key_pos = jnp.arange(2 * row_count, dtype=jnp.int32)[None, :]
-    allowed = (
-        (key_pos > query_pos)
-        & (key_pos <= query_pos + row_count)
-        & ((key_pos >= row_count) | (my_ctx > 0))
-    )
-    scores = jnp.where(allowed[None], scores, -jnp.inf)
-    highest = jnp.max(scores, axis=-1, keepdims=True)
-    weights_f = jnp.exp(scores - highest)
-    summed = jnp.sum(weights_f, axis=-1)
-    mixed = jnp.einsum(
-        "hij,jhd->hdi",
-        weights_f.astype(jnp.bfloat16),
-        window_values,
-        preferred_element_type=f32,
-    )
-    local_out = (mixed / summed[:, None, :]).reshape(features, row_count)
 
     chunk_pairs = CHUNK_HEADS // 2
     near_flops = 2 * 2 * half * 2 * mem_rows * features
@@ -330,6 +328,10 @@
     ]
     near_state = []
     for part in range(2):
+        if part == 1:
+            crossed.append(
+                swap(after(across(later_me, 2), crossed[0], near_state[0][1]), "mem", 2)
+            )
         near_state.append(
             pl.pallas_call(
                 near_kernel,
@@ -364,14 +366,46 @@
             )(me.reshape(1), q_halves[part], memory_keys, memory_values, near, near, bits[part])
         )
 
+    crossed.append(swap(after(across(later_me, 3), crossed[1], near_state[1][1]), "mem", 2))
+
+    window, _ = lax.optimization_barrier(((local_keys, local_values), q_blocks[-1]))
+    earlier_k = from_behind(window[0], "ctx", 1)
+    earlier_v = from_behind(window[1], "ctx", 1)
+    own_queries, _ = lax.optimization_barrier((queries, near_state[1][1]))
+    pair_spec = pl.BlockSpec((row_count, PAIR), lambda p, c: (0, p))
+    local_out = pl.pallas_call(
+        local_kernel,
+        grid_spec=pltpu.PrefetchScalarGridSpec(
+            num_scalar_prefetch=1,
+            grid=(pairs,),
+            in_specs=[pair_spec] * 5,
+            out_specs=pl.BlockSpec((PAIR, row_count), lambda p, c: (p, 0)),
+        ),
+        out_shape=jax.ShapeDtypeStruct((features, row_count), f32),
+        cost_estimate=pl.CostEstimate(
+            flops=8 * row_count * row_count * features,
+            transcendentals=2 * row_count * row_count * heads_here,
+            bytes_accessed=2 << 20,
+        ),
+        name="local_window",
+    )(my_ctx.reshape(1), own_queries, earlier_k, local_keys, earlier_v, local_values)
+
     gate = jax.nn.sigmoid(gate_bias)
     gate_rows = jnp.broadcast_to(gate[:, None], (heads_here, row_count)).reshape(
         chunks, CHUNK_HEADS, row_count
     )
     combined = []
+    messages = []
+    merges = []
     msg_rows = width + STAT_ROWS
     for j in range(chunks):
-        far2, far3 = far[j]
+        tokens = [near_state[0][1], near_state[1][1]]
+        if j >= 2:
+            tokens += messages[j - 2] + messages[j - 1]
+        if j == chunks - 1:
+            tokens += [local_out] + merges[: j - 1]
+        far2 = after(crossed[j], *tokens)
+        far3 = swap(far2[1], "mem", 1)
         message = [None, None]
         for part in (1, 0):
             acc, stat = near_state[part]
@@ -380,8 +414,8 @@
                 grid=(1,),
                 in_specs=[
                     pl.BlockSpec((half, width), lambda i, j=j: (0, j)),
-                    pl.BlockSpec((1, mem_rows, width), lambda i: (0, 0, 0)),
-                    pl.BlockSpec((1, mem_rows, width), lambda i: (1, 0, 0)),
+                    pl.BlockSpec((None, 1, mem_rows, width), lambda i: (0, 0, 0, 0)),
+                    pl.BlockSpec((None, 1, mem_rows, width), lambda i: (0, 1, 0, 0)),
                     pl.BlockSpec((1, mem_rows, width), lambda i: (0, 0, 0)),
                     pl.BlockSpec((1, mem_rows, width), lambda i: (1, 0, 0)),
                     pl.BlockSpec((1, half), lambda i: (0, 0)),
@@ -399,19 +433,28 @@
                 ),
                 name="far_tiles",
             )(q_halves[part], far2, far2, far3, far3, bits[part], acc, stat)
+        messages.append(message)
         other = swap(message[1], "ctx", 1)
         merged = pl.pallas_call(
             merge_kernel,
             out_shape=[jax.ShapeDtypeStruct((msg_rows, row_count), jnp.bfloat16)] * turns,
             name="merge_pair",
         )(message[0], other)
+        merges.append(merged[0])
         answers = [merged[0]] + [turn(merged[k], "ctx", -2 * k) for k in range(1, turns)]
         combined.append(
             pl.pallas_call(
                 final_kernel,
+                grid=(1,),
+                in_specs=[pl.BlockSpec((msg_rows, row_count), lambda i: (0, 0))] * turns
+                + [
+                    pl.BlockSpec((width, row_count), lambda i, j=j: (j, 0)),
+                    pl.BlockSpec((1, CHUNK_HEADS, row_count), lambda i, j=j: (j, 0, 0)),
+                ],
+                out_specs=pl.BlockSpec((width, row_count), lambda i: (0, 0)),
                 out_shape=jax.ShapeDtypeStruct((width, row_count), jnp.bfloat16),
                 name="merge_all",
-            )(*answers, local_out[j * width : (j + 1) * width], gate_rows[j])
+            )(*answers, local_out, gate_rows)
         )
     early = jnp.concatenate(combined[:-1], axis=0)
     cols = w_output.shape[1] // mem_size

time: 229 us -> 231 us (level)
  waiting for transfers between devices: 47.6 us -> 61.1 us
  other arithmetic: 14.8 us -> 5.28 us
  Pallas kernels: 59.2 us -> 67.9 us
  starting transfers between devices: 62 us -> 55.1 us
  matrix products: 20.4 us -> 18 us
    ppermute x2, waiting for transfers between devices: 0.01 us -> 14.2 us  [from_behind(): return lax.ppermute(block, axis, route)]
    ppermute x24, waiting for transfers between devices: 40.9 us -> 30.2 us  [swap(): lax.ppermute(block, axis, [(i, i ^ distance) for i in range(lax.axis_size...]
    ppermute x18, waiting for transfers between devices: 6.67 us -> 16.6 us  [turn(): lax.ppermute(block, axis, [(i, (i + distance) % size) for i in range(size)])]
    another operation x9 -> x1, other arithmetic: 8.45 us -> 1.49 us  [share(): jnp.stack([lax.dynamic_slice(memory_keys, (0, at), (mem_rows, cols)), lax...]
    pallas_call x4 -> x5, Pallas kernels: 7.05 us -> 13.4 us  [the longest x4 7.05 us: on_device(): pl.pallas_call(final_kernel, grid=(1,), in_specs=[pl.BlockSpec((msg_rows,...]
    unnamed x87 -> x75, local copies, waits for them, and re-layouts: 7.93 us -> 13.5 us
    ppermute x2, starting transfers between devices: 9.48 us -> 5.24 us  [from_behind(): return lax.ppermute(block, axis, route)]
    concatenate x2 -> x0, local copies, waits for them, and re-layouts: 4.09 us -> none  [the longest x1 2.05 us: on_device(): jnp.concatenate([earlier_v, local_values], 0)]
  transfers between devices with their start and end apart: 44 -> 44, of which waited for: 14 -> 12; matrix products, arithmetic and copies ran while one was open for 19% -> 7% of each run, Pallas kernels for 25% -> 29%
where the time goes in v3:
time: 231 us; the launch traced here: 230 us
  Pallas kernels  67.9 us (29%)
  waiting for transfers between devices  61.1 us (26%)
  starting transfers between devices  55.1 us (24%)
  local copies, waits for them, and re-layouts  21.9 us (9%)
  matrix products  18 us (8%)
  other arithmetic  5.28 us (2%)
    ppermute x18, starting transfers between devices, turn(): lax.ppermute(block, axis, [(i, (i + distance) % size) for i in range(size)])  30.6 us
    ppermute x24, waiting for transfers between devices, swap(): lax.ppermute(block, axis, [(i, i ^ distance) for i in range(lax.axis_size...  30.2 us
    pallas_call x8, Pallas kernels, on_device(): pl.pallas_call(far_kernel, grid=(1,), in_specs=[pl.BlockSpec((half, width...  26 us
    pallas_call x2, Pallas kernels, on_device(): pl.pallas_call(near_kernel, grid_spec=pltpu.PrefetchScalarGridSpec(num_sc...  21.2 us
    ppermute x24, starting transfers between devices, swap(): lax.ppermute(block, axis, [(i, i ^ distance) for i in range(lax.axis_size...  19.2 us
    ppermute x18, waiting for transfers between devices, turn(): lax.ppermute(block, axis, [(i, (i + distance) % size) for i in range(size)])  16.6 us
    ppermute x2, waiting for transfers between devices, from_behind(): return lax.ppermute(block, axis, route)  14.2 us
    unnamed x75, local copies, waits for them, and re-layouts  13.5 us
  transfers between devices with their start and end apart: 44, of which 12 were waited for; matrix products, arithmetic and copies ran while one was open for 7% of the time, Pallas kernels for 29%

profile of v3, /device:TPU:0, one launch (start us, length us, event | category | flops | bytes accessed | tf_op | source)
XLA Modules:
  0.0 229.8 jit_solution(3924169029690306606)
XLA Ops:
  0.0 2.9 %collective-permute-start.1 = (bf16[128,1024]{1,0:T(8,128)(2,1)}, bf16[128,1024]{1,0:T(8,128)(2,1)S(1)}, u32[]{:S(2)}, u32[]{:S(2)}) collective-permute-start(bf16[128,1024]{1,0:T(8,128)(2,1)} %param.10), channel_id=1, source_target_pairs={{0,2},{1,3},{2,0},{3,1},{4,6},{5,7},{6,4},{7,5},{8,10},{9,11},{10,... | collective-permute-start | bytes 786440 | tf_op jit(solution)/shard_map/ppermute | solution.py:20
  3.6 1.5 collective-permute-start.8
  5.2 2.1 collective-permute-done.8
  7.3 2.6 %collective-permute-start.10 = (s32[2,16,128]{2,1,0:T(8,128)S(1)}, s32[2,16,128]{2,1,0:T(8,128)S(1)}, u32[]{:S(2)}, u32[]{:S(2)}) collective-permute-start(s32[2,16,128]{2,1,0:T(8,128)S(1)} %get-tuple-element.86), channel_id=1, source_target_pairs={{0,16},{4,20},{8,24},{12,28},{16,0},{20,4},{24,8},{28,12},{1,17},{... | collective-permute-start | bytes 49160 | tf_op jit(solution)/shard_map/ppermute | solution.py:25
  9.9 1.6 collective-permute-start.9
  11.5 2.2 collective-permute-start.11
  15.7 4.6 %convolution_convert_fusion.q_ref = bf16[128,1024]{1,0:T(8,128)(2,1)S(1)} fusion(bf16[128,4096]{1,0:T(8,128)(2,1)S(1)} %constant_dynamic-update-slice_fusion.4, bf16[4096,1024]{1,0:T(8,128)(2,1)} %param.11), kind=kOutput, calls=%fused_computation.20 | convolution fusion | flops 1073872896 | bytes 9699328 | tf_op jit(solution)/shard_map/dot_general | solution.py:298
  20.3 1.8 dynamic-slice_bitcast_fusion
  22.2 1.5 pad_maximum_fusion
  23.7 1.6 collective-permute-start.12
  25.3 3.8 %collective-permute-start.5 = (bf16[128,1024]{1,0:T(8,128)(2,1)S(1)}, bf16[128,1024]{1,0:T(8,128)(2,1)}, u32[]{:S(2)}, u32[]{:S(2)}) collective-permute-start(bf16[128,1024]{1,0:T(8,128)(2,1)S(1)} %convolution_convert_fusion.q_ref), channel_id=1, source_target_pairs={{0,24},{4,28},{8,0},{12,4},{16,8},{20,12},{24,16},{28,20},{1,25},{... | collective-permute-start | bytes 786440 | tf_op jit(solution)/shard_map/ppermute | solution.py:25
  29.6 2.5 %dynamic-slice_bitcast_fusion.16 = (bf16[1,512,256]{2,1,0:T(8,128)(2,1)S(1)}, bf16[1,512,256]{2,1,0:T(8,128)(2,1)S(1)}, bf16[1,512,256]{2,1,0:T(8,128)(2,1)S(1)}...) fusion(bf16[512,4096]{1,0:T(8,128)(2,1)} %v0_ref.3, ...), kind=kLoop, calls=%fused_computation.62 | loop fusion | bytes 8388640 | tf_op jit(solution)/shard_map/stack | solution.py:301
  33.4 13.8 %collective-permute-done.3 = bf16[128,1024]{1,0:T(8,128)(2,1)} collective-permute-done((bf16[128,1024]{1,0:T(8,128)(2,1)S(1)}, bf16[128,1024]{1,0:T(8,128)(2,1)}, u32[]{:S(2)}, u32[]{:S(2)}) %collective-permute-start.3) | collective-permute-done | bytes 262176 | tf_op jit(solution)/shard_map/ppermute | solution.py:25
  48.4 1.5 collective-permute-done.4
  51.5 5.0 %collective-permute-done.13 = bf16[128,1024]{1,0:T(8,128)(2,1)S(1)} collective-permute-done((bf16[128,1024]{1,0:T(8,128)(2,1)}, bf16[128,1024]{1,0:T(8,128)(2,1)S(1)}, u32[]{:S(2)}, u32[]{:S(2)}) %collective-permute-start.13) | collective-permute-done | bytes 262176 | tf_op jit(solution)/shard_map/ppermute | solution.py:20
  58.1 4.1 %collective-permute-done.14 = bf16[128,1024]{1,0:T(8,128)(2,1)S(1)} collective-permute-done((bf16[128,1024]{1,0:T(8,128)(2,1)}, bf16[128,1024]{1,0:T(8,128)(2,1)S(1)}, u32[]{:S(2)}, u32[]{:S(2)}) %collective-permute-start.14) | collective-permute-done | bytes 262176 | tf_op jit(solution)/shard_map/ppermute | solution.py:20
  62.2 4.2 %collective-permute-done.15 = bf16[128,1024]{1,0:T(8,128)(2,1)S(1)} collective-permute-done((bf16[128,1024]{1,0:T(8,128)(2,1)}, bf16[128,1024]{1,0:T(8,128)(2,1)S(1)}, u32[]{:S(2)}, u32[]{:S(2)}) %collective-permute-start.15) | collective-permute-done | bytes 262176 | tf_op jit(solution)/shard_map/ppermute | solution.py:20
  66.4 1.3 copy-done.14
  67.8 1.6 copy-done.15
  69.4 10.6 %near_tiles.2 = (f32[1024,512]{1,0:T(8,128)S(1)}, f32[8,8,512]{2,1,0:T(8,128)S(1)}) custom-call(s32[1]{0:T(128)} %bitcast.6.m_ref, bf16[512,1024]{1,0:T(8,128)(2,1)S(1)} %pad_maximum_fusion.1.q_ref, bf16[512,4096]{1,0:T(8,128)(2,1)} %k0_ref.3, bf16[512,4096]{1,0:T(8,128)(2,1)} %v0_ref.3, bf16[2,512,1024]{2,1,0:T(8,128)(2,1)S(1)} %copy-done.15, ...), custom_call_target="tpu_custom_call" | custom-call | flops 2147483648 | bytes 8388608 | tf_op jit(solution)/shard_map/near_tiles/pallas_call | solution.py:336
  80.0 10.5 %near_tiles.3 = (f32[1024,512]{1,0:T(8,128)S(1)}, f32[8,8,512]{2,1,0:T(8,128)S(1)}) custom-call(s32[1]{0:T(128)} %bitcast.6.m_ref, bf16[512,1024]{1,0:T(8,128)(2,1)S(1)} %constant_dynamic-update-slice_fusion.q_ref, bf16[512,4096]{1,0:T(8,128)(2,1)} %k0_ref.3, bf16[512,4096]{1,0:T(8,128)(2,1)} %v0_ref.3, bf16[2,512,1024]{2,1,0:T(8,128)(2,1)S(1)} %copy-done.16, ...), custom_call_target="tpu_custom_call" | custom-call | flops 2147483648 | bytes 8388608 | tf_op jit(solution)/shard_map/near_tiles/pallas_call | solution.py:336
  93.1 2.6 %collective-permute-start.21 = (bf16[128,1024]{1,0:T(8,128)(2,1)S(1)}, bf16[128,1024]{1,0:T(8,128)(2,1)S(1)}, u32[]{:S(2)}, u32[]{:S(2)}) collective-permute-start(bf16[128,1024]{1,0:T(8,128)(2,1)S(1)} %copy-done.23), channel_id=1, source_target_pairs={{0,4},{4,8},{8,12},{12,16},{16,20},{20,24},{24,28},{1,5},{5,9},{9,... | collective-permute-start | bytes 786440 | tf_op jit(solution)/shard_map/ppermute | solution.py:31
  95.7 1.5 collective-permute-start.35
  97.2 3.1 %far_tiles.9 = bf16[4,272,128]{2,1,0:T(8,128)(2,1)} custom-call(bf16[512,1024]{1,0:T(8,128)(2,1)S(1)} %constant_dynamic-update-slice_fusion.q_ref, bf16[2,2,512,256]{3,2,1,0:T(8,128)(2,1)S(1)} %collective-permute-done.6.k2_ref.v2_ref, bf16[2,2,512,256]{3,2,1,0:T(8,128)(2,1)S(1)} %collective-permute-done.6.k2_ref.v2_ref, ...), custom_call_target="tpu_custom_call" | custom-call | flops 536870912 | bytes 3145728 | tf_op jit(solution)/shard_map/far_tiles/pallas_call | solution.py:412
  100.4 2.4 %far_tiles.8.a_ref = bf16[4,272,128]{2,1,0:T(8,128)(2,1)S(1)} custom-call(bf16[512,1024]{1,0:T(8,128)(2,1)S(1)} %pad_maximum_fusion.1.q_ref, bf16[2,2,512,256]{3,2,1,0:T(8,128)(2,1)S(1)} %collective-permute-done.6.k2_ref.v2_ref, bf16[2,2,512,256]{3,2,1,0:T(8,128)(2,1)S(1)} %collective-permute-done.6.k2_ref.v2_ref, ...), custom_call_target="tpu_custom_call" | custom-call | flops 536870912 | bytes 3145728 | tf_op jit(solution)/shard_map/far_tiles/pallas_call | solution.py:412
  102.8 3.1 %far_tiles.11 = bf16[4,272,128]{2,1,0:T(8,128)(2,1)} custom-call(bf16[512,1024]{1,0:T(8,128)(2,1)S(1)} %constant_dynamic-update-slice_fusion.q_ref, bf16[2,2,512,256]{3,2,1,0:T(8,128)(2,1)S(1)} %collective-permute-done.23.k2_ref.v2_ref, bf16[2,2,512,256]{3,2,1,0:T(8,128)(2,1)S(1)} %collective-permute-done.23.k2_ref.v2_ref, ...), custom_call_target="tpu_custom_call" | custom-call | flops 536870912 | bytes 3145728 | tf_op jit(solution)/shard_map/far_tiles/pallas_call | solution.py:412
  106.0 2.4 %far_tiles.10.a_ref = bf16[4,272,128]{2,1,0:T(8,128)(2,1)S(1)} custom-call(bf16[512,1024]{1,0:T(8,128)(2,1)S(1)} %pad_maximum_fusion.1.q_ref, bf16[2,2,512,256]{3,2,1,0:T(8,128)(2,1)S(1)} %collective-permute-done.23.k2_ref.v2_ref, bf16[2,2,512,256]{3,2,1,0:T(8,128)(2,1)S(1)} %collective-permute-done.23.k2_ref.v2_ref, ...), custom_call_target="tpu_custom_call" | custom-call | flops 536870912 | bytes 3145728 | tf_op jit(solution)/shard_map/far_tiles/pallas_call | solution.py:412
  108.4 8.3 %collective-permute-done.29.k2_ref.v2_ref = bf16[2,2,512,256]{3,2,1,0:T(8,128)(2,1)S(1)} collective-permute-done((bf16[2,2,512,256]{3,2,1,0:T(8,128)(2,1)S(1)}, bf16[2,2,512,256]{3,2,1,0:T(8,128)(2,1)S(1)}, u32[]{:S(2)}, u32[]{:S(2)}) %collective-permute-start.29) | collective-permute-done | bytes 1048608 | tf_op jit(solution)/shard_map/ppermute | solution.py:20
  119.1 1.5 collective-permute-start.25
  120.6 2.6 %collective-permute-start.22 = (bf16[128,1024]{1,0:T(8,128)(2,1)S(1)}, bf16[128,1024]{1,0:T(8,128)(2,1)S(1)}, u32[]{:S(2)}, u32[]{:S(2)}) collective-permute-start(bf16[128,1024]{1,0:T(8,128)(2,1)S(1)} %copy-done.24), channel_id=1, source_target_pairs={{0,4},{4,8},{8,12},{12,16},{16,20},{20,24},{24,28},{1,5},{5,9},{9,... | collective-permute-start | bytes 786440 | tf_op jit(solution)/shard_map/ppermute | solution.py:31
  123.2 14.2 %collective-permute-done.22.v0_ref = bf16[128,1024]{1,0:T(8,128)(2,1)S(1)} collective-permute-done((bf16[128,1024]{1,0:T(8,128)(2,1)S(1)}, bf16[128,1024]{1,0:T(8,128)(2,1)S(1)}, u32[]{:S(2)}, u32[]{:S(2)}) %collective-permute-start.22) | collective-permute-done | bytes 262176 | tf_op jit(solution)/shard_map/ppermute | solution.py:31
  138.2 6.3 %local_window.1.refs_4_ = f32[1024,128]{1,0:T(8,128)} custom-call(s32[1]{0:T(128)} %bitcast.19.ctx_ref, bf16[128,1024]{1,0:T(8,128)(2,1)} %copy-done.17, bf16[128,1024]{1,0:T(8,128)(2,1)} %copy-done.25, bf16[128,1024]{1,0:T(8,128)(2,1)} %k1_ref.1, bf16[128,1024]{1,0:T(8,128)(2,1)} %copy-done.26, bf16[128,1024]{1,0:T(8,128)(2,1)} %v1_ref.1), custom_call_target="tpu_custom_call" | custom-call | flops 134217728 | bytes 2097152 | tf_op jit(solution)/shard_map/local_window/pallas_call | solution.py:376
  144.5 1.8 merge_pair.4
  146.4 1.8 merge_pair.5
  148.2 1.6 copy-done.1
  149.8 1.2 copy-done.4
  151.0 1.2 copy-done.6
  152.2 3.5 %far_tiles.13 = bf16[4,272,128]{2,1,0:T(8,128)(2,1)S(1)} custom-call(bf16[512,1024]{1,0:T(8,128)(2,1)S(1)} %copy-done.6, bf16[2,2,512,256]{3,2,1,0:T(8,128)(2,1)S(1)} %copy-done.4, bf16[2,2,512,256]{3,2,1,0:T(8,128)(2,1)S(1)} %copy-done.4, bf16[2,512,256]{2,1,0:T(8,128)(2,1)} %collective-permute-done.30.k3_ref.v3_ref, ...), custom_call_target="tpu_custom_call" | custom-call | flops 536870912 | bytes 3145728 | tf_op jit(solution)/shard_map/far_tiles/pallas_call | solution.py:412
  155.7 3.6 %far_tiles.12.a_ref = bf16[4,272,128]{2,1,0:T(8,128)(2,1)S(1)} custom-call(bf16[512,1024]{1,0:T(8,128)(2,1)S(1)} %pad_maximum_fusion.1.q_ref, bf16[2,2,512,256]{3,2,1,0:T(8,128)(2,1)S(1)} %copy-done.4, bf16[2,2,512,256]{3,2,1,0:T(8,128)(2,1)S(1)} %copy-done.4, bf16[2,512,256]{2,1,0:T(8,128)(2,1)} %collective-permute-done.30.k3_ref.v3_ref, ...), custom_call_target="tpu_custom_call" | custom-call | flops 536870912 | bytes 3145728 | tf_op jit(solution)/shard_map/far_tiles/pallas_call | solution.py:412
  159.4 1.2 slice_bitcast_fusion
  160.6 2.5 %collective-permute-start.31 = (bf16[4,272,128]{2,1,0:T(8,128)(2,1)S(1)}, bf16[4,272,128]{2,1,0:T(8,128)(2,1)S(1)}, u32[]{:S(2)}, u32[]{:S(2)}) collective-permute-start(bf16[4,272,128]{2,1,0:T(8,128)(2,1)S(1)} %far_tiles.13), channel_id=1, source_target_pairs={{0,4},{4,0},{8,12},{12,8},{16,20},{20,16},{24,28},{28,24},{1,5},{5... | collective-permute-start | bytes 835592 | tf_op jit(solution)/shard_map/ppermute | solution.py:20
  163.2 4.3 %far_tiles.15 = bf16[4,272,128]{2,1,0:T(8,128)(2,1)} custom-call(bf16[512,1024]{1,0:T(8,128)(2,1)S(1)} %copy-done.7, bf16[2,2,512,256]{3,2,1,0:T(8,128)(2,1)} %collective-permute-done.35.k2_ref.v2_ref, bf16[2,2,512,256]{3,2,1,0:T(8,128)(2,1)} %collective-permute-done.35.k2_ref.v2_ref, bf16[2,512,256]{2,1,0:T(8,128)(2,1)S(1)} %collective-permute-done.36.k3_ref.v3_ref, ...), custom_call_target="tpu_custom_call" | custom-call | flops 536870912 | bytes 3145728 | tf_op jit(solution)/shard_map/far_tiles/pallas_call | solution.py:412
  167.5 1.8 collective-permute-start.37
  169.3 7.1 %collective-permute-start.19 = (bf16[272,128]{1,0:T(8,128)(2,1)}, bf16[272,128]{1,0:T(8,128)(2,1)S(1)}, u32[]{:S(2)}, u32[]{:S(2)}) collective-permute-start(bf16[272,128]{1,0:T(8,128)(2,1)} %get-tuple-element.46), channel_id=1, source_target_pairs={{0,16},{4,20},{8,24},{12,28},{16,0},{20,4},{24,8},{28,12},{1,17},{... | collective-permute-start | bytes 208904 | tf_op jit(solution)/shard_map/ppermute | solution.py:25
  176.4 2.0 collective-permute-start.20
  179.1 1.8 collective-permute-start.26
  180.9 1.9 merge_pair.6
  183.4 3.8 %collective-permute-start.32 = (bf16[272,128]{1,0:T(8,128)(2,1)}, bf16[272,128]{1,0:T(8,128)(2,1)}, u32[]{:S(2)}, u32[]{:S(2)}) collective-permute-start(bf16[272,128]{1,0:T(8,128)(2,1)} %get-tuple-element.60), channel_id=1, source_target_pairs={{0,24},{4,28},{8,0},{12,4},{16,8},{20,12},{24,16},{28,20},{1,25},{... | collective-permute-start | bytes 208904 | tf_op jit(solution)/shard_map/ppermute | solution.py:25
  188.3 3.4 %far_tiles.14.a_ref = bf16[4,272,128]{2,1,0:T(8,128)(2,1)S(1)} custom-call(bf16[512,1024]{1,0:T(8,128)(2,1)S(1)} %pad_maximum_fusion.1.q_ref, bf16[2,2,512,256]{3,2,1,0:T(8,128)(2,1)} %collective-permute-done.35.k2_ref.v2_ref, bf16[2,2,512,256]{3,2,1,0:T(8,128)(2,1)} %collective-permute-done.35.k2_ref.v2_ref, bf16[2,512,256]{2,1,0:T(8,128)(2,1)S(1)} %copy-done.9, ...), custom_call_target="tpu_custom_call" | custom-call | flops 536870912 | bytes 3145728 | tf_op jit(solution)/shard_map/far_tiles/pallas_call | solution.py:412
  192.4 1.8 merge_pair.7
  195.1 3.6 %collective-permute-start.38 = (bf16[272,128]{1,0:T(8,128)(2,1)}, bf16[272,128]{1,0:T(8,128)(2,1)S(1)}, u32[]{:S(2)}, u32[]{:S(2)}) collective-permute-start(bf16[272,128]{1,0:T(8,128)(2,1)} %get-tuple-element.66), channel_id=1, source_target_pairs={{0,24},{4,28},{8,0},{12,4},{16,8},{20,12},{24,16},{28,20},{1,25},{... | collective-permute-start | bytes 208904 | tf_op jit(solution)/shard_map/ppermute | solution.py:25
  200.2 1.8 merge_all.4
  201.9 1.8 merge_all.5
  204.4 1.8 merge_all.6
  207.0 1.8 merge_all.7
  208.8 1.4 fusion.41
  210.1 1.3 fusion.45
  211.5 1.9 fusion.35
  213.5 1.8 fusion.38
  215.9 1.3 fusion.43
  217.2 1.8 fusion.32
  219.6 1.3 fusion.47
  220.9 6.4 %collective-permute-done.43 = bf16[128,1024]{1,0:T(8,128)(2,1)S(1)} collective-permute-done((bf16[128,1024]{1,0:T(8,128)(2,1)S(1)}, bf16[128,1024]{1,0:T(8,128)(2,1)S(1)}, u32[]{:S(2)}, u32[]{:S(2)}) %collective-permute-start.43) | collective-permute-done | bytes 262176 | tf_op jit(solution)/shard_map/ppermute | solution.py:20
  227.3 2.5 %fusion.29 = bf16[128,1024]{1,0:T(8,128)(2,1)} fusion(f32[128,1024]{1,0:T(8,128)S(1)} %fusion.47, bf16[1024,4096]{1,0:T(8,128)(2,1)} %param.19, s32[]{:T(128)S(6)} %select_n.79, bf16[128,1024]{1,0:T(8,128)(2,1)S(1)} %collective-permute-done.43, bf16[128,1024]{1,0:T(8,128)(2,1)S(1)} %collective-permute-done.41, bf16[256,128]{1,0:T(8,128)(2,1)S(1)} %copy-done.20, ...), kind=kOutput, calls=%fused_computation.16 | convolution fusion | flops 202702848 | bytes 3080196 | tf_op jit(solution)/shard_map/dot_general | solution.py:466
  (160 shorter events, 22.4 us)
Async XLA Ops:
  0.0 13.7 %collective-permute-start.1 = (bf16[128,1024]{1,0:T(8,128)(2,1)}, bf16[128,1024]{1,0:T(8,128)(2,1)S(1)}, u32[]{:S(2)}, u32[]{:S(2)}) collective-permute-start(bf16[128,1024]{1,0:T(8,128)(2,1)} %param.10), channel_id=1, source_target_pairs={{0,2},{1,3},{2,0},{3,1},{4,6},{5,7},{6,4},{7,5},{8,10},{9,11},{10,... | collective-permute-start | bytes 786440 | tf_op jit(solution)/shard_map/ppermute | solution.py:20
  3.6 3.7 %collective-permute-start.8 = (s32[16,128]{1,0:T(8,128)S(1)}, s32[16,128]{1,0:T(8,128)S(1)}, u32[]{:S(2)}, u32[]{:S(2)}) collective-permute-start(s32[16,128]{1,0:T(8,128)S(1)} %get-tuple-element.88), channel_id=1, source_target_pairs={{0,4},{4,0},{8,12},{12,8},{16,20},{20,16},{24,28},{28,24},{1,5},{5... | collective-permute-start | bytes 24584 | tf_op jit(solution)/shard_map/ppermute | solution.py:20
  5.2 10.4 %collective-permute-start = (bf16[128,1024]{1,0:T(8,128)(2,1)}, bf16[128,1024]{1,0:T(8,128)(2,1)S(1)}, u32[]{:S(2)}, u32[]{:S(2)}) collective-permute-start(bf16[128,1024]{1,0:T(8,128)(2,1)} %param.10), channel_id=1, source_target_pairs={{0,1},{1,0},{2,3},{3,2},{4,5},{5,4},{6,7},{7,6},{8,9},{9,8},{10,11... | collective-permute-start | bytes 786440 | tf_op jit(solution)/shard_map/ppermute | solution.py:20
  7.3 7.5 %collective-permute-start.10 = (s32[2,16,128]{2,1,0:T(8,128)S(1)}, s32[2,16,128]{2,1,0:T(8,128)S(1)}, u32[]{:S(2)}, u32[]{:S(2)}) collective-permute-start(s32[2,16,128]{2,1,0:T(8,128)S(1)} %get-tuple-element.86), channel_id=1, source_target_pairs={{0,16},{4,20},{8,24},{12,28},{16,0},{20,4},{24,8},{28,12},{1,17},{... | collective-permute-start | bytes 49160 | tf_op jit(solution)/shard_map/ppermute | solution.py:25
  9.9 5.5 %collective-permute-start.9 = (s32[2,16,128]{2,1,0:T(8,128)S(1)}, s32[2,16,128]{2,1,0:T(8,128)S(1)}, u32[]{:S(2)}, u32[]{:S(2)}) collective-permute-start(s32[2,16,128]{2,1,0:T(8,128)S(1)} %get-tuple-element.86), channel_id=1, source_target_pairs={{0,8},{4,12},{8,16},{12,20},{16,24},{20,28},{24,0},{28,4},{1,9},{5... | collective-permute-start | bytes 49160 | tf_op jit(solution)/shard_map/ppermute | solution.py:25
  11.5 4.0 %collective-permute-start.11 = (s32[2,16,128]{2,1,0:T(8,128)S(1)}, s32[2,16,128]{2,1,0:T(8,128)S(1)}, u32[]{:S(2)}, u32[]{:S(2)}) collective-permute-start(s32[2,16,128]{2,1,0:T(8,128)S(1)} %get-tuple-element.86), channel_id=1, source_target_pairs={{0,24},{4,28},{8,0},{12,4},{16,8},{20,12},{24,16},{28,20},{1,25},{... | collective-permute-start | bytes 49160 | tf_op jit(solution)/shard_map/ppermute | solution.py:25
  13.7 1.9 collective-permute-start.2
  20.3 30.0 %copy-start.17 = (bf16[128,1024]{1,0:T(8,128)(2,1)}, bf16[128,1024]{1,0:T(8,128)(2,1)S(1)}, u32[]{:S(2)}) copy-start(bf16[128,1024]{1,0:T(8,128)(2,1)S(1)} %convolution_convert_fusion.q_ref) | copy-start | bytes 786436
  23.6 42.8 %collective-permute-start.7 = (bf16[2,512,1024]{2,1,0:T(8,128)(2,1)}, bf16[2,512,1024]{2,1,0:T(8,128)(2,1)S(1)}, u32[]{:S(2)}, u32[]{:S(2)}) collective-permute-start(bf16[2,512,1024]{2,1,0:T(8,128)(2,1)} %pad_maximum_fusion), channel_id=1, source_target_pairs={{0,1},{1,0},{2,3},{3,2},{4,5},{5,4},{6,7},{7,6},{8,9},{9,8},{10,11... | collective-permute-start | bytes 6291464 | tf_op jit(solution)/shard_map/ppermute | solution.py:20
  23.7 9.0 %collective-permute-start.12 = (bf16[128,1024]{1,0:T(8,128)(2,1)S(1)}, bf16[128,1024]{1,0:T(8,128)(2,1)}, u32[]{:S(2)}, u32[]{:S(2)}) collective-permute-start(bf16[128,1024]{1,0:T(8,128)(2,1)S(1)} %convolution_convert_fusion.q_ref), channel_id=1, source_target_pairs={{0,4},{4,0},{8,12},{12,8},{16,20},{20,16},{24,28},{28,24},{1,5},{5... | collective-permute-start | bytes 786440 | tf_op jit(solution)/shard_map/ppermute | solution.py:20
  25.3 22.5 %collective-permute-start.5 = (bf16[128,1024]{1,0:T(8,128)(2,1)S(1)}, bf16[128,1024]{1,0:T(8,128)(2,1)}, u32[]{:S(2)}, u32[]{:S(2)}) collective-permute-start(bf16[128,1024]{1,0:T(8,128)(2,1)S(1)} %convolution_convert_fusion.q_ref), channel_id=1, source_target_pairs={{0,24},{4,28},{8,0},{12,4},{16,8},{20,12},{24,16},{28,20},{1,25},{... | collective-permute-start | bytes 786440 | tf_op jit(solution)/shard_map/ppermute | solution.py:25
  29.1 20.8 %collective-permute-start.4 = (bf16[128,1024]{1,0:T(8,128)(2,1)S(1)}, bf16[128,1024]{1,0:T(8,128)(2,1)}, u32[]{:S(2)}, u32[]{:S(2)}) collective-permute-start(bf16[128,1024]{1,0:T(8,128)(2,1)S(1)} %convolution_convert_fusion.q_ref), channel_id=1, source_target_pairs={{0,16},{4,20},{8,24},{12,28},{16,0},{20,4},{24,8},{28,12},{1,17},{... | collective-permute-start | bytes 786440 | tf_op jit(solution)/shard_map/ppermute | solution.py:25
  29.1 18.1 %collective-permute-start.3 = (bf16[128,1024]{1,0:T(8,128)(2,1)S(1)}, bf16[128,1024]{1,0:T(8,128)(2,1)}, u32[]{:S(2)}, u32[]{:S(2)}) collective-permute-start(bf16[128,1024]{1,0:T(8,128)(2,1)S(1)} %convolution_convert_fusion.q_ref), channel_id=1, source_target_pairs={{0,8},{4,12},{8,16},{12,20},{16,24},{20,28},{24,0},{28,4},{1,9},{5... | collective-permute-start | bytes 786440 | tf_op jit(solution)/shard_map/ppermute | solution.py:25
  32.7 47.3 %collective-permute-start.6 = (bf16[2,2,512,256]{3,2,1,0:T(8,128)(2,1)S(1)}, bf16[2,2,512,256]{3,2,1,0:T(8,128)(2,1)S(1)}, u32[]{:S(2)}, u32[]{:S(2)}) collective-permute-start(bf16[2,2,512,256]{3,2,1,0:T(8,128)(2,1)S(1)} %pad_maximum_fusion.2), channel_id=1, source_target_pairs={{0,2},{1,3},{2,0},{3,1},{4,6},{5,7},{6,4},{7,5},{8,10},{9,11},{10,... | collective-permute-start | bytes 3145736 | tf_op jit(solution)/shard_map/ppermute | solution.py:20
  47.1 9.4 %collective-permute-start.13 = (bf16[128,1024]{1,0:T(8,128)(2,1)}, bf16[128,1024]{1,0:T(8,128)(2,1)S(1)}, u32[]{:S(2)}, u32[]{:S(2)}) collective-permute-start(bf16[128,1024]{1,0:T(8,128)(2,1)} %collective-permute-done.3), channel_id=1, source_target_pairs={{0,4},{4,0},{8,12},{12,8},{16,20},{20,16},{24,28},{28,24},{1,5},{5... | collective-permute-start | bytes 786440 | tf_op jit(solution)/shard_map/ppermute | solution.py:20
  47.8 43.5 %collective-permute-start.23 = (bf16[2,2,512,256]{3,2,1,0:T(8,128)(2,1)S(1)}, bf16[2,2,512,256]{3,2,1,0:T(8,128)(2,1)S(1)}, u32[]{:S(2)}, u32[]{:S(2)}) collective-permute-start(bf16[2,2,512,256]{3,2,1,0:T(8,128)(2,1)S(1)} %pad_maximum_fusion.3), channel_id=1, source_target_pairs={{0,2},{1,3},{2,0},{3,1},{4,6},{5,7},{6,4},{7,5},{8,10},{9,11},{10,... | collective-permute-start | bytes 3145736 | tf_op jit(solution)/shard_map/ppermute | solution.py:20
  49.8 12.4 %collective-permute-start.14 = (bf16[128,1024]{1,0:T(8,128)(2,1)}, bf16[128,1024]{1,0:T(8,128)(2,1)S(1)}, u32[]{:S(2)}, u32[]{:S(2)}) collective-permute-start(bf16[128,1024]{1,0:T(8,128)(2,1)} %collective-permute-done.4), channel_id=1, source_target_pairs={{0,4},{4,0},{8,12},{12,8},{16,20},{20,16},{24,28},{28,24},{1,5},{5... | collective-permute-start | bytes 786440 | tf_op jit(solution)/shard_map/ppermute | solution.py:20
  56.6 9.8 %collective-permute-start.15 = (bf16[128,1024]{1,0:T(8,128)(2,1)}, bf16[128,1024]{1,0:T(8,128)(2,1)S(1)}, u32[]{:S(2)}, u32[]{:S(2)}) collective-permute-start(bf16[128,1024]{1,0:T(8,128)(2,1)} %collective-permute-done.5), channel_id=1, source_target_pairs={{0,4},{4,0},{8,12},{12,8},{16,20},{20,16},{24,28},{28,24},{1,5},{5... | collective-permute-start | bytes 786440 | tf_op jit(solution)/shard_map/ppermute | solution.py:20
  66.4 36.4 %copy-start.5 = (bf16[512,1024]{1,0:T(8,128)(2,1)}, bf16[512,1024]{1,0:T(8,128)(2,1)S(1)}, u32[]{:S(2)}) copy-start(bf16[512,1024]{1,0:T(8,128)(2,1)S(1)} %constant_dynamic-update-slice_fusion.q_ref) | copy-start | bytes 3145732
  69.4 10.7 %copy-start.16 = (bf16[2,512,1024]{2,1,0:T(8,128)(2,1)S(1)}, bf16[2,512,1024]{2,1,0:T(8,128)(2,1)}, u32[]{:S(2)}) copy-start(bf16[2,512,1024]{2,1,0:T(8,128)(2,1)} %copy-done.14) | copy-start | bytes 6291460
  90.6 12.3 %copy-start = (f32[1024,512]{1,0:T(8,128)}, f32[1024,512]{1,0:T(8,128)S(1)}, u32[]{:S(2)}) copy-start(f32[1024,512]{1,0:T(8,128)S(1)} %get-tuple-element.43.acc_ref) | copy-start | bytes 6291460
  90.6 2.5 %copy-start.23 = (bf16[128,1024]{1,0:T(8,128)(2,1)S(1)}, bf16[128,1024]{1,0:T(8,128)(2,1)}, u32[]{:S(2)}) copy-start(bf16[128,1024]{1,0:T(8,128)(2,1)} %k1_ref.1) | copy-start | bytes 786436
  90.6 26.2 %collective-permute-start.29 = (bf16[2,2,512,256]{3,2,1,0:T(8,128)(2,1)S(1)}, bf16[2,2,512,256]{3,2,1,0:T(8,128)(2,1)S(1)}, u32[]{:S(2)}, u32[]{:S(2)}) collective-permute-start(bf16[2,2,512,256]{3,2,1,0:T(8,128)(2,1)S(1)} %pad_maximum_fusion.4), channel_id=1, source_target_pairs={{0,2},{1,3},{2,0},{3,1},{4,6},{5,7},{6,4},{7,5},{8,10},{9,11},{10,... | collective-permute-start | bytes 3145736 | tf_op jit(solution)/shard_map/ppermute | solution.py:20
  91.2 6.0 %collective-permute-start.16 = (bf16[2,512,256]{2,1,0:T(8,128)(2,1)S(1)}, bf16[2,512,256]{2,1,0:T(8,128)(2,1)S(1)}, u32[]{:S(2)}, u32[]{:S(2)}) collective-permute-start(bf16[2,512,256]{2,1,0:T(8,128)(2,1)S(1)} %slice_bitcast_fusion.3), channel_id=1, source_target_pairs={{0,1},{1,0},{2,3},{3,2},{4,5},{5,4},{6,7},{7,6},{8,9},{9,8},{10,11... | collective-permute-start | bytes 1572872 | tf_op jit(solution)/shard_map/ppermute | solution.py:20
  91.3 11.5 %collective-permute-start.24 = (bf16[2,512,256]{2,1,0:T(8,128)(2,1)S(1)}, bf16[2,512,256]{2,1,0:T(8,128)(2,1)S(1)}, u32[]{:S(2)}, u32[]{:S(2)}) collective-permute-start(bf16[2,512,256]{2,1,0:T(8,128)(2,1)S(1)} %slice_bitcast_fusion.2), channel_id=1, source_target_pairs={{0,1},{1,0},{2,3},{3,2},{4,5},{5,4},{6,7},{7,6},{8,9},{9,8},{10,11... | collective-permute-start | bytes 1572872 | tf_op jit(solution)/shard_map/ppermute | solution.py:20
  93.1 27.6 %collective-permute-start.21 = (bf16[128,1024]{1,0:T(8,128)(2,1)S(1)}, bf16[128,1024]{1,0:T(8,128)(2,1)S(1)}, u32[]{:S(2)}, u32[]{:S(2)}) collective-permute-start(bf16[128,1024]{1,0:T(8,128)(2,1)S(1)} %copy-done.23), channel_id=1, source_target_pairs={{0,4},{4,8},{8,12},{12,16},{16,20},{20,24},{24,28},{1,5},{5,9},{9,... | collective-permute-start | bytes 786440 | tf_op jit(solution)/shard_map/ppermute | solution.py:31
  95.7 63.7 %collective-permute-start.35 = (bf16[2,2,512,256]{3,2,1,0:T(8,128)(2,1)}, bf16[2,2,512,256]{3,2,1,0:T(8,128)(2,1)}, u32[]{:S(2)}, u32[]{:S(2)}) collective-permute-start(bf16[2,2,512,256]{3,2,1,0:T(8,128)(2,1)} %pad_maximum_fusion.5), channel_id=1, source_target_pairs={{0,2},{1,3},{2,0},{3,1},{4,6},{5,7},{6,4},{7,5},{8,10},{9,11},{10,... | collective-permute-start | bytes 3145736 | tf_op jit(solution)/shard_map/ppermute | solution.py:20
  102.8 5.6 %copy-start.12 = (bf16[4,272,128]{2,1,0:T(8,128)(2,1)}, bf16[4,272,128]{2,1,0:T(8,128)(2,1)S(1)}, u32[]{:S(2)}) copy-start(bf16[4,272,128]{2,1,0:T(8,128)(2,1)S(1)} %far_tiles.8.a_ref) | copy-start | bytes 835588
  106.0 14.7 %copy-start.24 = (bf16[128,1024]{1,0:T(8,128)(2,1)S(1)}, bf16[128,1024]{1,0:T(8,128)(2,1)}, u32[]{:S(2)}) copy-start(bf16[128,1024]{1,0:T(8,128)(2,1)} %v1_ref.1) | copy-start | bytes 786436
  108.4 9.2 %copy-start.10 = (bf16[4,272,128]{2,1,0:T(8,128)(2,1)}, bf16[4,272,128]{2,1,0:T(8,128)(2,1)S(1)}, u32[]{:S(2)}) copy-start(bf16[4,272,128]{2,1,0:T(8,128)(2,1)S(1)} %far_tiles.10.a_ref) | copy-start | bytes 835588
  118.6 29.6 %collective-permute-start.30 = (bf16[2,512,256]{2,1,0:T(8,128)(2,1)}, bf16[2,512,256]{2,1,0:T(8,128)(2,1)}, u32[]{:S(2)}, u32[]{:S(2)}) collective-permute-start(bf16[2,512,256]{2,1,0:T(8,128)(2,1)} %slice_bitcast_fusion.1), channel_id=1, source_target_pairs={{0,1},{1,0},{2,3},{3,2},{4,5},{5,4},{6,7},{7,6},{8,9},{9,8},{10,11... | collective-permute-start | bytes 1572872 | tf_op jit(solution)/shard_map/ppermute | solution.py:20
  118.6 25.9 %collective-permute-start.17 = (bf16[4,272,128]{2,1,0:T(8,128)(2,1)}, bf16[4,272,128]{2,1,0:T(8,128)(2,1)}, u32[]{:S(2)}, u32[]{:S(2)}) collective-permute-start(bf16[4,272,128]{2,1,0:T(8,128)(2,1)} %far_tiles.9), channel_id=1, source_target_pairs={{0,4},{4,0},{8,12},{12,8},{16,20},{20,16},{24,28},{28,24},{1,5},{5... | collective-permute-start | bytes 835592 | tf_op jit(solution)/shard_map/ppermute | solution.py:20
  119.1 27.3 %collective-permute-start.25 = (bf16[4,272,128]{2,1,0:T(8,128)(2,1)}, bf16[4,272,128]{2,1,0:T(8,128)(2,1)}, u32[]{:S(2)}, u32[]{:S(2)}) collective-permute-start(bf16[4,272,128]{2,1,0:T(8,128)(2,1)} %far_tiles.11), channel_id=1, source_target_pairs={{0,4},{4,0},{8,12},{12,8},{16,20},{20,16},{24,28},{28,24},{1,5},{5... | collective-permute-start | bytes 835592 | tf_op jit(solution)/shard_map/ppermute | solution.py:20
  120.6 16.8 %copy-start.25 = (bf16[128,1024]{1,0:T(8,128)(2,1)}, bf16[128,1024]{1,0:T(8,128)(2,1)S(1)}, u32[]{:S(2)}) copy-start(bf16[128,1024]{1,0:T(8,128)(2,1)S(1)} %collective-permute-done.21.k0_ref) | copy-start | bytes 786436
  120.6 16.8 %collective-permute-start.22 = (bf16[128,1024]{1,0:T(8,128)(2,1)S(1)}, bf16[128,1024]{1,0:T(8,128)(2,1)S(1)}, u32[]{:S(2)}, u32[]{:S(2)}) collective-permute-start(bf16[128,1024]{1,0:T(8,128)(2,1)S(1)} %copy-done.24), channel_id=1, source_target_pairs={{0,4},{4,8},{8,12},{12,16},{16,20},{20,24},{24,28},{1,5},{5,9},{9,... | collective-permute-start | bytes 786440 | tf_op jit(solution)/shard_map/ppermute | solution.py:31
  155.7 7.5 %copy-start.2 = (f32[1024,512]{1,0:T(8,128)S(1)}, f32[1024,512]{1,0:T(8,128)}, u32[]{:S(2)}) copy-start(f32[1024,512]{1,0:T(8,128)} %copy-done) | copy-start | bytes 6291460
  155.7 7.5 %copy-start.7 = (bf16[512,1024]{1,0:T(8,128)(2,1)S(1)}, bf16[512,1024]{1,0:T(8,128)(2,1)}, u32[]{:S(2)}) copy-start(bf16[512,1024]{1,0:T(8,128)(2,1)} %copy-done.5) | copy-start | bytes 3145732
  160.5 2.6 %collective-permute-start.36 = (bf16[2,512,256]{2,1,0:T(8,128)(2,1)S(1)}, bf16[2,512,256]{2,1,0:T(8,128)(2,1)S(1)}, u32[]{:S(2)}, u32[]{:S(2)}) collective-permute-start(bf16[2,512,256]{2,1,0:T(8,128)(2,1)S(1)} %slice_bitcast_fusion), channel_id=1, source_target_pairs={{0,1},{1,0},{2,3},{3,2},{4,5},{5,4},{6,7},{7,6},{8,9},{9,8},{10,11... | collective-permute-start | bytes 1572872 | tf_op jit(solution)/shard_map/ppermute | solution.py:20
  160.6 17.8 %collective-permute-start.31 = (bf16[4,272,128]{2,1,0:T(8,128)(2,1)S(1)}, bf16[4,272,128]{2,1,0:T(8,128)(2,1)S(1)}, u32[]{:S(2)}, u32[]{:S(2)}) collective-permute-start(bf16[4,272,128]{2,1,0:T(8,128)(2,1)S(1)} %far_tiles.13), channel_id=1, source_target_pairs={{0,4},{4,0},{8,12},{12,8},{16,20},{20,16},{24,28},{28,24},{1,5},{5... | collective-permute-start | bytes 835592 | tf_op jit(solution)/shard_map/ppermute | solution.py:20
  163.2 4.3 %copy-start.8 = (bf16[2,512,256]{2,1,0:T(8,128)(2,1)}, bf16[2,512,256]{2,1,0:T(8,128)(2,1)S(1)}, u32[]{:S(2)}) copy-start(bf16[2,512,256]{2,1,0:T(8,128)(2,1)S(1)} %collective-permute-done.36.k3_ref.v3_ref) | copy-start | bytes 1572868
  167.5 31.9 %copy-start.35 = (f32[16]{0:T(128)S(1)}, f32[16]{0:T(128)}, u32[]{:S(2)}) copy-start(f32[16]{0:T(128)} %param.18) | copy-start | bytes 196
  167.5 15.9 %collective-permute-start.37 = (bf16[4,272,128]{2,1,0:T(8,128)(2,1)}, bf16[4,272,128]{2,1,0:T(8,128)(2,1)}, u32[]{:S(2)}, u32[]{:S(2)}) collective-permute-start(bf16[4,272,128]{2,1,0:T(8,128)(2,1)} %far_tiles.15), channel_id=1, source_target_pairs={{0,4},{4,0},{8,12},{12,8},{16,20},{20,16},{24,28},{28,24},{1,5},{5... | collective-permute-start | bytes 835592 | tf_op jit(solution)/shard_map/ppermute | solution.py:20
  169.3 13.5 %collective-permute-start.18 = (bf16[272,128]{1,0:T(8,128)(2,1)}, bf16[272,128]{1,0:T(8,128)(2,1)S(1)}, u32[]{:S(2)}, u32[]{:S(2)}) collective-permute-start(bf16[272,128]{1,0:T(8,128)(2,1)} %get-tuple-element.45), channel_id=1, source_target_pairs={{0,24},{4,28},{8,0},{12,4},{16,8},{20,12},{24,16},{28,20},{1,25},{... | collective-permute-start | bytes 208904 | tf_op jit(solution)/shard_map/ppermute | solution.py:25
  169.3 14.1 %collective-permute-start.19 = (bf16[272,128]{1,0:T(8,128)(2,1)}, bf16[272,128]{1,0:T(8,128)(2,1)S(1)}, u32[]{:S(2)}, u32[]{:S(2)}) collective-permute-start(bf16[272,128]{1,0:T(8,128)(2,1)} %get-tuple-element.46), channel_id=1, source_target_pairs={{0,16},{4,20},{8,24},{12,28},{16,0},{20,4},{24,8},{28,12},{1,17},{... | collective-permute-start | bytes 208904 | tf_op jit(solution)/shard_map/ppermute | solution.py:25
  176.4 17.9 %collective-permute-start.20 = (bf16[272,128]{1,0:T(8,128)(2,1)}, bf16[272,128]{1,0:T(8,128)(2,1)S(1)}, u32[]{:S(2)}, u32[]{:S(2)}) collective-permute-start(bf16[272,128]{1,0:T(8,128)(2,1)} %get-tuple-element.47), channel_id=1, source_target_pairs={{0,8},{4,12},{8,16},{12,20},{16,24},{20,28},{24,0},{28,4},{1,9},{5... | collective-permute-start | bytes 208904 | tf_op jit(solution)/shard_map/ppermute | solution.py:25
  179.1 15.8 %collective-permute-start.26 = (bf16[272,128]{1,0:T(8,128)(2,1)}, bf16[272,128]{1,0:T(8,128)(2,1)}, u32[]{:S(2)}, u32[]{:S(2)}) collective-permute-start(bf16[272,128]{1,0:T(8,128)(2,1)} %get-tuple-element.54), channel_id=1, source_target_pairs={{0,24},{4,28},{8,0},{12,4},{16,8},{20,12},{24,16},{28,20},{1,25},{... | collective-permute-start | bytes 208904 | tf_op jit(solution)/shard_map/ppermute | solution.py:25
  182.8 17.4 %copy-start.27 = (bf16[272,128]{1,0:T(8,128)(2,1)}, bf16[272,128]{1,0:T(8,128)(2,1)S(1)}, u32[]{:S(2)}) copy-start(bf16[272,128]{1,0:T(8,128)(2,1)S(1)} %collective-permute-done.18.refs_1_) | copy-start | bytes 208900
  182.8 12.3 %collective-permute-start.27 = (bf16[272,128]{1,0:T(8,128)(2,1)}, bf16[272,128]{1,0:T(8,128)(2,1)}, u32[]{:S(2)}, u32[]{:S(2)}) collective-permute-start(bf16[272,128]{1,0:T(8,128)(2,1)} %get-tuple-element.55), channel_id=1, source_target_pairs={{0,16},{4,20},{8,24},{12,28},{16,0},{20,4},{24,8},{28,12},{1,17},{... | collective-permute-start | bytes 208904 | tf_op jit(solution)/shard_map/ppermute | solution.py:25
  183.4 16.8 %copy-start.28 = (bf16[272,128]{1,0:T(8,128)(2,1)}, bf16[272,128]{1,0:T(8,128)(2,1)S(1)}, u32[]{:S(2)}) copy-start(bf16[272,128]{1,0:T(8,128)(2,1)S(1)} %collective-permute-done.19.refs_2_) | copy-start | bytes 208900
  183.4 15.3 %collective-permute-start.28 = (bf16[272,128]{1,0:T(8,128)(2,1)}, bf16[272,128]{1,0:T(8,128)(2,1)}, u32[]{:S(2)}, u32[]{:S(2)}) collective-permute-start(bf16[272,128]{1,0:T(8,128)(2,1)} %get-tuple-element.56), channel_id=1, source_target_pairs={{0,8},{4,12},{8,16},{12,20},{16,24},{20,28},{24,0},{28,4},{1,9},{5... | collective-permute-start | bytes 208904 | tf_op jit(solution)/shard_map/ppermute | solution.py:25
  183.4 15.9 %collective-permute-start.32 = (bf16[272,128]{1,0:T(8,128)(2,1)}, bf16[272,128]{1,0:T(8,128)(2,1)}, u32[]{:S(2)}, u32[]{:S(2)}) collective-permute-start(bf16[272,128]{1,0:T(8,128)(2,1)} %get-tuple-element.60), channel_id=1, source_target_pairs={{0,24},{4,28},{8,0},{12,4},{16,8},{20,12},{24,16},{28,20},{1,25},{... | collective-permute-start | bytes 208904 | tf_op jit(solution)/shard_map/ppermute | solution.py:25
  194.3 5.9 %copy-start.29 = (bf16[272,128]{1,0:T(8,128)(2,1)}, bf16[272,128]{1,0:T(8,128)(2,1)S(1)}, u32[]{:S(2)}) copy-start(bf16[272,128]{1,0:T(8,128)(2,1)S(1)} %collective-permute-done.20.refs_3_) | copy-start | bytes 208900
  194.3 9.5 %collective-permute-start.33 = (bf16[272,128]{1,0:T(8,128)(2,1)}, bf16[272,128]{1,0:T(8,128)(2,1)S(1)}, u32[]{:S(2)}, u32[]{:S(2)}) collective-permute-start(bf16[272,128]{1,0:T(8,128)(2,1)} %get-tuple-element.61), channel_id=1, source_target_pairs={{0,16},{4,20},{8,24},{12,28},{16,0},{20,4},{24,8},{28,12},{1,17},{... | collective-permute-start | bytes 208904 | tf_op jit(solution)/shard_map/ppermute | solution.py:25
  194.9 8.8 %collective-permute-start.34 = (bf16[272,128]{1,0:T(8,128)(2,1)}, bf16[272,128]{1,0:T(8,128)(2,1)S(1)}, u32[]{:S(2)}, u32[]{:S(2)}) collective-permute-start(bf16[272,128]{1,0:T(8,128)(2,1)} %get-tuple-element.62), channel_id=1, source_target_pairs={{0,8},{4,12},{8,16},{12,20},{16,24},{20,28},{24,0},{28,4},{1,9},{5... | collective-permute-start | bytes 208904 | tf_op jit(solution)/shard_map/ppermute | solution.py:25
  195.1 11.0 %collective-permute-start.38 = (bf16[272,128]{1,0:T(8,128)(2,1)}, bf16[272,128]{1,0:T(8,128)(2,1)S(1)}, u32[]{:S(2)}, u32[]{:S(2)}) collective-permute-start(bf16[272,128]{1,0:T(8,128)(2,1)} %get-tuple-element.66), channel_id=1, source_target_pairs={{0,24},{4,28},{8,0},{12,4},{16,8},{20,12},{24,16},{28,20},{1,25},{... | collective-permute-start | bytes 208904 | tf_op jit(solution)/shard_map/ppermute | solution.py:25
  198.7 7.6 %collective-permute-start.39 = (bf16[272,128]{1,0:T(8,128)(2,1)}, bf16[272,128]{1,0:T(8,128)(2,1)S(1)}, u32[]{:S(2)}, u32[]{:S(2)}) collective-permute-start(bf16[272,128]{1,0:T(8,128)(2,1)} %get-tuple-element.67), channel_id=1, source_target_pairs={{0,16},{4,20},{8,24},{12,28},{16,0},{20,4},{24,8},{28,12},{1,17},{... | collective-permute-start | bytes 208904 | tf_op jit(solution)/shard_map/ppermute | solution.py:25
  199.3 7.1 %collective-permute-start.40 = (bf16[272,128]{1,0:T(8,128)(2,1)}, bf16[272,128]{1,0:T(8,128)(2,1)S(1)}, u32[]{:S(2)}, u32[]{:S(2)}) collective-permute-start(bf16[272,128]{1,0:T(8,128)(2,1)} %get-tuple-element.68), channel_id=1, source_target_pairs={{0,8},{4,12},{8,16},{12,20},{16,24},{20,28},{24,0},{28,4},{1,9},{5... | collective-permute-start | bytes 208904 | tf_op jit(solution)/shard_map/ppermute | solution.py:25
  201.9 9.6 %copy-start.18 = (bf16[256,128]{1,0:T(8,128)(2,1)S(1)}, bf16[256,128]{1,0:T(8,128)(2,1)}, u32[]{:S(2)}) copy-start(bf16[256,128]{1,0:T(8,128)(2,1)} %merge_all.4) | copy-start | bytes 196612
  203.7 9.7 %copy-start.19 = (bf16[256,128]{1,0:T(8,128)(2,1)S(1)}, bf16[256,128]{1,0:T(8,128)(2,1)}, u32[]{:S(2)}) copy-start(bf16[256,128]{1,0:T(8,128)(2,1)} %merge_all.5) | copy-start | bytes 196612
  206.1 7.3 %copy-start.20 = (bf16[256,128]{1,0:T(8,128)(2,1)S(1)}, bf16[256,128]{1,0:T(8,128)(2,1)}, u32[]{:S(2)}) copy-start(bf16[256,128]{1,0:T(8,128)(2,1)} %merge_all.6) | copy-start | bytes 196612
  208.8 7.1 %copy-start.21 = (bf16[256,128]{1,0:T(8,128)(2,1)S(1)}, bf16[256,128]{1,0:T(8,128)(2,1)}, u32[]{:S(2)}) copy-start(bf16[256,128]{1,0:T(8,128)(2,1)} %merge_all.7) | copy-start | bytes 196612
  213.4 3.8 %collective-permute-start.42 = (bf16[128,1024]{1,0:T(8,128)(2,1)S(1)}, bf16[128,1024]{1,0:T(8,128)(2,1)S(1)}, u32[]{:S(2)}, u32[]{:S(2)}) collective-permute-start(bf16[128,1024]{1,0:T(8,128)(2,1)S(1)} %fusion.35), channel_id=1, source_target_pairs={{0,1},{1,0},{2,3},{3,2},{4,5},{5,4},{6,7},{7,6},{8,9},{9,8},{10,11... | collective-permute-start | bytes 786440 | tf_op jit(solution)/shard_map/ppermute | solution.py:20
  215.3 5.6 %collective-permute-start.41 = (bf16[128,1024]{1,0:T(8,128)(2,1)S(1)}, bf16[128,1024]{1,0:T(8,128)(2,1)S(1)}, u32[]{:S(2)}, u32[]{:S(2)}) collective-permute-start(bf16[128,1024]{1,0:T(8,128)(2,1)S(1)} %fusion.38), channel_id=1, source_target_pairs={{0,1},{1,0},{2,3},{3,2},{4,5},{5,4},{6,7},{7,6},{8,9},{9,8},{10,11... | collective-permute-start | bytes 786440 | tf_op jit(solution)/shard_map/ppermute | solution.py:20
  219.0 8.3 %collective-permute-start.43 = (bf16[128,1024]{1,0:T(8,128)(2,1)S(1)}, bf16[128,1024]{1,0:T(8,128)(2,1)S(1)}, u32[]{:S(2)}, u32[]{:S(2)}) collective-permute-start(bf16[128,1024]{1,0:T(8,128)(2,1)S(1)} %fusion.32), channel_id=1, source_target_pairs={{0,2},{1,3},{2,0},{3,1},{4,6},{5,7},{6,4},{7,5},{8,10},{9,11},{10,... | collective-permute-start | bytes 786440 | tf_op jit(solution)/shard_map/ppermute | solution.py:20
  (16 other events, 15.6 us)

commit v4 on v3

--- a/solution.py
+++ b/solution.py
@@ -11,9 +11,17 @@
 PAIR = 2 * DH
 TILE_ROWS = 128
 QB = 256
-CHUNK_HEADS = 4
-STAT_ROWS = 16
+NEAR_HEADS = 4
 EMPTY = -1e38
+
+
+def chunk_heads(heads):
+    large = (3 * heads // 8) // 2 * 2
+    return [large, large, heads - 2 * large]
+
+
+def stat_rows(heads):
+    return -(-3 * heads // 16) * 16
 
 
 def swap(block, axis, distance):
@@ -38,7 +46,7 @@
     step = 2 if tiles % 2 == 0 else 1
     units = [
         (pair, block, head)
-        for pair in range(CHUNK_HEADS // 2)
+        for pair in range(q_ref.shape[1] // PAIR)
         for block in range(rows // QB)
         for head in range(2)
     ]
@@ -127,7 +135,7 @@
 
 def packed(lses):
     rows = [part for x in lses for part in three(x)]
-    rows.append(jnp.zeros((STAT_ROWS - len(rows), rows[0].shape[1]), jnp.float32))
+    rows.append(jnp.zeros((stat_rows(len(lses)) - len(rows), rows[0].shape[1]), jnp.float32))
     return jnp.concatenate(rows, axis=0).astype(jnp.bfloat16)
 
 
@@ -136,7 +144,7 @@
 ):
     vt_ref[0] = jnp.transpose(v2_ref[0])
     vt_ref[1] = jnp.transpose(v3_ref[0])
-    base = CHUNK_HEADS * DH
+    base = q_ref.shape[1]
     lses = {}
 
     def emit(pair, block, head, top, total, sums):
@@ -164,10 +172,10 @@
     )
     for block in range(q_ref.shape[0] // QB):
         stats = packed(
-            [lses[pair, block, head] for pair in range(CHUNK_HEADS // 2) for head in range(2)]
+            [lses[pair, block, head] for pair in range(base // PAIR) for head in range(2)]
         )
         for part in range(QB // TILE_ROWS):
-            out_ref[block * (QB // TILE_ROWS) + part, base : base + STAT_ROWS] = stats[
+            out_ref[block * (QB // TILE_ROWS) + part, base:] = stats[
                 :, part * TILE_ROWS : (part + 1) * TILE_ROWS
             ]
 
@@ -176,13 +184,13 @@
     return stats[3 * head : 3 * head + 1] + stats[3 * head + 1 : 3 * head + 2] + stats[3 * head + 2 : 3 * head + 3]
 
 
-def merge_kernel(a_ref, b_ref, *out_refs):
-    base = CHUNK_HEADS * DH
+def merge_kernel(heads, a_ref, b_ref, *out_refs):
+    base = heads * DH
     for k, out_ref in enumerate(out_refs):
         stats_a = a_ref[k, base:].astype(jnp.float32)
         stats_b = b_ref[k, base:].astype(jnp.float32)
         lses = []
-        for head in range(CHUNK_HEADS):
+        for head in range(heads):
             lse_a = lse_of(stats_a, head)
             lse_b = lse_of(stats_b, head)
             top = jnp.maximum(lse_a, lse_b)
@@ -226,11 +234,11 @@
         out_ref[head * DH : (head + 1) * DH] = o[:DH] / o[DH : DH + 1]
 
 
-def final_kernel(*refs):
+def final_kernel(heads, first, *refs):
     *msg_refs, local_ref, gate_ref, out_ref = refs
-    base = CHUNK_HEADS * DH
+    base = heads * DH
     stats = [r[base:].astype(jnp.float32) for r in msg_refs]
-    for head in range(CHUNK_HEADS):
+    for head in range(heads):
         lses = [lse_of(s, head) for s in stats]
         top = functools.reduce(jnp.maximum, lses)
         ws = [jnp.exp(x - top) for x in lses]
@@ -240,9 +248,10 @@
         for r, w in zip(msg_refs, ws):
             term = w * r[rows].astype(jnp.float32)
             mem = term if mem is None else mem + term
-        gate = gate_ref[0, head : head + 1]
+        gate = gate_ref[first + head : first + head + 1]
+        local_rows = slice((first + head) * DH, (first + head + 1) * DH)
         out_ref[rows] = (
-            (gate * inv) * mem + (1.0 - gate) * local_ref[rows].astype(jnp.float32)
+            (gate * inv) * mem + (1.0 - gate) * local_ref[local_rows]
         ).astype(jnp.bfloat16)
 
 
@@ -271,12 +280,18 @@
     all_rows = ctx_size * row_count
     me = lax.axis_index("mem")
     my_ctx = lax.axis_index("ctx")
-    chunks = heads_here // CHUNK_HEADS
-    width = CHUNK_HEADS * DH
+    sizes = chunk_heads(heads_here)
+    firsts = [sum(sizes[:j]) for j in range(len(sizes))]
+    chunks = len(sizes)
+    near_chunks = heads_here // NEAR_HEADS
+    width = NEAR_HEADS * DH
     pairs = heads_here // 2
 
     half = all_rows // 2
     f32 = jnp.float32
+
+    def after(value, *earlier):
+        return lax.optimization_barrier((value, earlier))[0]
 
     live = jnp.arange(pick_count, dtype=jnp.int32)[None, :] < tile_counts[:, None]
     ids = jnp.transpose(jnp.where(live, tile_ids, -1))
@@ -295,8 +310,6 @@
     hidden = jnp.zeros((row_count, mem_size * hidden_states.shape[1]), jnp.bfloat16)
     for k in range(mem_size):
         hidden = lax.dynamic_update_slice(hidden, have[k], (0, (me ^ k) * hidden_states.shape[1]))
-    queries = jnp.dot(hidden, w_query, preferred_element_type=f32).astype(jnp.bfloat16)
-
     def share(at, cols):
         return jnp.stack(
             [
@@ -306,29 +319,40 @@
         )
 
     def across(at, j):
-        return jnp.stack([share((at ^ k) * features + j * width, width) for k in (2, 3)])
-
-    def after(value, *earlier):
-        return lax.optimization_barrier((value, earlier))[0]
-
-    later_me = after(me, queries)
-    crossed = [swap(across(after(me, h1), 0), "mem", 2)]
-    near = swap(share((later_me ^ 1) * features, features), "mem", 1)
+        return jnp.stack(
+            [share((at ^ k) * features + firsts[j] * DH, sizes[j] * DH) for k in (2, 3)]
+        )
+
+    first_block = across(after(me, h1), 0)
+    queries = jnp.dot(
+        after(hidden, first_block, bits[0]), w_query, preferred_element_type=f32
+    ).astype(jnp.bfloat16)
+
+    crossed = [swap(first_block, "mem", 2)]
 
     q_blocks = [queries] + [turn(queries, "ctx", 2 * k) for k in range(1, turns)]
     q_blocks += [swap(q, "ctx", 1) for q in q_blocks]
-    crossed.append(swap(after(across(later_me, 1), q_blocks[turns]), "mem", 2))
+    later_me = after(me, q_blocks[1])
+    near = swap(share((later_me ^ 1) * features, features), "mem", 1)
+    crossed.append(swap(across(later_me, 1), "mem", 2))
+    window = jnp.stack([local_keys, after(local_values, q_blocks[-1])])
+    window = from_behind(window, "ctx", 1)
     q_halves = [jnp.concatenate(q_blocks[part * turns : (part + 1) * turns], 0) for part in range(2)]
 
-    chunk_pairs = CHUNK_HEADS // 2
     near_flops = 2 * 2 * half * 2 * mem_rows * features
-    scratch = [
-        pltpu.VMEM((2, width, mem_rows), jnp.bfloat16),
-        pltpu.VMEM((2, 2, mem_rows, QB), f32),
-    ]
+
+    def scratch(cols):
+        return [
+            pltpu.VMEM((2, cols, mem_rows), jnp.bfloat16),
+            pltpu.VMEM((2, 2, mem_rows, QB), f32),
+        ]
+
+    chunk_pairs = NEAR_HEADS // 2
     near_state = []
+    q_halves[0] = after(q_halves[0], crossed[0])
     for part in range(2):
         if part == 1:
+            q_halves[1] = after(q_halves[1], window, near_state[0][1])
             crossed.append(
                 swap(after(across(later_me, 2), crossed[0], near_state[0][1]), "mem", 2)
             )
@@ -337,11 +361,11 @@
                 near_kernel,
                 grid_spec=pltpu.PrefetchScalarGridSpec(
                     num_scalar_prefetch=1,
-                    grid=(chunks,),
+                    grid=(near_chunks,),
                     in_specs=[
                         pl.BlockSpec((half, width), lambda p, m: (0, p)),
-                        pl.BlockSpec((mem_rows, width), lambda p, m: (0, m[0] * chunks + p)),
-                        pl.BlockSpec((mem_rows, width), lambda p, m: (0, m[0] * chunks + p)),
+                        pl.BlockSpec((mem_rows, width), lambda p, m: (0, m[0] * near_chunks + p)),
+                        pl.BlockSpec((mem_rows, width), lambda p, m: (0, m[0] * near_chunks + p)),
                         pl.BlockSpec((1, mem_rows, width), lambda p, m: (0, 0, p)),
                         pl.BlockSpec((1, mem_rows, width), lambda p, m: (1, 0, p)),
                         pl.BlockSpec((1, half), lambda p, m: (0, 0)),
@@ -350,7 +374,7 @@
                         pl.BlockSpec((width, half), lambda p, m: (p, 0)),
                         pl.BlockSpec((chunk_pairs, 8, half), lambda p, m: (p, 0, 0)),
                     ],
-                    scratch_shapes=scratch,
+                    scratch_shapes=scratch(width),
                 ),
                 out_shape=[
                     jax.ShapeDtypeStruct((features, half), f32),
@@ -366,11 +390,6 @@
             )(me.reshape(1), q_halves[part], memory_keys, memory_values, near, near, bits[part])
         )
 
-    crossed.append(swap(after(across(later_me, 3), crossed[1], near_state[1][1]), "mem", 2))
-
-    window, _ = lax.optimization_barrier(((local_keys, local_values), q_blocks[-1]))
-    earlier_k = from_behind(window[0], "ctx", 1)
-    earlier_v = from_behind(window[1], "ctx", 1)
     own_queries, _ = lax.optimization_barrier((queries, near_state[1][1]))
     pair_spec = pl.BlockSpec((row_count, PAIR), lambda p, c: (0, p))
     local_out = pl.pallas_call(
@@ -378,7 +397,13 @@
         grid_spec=pltpu.PrefetchScalarGridSpec(
             num_scalar_prefetch=1,
             grid=(pairs,),
-            in_specs=[pair_spec] * 5,
+            in_specs=[
+                pair_spec,
+                pl.BlockSpec((None, row_count, PAIR), lambda p, c: (0, 0, p)),
+                pair_spec,
+                pl.BlockSpec((None, row_count, PAIR), lambda p, c: (1, 0, p)),
+                pair_spec,
+            ],
             out_specs=pl.BlockSpec((PAIR, row_count), lambda p, c: (p, 0)),
         ),
         out_shape=jax.ShapeDtypeStruct((features, row_count), f32),
@@ -388,22 +413,29 @@
             bytes_accessed=2 << 20,
         ),
         name="local_window",
-    )(my_ctx.reshape(1), own_queries, earlier_k, local_keys, earlier_v, local_values)
+    )(my_ctx.reshape(1), own_queries, window, local_keys, window, local_values)
 
     gate = jax.nn.sigmoid(gate_bias)
-    gate_rows = jnp.broadcast_to(gate[:, None], (heads_here, row_count)).reshape(
-        chunks, CHUNK_HEADS, row_count
-    )
+    gate_rows = jnp.broadcast_to(gate[:, None], (heads_here, row_count))
+    cols = w_output.shape[1] // mem_size
+    over_rows = (((0,), (0,)), ((), ()))
+
+    def weights(k, first, count):
+        return lax.dynamic_slice(w_output, (first * DH, (me ^ k) * cols), (count * DH, cols))
+
     combined = []
     messages = []
     merges = []
-    msg_rows = width + STAT_ROWS
+    early = None
     for j in range(chunks):
+        heads, first = sizes[j], firsts[j]
+        wide = heads * DH
+        msg_rows = wide + stat_rows(heads)
         tokens = [near_state[0][1], near_state[1][1]]
         if j >= 2:
             tokens += messages[j - 2] + messages[j - 1]
         if j == chunks - 1:
-            tokens += [local_out] + merges[: j - 1]
+            tokens += [local_out] + merges
         far2 = after(crossed[j], *tokens)
         far3 = swap(far2[1], "mem", 1)
         message = [None, None]
@@ -413,22 +445,25 @@
                 far_kernel,
                 grid=(1,),
                 in_specs=[
-                    pl.BlockSpec((half, width), lambda i, j=j: (0, j)),
-                    pl.BlockSpec((None, 1, mem_rows, width), lambda i: (0, 0, 0, 0)),
-                    pl.BlockSpec((None, 1, mem_rows, width), lambda i: (0, 1, 0, 0)),
-                    pl.BlockSpec((1, mem_rows, width), lambda i: (0, 0, 0)),
-                    pl.BlockSpec((1, mem_rows, width), lambda i: (1, 0, 0)),
+                    pl.BlockSpec((pl.Element(half), pl.Element(wide)), lambda i, c=first * DH: (0, c)),
+                    pl.BlockSpec((None, 1, mem_rows, wide), lambda i: (0, 0, 0, 0)),
+                    pl.BlockSpec((None, 1, mem_rows, wide), lambda i: (0, 1, 0, 0)),
+                    pl.BlockSpec((1, mem_rows, wide), lambda i: (0, 0, 0)),
+                    pl.BlockSpec((1, mem_rows, wide), lambda i: (1, 0, 0)),
                     pl.BlockSpec((1, half), lambda i: (0, 0)),
-                    pl.BlockSpec((width, half), lambda i, j=j: (j, 0)),
-                    pl.BlockSpec((chunk_pairs, 8, half), lambda i, j=j: (j, 0, 0)),
+                    pl.BlockSpec((pl.Element(wide), pl.Element(half)), lambda i, c=first * DH: (c, 0)),
+                    pl.BlockSpec(
+                        (pl.Element(heads // 2), pl.Element(8), pl.Element(half)),
+                        lambda i, c=first // 2: (c, 0, 0),
+                    ),
                 ],
                 out_specs=pl.BlockSpec((turns, msg_rows, row_count), lambda i: (0, 0, 0)),
                 out_shape=jax.ShapeDtypeStruct((turns, msg_rows, row_count), jnp.bfloat16),
-                scratch_shapes=scratch,
+                scratch_shapes=scratch(wide),
                 compiler_params=pltpu.CompilerParams(vmem_limit_bytes=48 << 20),
                 cost_estimate=pl.CostEstimate(
-                    flops=near_flops // chunks,
-                    transcendentals=half * 2 * mem_rows * CHUNK_HEADS,
+                    flops=near_flops * heads // heads_here,
+                    transcendentals=half * 2 * mem_rows * heads,
                     bytes_accessed=3 << 20,
                 ),
                 name="far_tiles",
@@ -436,35 +471,32 @@
         messages.append(message)
         other = swap(message[1], "ctx", 1)
         merged = pl.pallas_call(
-            merge_kernel,
+            functools.partial(merge_kernel, heads),
             out_shape=[jax.ShapeDtypeStruct((msg_rows, row_count), jnp.bfloat16)] * turns,
             name="merge_pair",
         )(message[0], other)
         merges.append(merged[0])
         answers = [merged[0]] + [turn(merged[k], "ctx", -2 * k) for k in range(1, turns)]
-        combined.append(
-            pl.pallas_call(
-                final_kernel,
-                grid=(1,),
-                in_specs=[pl.BlockSpec((msg_rows, row_count), lambda i: (0, 0))] * turns
-                + [
-                    pl.BlockSpec((width, row_count), lambda i, j=j: (j, 0)),
-                    pl.BlockSpec((1, CHUNK_HEADS, row_count), lambda i, j=j: (j, 0, 0)),
-                ],
-                out_specs=pl.BlockSpec((width, row_count), lambda i: (0, 0)),
-                out_shape=jax.ShapeDtypeStruct((width, row_count), jnp.bfloat16),
-                name="merge_all",
-            )(*answers, local_out, gate_rows)
-        )
-    early = jnp.concatenate(combined[:-1], axis=0)
-    cols = w_output.shape[1] // mem_size
-    over_rows = (((0,), (0,)), ((), ()))
+        if j == chunks - 1:
+            answers[0] = after(answers[0], early)
+        mixed = pl.pallas_call(
+            functools.partial(final_kernel, heads, first),
+            out_shape=jax.ShapeDtypeStruct((wide, row_count), jnp.bfloat16),
+            name="merge_all",
+        )(*answers, local_out, gate_rows)
+        combined.append(mixed)
+        if j == chunks - 2:
+            mixed = jnp.concatenate(combined, axis=0)
+            early = [
+                lax.dot_general(
+                    mixed, weights(k, 0, first + heads), over_rows, preferred_element_type=f32
+                )
+                for k in range(mem_size)
+            ]
 
     def piece(k):
-        w = lax.dynamic_slice(w_output, (0, (me ^ k) * cols), (features, cols))
-        split = early.shape[0]
-        return lax.dot_general(early, w[:split], over_rows, preferred_element_type=f32) + lax.dot_general(
-            combined[-1], w[split:], over_rows, preferred_element_type=f32
+        return early[k] + lax.dot_general(
+            combined[-1], weights(k, firsts[-1], sizes[-1]), over_rows, preferred_element_type=f32
         )
 
     away = piece(2) + swap(piece(3).astype(jnp.bfloat16), "mem", 1).astype(f32)

time: 231 us -> 219 us (0.948)
  starting transfers between devices: 55.1 us -> 41.7 us
  Pallas kernels: 67.9 us -> 62.5 us
  other arithmetic: 5.28 us -> 9.06 us
  local copies, waits for them, and re-layouts: 21.9 us -> 24.5 us
  waiting for transfers between devices: 61.1 us -> 63.7 us
    ppermute x18 -> x15, waiting for transfers between devices: 16.6 us -> 41.4 us  [turn(): lax.ppermute(block, axis, [(i, (i + distance) % size) for i in range(size)])]
    ppermute x2 -> x1, waiting for transfers between devices: 14.2 us -> 0.01 us  [from_behind(): return lax.ppermute(block, axis, route)]
    ppermute x18 -> x15, starting transfers between devices: 30.6 us -> 20.1 us  [turn(): lax.ppermute(block, axis, [(i, (i + distance) % size) for i in range(size)])]
    ppermute x24 -> x21, waiting for transfers between devices: 30.2 us -> 22.3 us  [swap(): lax.ppermute(block, axis, [(i, i ^ distance) for i in range(lax.axis_size...]
    pallas_call x16 -> x12, Pallas kernels: 40.4 us -> 34.7 us  [the longest x6 22.6 us: on_device(): pl.pallas_call(far_kernel, grid=(1,), in_specs=[pl.BlockSpec((pl.Element(...]
    another operation x2 -> x7, local copies, waits for them, and re-layouts: 4.36 us -> 8.82 us  [share(): jnp.stack([lax.dynamic_slice(memory_keys, (0, at), (mem_rows, cols)), lax...]
    unnamed x75 -> x70, local copies, waits for them, and re-layouts: 13.5 us -> 9.41 us
    another operation x12 -> x10, other arithmetic: 1.78 us -> 4.32 us  [the longest x9 4.26 us: across(): jnp.stack([share((at ^ k) * features + firsts[j] * DH, sizes[j] * DH) for...]
  transfers between devices with their start and end apart: 44 -> 37, of which waited for: 12 -> 14; matrix products, arithmetic and copies ran while one was open for 7% -> 13% of each run, Pallas kernels for 29% -> 25%
where the time goes in v4:
time: 219 us; the launch traced here: 218 us
  waiting for transfers between devices  63.7 us (29%)
  Pallas kernels  62.5 us (29%)
  starting transfers between devices  41.7 us (19%)
  local copies, waits for them, and re-layouts  24.5 us (11%)
  matrix products  15.7 us (7%)
  other arithmetic  9.06 us (4%)
    ppermute x15, waiting for transfers between devices, turn(): lax.ppermute(block, axis, [(i, (i + distance) % size) for i in range(size)])  41.4 us
    pallas_call x6, Pallas kernels, on_device(): pl.pallas_call(far_kernel, grid=(1,), in_specs=[pl.BlockSpec((pl.Element(...  22.6 us
    ppermute x21, waiting for transfers between devices, swap(): lax.ppermute(block, axis, [(i, i ^ distance) for i in range(lax.axis_size...  22.3 us
    pallas_call x2, Pallas kernels, on_device(): pl.pallas_call(near_kernel, grid_spec=pltpu.PrefetchScalarGridSpec(num_sc...  21.6 us
    ppermute x15, starting transfers between devices, turn(): lax.ppermute(block, axis, [(i, (i + distance) % size) for i in range(size)])  20.1 us
    ppermute x21, starting transfers between devices, swap(): lax.ppermute(block, axis, [(i, i ^ distance) for i in range(lax.axis_size...  18 us
    unnamed x70, local copies, waits for them, and re-layouts  9.41 us
    another operation x7, local copies, waits for them, and re-layouts, share(): jnp.stack([lax.dynamic_slice(memory_keys, (0, at), (mem_rows, cols)), lax...  8.82 us
  transfers between devices with their start and end apart: 37, of which 14 were waited for; matrix products, arithmetic and copies ran while one was open for 13% of the time, Pallas kernels for 25%

profile of v4, /device:TPU:0, one launch (start us, length us, event | category | flops | bytes accessed | tf_op | source)
XLA Modules:
  0.0 217.7 jit_solution(7795232441564308646)
XLA Ops:
  0.7 3.0 %collective-permute-start.3 = (s32[16,128]{1,0:T(8,128)S(1)}, s32[16,128]{1,0:T(8,128)S(1)}, u32[]{:S(2)}, u32[]{:S(2)}) collective-permute-start(s32[16,128]{1,0:T(8,128)S(1)} %get-tuple-element.76), channel_id=1, source_target_pairs={{0,4},{4,0},{8,12},{12,8},{16,20},{20,16},{24,28},{28,24},{1,5},{5... | collective-permute-start | bytes 24584 | tf_op jit(solution)/shard_map/ppermute | solution.py:28
  3.7 1.5 collective-permute-start.1
  5.3 4.1 %collective-permute-start.6 = (s32[2,16,128]{2,1,0:T(8,128)S(1)}, s32[2,16,128]{2,1,0:T(8,128)S(1)}, u32[]{:S(2)}, u32[]{:S(2)}) collective-permute-start(s32[2,16,128]{2,1,0:T(8,128)S(1)} %get-tuple-element.74), channel_id=1, source_target_pairs={{0,24},{4,28},{8,0},{12,4},{16,8},{20,12},{24,16},{28,20},{1,25},{... | collective-permute-start | bytes 49160 | tf_op jit(solution)/shard_map/ppermute | solution.py:33
  11.5 2.5 %collective-permute-done.5 = s32[2,16,128]{2,1,0:T(8,128)S(1)} collective-permute-done((s32[2,16,128]{2,1,0:T(8,128)S(1)}, s32[2,16,128]{2,1,0:T(8,128)S(1)}, u32[]{:S(2)}, u32[]{:S(2)}) %collective-permute-start.5) | collective-permute-done | bytes 16416 | tf_op jit(solution)/shard_map/ppermute | solution.py:33
  15.1 1.7 dynamic-slice_bitcast_fusion.8
  17.1 1.5 constant_dynamic-update-slice_fusion.2
  19.6 1.4 pad_maximum_fusion.1
  21.0 1.3 convolution_convert_fusion.q_ref
  22.4 10.1 %collective-permute-done.7 = bf16[128,1024]{1,0:T(8,128)(2,1)} collective-permute-done((bf16[128,1024]{1,0:T(8,128)(2,1)S(1)}, bf16[128,1024]{1,0:T(8,128)(2,1)}, u32[]{:S(2)}, u32[]{:S(2)}) %collective-permute-start.7) | collective-permute-done | bytes 262176 | tf_op jit(solution)/shard_map/ppermute | solution.py:33
  32.5 1.3 dynamic-slice_bitcast_fusion
  33.8 1.3 dynamic-slice_bitcast_fusion.1
  35.1 1.5 pad_maximum_fusion
  36.6 1.5 collective-permute-start.10
  38.1 1.2 dynamic-slice_bitcast_fusion.4
  39.3 1.2 dynamic-slice_bitcast_fusion.5
  40.7 1.3 pad_maximum_fusion.2
  42.6 5.3 %collective-permute-done.9 = bf16[128,1024]{1,0:T(8,128)(2,1)} collective-permute-done((bf16[128,1024]{1,0:T(8,128)(2,1)S(1)}, bf16[128,1024]{1,0:T(8,128)(2,1)}, u32[]{:S(2)}, u32[]{:S(2)}) %collective-permute-start.9) | collective-permute-done | bytes 262176 | tf_op jit(solution)/shard_map/ppermute | solution.py:33
  47.9 1.5 collective-permute-start.15
  49.4 8.0 %collective-permute-done.8 = bf16[128,1024]{1,0:T(8,128)(2,1)} collective-permute-done((bf16[128,1024]{1,0:T(8,128)(2,1)S(1)}, bf16[128,1024]{1,0:T(8,128)(2,1)}, u32[]{:S(2)}, u32[]{:S(2)}) %collective-permute-start.8) | collective-permute-done | bytes 262176 | tf_op jit(solution)/shard_map/ppermute | solution.py:33
  57.4 1.5 collective-permute-start.12
  61.7 5.0 %collective-permute-done.12 = bf16[128,1024]{1,0:T(8,128)(2,1)S(1)} collective-permute-done((bf16[128,1024]{1,0:T(8,128)(2,1)S(1)}, bf16[128,1024]{1,0:T(8,128)(2,1)S(1)}, u32[]{:S(2)}, u32[]{:S(2)}) %collective-permute-start.12) | collective-permute-done | bytes 262176 | tf_op jit(solution)/shard_map/ppermute | solution.py:28
  66.7 1.5 collective-permute-start.13
  68.2 4.1 %collective-permute-done.14 = bf16[128,1024]{1,0:T(8,128)(2,1)S(1)} collective-permute-done((bf16[128,1024]{1,0:T(8,128)(2,1)}, bf16[128,1024]{1,0:T(8,128)(2,1)S(1)}, u32[]{:S(2)}, u32[]{:S(2)}) %collective-permute-start.14) | collective-permute-done | bytes 262176 | tf_op jit(solution)/shard_map/ppermute | solution.py:28
  72.3 3.6 %collective-permute-start.16 = (bf16[2,128,1024]{2,1,0:T(8,128)(2,1)S(1)}, bf16[2,128,1024]{2,1,0:T(8,128)(2,1)S(1)}, u32[]{:S(2)}, u32[]{:S(2)}) collective-permute-start(bf16[2,128,1024]{2,1,0:T(8,128)(2,1)S(1)} %pad_maximum_fusion.6), channel_id=1, source_target_pairs={{0,4},{4,8},{8,12},{12,16},{16,20},{20,24},{24,28},{1,5},{5,9},{9,... | collective-permute-start | bytes 1572872 | tf_op jit(solution)/shard_map/ppermute | solution.py:39
  76.0 1.2 pad_maximum_fusion.3.q_ref
  77.2 1.2 pad_maximum_fusion.4.q_ref
  78.4 10.9 %near_tiles.2 = (f32[1024,512]{1,0:T(8,128)S(1)}, f32[8,8,512]{2,1,0:T(8,128)S(1)}) custom-call(s32[1]{0:T(128)} %bitcast.14.m_ref, bf16[512,1024]{1,0:T(8,128)(2,1)S(1)} %pad_maximum_fusion.3.q_ref, bf16[512,4096]{1,0:T(8,128)(2,1)} %k0_ref.3, bf16[512,4096]{1,0:T(8,128)(2,1)} %v0_ref.3, bf16[2,512,1024]{2,1,0:T(8,128)(2,1)} %collective-permute-done.11.k1_ref.v1_ref, ...), custom_call_target="tpu_custom_call" | custom-call | flops 2147483648 | bytes 8388608 | tf_op jit(solution)/shard_map/near_tiles/pallas_call | solution.py:360
  89.4 1.3 copy-done
  90.7 10.7 %near_tiles.3 = (f32[1024,512]{1,0:T(8,128)S(1)}, f32[8,8,512]{2,1,0:T(8,128)S(1)}) custom-call(s32[1]{0:T(128)} %bitcast.14.m_ref, bf16[512,1024]{1,0:T(8,128)(2,1)S(1)} %pad_maximum_fusion.4.q_ref, bf16[512,4096]{1,0:T(8,128)(2,1)} %k0_ref.3, bf16[512,4096]{1,0:T(8,128)(2,1)} %v0_ref.3, bf16[2,512,1024]{2,1,0:T(8,128)(2,1)} %collective-permute-done.11.k1_ref.v1_ref, ...), custom_call_target="tpu_custom_call" | custom-call | flops 2147483648 | bytes 8388608 | tf_op jit(solution)/shard_map/near_tiles/pallas_call | solution.py:360
  101.4 5.9 %collective-permute-done.22.k2_ref.v2_ref = bf16[2,2,512,384]{3,2,1,0:T(8,128)(2,1)S(1)} collective-permute-done((bf16[2,2,512,384]{3,2,1,0:T(8,128)(2,1)}, bf16[2,2,512,384]{3,2,1,0:T(8,128)(2,1)S(1)}, u32[]{:S(2)}, u32[]{:S(2)}) %collective-permute-start.22) | collective-permute-done | bytes 1572896 | tf_op jit(solution)/shard_map/ppermute | solution.py:28
  109.3 1.5 collective-permute-start.28
  110.8 4.2 %far_tiles.9 = bf16[4,416,128]{2,1,0:T(8,128)(2,1)} custom-call(bf16[512,1024]{1,0:T(8,128)(2,1)S(1)} %pad_maximum_fusion.4.q_ref, bf16[2,2,512,384]{3,2,1,0:T(8,128)(2,1)S(1)} %collective-permute-done.22.k2_ref.v2_ref, bf16[2,2,512,384]{3,2,1,0:T(8,128)(2,1)S(1)} %collective-permute-done.22.k2_ref.v2_ref, ...), custom_call_target="tpu_custom_call" | custom-call | flops 805306368 | bytes 3145728 | tf_op jit(solution)/shard_map/far_tiles/pallas_call | solution.py:444
  115.0 1.5 collective-permute-start.24
  116.5 4.2 %far_tiles.7 = bf16[4,416,128]{2,1,0:T(8,128)(2,1)} custom-call(bf16[512,1024]{1,0:T(8,128)(2,1)S(1)} %pad_maximum_fusion.4.q_ref, bf16[2,2,512,384]{3,2,1,0:T(8,128)(2,1)S(1)} %collective-permute-done.10.k2_ref.v2_ref, bf16[2,2,512,384]{3,2,1,0:T(8,128)(2,1)S(1)} %collective-permute-done.10.k2_ref.v2_ref, ...), custom_call_target="tpu_custom_call" | custom-call | flops 805306368 | bytes 3145728 | tf_op jit(solution)/shard_map/far_tiles/pallas_call | solution.py:444
  121.2 6.3 %local_window.1.refs_4_ = f32[1024,128]{1,0:T(8,128)} custom-call(s32[1]{0:T(128)} %bitcast.21.ctx_ref, bf16[128,1024]{1,0:T(8,128)(2,1)} %copy-done.21, bf16[2,128,1024]{2,1,0:T(8,128)(2,1)} %copy-done.22, bf16[128,1024]{1,0:T(8,128)(2,1)} %k1_ref.1, bf16[2,128,1024]{2,1,0:T(8,128)(2,1)} %copy-done.22, bf16[128,1024]{1,0:T(8,128)(2,1)} %v1_ref.1), custom_call_target="tpu_custom_call" | custom-call | flops 134217728 | bytes 2097152 | tf_op jit(solution)/shard_map/local_window/pallas_call | solution.py:395
  127.5 1.6 copy-done.1
  129.1 1.2 copy-done.6
  131.5 3.5 %far_tiles.8.a_ref = bf16[4,416,128]{2,1,0:T(8,128)(2,1)S(1)} custom-call(bf16[512,1024]{1,0:T(8,128)(2,1)S(1)} %copy-done.6, bf16[2,2,512,384]{3,2,1,0:T(8,128)(2,1)S(1)} %collective-permute-done.22.k2_ref.v2_ref, bf16[2,2,512,384]{3,2,1,0:T(8,128)(2,1)S(1)} %collective-permute-done.22.k2_ref.v2_ref, bf16[2,512,384]{2,1,0:T(8,128)(2,1)S(1)} %copy-done.11, ...), custom_call_target="tpu_custom_call" | custom-call | flops 805306368 | bytes 3145728 | tf_op jit(solution)/shard_map/far_tiles/pallas_call | solution.py:444
  135.0 3.5 %far_tiles.6.a_ref = bf16[4,416,128]{2,1,0:T(8,128)(2,1)S(1)} custom-call(bf16[512,1024]{1,0:T(8,128)(2,1)S(1)} %copy-done.6, bf16[2,2,512,384]{3,2,1,0:T(8,128)(2,1)S(1)} %collective-permute-done.10.k2_ref.v2_ref, bf16[2,2,512,384]{3,2,1,0:T(8,128)(2,1)S(1)} %collective-permute-done.10.k2_ref.v2_ref, bf16[2,512,384]{2,1,0:T(8,128)(2,1)S(1)} %copy-done.13, ...), custom_call_target="tpu_custom_call" | custom-call | flops 805306368 | bytes 3145728 | tf_op jit(solution)/shard_map/far_tiles/pallas_call | solution.py:444
  139.2 2.0 merge_pair.4
  141.3 2.0 merge_pair.3
  143.3 1.9 slice_bitcast_fusion.2
  145.2 6.3 %collective-permute-start.25 = (bf16[416,128]{1,0:T(8,128)(2,1)}, bf16[416,128]{1,0:T(8,128)(2,1)}, u32[]{:S(2)}, u32[]{:S(2)}) collective-permute-start(bf16[416,128]{1,0:T(8,128)(2,1)} %get-tuple-element.51), channel_id=1, source_target_pairs={{0,24},{4,28},{8,0},{12,4},{16,8},{20,12},{24,16},{28,20},{1,25},{... | collective-permute-start | bytes 319496 | tf_op jit(solution)/shard_map/ppermute | solution.py:33
  152.1 3.3 %collective-permute-start.19 = (bf16[416,128]{1,0:T(8,128)(2,1)}, bf16[416,128]{1,0:T(8,128)(2,1)S(1)}, u32[]{:S(2)}, u32[]{:S(2)}) collective-permute-start(bf16[416,128]{1,0:T(8,128)(2,1)} %get-tuple-element.45), channel_id=1, source_target_pairs={{0,24},{4,28},{8,0},{12,4},{16,8},{20,12},{24,16},{28,20},{1,25},{... | collective-permute-start | bytes 319496 | tf_op jit(solution)/shard_map/ppermute | solution.py:33
  156.5 6.2 %collective-permute-done.26.refs_2_ = bf16[416,128]{1,0:T(8,128)(2,1)} collective-permute-done((bf16[416,128]{1,0:T(8,128)(2,1)}, bf16[416,128]{1,0:T(8,128)(2,1)}, u32[]{:S(2)}, u32[]{:S(2)}) %collective-permute-start.26) | collective-permute-done | bytes 106528 | tf_op jit(solution)/shard_map/ppermute | solution.py:33
  164.0 2.2 merge_all.4
  166.2 5.3 %collective-permute-done.20.refs_2_ = bf16[416,128]{1,0:T(8,128)(2,1)} collective-permute-done((bf16[416,128]{1,0:T(8,128)(2,1)}, bf16[416,128]{1,0:T(8,128)(2,1)}, u32[]{:S(2)}, u32[]{:S(2)}) %collective-permute-start.20) | collective-permute-done | bytes 106528 | tf_op jit(solution)/shard_map/ppermute | solution.py:33
  171.5 2.0 merge_all.3
  173.5 2.7 %fusion.6 = f32[128,1024]{1,0:T(8,128)} fusion(bf16[1024,4096]{1,0:T(8,128)(2,1)} %param.19, s32[]{:T(128)S(6)} %select_n.75, bf16[384,128]{1,0:T(8,128)(2,1)} %merge_all.4, bf16[384,128]{1,0:T(8,128)(2,1)} %merge_all.3), kind=kOutput, calls=%fused_computation.9 | convolution fusion | flops 201719808 | bytes 2293764 | tf_op jit(solution)/shard_map/dot_general | solution.py:491
  176.2 3.6 %far_tiles.11 = bf16[4,272,128]{2,1,0:T(8,128)(2,1)S(1)} custom-call(bf16[512,1024]{1,0:T(8,128)(2,1)S(1)} %copy-done.9, bf16[2,2,512,256]{3,2,1,0:T(8,128)(2,1)} %collective-permute-done.28.k2_ref.v2_ref, bf16[2,2,512,256]{3,2,1,0:T(8,128)(2,1)} %collective-permute-done.28.k2_ref.v2_ref, bf16[2,512,256]{2,1,0:T(8,128)(2,1)} %collective-permute-done.29.k3_ref.v3_ref, ...), custom_call_target="tpu_custom_call" | custom-call | flops 536870912 | bytes 3145728 | tf_op jit(solution)/shard_map/far_tiles/pallas_call | solution.py:444
  180.0 2.0 fusion.4
  182.0 1.8 fusion.2
  183.8 3.6 %far_tiles.10.a_ref = bf16[4,272,128]{2,1,0:T(8,128)(2,1)S(1)} custom-call(bf16[512,1024]{1,0:T(8,128)(2,1)S(1)} %copy-done.7, bf16[2,2,512,256]{3,2,1,0:T(8,128)(2,1)} %collective-permute-done.28.k2_ref.v2_ref, bf16[2,2,512,256]{3,2,1,0:T(8,128)(2,1)} %collective-permute-done.28.k2_ref.v2_ref, bf16[2,512,256]{2,1,0:T(8,128)(2,1)} %collective-permute-done.29.k3_ref.v3_ref, ...), custom_call_target="tpu_custom_call" | custom-call | flops 536870912 | bytes 3145728 | tf_op jit(solution)/shard_map/far_tiles/pallas_call | solution.py:444
  189.2 1.8 merge_pair.5
  192.6 2.0 collective-permute-start.33
  194.6 1.8 fusion
  196.4 3.1 %collective-permute-done.32.refs_2_ = bf16[272,128]{1,0:T(8,128)(2,1)S(1)} collective-permute-done((bf16[272,128]{1,0:T(8,128)(2,1)}, bf16[272,128]{1,0:T(8,128)(2,1)S(1)}, u32[]{:S(2)}, u32[]{:S(2)}) %collective-permute-start.32) | collective-permute-done | bytes 69664 | tf_op jit(solution)/shard_map/ppermute | solution.py:33
  200.8 1.9 merge_all.5
  202.7 1.4 fusion.14
  204.2 1.3 fusion.13
  206.1 1.3 fusion.12
  207.4 1.5 collective-permute-start.36
  209.0 6.8 %collective-permute-done.36 = bf16[128,1024]{1,0:T(8,128)(2,1)S(1)} collective-permute-done((bf16[128,1024]{1,0:T(8,128)(2,1)S(1)}, bf16[128,1024]{1,0:T(8,128)(2,1)S(1)}, u32[]{:S(2)}, u32[]{:S(2)}) %collective-permute-start.36) | collective-permute-done | bytes 262176 | tf_op jit(solution)/shard_map/ppermute | solution.py:28
  215.7 2.0 fusion.11
  (138 shorter events, 21.5 us)
Async XLA Ops:
  0.7 4.6 %collective-permute-start.3 = (s32[16,128]{1,0:T(8,128)S(1)}, s32[16,128]{1,0:T(8,128)S(1)}, u32[]{:S(2)}, u32[]{:S(2)}) collective-permute-start(s32[16,128]{1,0:T(8,128)S(1)} %get-tuple-element.76), channel_id=1, source_target_pairs={{0,4},{4,0},{8,12},{12,8},{16,20},{20,16},{24,28},{28,24},{1,5},{5... | collective-permute-start | bytes 24584 | tf_op jit(solution)/shard_map/ppermute | solution.py:28
  3.7 11.4 %collective-permute-start = (bf16[128,1024]{1,0:T(8,128)(2,1)}, bf16[128,1024]{1,0:T(8,128)(2,1)S(1)}, u32[]{:S(2)}, u32[]{:S(2)}) collective-permute-start(bf16[128,1024]{1,0:T(8,128)(2,1)} %param.10), channel_id=1, source_target_pairs={{0,1},{1,0},{2,3},{3,2},{4,5},{5,4},{6,7},{7,6},{8,9},{9,8},{10,11... | collective-permute-start | bytes 786440 | tf_op jit(solution)/shard_map/ppermute | solution.py:28
  3.7 13.4 %collective-permute-start.1 = (bf16[128,1024]{1,0:T(8,128)(2,1)}, bf16[128,1024]{1,0:T(8,128)(2,1)}, u32[]{:S(2)}, u32[]{:S(2)}) collective-permute-start(bf16[128,1024]{1,0:T(8,128)(2,1)} %param.10), channel_id=1, source_target_pairs={{0,2},{1,3},{2,0},{3,1},{4,6},{5,7},{6,4},{7,5},{8,10},{9,11},{10,... | collective-permute-start | bytes 786440 | tf_op jit(solution)/shard_map/ppermute | solution.py:28
  5.3 6.2 %collective-permute-start.6 = (s32[2,16,128]{2,1,0:T(8,128)S(1)}, s32[2,16,128]{2,1,0:T(8,128)S(1)}, u32[]{:S(2)}, u32[]{:S(2)}) collective-permute-start(s32[2,16,128]{2,1,0:T(8,128)S(1)} %get-tuple-element.74), channel_id=1, source_target_pairs={{0,24},{4,28},{8,0},{12,4},{16,8},{20,12},{24,16},{28,20},{1,25},{... | collective-permute-start | bytes 49160 | tf_op jit(solution)/shard_map/ppermute | solution.py:33
  9.4 4.6 %collective-permute-start.5 = (s32[2,16,128]{2,1,0:T(8,128)S(1)}, s32[2,16,128]{2,1,0:T(8,128)S(1)}, u32[]{:S(2)}, u32[]{:S(2)}) collective-permute-start(s32[2,16,128]{2,1,0:T(8,128)S(1)} %get-tuple-element.74), channel_id=1, source_target_pairs={{0,16},{4,20},{8,24},{12,28},{16,0},{20,4},{24,8},{28,12},{1,17},{... | collective-permute-start | bytes 49160 | tf_op jit(solution)/shard_map/ppermute | solution.py:33
  9.4 5.5 %collective-permute-start.4 = (s32[2,16,128]{2,1,0:T(8,128)S(1)}, s32[2,16,128]{2,1,0:T(8,128)S(1)}, u32[]{:S(2)}, u32[]{:S(2)}) collective-permute-start(s32[2,16,128]{2,1,0:T(8,128)S(1)} %get-tuple-element.74), channel_id=1, source_target_pairs={{0,8},{4,12},{8,16},{12,20},{16,24},{20,28},{24,0},{28,4},{1,9},{5... | collective-permute-start | bytes 49160 | tf_op jit(solution)/shard_map/ppermute | solution.py:33
  15.1 1.7 copy-start.28
  15.1 5.9 %copy-start.17 = (bf16[4096,1024]{1,0:T(8,128)(2,1)S(1)}, bf16[4096,1024]{1,0:T(8,128)(2,1)}, u32[]{:S(2)}) copy-start(bf16[4096,1024]{1,0:T(8,128)(2,1)} %param.11) | copy-start | bytes 25165828
  17.0 3.9 %collective-permute-start.2 = (bf16[128,1024]{1,0:T(8,128)(2,1)}, bf16[128,1024]{1,0:T(8,128)(2,1)S(1)}, u32[]{:S(2)}, u32[]{:S(2)}) collective-permute-start(bf16[128,1024]{1,0:T(8,128)(2,1)} %collective-permute-done.1), channel_id=1, source_target_pairs={{0,1},{1,0},{2,3},{3,2},{4,5},{5,4},{6,7},{7,6},{8,9},{9,8},{10,11... | collective-permute-start | bytes 786440 | tf_op jit(solution)/shard_map/ppermute | solution.py:28
  22.3 53.6 %copy-start.21 = (bf16[128,1024]{1,0:T(8,128)(2,1)}, bf16[128,1024]{1,0:T(8,128)(2,1)S(1)}, u32[]{:S(2)}) copy-start(bf16[128,1024]{1,0:T(8,128)(2,1)S(1)} %convolution_convert_fusion.q_ref) | copy-start | bytes 786436
  22.3 10.2 %collective-permute-start.7 = (bf16[128,1024]{1,0:T(8,128)(2,1)S(1)}, bf16[128,1024]{1,0:T(8,128)(2,1)}, u32[]{:S(2)}, u32[]{:S(2)}) collective-permute-start(bf16[128,1024]{1,0:T(8,128)(2,1)S(1)} %convolution_convert_fusion.q_ref), channel_id=1, source_target_pairs={{0,8},{4,12},{8,16},{12,20},{16,24},{20,28},{24,0},{28,4},{1,9},{5... | collective-permute-start | bytes 786440 | tf_op jit(solution)/shard_map/ppermute | solution.py:33
  36.6 41.8 %collective-permute-start.11 = (bf16[2,512,1024]{2,1,0:T(8,128)(2,1)}, bf16[2,512,1024]{2,1,0:T(8,128)(2,1)}, u32[]{:S(2)}, u32[]{:S(2)}) collective-permute-start(bf16[2,512,1024]{2,1,0:T(8,128)(2,1)} %pad_maximum_fusion), channel_id=1, source_target_pairs={{0,1},{1,0},{2,3},{3,2},{4,5},{5,4},{6,7},{7,6},{8,9},{9,8},{10,11... | collective-permute-start | bytes 6291464 | tf_op jit(solution)/shard_map/ppermute | solution.py:28
  36.6 41.8 %collective-permute-start.10 = (bf16[2,2,512,384]{3,2,1,0:T(8,128)(2,1)}, bf16[2,2,512,384]{3,2,1,0:T(8,128)(2,1)S(1)}, u32[]{:S(2)}, u32[]{:S(2)}) collective-permute-start(bf16[2,2,512,384]{3,2,1,0:T(8,128)(2,1)} %pad_maximum_fusion.1), channel_id=1, source_target_pairs={{0,2},{1,3},{2,0},{3,1},{4,6},{5,7},{6,4},{7,5},{8,10},{9,11},{10,... | collective-permute-start | bytes 4718600 | tf_op jit(solution)/shard_map/ppermute | solution.py:28
  38.1 9.8 %collective-permute-start.9 = (bf16[128,1024]{1,0:T(8,128)(2,1)S(1)}, bf16[128,1024]{1,0:T(8,128)(2,1)}, u32[]{:S(2)}, u32[]{:S(2)}) collective-permute-start(bf16[128,1024]{1,0:T(8,128)(2,1)S(1)} %convolution_convert_fusion.q_ref), channel_id=1, source_target_pairs={{0,24},{4,28},{8,0},{12,4},{16,8},{20,12},{24,16},{28,20},{1,25},{... | collective-permute-start | bytes 786440 | tf_op jit(solution)/shard_map/ppermute | solution.py:33
  42.0 65.3 %collective-permute-start.22 = (bf16[2,2,512,384]{3,2,1,0:T(8,128)(2,1)}, bf16[2,2,512,384]{3,2,1,0:T(8,128)(2,1)S(1)}, u32[]{:S(2)}, u32[]{:S(2)}) collective-permute-start(bf16[2,2,512,384]{3,2,1,0:T(8,128)(2,1)} %pad_maximum_fusion.2), channel_id=1, source_target_pairs={{0,2},{1,3},{2,0},{3,1},{4,6},{5,7},{6,4},{7,5},{8,10},{9,11},{10,... | collective-permute-start | bytes 4718600 | tf_op jit(solution)/shard_map/ppermute | solution.py:28
  42.6 14.8 %collective-permute-start.8 = (bf16[128,1024]{1,0:T(8,128)(2,1)S(1)}, bf16[128,1024]{1,0:T(8,128)(2,1)}, u32[]{:S(2)}, u32[]{:S(2)}) collective-permute-start(bf16[128,1024]{1,0:T(8,128)(2,1)S(1)} %convolution_convert_fusion.q_ref), channel_id=1, source_target_pairs={{0,16},{4,20},{8,24},{12,28},{16,0},{20,4},{24,8},{28,12},{1,17},{... | collective-permute-start | bytes 786440 | tf_op jit(solution)/shard_map/ppermute | solution.py:33
  47.9 11.1 %collective-permute-start.15 = (bf16[128,1024]{1,0:T(8,128)(2,1)}, bf16[128,1024]{1,0:T(8,128)(2,1)}, u32[]{:S(2)}, u32[]{:S(2)}) collective-permute-start(bf16[128,1024]{1,0:T(8,128)(2,1)} %collective-permute-done.9), channel_id=1, source_target_pairs={{0,4},{4,0},{8,12},{12,8},{16,20},{20,16},{24,28},{28,24},{1,5},{5... | collective-permute-start | bytes 786440 | tf_op jit(solution)/shard_map/ppermute | solution.py:28
  49.4 12.2 %copy-start.25 = (bf16[128,1024]{1,0:T(8,128)(2,1)S(1)}, bf16[128,1024]{1,0:T(8,128)(2,1)}, u32[]{:S(2)}) copy-start(bf16[128,1024]{1,0:T(8,128)(2,1)} %v1_ref.1) | copy-start | bytes 786436
  49.4 12.2 %copy-start.26 = (bf16[128,1024]{1,0:T(8,128)(2,1)S(1)}, bf16[128,1024]{1,0:T(8,128)(2,1)}, u32[]{:S(2)}) copy-start(bf16[128,1024]{1,0:T(8,128)(2,1)} %k1_ref.1) | copy-start | bytes 786436
  57.4 9.3 %collective-permute-start.12 = (bf16[128,1024]{1,0:T(8,128)(2,1)S(1)}, bf16[128,1024]{1,0:T(8,128)(2,1)S(1)}, u32[]{:S(2)}, u32[]{:S(2)}) collective-permute-start(bf16[128,1024]{1,0:T(8,128)(2,1)S(1)} %convolution_convert_fusion.q_ref), channel_id=1, source_target_pairs={{0,4},{4,0},{8,12},{12,8},{16,20},{20,16},{24,28},{28,24},{1,5},{5... | collective-permute-start | bytes 786440 | tf_op jit(solution)/shard_map/ppermute | solution.py:28
  58.9 13.4 %collective-permute-start.14 = (bf16[128,1024]{1,0:T(8,128)(2,1)}, bf16[128,1024]{1,0:T(8,128)(2,1)S(1)}, u32[]{:S(2)}, u32[]{:S(2)}) collective-permute-start(bf16[128,1024]{1,0:T(8,128)(2,1)} %collective-permute-done.8), channel_id=1, source_target_pairs={{0,4},{4,0},{8,12},{12,8},{16,20},{20,16},{24,28},{28,24},{1,5},{5... | collective-permute-start | bytes 786440 | tf_op jit(solution)/shard_map/ppermute | solution.py:28
  66.7 10.5 %collective-permute-start.13 = (bf16[128,1024]{1,0:T(8,128)(2,1)}, bf16[128,1024]{1,0:T(8,128)(2,1)S(1)}, u32[]{:S(2)}, u32[]{:S(2)}) collective-permute-start(bf16[128,1024]{1,0:T(8,128)(2,1)} %collective-permute-done.7), channel_id=1, source_target_pairs={{0,4},{4,0},{8,12},{12,8},{16,20},{20,16},{24,28},{28,24},{1,5},{5... | collective-permute-start | bytes 786440 | tf_op jit(solution)/shard_map/ppermute | solution.py:28
  72.3 18.4 %collective-permute-start.16 = (bf16[2,128,1024]{2,1,0:T(8,128)(2,1)S(1)}, bf16[2,128,1024]{2,1,0:T(8,128)(2,1)S(1)}, u32[]{:S(2)}, u32[]{:S(2)}) collective-permute-start(bf16[2,128,1024]{2,1,0:T(8,128)(2,1)S(1)} %pad_maximum_fusion.6), channel_id=1, source_target_pairs={{0,4},{4,8},{8,12},{12,16},{16,20},{20,24},{24,28},{1,5},{5,9},{9,... | collective-permute-start | bytes 1572872 | tf_op jit(solution)/shard_map/ppermute | solution.py:39
  77.2 12.2 %copy-start.5 = (bf16[512,1024]{1,0:T(8,128)(2,1)}, bf16[512,1024]{1,0:T(8,128)(2,1)S(1)}, u32[]{:S(2)}) copy-start(bf16[512,1024]{1,0:T(8,128)(2,1)S(1)} %pad_maximum_fusion.3.q_ref) | copy-start | bytes 3145732
  78.4 38.1 %copy-start.8 = (bf16[512,1024]{1,0:T(8,128)(2,1)}, bf16[512,1024]{1,0:T(8,128)(2,1)S(1)}, u32[]{:S(2)}) copy-start(bf16[512,1024]{1,0:T(8,128)(2,1)S(1)} %pad_maximum_fusion.4.q_ref) | copy-start | bytes 3145732
  89.3 1.3 copy-start
  90.7 10.7 %copy-start.22 = (bf16[2,128,1024]{2,1,0:T(8,128)(2,1)}, bf16[2,128,1024]{2,1,0:T(8,128)(2,1)S(1)}, u32[]{:S(2)}) copy-start(bf16[2,128,1024]{2,1,0:T(8,128)(2,1)S(1)} %collective-permute-done.16.k0_ref.v0_ref) | copy-start | bytes 1572868
  101.4 15.1 %copy-start.3 = (f32[1024,512]{1,0:T(8,128)}, f32[1024,512]{1,0:T(8,128)S(1)}, u32[]{:S(2)}) copy-start(f32[1024,512]{1,0:T(8,128)S(1)} %get-tuple-element.43.acc_ref) | copy-start | bytes 6291460
  107.4 3.3 %collective-permute-start.23 = (bf16[2,512,384]{2,1,0:T(8,128)(2,1)S(1)}, bf16[2,512,384]{2,1,0:T(8,128)(2,1)S(1)}, u32[]{:S(2)}, u32[]{:S(2)}) collective-permute-start(bf16[2,512,384]{2,1,0:T(8,128)(2,1)S(1)} %slice_bitcast_fusion), channel_id=1, source_target_pairs={{0,1},{1,0},{2,3},{3,2},{4,5},{5,4},{6,7},{7,6},{8,9},{9,8},{10,11... | collective-permute-start | bytes 2359304 | tf_op jit(solution)/shard_map/ppermute | solution.py:28
  107.6 8.9 %collective-permute-start.17 = (bf16[2,512,384]{2,1,0:T(8,128)(2,1)S(1)}, bf16[2,512,384]{2,1,0:T(8,128)(2,1)S(1)}, u32[]{:S(2)}, u32[]{:S(2)}) collective-permute-start(bf16[2,512,384]{2,1,0:T(8,128)(2,1)S(1)} %slice_bitcast_fusion.1), channel_id=1, source_target_pairs={{0,1},{1,0},{2,3},{3,2},{4,5},{5,4},{6,7},{7,6},{8,9},{9,8},{10,11... | collective-permute-start | bytes 2359304 | tf_op jit(solution)/shard_map/ppermute | solution.py:28
  109.3 34.0 %collective-permute-start.28 = (bf16[2,2,512,256]{3,2,1,0:T(8,128)(2,1)}, bf16[2,2,512,256]{3,2,1,0:T(8,128)(2,1)}, u32[]{:S(2)}, u32[]{:S(2)}) collective-permute-start(bf16[2,2,512,256]{3,2,1,0:T(8,128)(2,1)} %pad_maximum_fusion.5), channel_id=1, source_target_pairs={{0,2},{1,3},{2,0},{3,1},{4,6},{5,7},{6,4},{7,5},{8,10},{9,11},{10,... | collective-permute-start | bytes 3145736 | tf_op jit(solution)/shard_map/ppermute | solution.py:28
  110.8 4.2 %copy-start.10 = (bf16[2,512,384]{2,1,0:T(8,128)(2,1)}, bf16[2,512,384]{2,1,0:T(8,128)(2,1)S(1)}, u32[]{:S(2)}) copy-start(bf16[2,512,384]{2,1,0:T(8,128)(2,1)S(1)} %collective-permute-done.23.k3_ref.v3_ref) | copy-start | bytes 2359300
  115.0 24.2 %collective-permute-start.24 = (bf16[4,416,128]{2,1,0:T(8,128)(2,1)}, bf16[4,416,128]{2,1,0:T(8,128)(2,1)}, u32[]{:S(2)}, u32[]{:S(2)}) collective-permute-start(bf16[4,416,128]{2,1,0:T(8,128)(2,1)} %far_tiles.9), channel_id=1, source_target_pairs={{0,4},{4,0},{8,12},{12,8},{16,20},{20,16},{24,28},{28,24},{1,5},{5... | collective-permute-start | bytes 1277960 | tf_op jit(solution)/shard_map/ppermute | solution.py:28
  116.5 4.2 %copy-start.12 = (bf16[2,512,384]{2,1,0:T(8,128)(2,1)}, bf16[2,512,384]{2,1,0:T(8,128)(2,1)S(1)}, u32[]{:S(2)}) copy-start(bf16[2,512,384]{2,1,0:T(8,128)(2,1)S(1)} %collective-permute-done.17.k3_ref.v3_ref) | copy-start | bytes 2359300
  120.7 20.5 %collective-permute-start.18 = (bf16[4,416,128]{2,1,0:T(8,128)(2,1)}, bf16[4,416,128]{2,1,0:T(8,128)(2,1)}, u32[]{:S(2)}, u32[]{:S(2)}) collective-permute-start(bf16[4,416,128]{2,1,0:T(8,128)(2,1)} %far_tiles.7), channel_id=1, source_target_pairs={{0,4},{4,0},{8,12},{12,8},{16,20},{20,16},{24,28},{28,24},{1,5},{5... | collective-permute-start | bytes 1277960 | tf_op jit(solution)/shard_map/ppermute | solution.py:28
  127.5 1.6 copy-start.1
  131.5 3.5 %copy-start.13 = (bf16[2,512,384]{2,1,0:T(8,128)(2,1)S(1)}, bf16[2,512,384]{2,1,0:T(8,128)(2,1)}, u32[]{:S(2)}) copy-start(bf16[2,512,384]{2,1,0:T(8,128)(2,1)} %copy-done.12) | copy-start | bytes 2359300
  135.0 3.5 %copy-start.15 = (bf16[4,416,128]{2,1,0:T(8,128)(2,1)}, bf16[4,416,128]{2,1,0:T(8,128)(2,1)S(1)}, u32[]{:S(2)}) copy-start(bf16[4,416,128]{2,1,0:T(8,128)(2,1)S(1)} %far_tiles.8.a_ref) | copy-start | bytes 1277956
  139.2 23.5 %copy-start.34 = (f32[16]{0:T(128)S(1)}, f32[16]{0:T(128)}, u32[]{:S(2)}) copy-start(f32[16]{0:T(128)} %param.18) | copy-start | bytes 196
  145.2 31.0 %collective-permute-start.29 = (bf16[2,512,256]{2,1,0:T(8,128)(2,1)}, bf16[2,512,256]{2,1,0:T(8,128)(2,1)}, u32[]{:S(2)}, u32[]{:S(2)}) collective-permute-start(bf16[2,512,256]{2,1,0:T(8,128)(2,1)} %slice_bitcast_fusion.2), channel_id=1, source_target_pairs={{0,1},{1,0},{2,3},{3,2},{4,5},{5,4},{6,7},{7,6},{8,9},{9,8},{10,11... | collective-permute-start | bytes 1572872 | tf_op jit(solution)/shard_map/ppermute | solution.py:28
  145.2 10.2 %collective-permute-start.25 = (bf16[416,128]{1,0:T(8,128)(2,1)}, bf16[416,128]{1,0:T(8,128)(2,1)}, u32[]{:S(2)}, u32[]{:S(2)}) collective-permute-start(bf16[416,128]{1,0:T(8,128)(2,1)} %get-tuple-element.51), channel_id=1, source_target_pairs={{0,24},{4,28},{8,0},{12,4},{16,8},{20,12},{24,16},{28,20},{1,25},{... | collective-permute-start | bytes 319496 | tf_op jit(solution)/shard_map/ppermute | solution.py:33
  151.5 11.1 %collective-permute-start.26 = (bf16[416,128]{1,0:T(8,128)(2,1)}, bf16[416,128]{1,0:T(8,128)(2,1)}, u32[]{:S(2)}, u32[]{:S(2)}) collective-permute-start(bf16[416,128]{1,0:T(8,128)(2,1)} %get-tuple-element.52), channel_id=1, source_target_pairs={{0,16},{4,20},{8,24},{12,28},{16,0},{20,4},{24,8},{28,12},{1,17},{... | collective-permute-start | bytes 319496 | tf_op jit(solution)/shard_map/ppermute | solution.py:33
  151.5 11.2 %collective-permute-start.27 = (bf16[416,128]{1,0:T(8,128)(2,1)}, bf16[416,128]{1,0:T(8,128)(2,1)S(1)}, u32[]{:S(2)}, u32[]{:S(2)}) collective-permute-start(bf16[416,128]{1,0:T(8,128)(2,1)} %get-tuple-element.53), channel_id=1, source_target_pairs={{0,8},{4,12},{8,16},{12,20},{16,24},{20,28},{24,0},{28,4},{1,9},{5... | collective-permute-start | bytes 319496 | tf_op jit(solution)/shard_map/ppermute | solution.py:33
  152.1 14.1 %collective-permute-start.19 = (bf16[416,128]{1,0:T(8,128)(2,1)}, bf16[416,128]{1,0:T(8,128)(2,1)S(1)}, u32[]{:S(2)}, u32[]{:S(2)}) collective-permute-start(bf16[416,128]{1,0:T(8,128)(2,1)} %get-tuple-element.45), channel_id=1, source_target_pairs={{0,24},{4,28},{8,0},{12,4},{16,8},{20,12},{24,16},{28,20},{1,25},{... | collective-permute-start | bytes 319496 | tf_op jit(solution)/shard_map/ppermute | solution.py:33
  155.4 16.1 %collective-permute-start.20 = (bf16[416,128]{1,0:T(8,128)(2,1)}, bf16[416,128]{1,0:T(8,128)(2,1)}, u32[]{:S(2)}, u32[]{:S(2)}) collective-permute-start(bf16[416,128]{1,0:T(8,128)(2,1)} %get-tuple-element.46), channel_id=1, source_target_pairs={{0,16},{4,20},{8,24},{12,28},{16,0},{20,4},{24,8},{28,12},{1,17},{... | collective-permute-start | bytes 319496 | tf_op jit(solution)/shard_map/ppermute | solution.py:33
  162.7 8.8 %collective-permute-start.21 = (bf16[416,128]{1,0:T(8,128)(2,1)}, bf16[416,128]{1,0:T(8,128)(2,1)}, u32[]{:S(2)}, u32[]{:S(2)}) collective-permute-start(bf16[416,128]{1,0:T(8,128)(2,1)} %get-tuple-element.47), channel_id=1, source_target_pairs={{0,8},{4,12},{8,16},{12,20},{16,24},{20,28},{24,0},{28,4},{1,9},{5... | collective-permute-start | bytes 319496 | tf_op jit(solution)/shard_map/ppermute | solution.py:33
  164.0 12.2 %copy-start.4 = (f32[1024,512]{1,0:T(8,128)S(1)}, f32[1024,512]{1,0:T(8,128)}, u32[]{:S(2)}) copy-start(f32[1024,512]{1,0:T(8,128)} %copy-done.3) | copy-start | bytes 6291460
  164.0 12.2 %copy-start.9 = (bf16[512,1024]{1,0:T(8,128)(2,1)S(1)}, bf16[512,1024]{1,0:T(8,128)(2,1)}, u32[]{:S(2)}) copy-start(bf16[512,1024]{1,0:T(8,128)(2,1)} %copy-done.8) | copy-start | bytes 3145732
  166.2 5.3 %copy-start.29 = (bf16[416,128]{1,0:T(8,128)(2,1)}, bf16[416,128]{1,0:T(8,128)(2,1)S(1)}, u32[]{:S(2)}) copy-start(bf16[416,128]{1,0:T(8,128)(2,1)S(1)} %collective-permute-done.19.refs_1_) | copy-start | bytes 319492
  176.2 3.8 %copy-start.18 = (bf16[384,128]{1,0:T(8,128)(2,1)S(1)}, bf16[384,128]{1,0:T(8,128)(2,1)}, u32[]{:S(2)}) copy-start(bf16[384,128]{1,0:T(8,128)(2,1)} %merge_all.4) | copy-start | bytes 294916
  176.2 3.8 %copy-start.19 = (bf16[384,128]{1,0:T(8,128)(2,1)S(1)}, bf16[384,128]{1,0:T(8,128)(2,1)}, u32[]{:S(2)}) copy-start(bf16[384,128]{1,0:T(8,128)(2,1)} %merge_all.3) | copy-start | bytes 294916
  179.9 3.9 %copy-start.2 = (f32[1024,512]{1,0:T(8,128)S(1)}, f32[1024,512]{1,0:T(8,128)}, u32[]{:S(2)}) copy-start(f32[1024,512]{1,0:T(8,128)} %copy-done) | copy-start | bytes 6291460
  179.9 3.9 %copy-start.7 = (bf16[512,1024]{1,0:T(8,128)(2,1)S(1)}, bf16[512,1024]{1,0:T(8,128)(2,1)}, u32[]{:S(2)}) copy-start(bf16[512,1024]{1,0:T(8,128)(2,1)} %copy-done.5) | copy-start | bytes 3145732
  179.9 8.6 %collective-permute-start.30 = (bf16[4,272,128]{2,1,0:T(8,128)(2,1)S(1)}, bf16[4,272,128]{2,1,0:T(8,128)(2,1)S(1)}, u32[]{:S(2)}, u32[]{:S(2)}) collective-permute-start(bf16[4,272,128]{2,1,0:T(8,128)(2,1)S(1)} %far_tiles.11), channel_id=1, source_target_pairs={{0,4},{4,0},{8,12},{12,8},{16,20},{20,16},{24,28},{28,24},{1,5},{5... | collective-permute-start | bytes 835592 | tf_op jit(solution)/shard_map/ppermute | solution.py:28
  183.8 10.8 %copy-start.20 = (bf16[384,128]{1,0:T(8,128)(2,1)S(1)}, bf16[384,128]{1,0:T(8,128)(2,1)}, u32[]{:S(2)}) copy-start(bf16[384,128]{1,0:T(8,128)(2,1)} %merge_all.3) | copy-start | bytes 294916
  191.1 5.4 %collective-permute-start.31 = (bf16[272,128]{1,0:T(8,128)(2,1)}, bf16[272,128]{1,0:T(8,128)(2,1)S(1)}, u32[]{:S(2)}, u32[]{:S(2)}) collective-permute-start(bf16[272,128]{1,0:T(8,128)(2,1)} %get-tuple-element.58), channel_id=1, source_target_pairs={{0,24},{4,28},{8,0},{12,4},{16,8},{20,12},{24,16},{28,20},{1,25},{... | collective-permute-start | bytes 208904 | tf_op jit(solution)/shard_map/ppermute | solution.py:33
  191.5 8.0 %collective-permute-start.32 = (bf16[272,128]{1,0:T(8,128)(2,1)}, bf16[272,128]{1,0:T(8,128)(2,1)S(1)}, u32[]{:S(2)}, u32[]{:S(2)}) collective-permute-start(bf16[272,128]{1,0:T(8,128)(2,1)} %get-tuple-element.59), channel_id=1, source_target_pairs={{0,16},{4,20},{8,24},{12,28},{16,0},{20,4},{24,8},{28,12},{1,17},{... | collective-permute-start | bytes 208904 | tf_op jit(solution)/shard_map/ppermute | solution.py:33
  192.6 7.0 %collective-permute-start.33 = (bf16[272,128]{1,0:T(8,128)(2,1)}, bf16[272,128]{1,0:T(8,128)(2,1)S(1)}, u32[]{:S(2)}, u32[]{:S(2)}) collective-permute-start(bf16[272,128]{1,0:T(8,128)(2,1)} %get-tuple-element.60), channel_id=1, source_target_pairs={{0,8},{4,12},{8,16},{12,20},{16,24},{20,28},{24,0},{28,4},{1,9},{5... | collective-permute-start | bytes 208904 | tf_op jit(solution)/shard_map/ppermute | solution.py:33
  196.4 3.1 %copy-start.31 = (bf16[272,128]{1,0:T(8,128)(2,1)}, bf16[272,128]{1,0:T(8,128)(2,1)S(1)}, u32[]{:S(2)}) copy-start(bf16[272,128]{1,0:T(8,128)(2,1)S(1)} %collective-permute-done.31.refs_1_) | copy-start | bytes 208900
  202.7 3.4 %copy-start.24 = (bf16[256,128]{1,0:T(8,128)(2,1)S(1)}, bf16[256,128]{1,0:T(8,128)(2,1)}, u32[]{:S(2)}) copy-start(bf16[256,128]{1,0:T(8,128)(2,1)} %merge_all.5) | copy-start | bytes 196612
  202.7 13.0 %copy-start.23 = (f32[128,1024]{1,0:T(8,128)S(1)}, f32[128,1024]{1,0:T(8,128)}, u32[]{:S(2)}) copy-start(f32[128,1024]{1,0:T(8,128)} %fusion.6) | copy-start | bytes 1572868
  204.1 2.0 collective-permute-start.35
  205.5 3.4 %collective-permute-start.34 = (bf16[128,1024]{1,0:T(8,128)(2,1)S(1)}, bf16[128,1024]{1,0:T(8,128)(2,1)S(1)}, u32[]{:S(2)}, u32[]{:S(2)}) collective-permute-start(bf16[128,1024]{1,0:T(8,128)(2,1)S(1)} %fusion.13), channel_id=1, source_target_pairs={{0,1},{1,0},{2,3},{3,2},{4,5},{5,4},{6,7},{7,6},{8,9},{9,8},{10,11... | collective-permute-start | bytes 786440 | tf_op jit(solution)/shard_map/ppermute | solution.py:28
  207.4 8.3 %collective-permute-start.36 = (bf16[128,1024]{1,0:T(8,128)(2,1)S(1)}, bf16[128,1024]{1,0:T(8,128)(2,1)S(1)}, u32[]{:S(2)}, u32[]{:S(2)}) collective-permute-start(bf16[128,1024]{1,0:T(8,128)(2,1)S(1)} %fusion.12), channel_id=1, source_target_pairs={{0,2},{1,3},{2,0},{3,1},{4,6},{5,7},{6,4},{7,5},{8,10},{9,11},{10,... | collective-permute-start | bytes 786440 | tf_op jit(solution)/shard_map/ppermute | solution.py:28
  (8 other events, 6.4 us)

commit v5 on v4

--- a/solution.py
+++ b/solution.py
@@ -37,6 +37,30 @@
     devices = range(lax.axis_size(axis))
     route = [(i - distance, i) for i in devices if i - distance in devices]
     return lax.ppermute(block, axis, route)
+
+
+def share_kernel(sizes, me_ref, keys_ref, values_ref, near_ref, *rest):
+    *far_refs, sems = rest
+    features = near_ref.shape[2]
+    copies = []
+
+    def copy(k, first, target, cols):
+        start = pl.multiple_of((me_ref[0] ^ k) * features + first * DH, PAIR)
+        for which, source in enumerate((keys_ref, values_ref)):
+            copies.append(
+                pltpu.make_async_copy(
+                    source.at[:, pl.ds(start, cols)], target.at[which], sems.at[len(copies)]
+                )
+            )
+
+    for j, far_ref in enumerate(far_refs):
+        for k in (2, 3):
+            copy(k, sum(sizes[:j]), far_ref.at[k - 2], sizes[j] * DH)
+    copy(1, 0, near_ref, features)
+    for one in copies:
+        one.start()
+    for one in copies:
+        one.wait()
 
 
 def pipelined(q_ref, key_refs, vt_ref, bits_ref, s_ref, first_bit, emit):
@@ -310,31 +334,28 @@
     hidden = jnp.zeros((row_count, mem_size * hidden_states.shape[1]), jnp.bfloat16)
     for k in range(mem_size):
         hidden = lax.dynamic_update_slice(hidden, have[k], (0, (me ^ k) * hidden_states.shape[1]))
-    def share(at, cols):
-        return jnp.stack(
-            [
-                lax.dynamic_slice(memory_keys, (0, at), (mem_rows, cols)),
-                lax.dynamic_slice(memory_values, (0, at), (mem_rows, cols)),
-            ]
-        )
-
-    def across(at, j):
-        return jnp.stack(
-            [share((at ^ k) * features + firsts[j] * DH, sizes[j] * DH) for k in (2, 3)]
-        )
-
-    first_block = across(after(me, h1), 0)
+    near_block, *far_blocks = pl.pallas_call(
+        functools.partial(share_kernel, sizes),
+        in_specs=[
+            pl.BlockSpec(memory_space=pltpu.SMEM),
+            pl.BlockSpec(memory_space=pl.ANY),
+            pl.BlockSpec(memory_space=pl.ANY),
+        ],
+        out_specs=[pl.BlockSpec(memory_space=pl.ANY)] * (1 + chunks),
+        out_shape=[jax.ShapeDtypeStruct((2, mem_rows, features), jnp.bfloat16)]
+        + [jax.ShapeDtypeStruct((2, 2, mem_rows, n * DH), jnp.bfloat16) for n in sizes],
+        scratch_shapes=[pltpu.SemaphoreType.DMA((2 + 4 * chunks,))],
+        name="share_tiles",
+    )(me.reshape(1), memory_keys, memory_values)
     queries = jnp.dot(
-        after(hidden, first_block, bits[0]), w_query, preferred_element_type=f32
+        after(hidden, far_blocks[0], bits[0]), w_query, preferred_element_type=f32
     ).astype(jnp.bfloat16)
-
-    crossed = [swap(first_block, "mem", 2)]
+    crossed = [swap(after(far_blocks[0], h1), "mem", 2)]
 
     q_blocks = [queries] + [turn(queries, "ctx", 2 * k) for k in range(1, turns)]
     q_blocks += [swap(q, "ctx", 1) for q in q_blocks]
-    later_me = after(me, q_blocks[1])
-    near = swap(share((later_me ^ 1) * features, features), "mem", 1)
-    crossed.append(swap(across(later_me, 1), "mem", 2))
+    near = swap(near_block, "mem", 1)
+    crossed.append(swap(after(far_blocks[1], queries), "mem", 2))
     window = jnp.stack([local_keys, after(local_values, q_blocks[-1])])
     window = from_behind(window, "ctx", 1)
     q_halves = [jnp.concatenate(q_blocks[part * turns : (part + 1) * turns], 0) for part in range(2)]
@@ -354,7 +375,7 @@
         if part == 1:
             q_halves[1] = after(q_halves[1], window, near_state[0][1])
             crossed.append(
-                swap(after(across(later_me, 2), crossed[0], near_state[0][1]), "mem", 2)
+                swap(after(far_blocks[2], near_state[0][1]), "mem", 2)
             )
         near_state.append(
             pl.pallas_call(
@@ -423,10 +444,9 @@
     def weights(k, first, count):
         return lax.dynamic_slice(w_output, (first * DH, (me ^ k) * cols), (count * DH, cols))
 
-    combined = []
     messages = []
     merges = []
-    early = None
+    answers = []
     for j in range(chunks):
         heads, first = sizes[j], firsts[j]
         wide = heads * DH
@@ -476,14 +496,18 @@
             name="merge_pair",
         )(message[0], other)
         merges.append(merged[0])
-        answers = [merged[0]] + [turn(merged[k], "ctx", -2 * k) for k in range(1, turns)]
-        if j == chunks - 1:
-            answers[0] = after(answers[0], early)
+        answers.append([merged[0]] + [turn(merged[k], "ctx", -2 * k) for k in range(1, turns)])
+
+    combined = []
+    early = None
+    for j in range(chunks):
+        heads, first = sizes[j], firsts[j]
+        token = messages[-1][0] if j < chunks - 1 else early
         mixed = pl.pallas_call(
             functools.partial(final_kernel, heads, first),
-            out_shape=jax.ShapeDtypeStruct((wide, row_count), jnp.bfloat16),
+            out_shape=jax.ShapeDtypeStruct((heads * DH, row_count), jnp.bfloat16),
             name="merge_all",
-        )(*answers, local_out, gate_rows)
+        )(after(answers[j][0], token), *answers[j][1:], local_out, gate_rows)
         combined.append(mixed)
         if j == chunks - 2:
             mixed = jnp.concatenate(combined, axis=0)

time: 219 us -> 391 us (1.79)
  Pallas kernels: 62.5 us -> 254 us
  waiting for transfers between devices: 63.7 us -> 45.3 us
  starting transfers between devices: 41.7 us -> 56.4 us
  local copies, waits for them, and re-layouts: 24.5 us -> 13.6 us
  other arithmetic: 9.06 us -> 1.03 us
    pallas_call x0 -> x1, Pallas kernels: none -> 192 us  [on_device(): pl.pallas_call(functools.partial(share_kernel, sizes), in_specs=[pl.Block...]
    ppermute x15, waiting for transfers between devices: 41.4 us -> 24.1 us  [turn(): lax.ppermute(block, axis, [(i, (i + distance) % size) for i in range(size)])]
    ppermute x15, starting transfers between devices: 20.1 us -> 32.7 us  [turn(): lax.ppermute(block, axis, [(i, (i + distance) % size) for i in range(size)])]
    another operation x7 -> x0, local copies, waits for them, and re-layouts: 8.82 us -> none  [share(): jnp.stack([lax.dynamic_slice(memory_keys, (0, at), (mem_rows, cols)), lax...]
    another operation x10 -> x0, other arithmetic: 5.75 us -> none  [the longest x9 4.26 us: across(): jnp.stack([share((at ^ k) * features + firsts[j] * DH, sizes[j] * DH) for...]
  transfers between devices with their start and end apart: 37 -> 37, of which waited for: 14 -> 11; matrix products, arithmetic and copies ran while one was open for 13% -> 4% of each run, Pallas kernels for 25% -> 64%
where the time goes in v5:
time: 391 us; the launch traced here: 389 us
  Pallas kernels  254 us (65%)
  starting transfers between devices  56.4 us (14%)
  waiting for transfers between devices  45.3 us (12%)
  matrix products  18.1 us (5%)
  local copies, waits for them, and re-layouts  13.6 us (3%)
    pallas_call x1, Pallas kernels, on_device(): pl.pallas_call(functools.partial(share_kernel, sizes), in_specs=[pl.Block...  192 us
    ppermute x15, starting transfers between devices, turn(): lax.ppermute(block, axis, [(i, (i + distance) % size) for i in range(size)])  32.7 us
    ppermute x15, waiting for transfers between devices, turn(): lax.ppermute(block, axis, [(i, (i + distance) % size) for i in range(size)])  24.1 us
    pallas_call x6, Pallas kernels, on_device(): pl.pallas_call(far_kernel, grid=(1,), in_specs=[pl.BlockSpec((pl.Element(...  22.4 us
    pallas_call x2, Pallas kernels, on_device(): pl.pallas_call(near_kernel, grid_spec=pltpu.PrefetchScalarGridSpec(num_sc...  21.5 us
    ppermute x21, waiting for transfers between devices, swap(): lax.ppermute(block, axis, [(i, i ^ distance) for i in range(lax.axis_size...  21.2 us
    ppermute x21, starting transfers between devices, swap(): lax.ppermute(block, axis, [(i, i ^ distance) for i in range(lax.axis_size...  20.1 us
    unnamed x70, local copies, waits for them, and re-layouts  10.6 us
  transfers between devices with their start and end apart: 37, of which 11 were waited for; matrix products, arithmetic and copies ran while one was open for 4% of the time, Pallas kernels for 64%

profile of v5, /device:TPU:0, one launch (start us, length us, event | category | flops | bytes accessed | tf_op | source)
XLA Modules:
  0.0 389.1 jit_solution(10278495975577669735)
XLA Ops:
  0.0 0.7 fusion.29
  0.7 3.0 collective-permute-start.3
  3.7 1.5 collective-permute-start.1
  5.3 2.1 collective-permute-start.4
  7.4 2.6 collective-permute-start.5
  10.0 1.3 collective-permute-start.6
  11.4 1.0 constant_dynamic-update-slice_fusion.3
  12.4 191.8 %share_tiles.1 = (bf16[2,512,1024]{2,1,0:T(8,128)(2,1)}, bf16[2,2,512,384]{3,2,1,0:T(8,128)(2,1)}, bf16[2,2,512,384]{3,2,1,0:T(8,128)(2,1)}, bf16[2,2,512,256]{3,2,1,0:T(8,128)(2,1)}) custom-call(s32[1]{0:T(128)} %bitcast.me_ref.m_ref, bf16[512,4096]{1,0:T(8,128)(2,1)} %k0_ref.3, bf16[512,4096]{1,0:T(8,128)(2,1)} %v0_ref.3), custom_call_target="tpu_custom_call" | custom-call | tf_op jit(solution)/shard_map/share_tiles/pallas_call | solution.py:337
  205.1 1.6 collective-permute-start.10
  206.7 2.0 collective-permute-done.2
  208.7 4.7 %convolution_convert_fusion.q_ref = bf16[128,1024]{1,0:T(8,128)(2,1)S(1)} fusion(bf16[128,4096]{1,0:T(8,128)(2,1)S(1)} %constant_dynamic-update-slice_fusion, bf16[4096,1024]{1,0:T(8,128)(2,1)} %param.11), kind=kOutput, calls=%fused_computation.17 | convolution fusion | flops 1073872896 | bytes 9699328 | tf_op jit(solution)/shard_map/dot_general | solution.py:350
  213.9 1.6 collective-permute-start.7
  215.6 11.8 %collective-permute-done.9 = bf16[128,1024]{1,0:T(8,128)(2,1)S(1)} collective-permute-done((bf16[128,1024]{1,0:T(8,128)(2,1)S(1)}, bf16[128,1024]{1,0:T(8,128)(2,1)S(1)}, u32[]{:S(2)}, u32[]{:S(2)}) %collective-permute-start.9) | collective-permute-done | bytes 262176 | tf_op jit(solution)/shard_map/ppermute | solution.py:33
  227.4 1.5 collective-permute-start.20
  228.9 1.5 collective-permute-start.15
  230.4 8.4 %collective-permute-done.8 = bf16[128,1024]{1,0:T(8,128)(2,1)S(1)} collective-permute-done((bf16[128,1024]{1,0:T(8,128)(2,1)S(1)}, bf16[128,1024]{1,0:T(8,128)(2,1)S(1)}, u32[]{:S(2)}, u32[]{:S(2)}) %collective-permute-start.8) | collective-permute-done | bytes 262176 | tf_op jit(solution)/shard_map/ppermute | solution.py:33
  238.9 1.5 collective-permute-start.12
  240.9 7.2 %collective-permute-done.12 = bf16[128,1024]{1,0:T(8,128)(2,1)S(1)} collective-permute-done((bf16[128,1024]{1,0:T(8,128)(2,1)S(1)}, bf16[128,1024]{1,0:T(8,128)(2,1)S(1)}, u32[]{:S(2)}, u32[]{:S(2)}) %collective-permute-start.12) | collective-permute-done | bytes 262176 | tf_op jit(solution)/shard_map/ppermute | solution.py:28
  248.1 1.5 collective-permute-start.14
  249.7 4.0 %collective-permute-done.13 = bf16[128,1024]{1,0:T(8,128)(2,1)S(1)} collective-permute-done((bf16[128,1024]{1,0:T(8,128)(2,1)S(1)}, bf16[128,1024]{1,0:T(8,128)(2,1)S(1)}, u32[]{:S(2)}, u32[]{:S(2)}) %collective-permute-start.13) | collective-permute-done | bytes 262176 | tf_op jit(solution)/shard_map/ppermute | solution.py:28
  253.7 3.6 collective-permute-start.16
  257.4 0.9 collective-permute-done.14
  258.5 10.8 %near_tiles.2 = (f32[1024,512]{1,0:T(8,128)S(1)}, f32[8,8,512]{2,1,0:T(8,128)S(1)}) custom-call(s32[1]{0:T(128)} %bitcast.me_ref.m_ref, bf16[512,1024]{1,0:T(8,128)(2,1)S(1)} %pad_maximum_fusion.q_ref, bf16[512,4096]{1,0:T(8,128)(2,1)} %k0_ref.3, bf16[512,4096]{1,0:T(8,128)(2,1)} %v0_ref.3, bf16[2,512,1024]{2,1,0:T(8,128)(2,1)S(1)} %collective-permute-done.11.k1_ref.v1_ref, ...), custom_call_target="tpu_custom_call" | custom-call | flops 2147483648 | bytes 8388608 | tf_op jit(solution)/shard_map/near_tiles/pallas_call | solution.py:381
  269.4 1.3 copy-done
  270.7 10.7 %near_tiles.3 = (f32[1024,512]{1,0:T(8,128)S(1)}, f32[8,8,512]{2,1,0:T(8,128)S(1)}) custom-call(s32[1]{0:T(128)} %bitcast.me_ref.m_ref, bf16[512,1024]{1,0:T(8,128)(2,1)S(1)} %pad_maximum_fusion.1.q_ref, bf16[512,4096]{1,0:T(8,128)(2,1)} %k0_ref.3, bf16[512,4096]{1,0:T(8,128)(2,1)} %v0_ref.3, ...), custom_call_target="tpu_custom_call" | custom-call | flops 2147483648 | bytes 8388608 | tf_op jit(solution)/shard_map/near_tiles/pallas_call | solution.py:381
  282.2 1.5 collective-permute-start.19
  283.8 4.2 %far_tiles.7 = bf16[4,416,128]{2,1,0:T(8,128)(2,1)} custom-call(bf16[512,1024]{1,0:T(8,128)(2,1)S(1)} %pad_maximum_fusion.1.q_ref, bf16[2,2,512,384]{3,2,1,0:T(8,128)(2,1)S(1)} %collective-permute-done.10.k2_ref.v2_ref, bf16[2,2,512,384]{3,2,1,0:T(8,128)(2,1)S(1)} %collective-permute-done.10.k2_ref.v2_ref, ...), custom_call_target="tpu_custom_call" | custom-call | flops 805306368 | bytes 3145728 | tf_op jit(solution)/shard_map/far_tiles/pallas_call | solution.py:464
  288.0 2.5 collective-permute-start.18
  290.5 4.2 %far_tiles.9 = bf16[4,416,128]{2,1,0:T(8,128)(2,1)} custom-call(bf16[512,1024]{1,0:T(8,128)(2,1)S(1)} %pad_maximum_fusion.1.q_ref, bf16[2,2,512,384]{3,2,1,0:T(8,128)(2,1)S(1)} %collective-permute-done.20.k2_ref.v2_ref, bf16[2,2,512,384]{3,2,1,0:T(8,128)(2,1)S(1)} %collective-permute-done.20.k2_ref.v2_ref, ...), custom_call_target="tpu_custom_call" | custom-call | flops 805306368 | bytes 3145728 | tf_op jit(solution)/shard_map/far_tiles/pallas_call | solution.py:464
  294.7 6.3 %local_window.1.refs_4_ = f32[1024,128]{1,0:T(8,128)} custom-call(s32[1]{0:T(128)} %bitcast.14.ctx_ref, bf16[128,1024]{1,0:T(8,128)(2,1)} %copy-done.19, bf16[2,128,1024]{2,1,0:T(8,128)(2,1)} %copy-done.20, bf16[128,1024]{1,0:T(8,128)(2,1)} %k1_ref.1, bf16[2,128,1024]{2,1,0:T(8,128)(2,1)} %copy-done.20, bf16[128,1024]{1,0:T(8,128)(2,1)} %v1_ref.1), custom_call_target="tpu_custom_call" | custom-call | flops 134217728 | bytes 2097152 | tf_op jit(solution)/shard_map/local_window/pallas_call | solution.py:416
  301.0 1.6 copy-done.1
  302.6 1.2 copy-done.6
  303.8 1.1 copy-done.11
  304.9 3.5 far_tiles.6.a_ref
  308.4 3.5 far_tiles.8.a_ref
  311.9 0.8 copy-done.14
  312.6 2.2 merge_pair.3
  314.9 2.0 merge_pair.4
  316.9 1.1 slice_bitcast_fusion.2
  318.1 12.9 %collective-permute-start.24 = (bf16[416,128]{1,0:T(8,128)(2,1)}, bf16[416,128]{1,0:T(8,128)(2,1)S(1)}, u32[]{:S(2)}, u32[]{:S(2)}) collective-permute-start(bf16[416,128]{1,0:T(8,128)(2,1)} %get-tuple-element.61), channel_id=1, source_target_pairs={{0,24},{4,28},{8,0},{12,4},{16,8},{20,12},{24,16},{28,20},{1,25},{... | collective-permute-start | bytes 319496 | tf_op jit(solution)/shard_map/ppermute | solution.py:33
  331.6 3.4 collective-permute-start.27
  335.0 0.9 collective-permute-start.28
  335.9 3.5 collective-permute-start.29
  339.4 1.2 copy-done.7
  340.7 3.6 far_tiles.10.a_ref
  344.3 3.5 far_tiles.11
  348.7 2.0 merge_all.3
  352.0 2.0 merge_all.4
  354.1 1.9 fusion
  356.1 1.8 fusion.2
  357.9 1.8 fusion.4
  359.7 0.7 copy-done.24
  360.4 1.8 merge_pair.5
  362.3 0.9 collective-permute-start.31
  363.7 1.6 collective-permute-start.33
  365.4 1.8 fusion.6
  367.4 3.6 collective-permute-done.32.refs_2_
  372.3 1.9 merge_all.5
  374.2 1.4 fusion.14
  375.6 1.3 fusion.13
  377.5 1.3 fusion.12
  378.8 1.6 collective-permute-start.36
  380.4 6.8 %collective-permute-done.36 = bf16[128,1024]{1,0:T(8,128)(2,1)S(1)} collective-permute-done((bf16[128,1024]{1,0:T(8,128)(2,1)S(1)}, bf16[128,1024]{1,0:T(8,128)(2,1)S(1)}, u32[]{:S(2)}, u32[]{:S(2)}) %collective-permute-start.36) | collective-permute-done | bytes 262176 | tf_op jit(solution)/shard_map/ppermute | solution.py:28
  387.1 2.0 fusion.11
  (122 shorter events, 9.0 us)
Async XLA Ops:
  0.7 4.6 %collective-permute-start.3 = (s32[16,128]{1,0:T(8,128)S(1)}, s32[16,128]{1,0:T(8,128)S(1)}, u32[]{:S(2)}, u32[]{:S(2)}) collective-permute-start(s32[16,128]{1,0:T(8,128)S(1)} %get-tuple-element.76), channel_id=1, source_target_pairs={{0,4},{4,0},{8,12},{12,8},{16,20},{20,16},{24,28},{28,24},{1,5},{5... | collective-permute-start | bytes 24584 | tf_op jit(solution)/shard_map/ppermute | solution.py:28
  3.7 200.8 %collective-permute-start.1 = (bf16[128,1024]{1,0:T(8,128)(2,1)}, bf16[128,1024]{1,0:T(8,128)(2,1)S(1)}, u32[]{:S(2)}, u32[]{:S(2)}) collective-permute-start(bf16[128,1024]{1,0:T(8,128)(2,1)} %param.10), channel_id=1, source_target_pairs={{0,2},{1,3},{2,0},{3,1},{4,6},{5,7},{6,4},{7,5},{8,10},{9,11},{10,... | collective-permute-start | bytes 786440 | tf_op jit(solution)/shard_map/ppermute | solution.py:28
  5.2 199.9 %collective-permute-start = (bf16[128,1024]{1,0:T(8,128)(2,1)}, bf16[128,1024]{1,0:T(8,128)(2,1)S(1)}, u32[]{:S(2)}, u32[]{:S(2)}) collective-permute-start(bf16[128,1024]{1,0:T(8,128)(2,1)} %param.10), channel_id=1, source_target_pairs={{0,1},{1,0},{2,3},{3,2},{4,5},{5,4},{6,7},{7,6},{8,9},{9,8},{10,11... | collective-permute-start | bytes 786440 | tf_op jit(solution)/shard_map/ppermute | solution.py:28
  5.3 199.0 %collective-permute-start.4 = (s32[2,16,128]{2,1,0:T(8,128)S(1)}, s32[2,16,128]{2,1,0:T(8,128)S(1)}, u32[]{:S(2)}, u32[]{:S(2)}) collective-permute-start(s32[2,16,128]{2,1,0:T(8,128)S(1)} %get-tuple-element.74), channel_id=1, source_target_pairs={{0,8},{4,12},{8,16},{12,20},{16,24},{20,28},{24,0},{28,4},{1,9},{5... | collective-permute-start | bytes 49160 | tf_op jit(solution)/shard_map/ppermute | solution.py:33
  7.4 197.0 %collective-permute-start.5 = (s32[2,16,128]{2,1,0:T(8,128)S(1)}, s32[2,16,128]{2,1,0:T(8,128)S(1)}, u32[]{:S(2)}, u32[]{:S(2)}) collective-permute-start(s32[2,16,128]{2,1,0:T(8,128)S(1)} %get-tuple-element.74), channel_id=1, source_target_pairs={{0,16},{4,20},{8,24},{12,28},{16,0},{20,4},{24,8},{28,12},{1,17},{... | collective-permute-start | bytes 49160 | tf_op jit(solution)/shard_map/ppermute | solution.py:33
  10.0 194.4 %collective-permute-start.6 = (s32[2,16,128]{2,1,0:T(8,128)S(1)}, s32[2,16,128]{2,1,0:T(8,128)S(1)}, u32[]{:S(2)}, u32[]{:S(2)}) collective-permute-start(s32[2,16,128]{2,1,0:T(8,128)S(1)} %get-tuple-element.74), channel_id=1, source_target_pairs={{0,24},{4,28},{8,0},{12,4},{16,8},{20,12},{24,16},{28,20},{1,25},{... | collective-permute-start | bytes 49160 | tf_op jit(solution)/shard_map/ppermute | solution.py:33
  204.3 54.2 %collective-permute-start.11 = (bf16[2,512,1024]{2,1,0:T(8,128)(2,1)}, bf16[2,512,1024]{2,1,0:T(8,128)(2,1)S(1)}, u32[]{:S(2)}, u32[]{:S(2)}) collective-permute-start(bf16[2,512,1024]{2,1,0:T(8,128)(2,1)} %get-tuple-element.43), channel_id=1, source_target_pairs={{0,1},{1,0},{2,3},{3,2},{4,5},{5,4},{6,7},{7,6},{8,9},{9,8},{10,11... | collective-permute-start | bytes 6291464 | tf_op jit(solution)/shard_map/ppermute | solution.py:28
  204.5 4.1 %collective-permute-start.2 = (bf16[128,1024]{1,0:T(8,128)(2,1)S(1)}, bf16[128,1024]{1,0:T(8,128)(2,1)S(1)}, u32[]{:S(2)}, u32[]{:S(2)}) collective-permute-start(bf16[128,1024]{1,0:T(8,128)(2,1)S(1)} %collective-permute-done.1), channel_id=1, source_target_pairs={{0,1},{1,0},{2,3},{3,2},{4,5},{5,4},{6,7},{7,6},{8,9},{9,8},{10,11... | collective-permute-start | bytes 786440 | tf_op jit(solution)/shard_map/ppermute | solution.py:28
  205.1 53.4 %collective-permute-start.10 = (bf16[2,2,512,384]{3,2,1,0:T(8,128)(2,1)}, bf16[2,2,512,384]{3,2,1,0:T(8,128)(2,1)S(1)}, u32[]{:S(2)}, u32[]{:S(2)}) collective-permute-start(bf16[2,2,512,384]{3,2,1,0:T(8,128)(2,1)} %get-tuple-element.41), channel_id=1, source_target_pairs={{0,2},{1,3},{2,0},{3,1},{4,6},{5,7},{6,4},{7,5},{8,10},{9,11},{10,... | collective-permute-start | bytes 4718600 | tf_op jit(solution)/shard_map/ppermute | solution.py:28
  208.7 41.0 %copy-start.22 = (bf16[128,1024]{1,0:T(8,128)(2,1)S(1)}, bf16[128,1024]{1,0:T(8,128)(2,1)}, u32[]{:S(2)}) copy-start(bf16[128,1024]{1,0:T(8,128)(2,1)} %v1_ref.1) | copy-start | bytes 786436
  208.7 41.0 %copy-start.23 = (bf16[128,1024]{1,0:T(8,128)(2,1)S(1)}, bf16[128,1024]{1,0:T(8,128)(2,1)}, u32[]{:S(2)}) copy-start(bf16[128,1024]{1,0:T(8,128)(2,1)} %k1_ref.1) | copy-start | bytes 786436
  213.4 45.1 %copy-start.19 = (bf16[128,1024]{1,0:T(8,128)(2,1)}, bf16[128,1024]{1,0:T(8,128)(2,1)S(1)}, u32[]{:S(2)}) copy-start(bf16[128,1024]{1,0:T(8,128)(2,1)S(1)} %convolution_convert_fusion.q_ref) | copy-start | bytes 786436
  213.4 14.0 %collective-permute-start.9 = (bf16[128,1024]{1,0:T(8,128)(2,1)S(1)}, bf16[128,1024]{1,0:T(8,128)(2,1)S(1)}, u32[]{:S(2)}, u32[]{:S(2)}) collective-permute-start(bf16[128,1024]{1,0:T(8,128)(2,1)S(1)} %convolution_convert_fusion.q_ref), channel_id=1, source_target_pairs={{0,24},{4,28},{8,0},{12,4},{16,8},{20,12},{24,16},{28,20},{1,25},{... | collective-permute-start | bytes 786440 | tf_op jit(solution)/shard_map/ppermute | solution.py:33
  213.9 15.0 %collective-permute-start.7 = (bf16[128,1024]{1,0:T(8,128)(2,1)S(1)}, bf16[128,1024]{1,0:T(8,128)(2,1)S(1)}, u32[]{:S(2)}, u32[]{:S(2)}) collective-permute-start(bf16[128,1024]{1,0:T(8,128)(2,1)S(1)} %convolution_convert_fusion.q_ref), channel_id=1, source_target_pairs={{0,8},{4,12},{8,16},{12,20},{16,24},{20,28},{24,0},{28,4},{1,9},{5... | collective-permute-start | bytes 786440 | tf_op jit(solution)/shard_map/ppermute | solution.py:33
  215.5 23.4 %collective-permute-start.8 = (bf16[128,1024]{1,0:T(8,128)(2,1)S(1)}, bf16[128,1024]{1,0:T(8,128)(2,1)S(1)}, u32[]{:S(2)}, u32[]{:S(2)}) collective-permute-start(bf16[128,1024]{1,0:T(8,128)(2,1)S(1)} %convolution_convert_fusion.q_ref), channel_id=1, source_target_pairs={{0,16},{4,20},{8,24},{12,28},{16,0},{20,4},{24,8},{28,12},{1,17},{... | collective-permute-start | bytes 786440 | tf_op jit(solution)/shard_map/ppermute | solution.py:33
  227.4 54.1 %collective-permute-start.20 = (bf16[2,2,512,384]{3,2,1,0:T(8,128)(2,1)}, bf16[2,2,512,384]{3,2,1,0:T(8,128)(2,1)S(1)}, u32[]{:S(2)}, u32[]{:S(2)}) collective-permute-start(bf16[2,2,512,384]{3,2,1,0:T(8,128)(2,1)} %get-tuple-element.55), channel_id=1, source_target_pairs={{0,2},{1,3},{2,0},{3,1},{4,6},{5,7},{6,4},{7,5},{8,10},{9,11},{10,... | collective-permute-start | bytes 4718600 | tf_op jit(solution)/shard_map/ppermute | solution.py:28
  228.9 11.5 %collective-permute-start.15 = (bf16[128,1024]{1,0:T(8,128)(2,1)S(1)}, bf16[128,1024]{1,0:T(8,128)(2,1)S(1)}, u32[]{:S(2)}, u32[]{:S(2)}) collective-permute-start(bf16[128,1024]{1,0:T(8,128)(2,1)S(1)} %collective-permute-done.9), channel_id=1, source_target_pairs={{0,4},{4,0},{8,12},{12,8},{16,20},{20,16},{24,28},{28,24},{1,5},{5... | collective-permute-start | bytes 786440 | tf_op jit(solution)/shard_map/ppermute | solution.py:28
  238.9 9.2 %collective-permute-start.12 = (bf16[128,1024]{1,0:T(8,128)(2,1)S(1)}, bf16[128,1024]{1,0:T(8,128)(2,1)S(1)}, u32[]{:S(2)}, u32[]{:S(2)}) collective-permute-start(bf16[128,1024]{1,0:T(8,128)(2,1)S(1)} %convolution_convert_fusion.q_ref), channel_id=1, source_target_pairs={{0,4},{4,0},{8,12},{12,8},{16,20},{20,16},{24,28},{28,24},{1,5},{5... | collective-permute-start | bytes 786440 | tf_op jit(solution)/shard_map/ppermute | solution.py:28
  240.4 13.3 %collective-permute-start.13 = (bf16[128,1024]{1,0:T(8,128)(2,1)S(1)}, bf16[128,1024]{1,0:T(8,128)(2,1)S(1)}, u32[]{:S(2)}, u32[]{:S(2)}) collective-permute-start(bf16[128,1024]{1,0:T(8,128)(2,1)S(1)} %collective-permute-done.7), channel_id=1, source_target_pairs={{0,4},{4,0},{8,12},{12,8},{16,20},{20,16},{24,28},{28,24},{1,5},{5... | collective-permute-start | bytes 786440 | tf_op jit(solution)/shard_map/ppermute | solution.py:28
  248.1 10.3 %collective-permute-start.14 = (bf16[128,1024]{1,0:T(8,128)(2,1)S(1)}, bf16[128,1024]{1,0:T(8,128)(2,1)S(1)}, u32[]{:S(2)}, u32[]{:S(2)}) collective-permute-start(bf16[128,1024]{1,0:T(8,128)(2,1)S(1)} %collective-permute-done.8), channel_id=1, source_target_pairs={{0,4},{4,0},{8,12},{12,8},{16,20},{20,16},{24,28},{28,24},{1,5},{5... | collective-permute-start | bytes 786440 | tf_op jit(solution)/shard_map/ppermute | solution.py:28
  253.7 16.9 %collective-permute-start.16 = (bf16[2,128,1024]{2,1,0:T(8,128)(2,1)S(1)}, bf16[2,128,1024]{2,1,0:T(8,128)(2,1)S(1)}, u32[]{:S(2)}, u32[]{:S(2)}) collective-permute-start(bf16[2,128,1024]{2,1,0:T(8,128)(2,1)S(1)} %pad_maximum_fusion.2), channel_id=1, source_target_pairs={{0,4},{4,8},{8,12},{12,16},{16,20},{20,24},{24,28},{1,5},{5,9},{9,... | collective-permute-start | bytes 1572872 | tf_op jit(solution)/shard_map/ppermute | solution.py:39
  257.4 11.9 %copy-start.5 = (bf16[512,1024]{1,0:T(8,128)(2,1)}, bf16[512,1024]{1,0:T(8,128)(2,1)S(1)}, u32[]{:S(2)}) copy-start(bf16[512,1024]{1,0:T(8,128)(2,1)S(1)} %pad_maximum_fusion.q_ref) | copy-start | bytes 3145732
  258.5 32.0 %copy-start.8 = (bf16[512,1024]{1,0:T(8,128)(2,1)}, bf16[512,1024]{1,0:T(8,128)(2,1)S(1)}, u32[]{:S(2)}) copy-start(bf16[512,1024]{1,0:T(8,128)(2,1)S(1)} %pad_maximum_fusion.1.q_ref) | copy-start | bytes 3145732
  269.3 1.3 copy-start
  270.7 10.7 %copy-start.20 = (bf16[2,128,1024]{2,1,0:T(8,128)(2,1)}, bf16[2,128,1024]{2,1,0:T(8,128)(2,1)S(1)}, u32[]{:S(2)}) copy-start(bf16[2,128,1024]{2,1,0:T(8,128)(2,1)S(1)} %collective-permute-done.16.k0_ref.v0_ref) | copy-start | bytes 1572868
  281.4 9.1 %copy-start.3 = (f32[1024,512]{1,0:T(8,128)}, f32[1024,512]{1,0:T(8,128)S(1)}, u32[]{:S(2)}) copy-start(f32[1024,512]{1,0:T(8,128)S(1)} %get-tuple-element.50.acc_ref) | copy-start | bytes 6291460
  281.5 2.4 collective-permute-start.17
  281.6 8.8 %collective-permute-start.21 = (bf16[2,512,384]{2,1,0:T(8,128)(2,1)S(1)}, bf16[2,512,384]{2,1,0:T(8,128)(2,1)S(1)}, u32[]{:S(2)}, u32[]{:S(2)}) collective-permute-start(bf16[2,512,384]{2,1,0:T(8,128)(2,1)S(1)} %slice_bitcast_fusion), channel_id=1, source_target_pairs={{0,1},{1,0},{2,3},{3,2},{4,5},{5,4},{6,7},{7,6},{8,9},{9,8},{10,11... | collective-permute-start | bytes 2359304 | tf_op jit(solution)/shard_map/ppermute | solution.py:28
  282.2 34.7 %collective-permute-start.19 = (bf16[2,2,512,256]{3,2,1,0:T(8,128)(2,1)}, bf16[2,2,512,256]{3,2,1,0:T(8,128)(2,1)}, u32[]{:S(2)}, u32[]{:S(2)}) collective-permute-start(bf16[2,2,512,256]{3,2,1,0:T(8,128)(2,1)} %get-tuple-element.53), channel_id=1, source_target_pairs={{0,2},{1,3},{2,0},{3,1},{4,6},{5,7},{6,4},{7,5},{8,10},{9,11},{10,... | collective-permute-start | bytes 3145736 | tf_op jit(solution)/shard_map/ppermute | solution.py:28
  283.8 4.2 %copy-start.10 = (bf16[2,512,384]{2,1,0:T(8,128)(2,1)}, bf16[2,512,384]{2,1,0:T(8,128)(2,1)S(1)}, u32[]{:S(2)}) copy-start(bf16[2,512,384]{2,1,0:T(8,128)(2,1)S(1)} %collective-permute-done.17.k3_ref.v3_ref) | copy-start | bytes 2359300
  288.0 24.7 %collective-permute-start.18 = (bf16[4,416,128]{2,1,0:T(8,128)(2,1)}, bf16[4,416,128]{2,1,0:T(8,128)(2,1)}, u32[]{:S(2)}, u32[]{:S(2)}) collective-permute-start(bf16[4,416,128]{2,1,0:T(8,128)(2,1)} %far_tiles.7), channel_id=1, source_target_pairs={{0,4},{4,0},{8,12},{12,8},{16,20},{20,16},{24,28},{28,24},{1,5},{5... | collective-permute-start | bytes 1277960 | tf_op jit(solution)/shard_map/ppermute | solution.py:28
  290.5 4.2 %copy-start.12 = (bf16[2,512,384]{2,1,0:T(8,128)(2,1)}, bf16[2,512,384]{2,1,0:T(8,128)(2,1)S(1)}, u32[]{:S(2)}) copy-start(bf16[2,512,384]{2,1,0:T(8,128)(2,1)S(1)} %collective-permute-done.21.k3_ref.v3_ref) | copy-start | bytes 2359300
  294.7 20.2 %collective-permute-start.22 = (bf16[4,416,128]{2,1,0:T(8,128)(2,1)}, bf16[4,416,128]{2,1,0:T(8,128)(2,1)}, u32[]{:S(2)}, u32[]{:S(2)}) collective-permute-start(bf16[4,416,128]{2,1,0:T(8,128)(2,1)} %far_tiles.9), channel_id=1, source_target_pairs={{0,4},{4,0},{8,12},{12,8},{16,20},{20,16},{24,28},{28,24},{1,5},{5... | collective-permute-start | bytes 1277960 | tf_op jit(solution)/shard_map/ppermute | solution.py:28
  301.0 1.6 copy-start.1
  302.6 1.2 copy-start.6
  303.8 1.1 copy-start.11
  304.9 3.5 copy-start.13
  308.4 3.5 copy-start.15
  312.6 26.8 %copy-start.34 = (f32[16]{0:T(128)S(1)}, f32[16]{0:T(128)}, u32[]{:S(2)}) copy-start(f32[16]{0:T(128)} %param.18) | copy-start | bytes 196
  312.6 26.8 %copy-start.2 = (f32[1024,512]{1,0:T(8,128)S(1)}, f32[1024,512]{1,0:T(8,128)}, u32[]{:S(2)}) copy-start(f32[1024,512]{1,0:T(8,128)} %copy-done) | copy-start | bytes 6291460
  318.0 17.9 %collective-permute-start.23 = (bf16[2,512,256]{2,1,0:T(8,128)(2,1)S(1)}, bf16[2,512,256]{2,1,0:T(8,128)(2,1)S(1)}, u32[]{:S(2)}, u32[]{:S(2)}) collective-permute-start(bf16[2,512,256]{2,1,0:T(8,128)(2,1)S(1)} %slice_bitcast_fusion.2), channel_id=1, source_target_pairs={{0,1},{1,0},{2,3},{3,2},{4,5},{5,4},{6,7},{7,6},{8,9},{9,8},{10,11... | collective-permute-start | bytes 1572872 | tf_op jit(solution)/shard_map/ppermute | solution.py:28
  318.1 16.9 %collective-permute-start.24 = (bf16[416,128]{1,0:T(8,128)(2,1)}, bf16[416,128]{1,0:T(8,128)(2,1)S(1)}, u32[]{:S(2)}, u32[]{:S(2)}) collective-permute-start(bf16[416,128]{1,0:T(8,128)(2,1)} %get-tuple-element.61), channel_id=1, source_target_pairs={{0,24},{4,28},{8,0},{12,4},{16,8},{20,12},{24,16},{28,20},{1,25},{... | collective-permute-start | bytes 319496 | tf_op jit(solution)/shard_map/ppermute | solution.py:33
  331.0 16.9 %collective-permute-start.25 = (bf16[416,128]{1,0:T(8,128)(2,1)}, bf16[416,128]{1,0:T(8,128)(2,1)S(1)}, u32[]{:S(2)}, u32[]{:S(2)}) collective-permute-start(bf16[416,128]{1,0:T(8,128)(2,1)} %get-tuple-element.62), channel_id=1, source_target_pairs={{0,16},{4,20},{8,24},{12,28},{16,0},{20,4},{24,8},{28,12},{1,17},{... | collective-permute-start | bytes 319496 | tf_op jit(solution)/shard_map/ppermute | solution.py:33
  331.2 16.8 %collective-permute-start.26 = (bf16[416,128]{1,0:T(8,128)(2,1)}, bf16[416,128]{1,0:T(8,128)(2,1)S(1)}, u32[]{:S(2)}, u32[]{:S(2)}) collective-permute-start(bf16[416,128]{1,0:T(8,128)(2,1)} %get-tuple-element.63), channel_id=1, source_target_pairs={{0,8},{4,12},{8,16},{12,20},{16,24},{20,28},{24,0},{28,4},{1,9},{5... | collective-permute-start | bytes 319496 | tf_op jit(solution)/shard_map/ppermute | solution.py:33
  331.6 19.1 %collective-permute-start.27 = (bf16[416,128]{1,0:T(8,128)(2,1)}, bf16[416,128]{1,0:T(8,128)(2,1)S(1)}, u32[]{:S(2)}, u32[]{:S(2)}) collective-permute-start(bf16[416,128]{1,0:T(8,128)(2,1)} %get-tuple-element.65), channel_id=1, source_target_pairs={{0,24},{4,28},{8,0},{12,4},{16,8},{20,12},{24,16},{28,20},{1,25},{... | collective-permute-start | bytes 319496 | tf_op jit(solution)/shard_map/ppermute | solution.py:33
  335.0 9.3 %copy-start.26 = (bf16[416,128]{1,0:T(8,128)(2,1)}, bf16[416,128]{1,0:T(8,128)(2,1)S(1)}, u32[]{:S(2)}) copy-start(bf16[416,128]{1,0:T(8,128)(2,1)S(1)} %collective-permute-done.24.refs_1_) | copy-start | bytes 319492
  335.0 15.7 %collective-permute-start.28 = (bf16[416,128]{1,0:T(8,128)(2,1)}, bf16[416,128]{1,0:T(8,128)(2,1)S(1)}, u32[]{:S(2)}, u32[]{:S(2)}) collective-permute-start(bf16[416,128]{1,0:T(8,128)(2,1)} %get-tuple-element.66), channel_id=1, source_target_pairs={{0,16},{4,20},{8,24},{12,28},{16,0},{20,4},{24,8},{28,12},{1,17},{... | collective-permute-start | bytes 319496 | tf_op jit(solution)/shard_map/ppermute | solution.py:33
  335.9 14.8 %collective-permute-start.29 = (bf16[416,128]{1,0:T(8,128)(2,1)}, bf16[416,128]{1,0:T(8,128)(2,1)S(1)}, u32[]{:S(2)}, u32[]{:S(2)}) collective-permute-start(bf16[416,128]{1,0:T(8,128)(2,1)} %get-tuple-element.67), channel_id=1, source_target_pairs={{0,8},{4,12},{8,16},{12,20},{16,24},{20,28},{24,0},{28,4},{1,9},{5... | collective-permute-start | bytes 319496 | tf_op jit(solution)/shard_map/ppermute | solution.py:33
  339.4 1.2 copy-start.7
  340.7 3.6 copy-start.4
  340.7 3.6 copy-start.9
  344.3 3.6 copy-start.16
  347.9 0.8 copy-start.27
  347.9 11.8 %collective-permute-start.30 = (bf16[4,272,128]{2,1,0:T(8,128)(2,1)S(1)}, bf16[4,272,128]{2,1,0:T(8,128)(2,1)S(1)}, u32[]{:S(2)}, u32[]{:S(2)}) collective-permute-start(bf16[4,272,128]{2,1,0:T(8,128)(2,1)S(1)} %far_tiles.11), channel_id=1, source_target_pairs={{0,4},{4,0},{8,12},{12,8},{16,20},{20,16},{24,28},{28,24},{1,5},{5... | collective-permute-start | bytes 835592 | tf_op jit(solution)/shard_map/ppermute | solution.py:28
  350.7 5.3 %copy-start.17 = (bf16[384,128]{1,0:T(8,128)(2,1)S(1)}, bf16[384,128]{1,0:T(8,128)(2,1)}, u32[]{:S(2)}) copy-start(bf16[384,128]{1,0:T(8,128)(2,1)} %merge_all.3) | copy-start | bytes 294916
  354.1 2.0 copy-start.18
  362.3 5.1 %collective-permute-start.31 = (bf16[272,128]{1,0:T(8,128)(2,1)}, bf16[272,128]{1,0:T(8,128)(2,1)S(1)}, u32[]{:S(2)}, u32[]{:S(2)}) collective-permute-start(bf16[272,128]{1,0:T(8,128)(2,1)} %get-tuple-element.70), channel_id=1, source_target_pairs={{0,24},{4,28},{8,0},{12,4},{16,8},{20,12},{24,16},{28,20},{1,25},{... | collective-permute-start | bytes 208904 | tf_op jit(solution)/shard_map/ppermute | solution.py:33
  363.2 7.9 %collective-permute-start.32 = (bf16[272,128]{1,0:T(8,128)(2,1)}, bf16[272,128]{1,0:T(8,128)(2,1)S(1)}, u32[]{:S(2)}, u32[]{:S(2)}) collective-permute-start(bf16[272,128]{1,0:T(8,128)(2,1)} %get-tuple-element.71), channel_id=1, source_target_pairs={{0,16},{4,20},{8,24},{12,28},{16,0},{20,4},{24,8},{28,12},{1,17},{... | collective-permute-start | bytes 208904 | tf_op jit(solution)/shard_map/ppermute | solution.py:33
  363.7 7.3 %collective-permute-start.33 = (bf16[272,128]{1,0:T(8,128)(2,1)}, bf16[272,128]{1,0:T(8,128)(2,1)S(1)}, u32[]{:S(2)}, u32[]{:S(2)}) collective-permute-start(bf16[272,128]{1,0:T(8,128)(2,1)} %get-tuple-element.72), channel_id=1, source_target_pairs={{0,8},{4,12},{8,16},{12,20},{16,24},{20,28},{24,0},{28,4},{1,9},{5... | collective-permute-start | bytes 208904 | tf_op jit(solution)/shard_map/ppermute | solution.py:33
  367.4 3.6 copy-start.31
  374.2 3.3 copy-start.21
  375.5 2.0 collective-permute-start.35
  377.0 3.4 collective-permute-start.34
  378.8 8.3 %collective-permute-start.36 = (bf16[128,1024]{1,0:T(8,128)(2,1)S(1)}, bf16[128,1024]{1,0:T(8,128)(2,1)S(1)}, u32[]{:S(2)}, u32[]{:S(2)}) collective-permute-start(bf16[128,1024]{1,0:T(8,128)(2,1)S(1)} %fusion.12), channel_id=1, source_target_pairs={{0,2},{1,3},{2,0},{3,1},{4,6},{5,7},{6,4},{7,5},{8,10},{9,11},{10,... | collective-permute-start | bytes 786440 | tf_op jit(solution)/shard_map/ppermute | solution.py:28
  (8 other events, 5.3 us)

commit v6 on v5

--- a/solution.py
+++ b/solution.py
@@ -39,28 +39,18 @@
     return lax.ppermute(block, axis, route)
 
 
-def share_kernel(sizes, me_ref, keys_ref, values_ref, near_ref, *rest):
-    *far_refs, sems = rest
+def share_kernel(sizes, me_ref, keys_ref, values_ref, near_ref, *far_refs):
     features = near_ref.shape[2]
-    copies = []
-
-    def copy(k, first, target, cols):
+
+    def block(source, k, first, cols):
         start = pl.multiple_of((me_ref[0] ^ k) * features + first * DH, PAIR)
-        for which, source in enumerate((keys_ref, values_ref)):
-            copies.append(
-                pltpu.make_async_copy(
-                    source.at[:, pl.ds(start, cols)], target.at[which], sems.at[len(copies)]
-                )
-            )
-
-    for j, far_ref in enumerate(far_refs):
-        for k in (2, 3):
-            copy(k, sum(sizes[:j]), far_ref.at[k - 2], sizes[j] * DH)
-    copy(1, 0, near_ref, features)
-    for one in copies:
-        one.start()
-    for one in copies:
-        one.wait()
+        return source[:, pl.ds(start, cols)]
+
+    for which, source in enumerate((keys_ref, values_ref)):
+        for j, far_ref in enumerate(far_refs):
+            for k in (2, 3):
+                far_ref[k - 2, which] = block(source, k, sum(sizes[:j]), sizes[j] * DH)
+        near_ref[which] = block(source, 1, 0, features)
 
 
 def pipelined(q_ref, key_refs, vt_ref, bits_ref, s_ref, first_bit, emit):
@@ -334,17 +324,22 @@
     hidden = jnp.zeros((row_count, mem_size * hidden_states.shape[1]), jnp.bfloat16)
     for k in range(mem_size):
         hidden = lax.dynamic_update_slice(hidden, have[k], (0, (me ^ k) * hidden_states.shape[1]))
+    share_rows = mem_rows // 4
     near_block, *far_blocks = pl.pallas_call(
         functools.partial(share_kernel, sizes),
-        in_specs=[
-            pl.BlockSpec(memory_space=pltpu.SMEM),
-            pl.BlockSpec(memory_space=pl.ANY),
-            pl.BlockSpec(memory_space=pl.ANY),
-        ],
-        out_specs=[pl.BlockSpec(memory_space=pl.ANY)] * (1 + chunks),
+        grid_spec=pltpu.PrefetchScalarGridSpec(
+            num_scalar_prefetch=1,
+            grid=(4,),
+            in_specs=[pl.BlockSpec((share_rows, memory_keys.shape[1]), lambda i, m: (i, 0))] * 2,
+            out_specs=[pl.BlockSpec((2, share_rows, features), lambda i, m: (0, i, 0))]
+            + [
+                pl.BlockSpec((2, 2, share_rows, n * DH), lambda i, m: (0, 0, i, 0)) for n in sizes
+            ],
+        ),
         out_shape=[jax.ShapeDtypeStruct((2, mem_rows, features), jnp.bfloat16)]
         + [jax.ShapeDtypeStruct((2, 2, mem_rows, n * DH), jnp.bfloat16) for n in sizes],
-        scratch_shapes=[pltpu.SemaphoreType.DMA((2 + 4 * chunks,))],
+        compiler_params=pltpu.CompilerParams(vmem_limit_bytes=48 << 20),
+        cost_estimate=pl.CostEstimate(flops=0, transcendentals=0, bytes_accessed=14 << 20),
         name="share_tiles",
     )(me.reshape(1), memory_keys, memory_values)
     queries = jnp.dot(
@@ -356,9 +351,32 @@
     q_blocks += [swap(q, "ctx", 1) for q in q_blocks]
     near = swap(near_block, "mem", 1)
     crossed.append(swap(after(far_blocks[1], queries), "mem", 2))
-    window = jnp.stack([local_keys, after(local_values, q_blocks[-1])])
-    window = from_behind(window, "ctx", 1)
     q_halves = [jnp.concatenate(q_blocks[part * turns : (part + 1) * turns], 0) for part in range(2)]
+
+    window = from_behind(jnp.stack([local_keys, local_values]), "ctx", 1)
+    pair_spec = pl.BlockSpec((row_count, PAIR), lambda p, c: (0, p))
+    local_out = pl.pallas_call(
+        local_kernel,
+        grid_spec=pltpu.PrefetchScalarGridSpec(
+            num_scalar_prefetch=1,
+            grid=(pairs,),
+            in_specs=[
+                pair_spec,
+                pl.BlockSpec((None, row_count, PAIR), lambda p, c: (0, 0, p)),
+                pair_spec,
+                pl.BlockSpec((None, row_count, PAIR), lambda p, c: (1, 0, p)),
+                pair_spec,
+            ],
+            out_specs=pl.BlockSpec((PAIR, row_count), lambda p, c: (p, 0)),
+        ),
+        out_shape=jax.ShapeDtypeStruct((features, row_count), f32),
+        cost_estimate=pl.CostEstimate(
+            flops=8 * row_count * row_count * features,
+            transcendentals=2 * row_count * row_count * heads_here,
+            bytes_accessed=2 << 20,
+        ),
+        name="local_window",
+    )(my_ctx.reshape(1), queries, window, local_keys, window, local_values)
 
     near_flops = 2 * 2 * half * 2 * mem_rows * features
 
@@ -370,10 +388,10 @@
 
     chunk_pairs = NEAR_HEADS // 2
     near_state = []
-    q_halves[0] = after(q_halves[0], crossed[0])
+    q_halves[0] = after(q_halves[0], crossed[0], local_out)
     for part in range(2):
         if part == 1:
-            q_halves[1] = after(q_halves[1], window, near_state[0][1])
+            q_halves[1] = after(q_halves[1], near_state[0][1])
             crossed.append(
                 swap(after(far_blocks[2], near_state[0][1]), "mem", 2)
             )
@@ -411,31 +429,6 @@
             )(me.reshape(1), q_halves[part], memory_keys, memory_values, near, near, bits[part])
         )
 
-    own_queries, _ = lax.optimization_barrier((queries, near_state[1][1]))
-    pair_spec = pl.BlockSpec((row_count, PAIR), lambda p, c: (0, p))
-    local_out = pl.pallas_call(
-        local_kernel,
-        grid_spec=pltpu.PrefetchScalarGridSpec(
-            num_scalar_prefetch=1,
-            grid=(pairs,),
-            in_specs=[
-                pair_spec,
-                pl.BlockSpec((None, row_count, PAIR), lambda p, c: (0, 0, p)),
-                pair_spec,
-                pl.BlockSpec((None, row_count, PAIR), lambda p, c: (1, 0, p)),
-                pair_spec,
-            ],
-            out_specs=pl.BlockSpec((PAIR, row_count), lambda p, c: (p, 0)),
-        ),
-        out_shape=jax.ShapeDtypeStruct((features, row_count), f32),
-        cost_estimate=pl.CostEstimate(
-            flops=8 * row_count * row_count * features,
-            transcendentals=2 * row_count * row_count * heads_here,
-            bytes_accessed=2 << 20,
-        ),
-        name="local_window",
-    )(my_ctx.reshape(1), own_queries, window, local_keys, window, local_values)
-
     gate = jax.nn.sigmoid(gate_bias)
     gate_rows = jnp.broadcast_to(gate[:, None], (heads_here, row_count))
     cols = w_output.shape[1] // mem_size
@@ -452,15 +445,18 @@
         wide = heads * DH
         msg_rows = wide + stat_rows(heads)
         tokens = [near_state[0][1], near_state[1][1]]
-        if j >= 2:
-            tokens += messages[j - 2] + messages[j - 1]
+        if j >= 1:
+            tokens += messages[j - 1]
         if j == chunks - 1:
-            tokens += [local_out] + merges
+            tokens += merges + answers[0]
         far2 = after(crossed[j], *tokens)
         far3 = swap(far2[1], "mem", 1)
         message = [None, None]
         for part in (1, 0):
             acc, stat = near_state[part]
+            asked = q_halves[part]
+            if part == 0 and j == chunks - 1:
+                asked = after(asked, message[1])
             message[part] = pl.pallas_call(
                 far_kernel,
                 grid=(1,),
@@ -487,7 +483,7 @@
                     bytes_accessed=3 << 20,
                 ),
                 name="far_tiles",
-            )(q_halves[part], far2, far2, far3, far3, bits[part], acc, stat)
+            )(asked, far2, far2, far3, far3, bits[part], acc, stat)
         messages.append(message)
         other = swap(message[1], "ctx", 1)
         merged = pl.pallas_call(

time: 391 us -> 192 us (0.49)
  Pallas kernels: 254 us -> 66.3 us
  starting transfers between devices: 56.4 us -> 44.4 us
  other arithmetic: 1.03 us -> 5.2 us
    pallas_call x1, Pallas kernels: 192 us -> 6.24 us  [on_device(): pl.pallas_call(functools.partial(share_kernel, sizes), grid_spec=pltpu.Pr...]
    ppermute x15, starting transfers between devices: 32.7 us -> 24.5 us  [turn(): lax.ppermute(block, axis, [(i, (i + distance) % size) for i in range(size)])]
    ppermute x15, waiting for transfers between devices: 24.1 us -> 18.4 us  [turn(): lax.ppermute(block, axis, [(i, (i + distance) % size) for i in range(size)])]
    ppermute x21, waiting for transfers between devices: 21.2 us -> 25.9 us  [swap(): lax.ppermute(block, axis, [(i, i ^ distance) for i in range(lax.axis_size...]
    unnamed x70 -> x68, local copies, waits for them, and re-layouts: 10.6 us -> 11.5 us
  transfers between devices with their start and end apart: 37 -> 37, of which waited for: 11 -> 11; matrix products, arithmetic and copies ran while one was open for 4% -> 11% of each run, Pallas kernels for 64% -> 33%
where the time goes in v6:
time: 192 us; the launch traced here: 191 us
  Pallas kernels  66.3 us (35%)
  starting transfers between devices  44.4 us (23%)
  waiting for transfers between devices  44.3 us (23%)
  matrix products  15.4 us (8%)
  local copies, waits for them, and re-layouts  14.5 us (8%)
  other arithmetic  5.2 us (3%)
    ppermute x21, waiting for transfers between devices, swap(): lax.ppermute(block, axis, [(i, i ^ distance) for i in range(lax.axis_size...  25.9 us
    ppermute x15, starting transfers between devices, turn(): lax.ppermute(block, axis, [(i, (i + distance) % size) for i in range(size)])  24.5 us
    pallas_call x2, Pallas kernels, on_device(): pl.pallas_call(near_kernel, grid_spec=pltpu.PrefetchScalarGridSpec(num_sc...  22.3 us
    pallas_call x6, Pallas kernels, on_device(): pl.pallas_call(far_kernel, grid=(1,), in_specs=[pl.BlockSpec((pl.Element(...  19.5 us
    ppermute x15, waiting for transfers between devices, turn(): lax.ppermute(block, axis, [(i, (i + distance) % size) for i in range(size)])  18.4 us
    ppermute x21, starting transfers between devices, swap(): lax.ppermute(block, axis, [(i, i ^ distance) for i in range(lax.axis_size...  16.3 us
    unnamed x68, local copies, waits for them, and re-layouts  11.5 us
    dot_general x4, matrix products, on_device(): lax.dot_general(mixed, weights(k, 0, first + heads), over_rows, preferred...  7.38 us
  transfers between devices with their start and end apart: 37, of which 11 were waited for; matrix products, arithmetic and copies ran while one was open for 11% of the time, Pallas kernels for 33%

profile of v6, /device:TPU:0, one launch (start us, length us, event | category | flops | bytes accessed | tf_op | source)
XLA Modules:
  0.0 190.6 jit_solution(4720375902041807750)
XLA Ops:
  0.5 2.5 %collective-permute-start.1 = (bf16[128,1024]{1,0:T(8,128)(2,1)}, bf16[128,1024]{1,0:T(8,128)(2,1)}, u32[]{:S(2)}, u32[]{:S(2)}) collective-permute-start(bf16[128,1024]{1,0:T(8,128)(2,1)} %param.10), channel_id=1, source_target_pairs={{0,2},{1,3},{2,0},{3,1},{4,6},{5,7},{6,4},{7,5},{8,10},{9,11},{10,... | collective-permute-start | bytes 786440 | tf_op jit(solution)/shard_map/ppermute | solution.py:28
  3.0 0.7 fusion.29
  3.7 1.5 collective-permute-start.3
  5.2 1.9 pad_maximum_fusion.2
  7.4 3.6 %collective-permute-start.6 = (s32[2,16,128]{2,1,0:T(8,128)S(1)}, s32[2,16,128]{2,1,0:T(8,128)S(1)}, u32[]{:S(2)}, u32[]{:S(2)}) collective-permute-start(s32[2,16,128]{2,1,0:T(8,128)S(1)} %get-tuple-element.72), channel_id=1, source_target_pairs={{0,24},{4,28},{8,0},{12,4},{16,8},{20,12},{24,16},{28,20},{1,25},{... | collective-permute-start | bytes 49160 | tf_op jit(solution)/shard_map/ppermute | solution.py:33
  11.0 1.0 collective-permute-start.4
  12.2 6.2 %share_tiles.1 = (bf16[2,512,1024]{2,1,0:T(8,128)(2,1)}, bf16[2,2,512,384]{3,2,1,0:T(8,128)(2,1)}, bf16[2,2,512,384]{3,2,1,0:T(8,128)(2,1)S(1)}, bf16[2,2,512,256]{3,2,1,0:T(8,128)(2,1)}) custom-call(s32[1]{0:T(128)} %bitcast.me_ref.m_ref, bf16[512,4096]{1,0:T(8,128)(2,1)} %k0_ref.3, bf16[512,4096]{1,0:T(8,128)(2,1)} %v0_ref.3), custom_call_target="tpu_custom_call" | custom-call | bytes 14680064 | tf_op jit(solution)/shard_map/share_tiles/pallas_call | solution.py:328
  18.4 3.7 %collective-permute-start.11 = (bf16[2,128,1024]{2,1,0:T(8,128)(2,1)}, bf16[2,128,1024]{2,1,0:T(8,128)(2,1)S(1)}, u32[]{:S(2)}, u32[]{:S(2)}) collective-permute-start(bf16[2,128,1024]{2,1,0:T(8,128)(2,1)} %pad_maximum_fusion.2), channel_id=1, source_target_pairs={{0,4},{4,8},{8,12},{12,16},{16,20},{20,24},{24,28},{1,5},{5,9},{9,... | collective-permute-start | bytes 1572872 | tf_op jit(solution)/shard_map/ppermute | solution.py:39
  22.9 0.7 copy-done.24
  24.2 1.0 constant_dynamic-update-slice_fusion.2
  25.1 1.0 constant_dynamic-update-slice_fusion.1
  26.7 2.0 %convolution_convert_fusion.q_ref = bf16[128,1024]{1,0:T(8,128)(2,1)} fusion(bf16[128,4096]{1,0:T(8,128)(2,1)S(1)} %constant_dynamic-update-slice_fusion, bf16[4096,1024]{1,0:T(8,128)(2,1)S(1)} %copy-done.17), kind=kOutput, calls=%fused_computation.17 | convolution fusion | flops 1073872896 | bytes 9699328 | tf_op jit(solution)/shard_map/dot_general | solution.py:345
  28.7 2.8 %collective-permute-start.9 = (bf16[128,1024]{1,0:T(8,128)(2,1)}, bf16[128,1024]{1,0:T(8,128)(2,1)S(1)}, u32[]{:S(2)}, u32[]{:S(2)}) collective-permute-start(bf16[128,1024]{1,0:T(8,128)(2,1)} %convolution_convert_fusion.q_ref), channel_id=1, source_target_pairs={{0,24},{4,28},{8,0},{12,4},{16,8},{20,12},{24,16},{28,20},{1,25},{... | collective-permute-start | bytes 786440 | tf_op jit(solution)/shard_map/ppermute | solution.py:33
  31.5 1.1 collective-permute-start.8
  32.6 6.4 %collective-permute-start.7 = (bf16[128,1024]{1,0:T(8,128)(2,1)}, bf16[128,1024]{1,0:T(8,128)(2,1)}, u32[]{:S(2)}, u32[]{:S(2)}) collective-permute-start(bf16[128,1024]{1,0:T(8,128)(2,1)} %convolution_convert_fusion.q_ref), channel_id=1, source_target_pairs={{0,8},{4,12},{8,16},{12,20},{16,24},{20,28},{24,0},{28,4},{1,9},{5... | collective-permute-start | bytes 786440 | tf_op jit(solution)/shard_map/ppermute | solution.py:33
  39.0 3.8 %collective-permute-start.13 = (bf16[128,1024]{1,0:T(8,128)(2,1)}, bf16[128,1024]{1,0:T(8,128)(2,1)S(1)}, u32[]{:S(2)}, u32[]{:S(2)}) collective-permute-start(bf16[128,1024]{1,0:T(8,128)(2,1)} %convolution_convert_fusion.q_ref), channel_id=1, source_target_pairs={{0,4},{4,0},{8,12},{12,8},{16,20},{20,16},{24,28},{28,24},{1,5},{5... | collective-permute-start | bytes 786440 | tf_op jit(solution)/shard_map/ppermute | solution.py:28
  42.9 13.3 %collective-permute-done.8 = bf16[128,1024]{1,0:T(8,128)(2,1)S(1)} collective-permute-done((bf16[128,1024]{1,0:T(8,128)(2,1)}, bf16[128,1024]{1,0:T(8,128)(2,1)S(1)}, u32[]{:S(2)}, u32[]{:S(2)}) %collective-permute-start.8) | collective-permute-done | bytes 262176 | tf_op jit(solution)/shard_map/ppermute | solution.py:33
  56.2 2.0 %collective-permute-start.15 = (bf16[128,1024]{1,0:T(8,128)(2,1)S(1)}, bf16[128,1024]{1,0:T(8,128)(2,1)}, u32[]{:S(2)}, u32[]{:S(2)}) collective-permute-start(bf16[128,1024]{1,0:T(8,128)(2,1)S(1)} %collective-permute-done.8), channel_id=1, source_target_pairs={{0,4},{4,0},{8,12},{12,8},{16,20},{20,16},{24,28},{28,24},{1,5},{5... | collective-permute-start | bytes 786440 | tf_op jit(solution)/shard_map/ppermute | solution.py:28
  58.3 6.3 %local_window.1.refs_4_ = f32[1024,128]{1,0:T(8,128)} custom-call(s32[1]{0:T(128)} %bitcast.9.ctx_ref, bf16[128,1024]{1,0:T(8,128)(2,1)} %convolution_convert_fusion.q_ref, bf16[2,128,1024]{2,1,0:T(8,128)(2,1)} %copy-done.20, bf16[128,1024]{1,0:T(8,128)(2,1)} %k1_ref.1, bf16[2,128,1024]{2,1,0:T(8,128)(2,1)} %copy-done.20, bf16[128,1024]{1,0:T(8,128)(2,1)} %v1_ref.1), custom_call_target="tpu_custom_call" | custom-call | flops 134217728 | bytes 2097152 | tf_op jit(solution)/shard_map/local_window/pallas_call | solution.py:358
  64.6 1.2 pad_maximum_fusion.q_ref
  66.7 4.4 %collective-permute-done.15 = bf16[128,1024]{1,0:T(8,128)(2,1)} collective-permute-done((bf16[128,1024]{1,0:T(8,128)(2,1)S(1)}, bf16[128,1024]{1,0:T(8,128)(2,1)}, u32[]{:S(2)}, u32[]{:S(2)}) %collective-permute-start.15) | collective-permute-done | bytes 262176 | tf_op jit(solution)/shard_map/ppermute | solution.py:28
  71.1 4.1 %collective-permute-done.14 = bf16[128,1024]{1,0:T(8,128)(2,1)} collective-permute-done((bf16[128,1024]{1,0:T(8,128)(2,1)}, bf16[128,1024]{1,0:T(8,128)(2,1)}, u32[]{:S(2)}, u32[]{:S(2)}) %collective-permute-start.14) | collective-permute-done | bytes 262176 | tf_op jit(solution)/shard_map/ppermute | solution.py:28
  75.2 1.3 pad_maximum_fusion.1.q_ref
  76.5 10.8 %near_tiles.2 = (f32[1024,512]{1,0:T(8,128)S(1)}, f32[8,8,512]{2,1,0:T(8,128)S(1)}) custom-call(s32[1]{0:T(128)} %bitcast.me_ref.m_ref, bf16[512,1024]{1,0:T(8,128)(2,1)S(1)} %pad_maximum_fusion.q_ref, bf16[512,4096]{1,0:T(8,128)(2,1)} %k0_ref.3, bf16[512,4096]{1,0:T(8,128)(2,1)} %v0_ref.3, bf16[2,512,1024]{2,1,0:T(8,128)(2,1)} %collective-permute-done.12.k1_ref.v1_ref, ...), custom_call_target="tpu_custom_call" | custom-call | flops 2147483648 | bytes 8388608 | tf_op jit(solution)/shard_map/near_tiles/pallas_call | solution.py:399
  87.4 11.4 %near_tiles.3 = (f32[1024,512]{1,0:T(8,128)S(1)}, f32[8,8,512]{2,1,0:T(8,128)S(1)}) custom-call(s32[1]{0:T(128)} %bitcast.me_ref.m_ref, bf16[512,1024]{1,0:T(8,128)(2,1)S(1)} %pad_maximum_fusion.1.q_ref, bf16[512,4096]{1,0:T(8,128)(2,1)} %k0_ref.3, bf16[512,4096]{1,0:T(8,128)(2,1)} %v0_ref.3, bf16[2,512,1024]{2,1,0:T(8,128)(2,1)} %collective-permute-done.12.k1_ref.v1_ref, ...), custom_call_target="tpu_custom_call" | custom-call | flops 2147483648 | bytes 8388608 | tf_op jit(solution)/shard_map/near_tiles/pallas_call | solution.py:399
  99.0 2.3 %collective-permute-done.17.k3_ref.v3_ref = bf16[2,512,384]{2,1,0:T(8,128)(2,1)S(1)} collective-permute-done((bf16[2,512,384]{2,1,0:T(8,128)(2,1)S(1)}, bf16[2,512,384]{2,1,0:T(8,128)(2,1)S(1)}, u32[]{:S(2)}, u32[]{:S(2)}) %collective-permute-start.17) | collective-permute-done | bytes 786464 | tf_op jit(solution)/shard_map/ppermute | solution.py:28
  101.3 3.4 %far_tiles.6.a_ref = bf16[4,416,128]{2,1,0:T(8,128)(2,1)S(1)} custom-call(bf16[512,1024]{1,0:T(8,128)(2,1)S(1)} %pad_maximum_fusion.q_ref, bf16[2,2,512,384]{3,2,1,0:T(8,128)(2,1)S(1)} %collective-permute-done.10.k2_ref.v2_ref, bf16[2,2,512,384]{3,2,1,0:T(8,128)(2,1)S(1)} %collective-permute-done.10.k2_ref.v2_ref, ...), custom_call_target="tpu_custom_call" | custom-call | flops 805306368 | bytes 3145728 | tf_op jit(solution)/shard_map/far_tiles/pallas_call | solution.py:460
  104.7 3.4 %far_tiles.7 = bf16[4,416,128]{2,1,0:T(8,128)(2,1)S(1)} custom-call(bf16[512,1024]{1,0:T(8,128)(2,1)S(1)} %pad_maximum_fusion.1.q_ref, bf16[2,2,512,384]{3,2,1,0:T(8,128)(2,1)S(1)} %collective-permute-done.10.k2_ref.v2_ref, bf16[2,2,512,384]{3,2,1,0:T(8,128)(2,1)S(1)} %collective-permute-done.10.k2_ref.v2_ref, ...), custom_call_target="tpu_custom_call" | custom-call | flops 805306368 | bytes 3145728 | tf_op jit(solution)/shard_map/far_tiles/pallas_call | solution.py:460
  108.9 1.8 collective-permute-done.21.k3_ref.v3_ref
  110.6 4.2 %far_tiles.9 = bf16[4,416,128]{2,1,0:T(8,128)(2,1)} custom-call(bf16[512,1024]{1,0:T(8,128)(2,1)S(1)} %pad_maximum_fusion.1.q_ref, bf16[2,2,512,384]{3,2,1,0:T(8,128)(2,1)S(1)} %collective-permute-done.20.k2_ref.v2_ref, bf16[2,2,512,384]{3,2,1,0:T(8,128)(2,1)S(1)} %collective-permute-done.20.k2_ref.v2_ref, ...), custom_call_target="tpu_custom_call" | custom-call | flops 805306368 | bytes 3145728 | tf_op jit(solution)/shard_map/far_tiles/pallas_call | solution.py:460
  115.2 6.0 %collective-permute-done.18.b_ref = bf16[4,416,128]{2,1,0:T(8,128)(2,1)} collective-permute-done((bf16[4,416,128]{2,1,0:T(8,128)(2,1)S(1)}, bf16[4,416,128]{2,1,0:T(8,128)(2,1)}, u32[]{:S(2)}, u32[]{:S(2)}) %collective-permute-start.18) | collective-permute-done | bytes 426016 | tf_op jit(solution)/shard_map/ppermute | solution.py:28
  121.3 2.0 %merge_pair.3 = (bf16[416,128]{1,0:T(8,128)(2,1)}, bf16[416,128]{1,0:T(8,128)(2,1)}, bf16[416,128]{1,0:T(8,128)(2,1)}, bf16[416,128]{1,0:T(8,128)(2,1)}) custom-call(bf16[4,416,128]{2,1,0:T(8,128)(2,1)} %copy-done.12, bf16[4,416,128]{2,1,0:T(8,128)(2,1)} %collective-permute-done.18.b_ref), custom_call_target="tpu_custom_call" | custom-call | tf_op jit(solution)/shard_map/merge_pair/pallas_call | solution.py:489
  123.5 2.0 %collective-permute-start.25 = (bf16[416,128]{1,0:T(8,128)(2,1)}, bf16[416,128]{1,0:T(8,128)(2,1)}, u32[]{:S(2)}, u32[]{:S(2)}) collective-permute-start(bf16[416,128]{1,0:T(8,128)(2,1)} %get-tuple-element.58), channel_id=1, source_target_pairs={{0,8},{4,12},{8,16},{12,20},{16,24},{20,28},{24,0},{28,4},{1,9},{5... | collective-permute-start | bytes 319496 | tf_op jit(solution)/shard_map/ppermute | solution.py:33
  125.5 1.6 copy-done.1
  127.1 1.2 copy-done.6
  128.3 1.1 copy-done.11
  129.5 3.4 %far_tiles.8.a_ref = bf16[4,416,128]{2,1,0:T(8,128)(2,1)S(1)} custom-call(bf16[512,1024]{1,0:T(8,128)(2,1)S(1)} %copy-done.6, bf16[2,2,512,384]{3,2,1,0:T(8,128)(2,1)S(1)} %collective-permute-done.20.k2_ref.v2_ref, bf16[2,2,512,384]{3,2,1,0:T(8,128)(2,1)S(1)} %collective-permute-done.20.k2_ref.v2_ref, bf16[2,512,384]{2,1,0:T(8,128)(2,1)S(1)} %copy-done.11, ...), custom_call_target="tpu_custom_call" | custom-call | flops 805306368 | bytes 3145728 | tf_op jit(solution)/shard_map/far_tiles/pallas_call | solution.py:460
  132.9 0.8 copy-done.13
  133.7 2.1 %merge_pair.4 = (bf16[416,128]{1,0:T(8,128)(2,1)}, bf16[416,128]{1,0:T(8,128)(2,1)}, bf16[416,128]{1,0:T(8,128)(2,1)}, bf16[416,128]{1,0:T(8,128)(2,1)}) custom-call(bf16[4,416,128]{2,1,0:T(8,128)(2,1)} %copy-done.13, bf16[4,416,128]{2,1,0:T(8,128)(2,1)} %collective-permute-done.22.b_ref), custom_call_target="tpu_custom_call" | custom-call | tf_op jit(solution)/shard_map/merge_pair/pallas_call | solution.py:489
  136.0 2.2 %collective-permute-start.27 = (bf16[416,128]{1,0:T(8,128)(2,1)}, bf16[416,128]{1,0:T(8,128)(2,1)S(1)}, u32[]{:S(2)}, u32[]{:S(2)}) collective-permute-start(bf16[416,128]{1,0:T(8,128)(2,1)} %get-tuple-element.63), channel_id=1, source_target_pairs={{0,24},{4,28},{8,0},{12,4},{16,8},{20,12},{24,16},{28,20},{1,25},{... | collective-permute-start | bytes 319496 | tf_op jit(solution)/shard_map/ppermute | solution.py:33
  138.2 0.7 collective-permute-start.28
  138.9 1.9 %collective-permute-start.29 = (bf16[416,128]{1,0:T(8,128)(2,1)}, bf16[416,128]{1,0:T(8,128)(2,1)S(1)}, u32[]{:S(2)}, u32[]{:S(2)}) collective-permute-start(bf16[416,128]{1,0:T(8,128)(2,1)} %get-tuple-element.65), channel_id=1, source_target_pairs={{0,8},{4,12},{8,16},{12,20},{16,24},{20,28},{24,0},{28,4},{1,9},{5... | collective-permute-start | bytes 319496 | tf_op jit(solution)/shard_map/ppermute | solution.py:33
  140.8 1.7 copy-done.4
  142.6 2.5 %far_tiles.10 = bf16[4,272,128]{2,1,0:T(8,128)(2,1)S(1)} custom-call(bf16[512,1024]{1,0:T(8,128)(2,1)S(1)} %copy-done.9, bf16[2,2,512,256]{3,2,1,0:T(8,128)(2,1)S(1)} %collective-permute-done.19.k2_ref.v2_ref, bf16[2,2,512,256]{3,2,1,0:T(8,128)(2,1)S(1)} %collective-permute-done.19.k2_ref.v2_ref, ...), custom_call_target="tpu_custom_call" | custom-call | flops 536870912 | bytes 3145728 | tf_op jit(solution)/shard_map/far_tiles/pallas_call | solution.py:460
  145.1 2.5 %far_tiles.11.a_ref = bf16[4,272,128]{2,1,0:T(8,128)(2,1)S(1)} custom-call(bf16[512,1024]{1,0:T(8,128)(2,1)S(1)} %copy-done.7, bf16[2,2,512,256]{3,2,1,0:T(8,128)(2,1)S(1)} %collective-permute-done.19.k2_ref.v2_ref, bf16[2,2,512,256]{3,2,1,0:T(8,128)(2,1)S(1)} %collective-permute-done.19.k2_ref.v2_ref, ...), custom_call_target="tpu_custom_call" | custom-call | flops 536870912 | bytes 3145728 | tf_op jit(solution)/shard_map/far_tiles/pallas_call | solution.py:460
  147.5 0.7 copy-done.14
  148.6 0.7 broadcast_in_dim.20.refs_5_
  149.3 2.0 %merge_all.3 = bf16[384,128]{1,0:T(8,128)(2,1)} custom-call(bf16[416,128]{1,0:T(8,128)(2,1)} %get-tuple-element.61.refs_0_, bf16[416,128]{1,0:T(8,128)(2,1)} %copy-done.26, bf16[416,128]{1,0:T(8,128)(2,1)} %collective-permute-done.24.refs_2_, bf16[416,128]{1,0:T(8,128)(2,1)} %collective-permute-done.25.refs_3_, f32[1024,128]{1,0:T(8,128)} %local_window.1.refs_4_, ...), custom_call_target="tpu_custom_call" | custom-call | tf_op jit(solution)/shard_map/merge_all/pallas_call | solution.py:502
  152.6 2.0 %merge_all.4 = bf16[384,128]{1,0:T(8,128)(2,1)} custom-call(bf16[416,128]{1,0:T(8,128)(2,1)} %get-tuple-element.62.refs_0_, bf16[416,128]{1,0:T(8,128)(2,1)} %copy-done.27, bf16[416,128]{1,0:T(8,128)(2,1)} %copy-done.28, bf16[416,128]{1,0:T(8,128)(2,1)} %copy-done.29, f32[1024,128]{1,0:T(8,128)} %local_window.1.refs_4_, f32[16,128]{1,0:T(8,128)} %broadcast_in_dim.20.refs_5_), custom_call_target="tpu_custom_call" | custom-call | tf_op jit(solution)/shard_map/merge_all/pallas_call | solution.py:502
  154.7 1.9 %fusion.6 = f32[128,1024]{1,0:T(8,128)S(1)} fusion(bf16[1024,4096]{1,0:T(8,128)(2,1)} %param.19, s32[]{:T(128)S(6)} %select_n.47, bf16[384,128]{1,0:T(8,128)(2,1)} %merge_all.4, bf16[384,128]{1,0:T(8,128)(2,1)} %merge_all.3), kind=kOutput, calls=%fused_computation.6 | convolution fusion | flops 201719808 | bytes 2293764 | tf_op jit(solution)/shard_map/dot_general | solution.py:511
  156.6 1.8 fusion.4
  158.5 1.8 fusion.2
  160.3 0.7 copy-done.22
  161.0 1.8 merge_pair.5
  162.8 1.9 collective-permute-start.31
  165.3 1.8 fusion
  167.7 4.5 %collective-permute-done.32.refs_2_ = bf16[272,128]{1,0:T(8,128)(2,1)S(1)} collective-permute-done((bf16[272,128]{1,0:T(8,128)(2,1)}, bf16[272,128]{1,0:T(8,128)(2,1)S(1)}, u32[]{:S(2)}, u32[]{:S(2)}) %collective-permute-start.32) | collective-permute-done | bytes 69664 | tf_op jit(solution)/shard_map/ppermute | solution.py:33
  173.4 1.9 %merge_all.5 = bf16[256,128]{1,0:T(8,128)(2,1)} custom-call(bf16[272,128]{1,0:T(8,128)(2,1)} %get-tuple-element.67.refs_0_, bf16[272,128]{1,0:T(8,128)(2,1)} %copy-done.30, bf16[272,128]{1,0:T(8,128)(2,1)} %copy-done.31, bf16[272,128]{1,0:T(8,128)(2,1)} %copy-done.32, f32[1024,128]{1,0:T(8,128)} %local_window.1.refs_4_, f32[16,128]{1,0:T(8,128)} %broadcast_in_dim.20.refs_5_), custom_call_target="tpu_custom_call" | custom-call | tf_op jit(solution)/shard_map/merge_all/pallas_call | solution.py:502
  175.4 1.4 fusion.14
  176.8 1.3 fusion.13
  178.7 1.3 fusion.12
  180.0 2.1 %collective-permute-start.36 = (bf16[128,1024]{1,0:T(8,128)(2,1)S(1)}, bf16[128,1024]{1,0:T(8,128)(2,1)S(1)}, u32[]{:S(2)}, u32[]{:S(2)}) collective-permute-start(bf16[128,1024]{1,0:T(8,128)(2,1)S(1)} %fusion.12), channel_id=1, source_target_pairs={{0,2},{1,3},{2,0},{3,1},{4,6},{5,7},{6,4},{7,5},{8,10},{9,11},{10,... | collective-permute-start | bytes 786440 | tf_op jit(solution)/shard_map/ppermute | solution.py:28
  182.1 6.5 %collective-permute-done.36 = bf16[128,1024]{1,0:T(8,128)(2,1)S(1)} collective-permute-done((bf16[128,1024]{1,0:T(8,128)(2,1)S(1)}, bf16[128,1024]{1,0:T(8,128)(2,1)S(1)}, u32[]{:S(2)}, u32[]{:S(2)}) %collective-permute-start.36) | collective-permute-done | bytes 262176 | tf_op jit(solution)/shard_map/ppermute | solution.py:28
  188.6 2.0 %fusion.11 = bf16[128,1024]{1,0:T(8,128)(2,1)} fusion(f32[128,1024]{1,0:T(8,128)S(1)} %fusion.6, bf16[256,128]{1,0:T(8,128)(2,1)S(1)} %copy-done.21, bf16[128,1024]{1,0:T(8,128)(2,1)S(1)} %collective-permute-done.36, bf16[128,1024]{1,0:T(8,128)(2,1)S(1)} %collective-permute-done.34, bf16[1024,4096]{1,0:T(8,128)(2,1)} %param.19, s32[]{:T(128)S(6)} %select_n.47), kind=kOutput, calls=%fused_computation.15 | convolution fusion | flops 67895296 | bytes 1900548 | tf_op jit(solution)/shard_map/dot_general | solution.py:518
  (120 shorter events, 9.8 us)
Async XLA Ops:
  0.0 12.1 %copy-start.23 = (bf16[128,1024]{1,0:T(8,128)(2,1)S(1)}, bf16[128,1024]{1,0:T(8,128)(2,1)}, u32[]{:S(2)}) copy-start(bf16[128,1024]{1,0:T(8,128)(2,1)} %param.10) | copy-start | bytes 786436
  0.0 22.9 %collective-permute-start = (bf16[128,1024]{1,0:T(8,128)(2,1)}, bf16[128,1024]{1,0:T(8,128)(2,1)S(1)}, u32[]{:S(2)}, u32[]{:S(2)}) collective-permute-start(bf16[128,1024]{1,0:T(8,128)(2,1)} %param.10), channel_id=1, source_target_pairs={{0,1},{1,0},{2,3},{3,2},{4,5},{5,4},{6,7},{7,6},{8,9},{9,8},{10,11... | collective-permute-start | bytes 786440 | tf_op jit(solution)/shard_map/ppermute | solution.py:28
  0.5 21.9 %collective-permute-start.1 = (bf16[128,1024]{1,0:T(8,128)(2,1)}, bf16[128,1024]{1,0:T(8,128)(2,1)}, u32[]{:S(2)}, u32[]{:S(2)}) collective-permute-start(bf16[128,1024]{1,0:T(8,128)(2,1)} %param.10), channel_id=1, source_target_pairs={{0,2},{1,3},{2,0},{3,1},{4,6},{5,7},{6,4},{7,5},{8,10},{9,11},{10,... | collective-permute-start | bytes 786440 | tf_op jit(solution)/shard_map/ppermute | solution.py:28
  3.7 3.7 %collective-permute-start.3 = (s32[16,128]{1,0:T(8,128)S(1)}, s32[16,128]{1,0:T(8,128)S(1)}, u32[]{:S(2)}, u32[]{:S(2)}) collective-permute-start(s32[16,128]{1,0:T(8,128)S(1)} %get-tuple-element.74), channel_id=1, source_target_pairs={{0,4},{4,0},{8,12},{12,8},{16,20},{20,16},{24,28},{28,24},{1,5},{5... | collective-permute-start | bytes 24584 | tf_op jit(solution)/shard_map/ppermute | solution.py:28
  7.4 11.0 %collective-permute-start.6 = (s32[2,16,128]{2,1,0:T(8,128)S(1)}, s32[2,16,128]{2,1,0:T(8,128)S(1)}, u32[]{:S(2)}, u32[]{:S(2)}) collective-permute-start(s32[2,16,128]{2,1,0:T(8,128)S(1)} %get-tuple-element.72), channel_id=1, source_target_pairs={{0,24},{4,28},{8,0},{12,4},{16,8},{20,12},{24,16},{28,20},{1,25},{... | collective-permute-start | bytes 49160 | tf_op jit(solution)/shard_map/ppermute | solution.py:33
  11.0 11.2 %collective-permute-start.5 = (s32[2,16,128]{2,1,0:T(8,128)S(1)}, s32[2,16,128]{2,1,0:T(8,128)S(1)}, u32[]{:S(2)}, u32[]{:S(2)}) collective-permute-start(s32[2,16,128]{2,1,0:T(8,128)S(1)} %get-tuple-element.72), channel_id=1, source_target_pairs={{0,16},{4,20},{8,24},{12,28},{16,0},{20,4},{24,8},{28,12},{1,17},{... | collective-permute-start | bytes 49160 | tf_op jit(solution)/shard_map/ppermute | solution.py:33
  11.0 11.3 %collective-permute-start.4 = (s32[2,16,128]{2,1,0:T(8,128)S(1)}, s32[2,16,128]{2,1,0:T(8,128)S(1)}, u32[]{:S(2)}, u32[]{:S(2)}) collective-permute-start(s32[2,16,128]{2,1,0:T(8,128)S(1)} %get-tuple-element.72), channel_id=1, source_target_pairs={{0,8},{4,12},{8,16},{12,20},{16,24},{20,28},{24,0},{28,4},{1,9},{5... | collective-permute-start | bytes 49160 | tf_op jit(solution)/shard_map/ppermute | solution.py:33
  12.2 14.5 %copy-start.17 = (bf16[4096,1024]{1,0:T(8,128)(2,1)S(1)}, bf16[4096,1024]{1,0:T(8,128)(2,1)}, u32[]{:S(2)}) copy-start(bf16[4096,1024]{1,0:T(8,128)(2,1)} %param.11) | copy-start | bytes 25165828
  18.4 10.3 %copy-start.15 = (bf16[2,2,512,384]{3,2,1,0:T(8,128)(2,1)}, bf16[2,2,512,384]{3,2,1,0:T(8,128)(2,1)S(1)}, u32[]{:S(2)}) copy-start(bf16[2,2,512,384]{3,2,1,0:T(8,128)(2,1)S(1)} %get-tuple-element.53) | copy-start | bytes 4718596
  18.4 14.2 %collective-permute-start.11 = (bf16[2,128,1024]{2,1,0:T(8,128)(2,1)}, bf16[2,128,1024]{2,1,0:T(8,128)(2,1)S(1)}, u32[]{:S(2)}, u32[]{:S(2)}) collective-permute-start(bf16[2,128,1024]{2,1,0:T(8,128)(2,1)} %pad_maximum_fusion.2), channel_id=1, source_target_pairs={{0,4},{4,8},{8,12},{12,16},{16,20},{20,24},{24,28},{1,5},{5,9},{9,... | collective-permute-start | bytes 1572872 | tf_op jit(solution)/shard_map/ppermute | solution.py:39
  22.1 54.4 %collective-permute-start.12 = (bf16[2,512,1024]{2,1,0:T(8,128)(2,1)}, bf16[2,512,1024]{2,1,0:T(8,128)(2,1)}, u32[]{:S(2)}, u32[]{:S(2)}) collective-permute-start(bf16[2,512,1024]{2,1,0:T(8,128)(2,1)} %get-tuple-element.42), channel_id=1, source_target_pairs={{0,1},{1,0},{2,3},{3,2},{4,5},{5,4},{6,7},{7,6},{8,9},{9,8},{10,11... | collective-permute-start | bytes 6291464 | tf_op jit(solution)/shard_map/ppermute | solution.py:28
  22.4 4.3 %collective-permute-start.2 = (bf16[128,1024]{1,0:T(8,128)(2,1)}, bf16[128,1024]{1,0:T(8,128)(2,1)S(1)}, u32[]{:S(2)}, u32[]{:S(2)}) collective-permute-start(bf16[128,1024]{1,0:T(8,128)(2,1)} %collective-permute-done.1), channel_id=1, source_target_pairs={{0,1},{1,0},{2,3},{3,2},{4,5},{5,4},{6,7},{7,6},{8,9},{9,8},{10,11... | collective-permute-start | bytes 786440 | tf_op jit(solution)/shard_map/ppermute | solution.py:28
  23.6 52.9 %collective-permute-start.10 = (bf16[2,2,512,384]{3,2,1,0:T(8,128)(2,1)}, bf16[2,2,512,384]{3,2,1,0:T(8,128)(2,1)S(1)}, u32[]{:S(2)}, u32[]{:S(2)}) collective-permute-start(bf16[2,2,512,384]{3,2,1,0:T(8,128)(2,1)} %get-tuple-element.40), channel_id=1, source_target_pairs={{0,2},{1,3},{2,0},{3,1},{4,6},{5,7},{6,4},{7,5},{8,10},{9,11},{10,... | collective-permute-start | bytes 4718600 | tf_op jit(solution)/shard_map/ppermute | solution.py:28
  28.7 10.4 %collective-permute-start.9 = (bf16[128,1024]{1,0:T(8,128)(2,1)}, bf16[128,1024]{1,0:T(8,128)(2,1)S(1)}, u32[]{:S(2)}, u32[]{:S(2)}) collective-permute-start(bf16[128,1024]{1,0:T(8,128)(2,1)} %convolution_convert_fusion.q_ref), channel_id=1, source_target_pairs={{0,24},{4,28},{8,0},{12,4},{16,8},{20,12},{24,16},{28,20},{1,25},{... | collective-permute-start | bytes 786440 | tf_op jit(solution)/shard_map/ppermute | solution.py:33
  31.5 24.7 %collective-permute-start.8 = (bf16[128,1024]{1,0:T(8,128)(2,1)}, bf16[128,1024]{1,0:T(8,128)(2,1)S(1)}, u32[]{:S(2)}, u32[]{:S(2)}) collective-permute-start(bf16[128,1024]{1,0:T(8,128)(2,1)} %convolution_convert_fusion.q_ref), channel_id=1, source_target_pairs={{0,16},{4,20},{8,24},{12,28},{16,0},{20,4},{24,8},{28,12},{1,17},{... | collective-permute-start | bytes 786440 | tf_op jit(solution)/shard_map/ppermute | solution.py:33
  32.6 25.7 %copy-start.20 = (bf16[2,128,1024]{2,1,0:T(8,128)(2,1)}, bf16[2,128,1024]{2,1,0:T(8,128)(2,1)S(1)}, u32[]{:S(2)}) copy-start(bf16[2,128,1024]{2,1,0:T(8,128)(2,1)S(1)} %collective-permute-done.11.k0_ref.v0_ref) | copy-start | bytes 1572868
  32.6 23.6 %collective-permute-start.7 = (bf16[128,1024]{1,0:T(8,128)(2,1)}, bf16[128,1024]{1,0:T(8,128)(2,1)}, u32[]{:S(2)}, u32[]{:S(2)}) collective-permute-start(bf16[128,1024]{1,0:T(8,128)(2,1)} %convolution_convert_fusion.q_ref), channel_id=1, source_target_pairs={{0,8},{4,12},{8,16},{12,20},{16,24},{20,28},{24,0},{28,4},{1,9},{5... | collective-permute-start | bytes 786440 | tf_op jit(solution)/shard_map/ppermute | solution.py:33
  39.0 19.2 %collective-permute-start.13 = (bf16[128,1024]{1,0:T(8,128)(2,1)}, bf16[128,1024]{1,0:T(8,128)(2,1)S(1)}, u32[]{:S(2)}, u32[]{:S(2)}) collective-permute-start(bf16[128,1024]{1,0:T(8,128)(2,1)} %convolution_convert_fusion.q_ref), channel_id=1, source_target_pairs={{0,4},{4,0},{8,12},{12,8},{16,20},{20,16},{24,28},{28,24},{1,5},{5... | collective-permute-start | bytes 786440 | tf_op jit(solution)/shard_map/ppermute | solution.py:28
  56.2 9.7 %collective-permute-start.16 = (bf16[128,1024]{1,0:T(8,128)(2,1)S(1)}, bf16[128,1024]{1,0:T(8,128)(2,1)}, u32[]{:S(2)}, u32[]{:S(2)}) collective-permute-start(bf16[128,1024]{1,0:T(8,128)(2,1)S(1)} %collective-permute-done.9), channel_id=1, source_target_pairs={{0,4},{4,0},{8,12},{12,8},{16,20},{20,16},{24,28},{28,24},{1,5},{5... | collective-permute-start | bytes 786440 | tf_op jit(solution)/shard_map/ppermute | solution.py:28
  56.2 14.9 %collective-permute-start.15 = (bf16[128,1024]{1,0:T(8,128)(2,1)S(1)}, bf16[128,1024]{1,0:T(8,128)(2,1)}, u32[]{:S(2)}, u32[]{:S(2)}) collective-permute-start(bf16[128,1024]{1,0:T(8,128)(2,1)S(1)} %collective-permute-done.8), channel_id=1, source_target_pairs={{0,4},{4,0},{8,12},{12,8},{16,20},{20,16},{24,28},{28,24},{1,5},{5... | collective-permute-start | bytes 786440 | tf_op jit(solution)/shard_map/ppermute | solution.py:28
  58.2 7.6 %copy-start.25 = (bf16[128,1024]{1,0:T(8,128)(2,1)}, bf16[128,1024]{1,0:T(8,128)(2,1)S(1)}, u32[]{:S(2)}) copy-start(bf16[128,1024]{1,0:T(8,128)(2,1)S(1)} %collective-permute-done.13) | copy-start | bytes 786436
  58.2 17.0 %collective-permute-start.14 = (bf16[128,1024]{1,0:T(8,128)(2,1)}, bf16[128,1024]{1,0:T(8,128)(2,1)}, u32[]{:S(2)}, u32[]{:S(2)}) collective-permute-start(bf16[128,1024]{1,0:T(8,128)(2,1)} %collective-permute-done.7), channel_id=1, source_target_pairs={{0,4},{4,0},{8,12},{12,8},{16,20},{20,16},{24,28},{28,24},{1,5},{5... | collective-permute-start | bytes 786440 | tf_op jit(solution)/shard_map/ppermute | solution.py:28
  64.6 1.6 copy-start.16
  65.8 35.5 %copy-start.5 = (bf16[512,1024]{1,0:T(8,128)(2,1)}, bf16[512,1024]{1,0:T(8,128)(2,1)S(1)}, u32[]{:S(2)}) copy-start(bf16[512,1024]{1,0:T(8,128)(2,1)S(1)} %pad_maximum_fusion.q_ref) | copy-start | bytes 3145732
  66.2 42.0 %collective-permute-start.20 = (bf16[2,2,512,384]{3,2,1,0:T(8,128)(2,1)S(1)}, bf16[2,2,512,384]{3,2,1,0:T(8,128)(2,1)S(1)}, u32[]{:S(2)}, u32[]{:S(2)}) collective-permute-start(bf16[2,2,512,384]{3,2,1,0:T(8,128)(2,1)S(1)} %copy-done.16), channel_id=1, source_target_pairs={{0,2},{1,3},{2,0},{3,1},{4,6},{5,7},{6,4},{7,5},{8,10},{9,11},{10,... | collective-permute-start | bytes 4718600 | tf_op jit(solution)/shard_map/ppermute | solution.py:28
  76.5 34.1 %copy-start.8 = (bf16[512,1024]{1,0:T(8,128)(2,1)}, bf16[512,1024]{1,0:T(8,128)(2,1)S(1)}, u32[]{:S(2)}) copy-start(bf16[512,1024]{1,0:T(8,128)(2,1)S(1)} %pad_maximum_fusion.1.q_ref) | copy-start | bytes 3145732
  87.4 13.9 %copy-start = (f32[1024,512]{1,0:T(8,128)}, f32[1024,512]{1,0:T(8,128)S(1)}, u32[]{:S(2)}) copy-start(f32[1024,512]{1,0:T(8,128)S(1)} %get-tuple-element.47.acc_ref) | copy-start | bytes 6291460
  98.8 11.8 %copy-start.3 = (f32[1024,512]{1,0:T(8,128)}, f32[1024,512]{1,0:T(8,128)S(1)}, u32[]{:S(2)}) copy-start(f32[1024,512]{1,0:T(8,128)S(1)} %get-tuple-element.48.acc_ref) | copy-start | bytes 6291460
  98.9 2.4 %collective-permute-start.17 = (bf16[2,512,384]{2,1,0:T(8,128)(2,1)S(1)}, bf16[2,512,384]{2,1,0:T(8,128)(2,1)S(1)}, u32[]{:S(2)}, u32[]{:S(2)}) collective-permute-start(bf16[2,512,384]{2,1,0:T(8,128)(2,1)S(1)} %slice_bitcast_fusion.1), channel_id=1, source_target_pairs={{0,1},{1,0},{2,3},{3,2},{4,5},{5,4},{6,7},{7,6},{8,9},{9,8},{10,11... | collective-permute-start | bytes 2359304 | tf_op jit(solution)/shard_map/ppermute | solution.py:28
  104.7 3.4 %copy-start.12 = (bf16[4,416,128]{2,1,0:T(8,128)(2,1)}, bf16[4,416,128]{2,1,0:T(8,128)(2,1)S(1)}, u32[]{:S(2)}) copy-start(bf16[4,416,128]{2,1,0:T(8,128)(2,1)S(1)} %far_tiles.6.a_ref) | copy-start | bytes 1277956
  108.3 2.4 %collective-permute-start.21 = (bf16[2,512,384]{2,1,0:T(8,128)(2,1)S(1)}, bf16[2,512,384]{2,1,0:T(8,128)(2,1)S(1)}, u32[]{:S(2)}, u32[]{:S(2)}) collective-permute-start(bf16[2,512,384]{2,1,0:T(8,128)(2,1)S(1)} %slice_bitcast_fusion), channel_id=1, source_target_pairs={{0,1},{1,0},{2,3},{3,2},{4,5},{5,4},{6,7},{7,6},{8,9},{9,8},{10,11... | collective-permute-start | bytes 2359304 | tf_op jit(solution)/shard_map/ppermute | solution.py:28
  108.5 27.4 %collective-permute-start.19 = (bf16[2,2,512,256]{3,2,1,0:T(8,128)(2,1)}, bf16[2,2,512,256]{3,2,1,0:T(8,128)(2,1)S(1)}, u32[]{:S(2)}, u32[]{:S(2)}) collective-permute-start(bf16[2,2,512,256]{3,2,1,0:T(8,128)(2,1)} %get-tuple-element.51), channel_id=1, source_target_pairs={{0,2},{1,3},{2,0},{3,1},{4,6},{5,7},{6,4},{7,5},{8,10},{9,11},{10,... | collective-permute-start | bytes 3145736 | tf_op jit(solution)/shard_map/ppermute | solution.py:28
  108.5 12.8 %collective-permute-start.18 = (bf16[4,416,128]{2,1,0:T(8,128)(2,1)S(1)}, bf16[4,416,128]{2,1,0:T(8,128)(2,1)}, u32[]{:S(2)}, u32[]{:S(2)}) collective-permute-start(bf16[4,416,128]{2,1,0:T(8,128)(2,1)S(1)} %far_tiles.7), channel_id=1, source_target_pairs={{0,4},{4,0},{8,12},{12,8},{16,20},{20,16},{24,28},{28,24},{1,5},{5... | collective-permute-start | bytes 1277960 | tf_op jit(solution)/shard_map/ppermute | solution.py:28
  110.6 4.2 %copy-start.10 = (bf16[2,512,384]{2,1,0:T(8,128)(2,1)}, bf16[2,512,384]{2,1,0:T(8,128)(2,1)S(1)}, u32[]{:S(2)}) copy-start(bf16[2,512,384]{2,1,0:T(8,128)(2,1)S(1)} %collective-permute-done.21.k3_ref.v3_ref) | copy-start | bytes 2359300
  114.9 18.8 %collective-permute-start.22 = (bf16[4,416,128]{2,1,0:T(8,128)(2,1)}, bf16[4,416,128]{2,1,0:T(8,128)(2,1)}, u32[]{:S(2)}, u32[]{:S(2)}) collective-permute-start(bf16[4,416,128]{2,1,0:T(8,128)(2,1)} %far_tiles.9), channel_id=1, source_target_pairs={{0,4},{4,0},{8,12},{12,8},{16,20},{20,16},{24,28},{28,24},{1,5},{5... | collective-permute-start | bytes 1277960 | tf_op jit(solution)/shard_map/ppermute | solution.py:28
  123.3 12.5 %collective-permute-start.23 = (bf16[416,128]{1,0:T(8,128)(2,1)}, bf16[416,128]{1,0:T(8,128)(2,1)S(1)}, u32[]{:S(2)}, u32[]{:S(2)}) collective-permute-start(bf16[416,128]{1,0:T(8,128)(2,1)} %get-tuple-element.56), channel_id=1, source_target_pairs={{0,24},{4,28},{8,0},{12,4},{16,8},{20,12},{24,16},{28,20},{1,25},{... | collective-permute-start | bytes 319496 | tf_op jit(solution)/shard_map/ppermute | solution.py:33
  123.3 12.6 %collective-permute-start.24 = (bf16[416,128]{1,0:T(8,128)(2,1)}, bf16[416,128]{1,0:T(8,128)(2,1)}, u32[]{:S(2)}, u32[]{:S(2)}) collective-permute-start(bf16[416,128]{1,0:T(8,128)(2,1)} %get-tuple-element.57), channel_id=1, source_target_pairs={{0,16},{4,20},{8,24},{12,28},{16,0},{20,4},{24,8},{28,12},{1,17},{... | collective-permute-start | bytes 319496 | tf_op jit(solution)/shard_map/ppermute | solution.py:33
  123.5 12.4 %collective-permute-start.25 = (bf16[416,128]{1,0:T(8,128)(2,1)}, bf16[416,128]{1,0:T(8,128)(2,1)}, u32[]{:S(2)}, u32[]{:S(2)}) collective-permute-start(bf16[416,128]{1,0:T(8,128)(2,1)} %get-tuple-element.58), channel_id=1, source_target_pairs={{0,8},{4,12},{8,16},{12,20},{16,24},{20,28},{24,0},{28,4},{1,9},{5... | collective-permute-start | bytes 319496 | tf_op jit(solution)/shard_map/ppermute | solution.py:33
  125.5 1.6 copy-start.1
  127.1 1.2 copy-start.6
  128.3 1.1 copy-start.11
  129.5 11.3 %copy-start.33 = (f32[16]{0:T(128)S(1)}, f32[16]{0:T(128)}, u32[]{:S(2)}) copy-start(f32[16]{0:T(128)} %param.18) | copy-start | bytes 196
  132.9 0.8 copy-start.13
  133.7 7.1 %copy-start.9 = (bf16[512,1024]{1,0:T(8,128)(2,1)S(1)}, bf16[512,1024]{1,0:T(8,128)(2,1)}, u32[]{:S(2)}) copy-start(bf16[512,1024]{1,0:T(8,128)(2,1)} %copy-done.8) | copy-start | bytes 3145732
  135.8 9.2 %copy-start.26 = (bf16[416,128]{1,0:T(8,128)(2,1)}, bf16[416,128]{1,0:T(8,128)(2,1)S(1)}, u32[]{:S(2)}) copy-start(bf16[416,128]{1,0:T(8,128)(2,1)S(1)} %collective-permute-done.23.refs_1_) | copy-start | bytes 319492
  135.9 4.9 %collective-permute-start.26 = (bf16[2,512,256]{2,1,0:T(8,128)(2,1)S(1)}, bf16[2,512,256]{2,1,0:T(8,128)(2,1)S(1)}, u32[]{:S(2)}, u32[]{:S(2)}) collective-permute-start(bf16[2,512,256]{2,1,0:T(8,128)(2,1)S(1)} %slice_bitcast_fusion.2), channel_id=1, source_target_pairs={{0,1},{1,0},{2,3},{3,2},{4,5},{5,4},{6,7},{7,6},{8,9},{9,8},{10,11... | collective-permute-start | bytes 1572872 | tf_op jit(solution)/shard_map/ppermute | solution.py:28
  136.0 15.3 %collective-permute-start.27 = (bf16[416,128]{1,0:T(8,128)(2,1)}, bf16[416,128]{1,0:T(8,128)(2,1)S(1)}, u32[]{:S(2)}, u32[]{:S(2)}) collective-permute-start(bf16[416,128]{1,0:T(8,128)(2,1)} %get-tuple-element.63), channel_id=1, source_target_pairs={{0,24},{4,28},{8,0},{12,4},{16,8},{20,12},{24,16},{28,20},{1,25},{... | collective-permute-start | bytes 319496 | tf_op jit(solution)/shard_map/ppermute | solution.py:33
  138.2 13.1 %collective-permute-start.28 = (bf16[416,128]{1,0:T(8,128)(2,1)}, bf16[416,128]{1,0:T(8,128)(2,1)S(1)}, u32[]{:S(2)}, u32[]{:S(2)}) collective-permute-start(bf16[416,128]{1,0:T(8,128)(2,1)} %get-tuple-element.64), channel_id=1, source_target_pairs={{0,16},{4,20},{8,24},{12,28},{16,0},{20,4},{24,8},{28,12},{1,17},{... | collective-permute-start | bytes 319496 | tf_op jit(solution)/shard_map/ppermute | solution.py:33
  138.9 12.5 %collective-permute-start.29 = (bf16[416,128]{1,0:T(8,128)(2,1)}, bf16[416,128]{1,0:T(8,128)(2,1)S(1)}, u32[]{:S(2)}, u32[]{:S(2)}) collective-permute-start(bf16[416,128]{1,0:T(8,128)(2,1)} %get-tuple-element.65), channel_id=1, source_target_pairs={{0,8},{4,12},{8,16},{12,20},{16,24},{20,28},{24,0},{28,4},{1,9},{5... | collective-permute-start | bytes 319496 | tf_op jit(solution)/shard_map/ppermute | solution.py:33
  140.8 4.2 %copy-start.2 = (f32[1024,512]{1,0:T(8,128)S(1)}, f32[1024,512]{1,0:T(8,128)}, u32[]{:S(2)}) copy-start(f32[1024,512]{1,0:T(8,128)} %copy-done) | copy-start | bytes 6291460
  140.8 1.7 copy-start.4
  142.6 2.5 %copy-start.7 = (bf16[512,1024]{1,0:T(8,128)(2,1)S(1)}, bf16[512,1024]{1,0:T(8,128)(2,1)}, u32[]{:S(2)}) copy-start(bf16[512,1024]{1,0:T(8,128)(2,1)} %copy-done.5) | copy-start | bytes 3145732
  147.5 0.7 copy-start.14
  148.3 12.0 %collective-permute-start.30 = (bf16[4,272,128]{2,1,0:T(8,128)(2,1)S(1)}, bf16[4,272,128]{2,1,0:T(8,128)(2,1)S(1)}, u32[]{:S(2)}, u32[]{:S(2)}) collective-permute-start(bf16[4,272,128]{2,1,0:T(8,128)(2,1)S(1)} %far_tiles.10), channel_id=1, source_target_pairs={{0,4},{4,0},{8,12},{12,8},{16,20},{20,16},{24,28},{28,24},{1,5},{5... | collective-permute-start | bytes 835592 | tf_op jit(solution)/shard_map/ppermute | solution.py:28
  151.3 5.3 %copy-start.18 = (bf16[384,128]{1,0:T(8,128)(2,1)S(1)}, bf16[384,128]{1,0:T(8,128)(2,1)}, u32[]{:S(2)}) copy-start(bf16[384,128]{1,0:T(8,128)(2,1)} %merge_all.3) | copy-start | bytes 294916
  154.7 2.0 %copy-start.19 = (bf16[384,128]{1,0:T(8,128)(2,1)S(1)}, bf16[384,128]{1,0:T(8,128)(2,1)}, u32[]{:S(2)}) copy-start(bf16[384,128]{1,0:T(8,128)(2,1)} %merge_all.4) | copy-start | bytes 294916
  162.8 4.8 %collective-permute-start.31 = (bf16[272,128]{1,0:T(8,128)(2,1)}, bf16[272,128]{1,0:T(8,128)(2,1)S(1)}, u32[]{:S(2)}, u32[]{:S(2)}) collective-permute-start(bf16[272,128]{1,0:T(8,128)(2,1)} %get-tuple-element.68), channel_id=1, source_target_pairs={{0,24},{4,28},{8,0},{12,4},{16,8},{20,12},{24,16},{28,20},{1,25},{... | collective-permute-start | bytes 208904 | tf_op jit(solution)/shard_map/ppermute | solution.py:33
  164.7 7.4 %collective-permute-start.32 = (bf16[272,128]{1,0:T(8,128)(2,1)}, bf16[272,128]{1,0:T(8,128)(2,1)S(1)}, u32[]{:S(2)}, u32[]{:S(2)}) collective-permute-start(bf16[272,128]{1,0:T(8,128)(2,1)} %get-tuple-element.69), channel_id=1, source_target_pairs={{0,16},{4,20},{8,24},{12,28},{16,0},{20,4},{24,8},{28,12},{1,17},{... | collective-permute-start | bytes 208904 | tf_op jit(solution)/shard_map/ppermute | solution.py:33
  165.2 7.0 %collective-permute-start.33 = (bf16[272,128]{1,0:T(8,128)(2,1)}, bf16[272,128]{1,0:T(8,128)(2,1)S(1)}, u32[]{:S(2)}, u32[]{:S(2)}) collective-permute-start(bf16[272,128]{1,0:T(8,128)(2,1)} %get-tuple-element.70), channel_id=1, source_target_pairs={{0,8},{4,12},{8,16},{12,20},{16,24},{20,28},{24,0},{28,4},{1,9},{5... | collective-permute-start | bytes 208904 | tf_op jit(solution)/shard_map/ppermute | solution.py:33
  167.7 4.5 %copy-start.30 = (bf16[272,128]{1,0:T(8,128)(2,1)}, bf16[272,128]{1,0:T(8,128)(2,1)S(1)}, u32[]{:S(2)}) copy-start(bf16[272,128]{1,0:T(8,128)(2,1)S(1)} %collective-permute-done.31.refs_1_) | copy-start | bytes 208900
  175.4 3.3 %copy-start.21 = (bf16[256,128]{1,0:T(8,128)(2,1)S(1)}, bf16[256,128]{1,0:T(8,128)(2,1)}, u32[]{:S(2)}) copy-start(bf16[256,128]{1,0:T(8,128)(2,1)} %merge_all.5) | copy-start | bytes 196612
  176.7 2.0 %collective-permute-start.35 = (bf16[128,1024]{1,0:T(8,128)(2,1)S(1)}, bf16[128,1024]{1,0:T(8,128)(2,1)S(1)}, u32[]{:S(2)}, u32[]{:S(2)}) collective-permute-start(bf16[128,1024]{1,0:T(8,128)(2,1)S(1)} %fusion.14), channel_id=1, source_target_pairs={{0,1},{1,0},{2,3},{3,2},{4,5},{5,4},{6,7},{7,6},{8,9},{9,8},{10,11... | collective-permute-start | bytes 786440 | tf_op jit(solution)/shard_map/ppermute | solution.py:28
  178.1 4.0 %collective-permute-start.34 = (bf16[128,1024]{1,0:T(8,128)(2,1)S(1)}, bf16[128,1024]{1,0:T(8,128)(2,1)S(1)}, u32[]{:S(2)}, u32[]{:S(2)}) collective-permute-start(bf16[128,1024]{1,0:T(8,128)(2,1)S(1)} %fusion.13), channel_id=1, source_target_pairs={{0,1},{1,0},{2,3},{3,2},{4,5},{5,4},{6,7},{7,6},{8,9},{9,8},{10,11... | collective-permute-start | bytes 786440 | tf_op jit(solution)/shard_map/ppermute | solution.py:28
  180.0 8.6 %collective-permute-start.36 = (bf16[128,1024]{1,0:T(8,128)(2,1)S(1)}, bf16[128,1024]{1,0:T(8,128)(2,1)S(1)}, u32[]{:S(2)}, u32[]{:S(2)}) collective-permute-start(bf16[128,1024]{1,0:T(8,128)(2,1)S(1)} %fusion.12), channel_id=1, source_target_pairs={{0,2},{1,3},{2,0},{3,1},{4,6},{5,7},{6,4},{7,5},{8,10},{9,11},{10,... | collective-permute-start | bytes 786440 | tf_op jit(solution)/shard_map/ppermute | solution.py:28
  (7 other events, 4.6 us)

commit v7 on v6

--- a/solution.py
+++ b/solution.py
@@ -317,6 +317,7 @@
     bits = jnp.sum(jnp.where(here, 1 << jnp.where(here, place, 0), 0), axis=2)
     bits = [bits[part].reshape(1, half) for part in range(2)]
 
+
     h1 = swap(hidden_states, "mem", 1)
     h2 = swap(hidden_states, "mem", 2)
     h3 = swap(h2, "mem", 1)
@@ -342,16 +343,20 @@
         cost_estimate=pl.CostEstimate(flops=0, transcendentals=0, bytes_accessed=14 << 20),
         name="share_tiles",
     )(me.reshape(1), memory_keys, memory_values)
+    near = swap(near_block, "mem", 1)
     queries = jnp.dot(
-        after(hidden, far_blocks[0], bits[0]), w_query, preferred_element_type=f32
+        after(hidden, far_blocks[0], bits[0], near), w_query, preferred_element_type=f32
     ).astype(jnp.bfloat16)
     crossed = [swap(after(far_blocks[0], h1), "mem", 2)]
 
-    q_blocks = [queries] + [turn(queries, "ctx", 2 * k) for k in range(1, turns)]
-    q_blocks += [swap(q, "ctx", 1) for q in q_blocks]
-    near = swap(near_block, "mem", 1)
+    own_swapped = swap(queries, "ctx", 1)
+    q_blocks = [queries]
+    for k in range(1, turns):
+        near_by = k in (1, turns - 1)
+        q_blocks.append(turn(queries if near_by else after(queries, own_swapped), "ctx", 2 * k))
+    q_blocks += [own_swapped] + [swap(q, "ctx", 1) for q in q_blocks[1:]]
     crossed.append(swap(after(far_blocks[1], queries), "mem", 2))
-    q_halves = [jnp.concatenate(q_blocks[part * turns : (part + 1) * turns], 0) for part in range(2)]
+    q_halves = [jnp.concatenate(q_blocks[:turns], 0), None]
 
     window = from_behind(jnp.stack([local_keys, local_values]), "ctx", 1)
     pair_spec = pl.BlockSpec((row_count, PAIR), lambda p, c: (0, p))
@@ -391,7 +396,7 @@
     q_halves[0] = after(q_halves[0], crossed[0], local_out)
     for part in range(2):
         if part == 1:
-            q_halves[1] = after(q_halves[1], near_state[0][1])
+            q_halves[1] = jnp.concatenate(after(q_blocks[turns:], near_state[0][1]), 0)
             crossed.append(
                 swap(after(far_blocks[2], near_state[0][1]), "mem", 2)
             )
@@ -434,9 +439,6 @@
     cols = w_output.shape[1] // mem_size
     over_rows = (((0,), (0,)), ((), ()))
 
-    def weights(k, first, count):
-        return lax.dynamic_slice(w_output, (first * DH, (me ^ k) * cols), (count * DH, cols))
-
     messages = []
     merges = []
     answers = []
@@ -444,17 +446,15 @@
         heads, first = sizes[j], firsts[j]
         wide = heads * DH
         msg_rows = wide + stat_rows(heads)
-        tokens = [near_state[0][1], near_state[1][1]]
-        if j >= 1:
-            tokens += messages[j - 1]
+        tokens = messages[j - 1] if j >= 1 else [near_state[0][1]]
         if j == chunks - 1:
-            tokens += merges + answers[0]
+            tokens = tokens + merges + answers[0]
         far2 = after(crossed[j], *tokens)
         far3 = swap(far2[1], "mem", 1)
         message = [None, None]
         for part in (1, 0):
             acc, stat = near_state[part]
-            asked = q_halves[part]
+            asked = after(q_halves[part], near_state[1][1])
             if part == 0 and j == chunks - 1:
                 asked = after(asked, message[1])
             message[part] = pl.pallas_call(
@@ -495,33 +495,29 @@
         answers.append([merged[0]] + [turn(merged[k], "ctx", -2 * k) for k in range(1, turns)])
 
     combined = []
-    early = None
     for j in range(chunks):
         heads, first = sizes[j], firsts[j]
-        token = messages[-1][0] if j < chunks - 1 else early
-        mixed = pl.pallas_call(
-            functools.partial(final_kernel, heads, first),
-            out_shape=jax.ShapeDtypeStruct((heads * DH, row_count), jnp.bfloat16),
-            name="merge_all",
-        )(after(answers[j][0], token), *answers[j][1:], local_out, gate_rows)
-        combined.append(mixed)
-        if j == chunks - 2:
-            mixed = jnp.concatenate(combined, axis=0)
-            early = [
-                lax.dot_general(
-                    mixed, weights(k, 0, first + heads), over_rows, preferred_element_type=f32
-                )
-                for k in range(mem_size)
-            ]
-
-    def piece(k):
-        return early[k] + lax.dot_general(
-            combined[-1], weights(k, firsts[-1], sizes[-1]), over_rows, preferred_element_type=f32
+        got = answers[j]
+        if j < chunks - 1:
+            got = [after(got[0], messages[-1][0])] + got[1:]
+        combined.append(
+            pl.pallas_call(
+                functools.partial(final_kernel, heads, first),
+                out_shape=jax.ShapeDtypeStruct((heads * DH, row_count), jnp.bfloat16),
+                name="merge_all",
+            )(*got, local_out, gate_rows)
         )
-
-    away = piece(2) + swap(piece(3).astype(jnp.bfloat16), "mem", 1).astype(f32)
-    away = swap(away.astype(jnp.bfloat16), "mem", 2)
-    result = piece(0) + swap(piece(1).astype(jnp.bfloat16), "mem", 1).astype(f32)
+    combined = jnp.concatenate(combined, axis=0)
+
+    def piece(k, rows):
+        w = lax.dynamic_slice(w_output, (0, (me ^ k) * cols), (features, cols))
+        return lax.dot_general(rows, w, over_rows, preferred_element_type=f32)
+
+    away = swap(piece(3, combined).astype(jnp.bfloat16), "mem", 1)
+    away = (piece(2, combined) + away.astype(f32)).astype(jnp.bfloat16)
+    rest = after(combined, away)
+    away = swap(away, "mem", 2)
+    result = piece(0, rest) + swap(piece(1, rest).astype(jnp.bfloat16), "mem", 1).astype(f32)
     return (result + away.astype(f32)).astype(jnp.bfloat16)
 
 

time: 192 us -> 179 us (0.932)
  waiting for transfers between devices: 44.3 us -> 40.4 us
  starting transfers between devices: 44.4 us -> 41.2 us
  other arithmetic: 5.2 us -> 2.26 us
  matrix products: 15.4 us -> 13.1 us
    ppermute x15, waiting for transfers between devices: 18.4 us -> 8.22 us  [turn(): lax.ppermute(block, axis, [(i, (i + distance) % size) for i in range(size)])]
    ppermute x21, waiting for transfers between devices: 25.9 us -> 32.2 us  [swap(): lax.ppermute(block, axis, [(i, i ^ distance) for i in range(lax.axis_size...]
    dot_general x9 -> x5, matrix products: 15.4 us -> 13.1 us  [the longest x4 8.42 us: piece(): return lax.dot_general(rows, w, over_rows, preferred_element_type=f32)]
    unnamed x68 -> x75, local copies, waits for them, and re-layouts: 11.5 us -> 12.1 us
  transfers between devices with their start and end apart: 37 -> 37, of which waited for: 11 -> 10; matrix products, arithmetic and copies ran while one was open for 11% -> 6% of each run, Pallas kernels for 33% -> 31%
where the time goes in v7:
time: 179 us; the launch traced here: 178 us
  Pallas kernels  65.9 us (37%)
  starting transfers between devices  41.2 us (23%)
  waiting for transfers between devices  40.4 us (23%)
  local copies, waits for them, and re-layouts  14.2 us (8%)
  matrix products  13.1 us (7%)
  other arithmetic  2.26 us (1%)
    ppermute x21, waiting for transfers between devices, swap(): lax.ppermute(block, axis, [(i, i ^ distance) for i in range(lax.axis_size...  32.2 us
    ppermute x15, starting transfers between devices, turn(): lax.ppermute(block, axis, [(i, (i + distance) % size) for i in range(size)])  22.6 us
    pallas_call x2, Pallas kernels, on_device(): pl.pallas_call(near_kernel, grid_spec=pltpu.PrefetchScalarGridSpec(num_sc...  21.6 us
    pallas_call x6, Pallas kernels, on_device(): pl.pallas_call(far_kernel, grid=(1,), in_specs=[pl.BlockSpec((pl.Element(...  19.6 us
    ppermute x21, starting transfers between devices, swap(): lax.ppermute(block, axis, [(i, i ^ distance) for i in range(lax.axis_size...  14.4 us
    unnamed x75, local copies, waits for them, and re-layouts  12.1 us
    dot_general x4, matrix products, piece(): return lax.dot_general(rows, w, over_rows, preferred_element_type=f32)  8.42 us
    ppermute x15, waiting for transfers between devices, turn(): lax.ppermute(block, axis, [(i, (i + distance) % size) for i in range(size)])  8.22 us
  transfers between devices with their start and end apart: 37, of which 10 were waited for; matrix products, arithmetic and copies ran while one was open for 6% of the time, Pallas kernels for 31%

profile of v7, /device:TPU:0, one launch (start us, length us, event | category | flops | bytes accessed | tf_op | source)
XLA Modules:
  0.0 177.6 jit_solution(13458043351973718421)
XLA Ops:
  0.0 6.4 %share_tiles.1 = (bf16[2,512,1024]{2,1,0:T(8,128)(2,1)}, bf16[2,2,512,384]{3,2,1,0:T(8,128)(2,1)}, bf16[2,2,512,384]{3,2,1,0:T(8,128)(2,1)}, bf16[2,2,512,256]{3,2,1,0:T(8,128)(2,1)}) custom-call(s32[1]{0:T(128)} %bitcast.me_ref.m_ref, bf16[512,4096]{1,0:T(8,128)(2,1)} %k0_ref.3, bf16[512,4096]{1,0:T(8,128)(2,1)} %v0_ref.3), custom_call_target="tpu_custom_call" | custom-call | bytes 14680064 | tf_op jit(solution)/shard_map/share_tiles/pallas_call | solution.py:329
  6.9 2.6 %collective-permute-start.3 = (s32[16,128]{1,0:T(8,128)S(1)}, s32[16,128]{1,0:T(8,128)S(1)}, u32[]{:S(2)}, u32[]{:S(2)}) collective-permute-start(s32[16,128]{1,0:T(8,128)S(1)} %get-tuple-element.86), channel_id=1, source_target_pairs={{0,4},{4,0},{8,12},{12,8},{16,20},{20,16},{24,28},{28,24},{1,5},{5... | collective-permute-start | bytes 24584 | tf_op jit(solution)/shard_map/ppermute | solution.py:28
  9.5 1.5 collective-permute-start.1
  11.2 3.1 %collective-permute-start.5 = (s32[2,16,128]{2,1,0:T(8,128)S(1)}, s32[2,16,128]{2,1,0:T(8,128)S(1)}, u32[]{:S(2)}, u32[]{:S(2)}) collective-permute-start(s32[2,16,128]{2,1,0:T(8,128)S(1)} %get-tuple-element.84), channel_id=1, source_target_pairs={{0,16},{4,20},{8,24},{12,28},{16,0},{20,4},{24,8},{28,12},{1,17},{... | collective-permute-start | bytes 49160 | tf_op jit(solution)/shard_map/ppermute | solution.py:33
  14.3 1.6 collective-permute-start.4
  16.0 4.0 %collective-permute-start.6 = (s32[2,16,128]{2,1,0:T(8,128)S(1)}, s32[2,16,128]{2,1,0:T(8,128)S(1)}, u32[]{:S(2)}, u32[]{:S(2)}) collective-permute-start(s32[2,16,128]{2,1,0:T(8,128)S(1)} %get-tuple-element.84), channel_id=1, source_target_pairs={{0,24},{4,28},{8,0},{12,4},{16,8},{20,12},{24,16},{28,20},{1,25},{... | collective-permute-start | bytes 49160 | tf_op jit(solution)/shard_map/ppermute | solution.py:33
  20.2 4.2 %collective-permute-start.13 = (bf16[2,128,1024]{2,1,0:T(8,128)(2,1)S(1)}, bf16[2,128,1024]{2,1,0:T(8,128)(2,1)}, u32[]{:S(2)}, u32[]{:S(2)}) collective-permute-start(bf16[2,128,1024]{2,1,0:T(8,128)(2,1)S(1)} %pad_maximum_fusion.1), channel_id=1, source_target_pairs={{0,4},{4,8},{8,12},{12,16},{16,20},{20,24},{24,28},{1,5},{5,9},{9,... | collective-permute-start | bytes 1572872 | tf_op jit(solution)/shard_map/ppermute | solution.py:39
  24.6 0.7 copy-done.23
  25.3 1.5 collective-permute-start.12
  26.8 1.0 constant_dynamic-update-slice_fusion.6
  27.9 4.7 %convolution_convert_fusion.q_ref = bf16[128,1024]{1,0:T(8,128)(2,1)S(1)} fusion(bf16[128,4096]{1,0:T(8,128)(2,1)S(1)} %constant_dynamic-update-slice_fusion.4, bf16[4096,1024]{1,0:T(8,128)(2,1)} %param.11), kind=kOutput, calls=%fused_computation.12 | convolution fusion | flops 1073872896 | bytes 9699328 | tf_op jit(solution)/shard_map/dot_general | solution.py:347
  32.7 2.8 %collective-permute-start.11 = (bf16[128,1024]{1,0:T(8,128)(2,1)S(1)}, bf16[128,1024]{1,0:T(8,128)(2,1)}, u32[]{:S(2)}, u32[]{:S(2)}) collective-permute-start(bf16[128,1024]{1,0:T(8,128)(2,1)S(1)} %convolution_convert_fusion.q_ref), channel_id=1, source_target_pairs={{0,24},{4,28},{8,0},{12,4},{16,8},{20,12},{24,16},{28,20},{1,25},{... | collective-permute-start | bytes 786440 | tf_op jit(solution)/shard_map/ppermute | solution.py:33
  35.5 5.6 %collective-permute-done.9 = bf16[128,1024]{1,0:T(8,128)(2,1)S(1)} collective-permute-done((bf16[128,1024]{1,0:T(8,128)(2,1)S(1)}, bf16[128,1024]{1,0:T(8,128)(2,1)S(1)}, u32[]{:S(2)}, u32[]{:S(2)}) %collective-permute-start.9) | collective-permute-done | bytes 262176 | tf_op jit(solution)/shard_map/ppermute | solution.py:28
  41.1 0.7 copy-done.24
  42.3 6.3 %local_window.1.refs_4_ = f32[1024,128]{1,0:T(8,128)} custom-call(s32[1]{0:T(128)} %bitcast.9.ctx_ref, bf16[128,1024]{1,0:T(8,128)(2,1)} %copy-done.15, bf16[2,128,1024]{2,1,0:T(8,128)(2,1)} %collective-permute-done.13.k0_ref.v0_ref, bf16[128,1024]{1,0:T(8,128)(2,1)} %k1_ref.1, bf16[2,128,1024]{2,1,0:T(8,128)(2,1)} %collective-permute-done.13.k0_ref.v0_ref, ...), custom_call_target="tpu_custom_call" | custom-call | flops 134217728 | bytes 2097152 | tf_op jit(solution)/shard_map/local_window/pallas_call | solution.py:363
  48.6 0.8 collective-permute-start.16
  49.4 1.2 collective-permute-start.14
  50.6 8.2 %collective-permute-done.10 = bf16[128,1024]{1,0:T(8,128)(2,1)} collective-permute-done((bf16[128,1024]{1,0:T(8,128)(2,1)S(1)}, bf16[128,1024]{1,0:T(8,128)(2,1)}, u32[]{:S(2)}, u32[]{:S(2)}) %collective-permute-start.10) | collective-permute-done | bytes 262176 | tf_op jit(solution)/shard_map/ppermute | solution.py:33
  58.8 1.3 pad_maximum_fusion.q_ref
  60.1 2.6 %collective-permute-done.12.k2_ref.v2_ref = bf16[2,2,512,384]{3,2,1,0:T(8,128)(2,1)S(1)} collective-permute-done((bf16[2,2,512,384]{3,2,1,0:T(8,128)(2,1)}, bf16[2,2,512,384]{3,2,1,0:T(8,128)(2,1)S(1)}, u32[]{:S(2)}, u32[]{:S(2)}) %collective-permute-start.12) | collective-permute-done | bytes 1572896 | tf_op jit(solution)/shard_map/ppermute | solution.py:28
  62.7 10.5 %near_tiles.2 = (f32[1024,512]{1,0:T(8,128)S(1)}, f32[8,8,512]{2,1,0:T(8,128)S(1)}) custom-call(s32[1]{0:T(128)} %bitcast.me_ref.m_ref, bf16[512,1024]{1,0:T(8,128)(2,1)S(1)} %pad_maximum_fusion.q_ref, bf16[512,4096]{1,0:T(8,128)(2,1)} %k0_ref.3, bf16[512,4096]{1,0:T(8,128)(2,1)} %v0_ref.3, bf16[2,512,1024]{2,1,0:T(8,128)(2,1)} %collective-permute-done.7.k1_ref.v1_ref, ...), custom_call_target="tpu_custom_call" | custom-call | flops 2147483648 | bytes 8388608 | tf_op jit(solution)/shard_map/near_tiles/pallas_call | solution.py:404
  73.6 7.5 %collective-permute-done.15 = bf16[128,1024]{1,0:T(8,128)(2,1)S(1)} collective-permute-done((bf16[128,1024]{1,0:T(8,128)(2,1)}, bf16[128,1024]{1,0:T(8,128)(2,1)S(1)}, u32[]{:S(2)}, u32[]{:S(2)}) %collective-permute-start.15) | collective-permute-done | bytes 262176 | tf_op jit(solution)/shard_map/ppermute | solution.py:28
  81.2 11.1 %near_tiles.3 = (f32[1024,512]{1,0:T(8,128)S(1)}, f32[8,8,512]{2,1,0:T(8,128)S(1)}) custom-call(s32[1]{0:T(128)} %bitcast.me_ref.m_ref, bf16[512,1024]{1,0:T(8,128)(2,1)S(1)} %constant_dynamic-update-slice_fusion.q_ref, bf16[512,4096]{1,0:T(8,128)(2,1)} %k0_ref.3, bf16[512,4096]{1,0:T(8,128)(2,1)} %v0_ref.3, ...), custom_call_target="tpu_custom_call" | custom-call | flops 2147483648 | bytes 8388608 | tf_op jit(solution)/shard_map/near_tiles/pallas_call | solution.py:404
  92.3 3.4 %far_tiles.7 = bf16[4,416,128]{2,1,0:T(8,128)(2,1)S(1)} custom-call(bf16[512,1024]{1,0:T(8,128)(2,1)S(1)} %constant_dynamic-update-slice_fusion.q_ref, bf16[2,2,512,384]{3,2,1,0:T(8,128)(2,1)S(1)} %collective-permute-done.12.k2_ref.v2_ref, bf16[2,2,512,384]{3,2,1,0:T(8,128)(2,1)S(1)} %collective-permute-done.12.k2_ref.v2_ref, ...), custom_call_target="tpu_custom_call" | custom-call | flops 805306368 | bytes 3145728 | tf_op jit(solution)/shard_map/far_tiles/pallas_call | solution.py:460
  95.7 3.4 %far_tiles.6.a_ref = bf16[4,416,128]{2,1,0:T(8,128)(2,1)S(1)} custom-call(bf16[512,1024]{1,0:T(8,128)(2,1)S(1)} %pad_maximum_fusion.q_ref, bf16[2,2,512,384]{3,2,1,0:T(8,128)(2,1)S(1)} %collective-permute-done.12.k2_ref.v2_ref, bf16[2,2,512,384]{3,2,1,0:T(8,128)(2,1)S(1)} %collective-permute-done.12.k2_ref.v2_ref, ...), custom_call_target="tpu_custom_call" | custom-call | flops 805306368 | bytes 3145728 | tf_op jit(solution)/shard_map/far_tiles/pallas_call | solution.py:460
  99.4 1.5 collective-permute-start.19
  101.7 4.3 %far_tiles.9 = bf16[4,416,128]{2,1,0:T(8,128)(2,1)} custom-call(bf16[512,1024]{1,0:T(8,128)(2,1)S(1)} %constant_dynamic-update-slice_fusion.q_ref, bf16[2,2,512,384]{3,2,1,0:T(8,128)(2,1)S(1)} %collective-permute-done.20.k2_ref.v2_ref, bf16[2,2,512,384]{3,2,1,0:T(8,128)(2,1)S(1)} %collective-permute-done.20.k2_ref.v2_ref, ...), custom_call_target="tpu_custom_call" | custom-call | flops 805306368 | bytes 3145728 | tf_op jit(solution)/shard_map/far_tiles/pallas_call | solution.py:460
  106.0 1.3 collective-permute-start.22
  107.3 6.4 %collective-permute-done.18.b_ref = bf16[4,416,128]{2,1,0:T(8,128)(2,1)} collective-permute-done((bf16[4,416,128]{2,1,0:T(8,128)(2,1)S(1)}, bf16[4,416,128]{2,1,0:T(8,128)(2,1)}, u32[]{:S(2)}, u32[]{:S(2)}) %collective-permute-start.18) | collective-permute-done | bytes 426016 | tf_op jit(solution)/shard_map/ppermute | solution.py:28
  113.7 2.0 %merge_pair.3 = (bf16[416,128]{1,0:T(8,128)(2,1)}, bf16[416,128]{1,0:T(8,128)(2,1)}, bf16[416,128]{1,0:T(8,128)(2,1)}, bf16[416,128]{1,0:T(8,128)(2,1)}) custom-call(bf16[4,416,128]{2,1,0:T(8,128)(2,1)} %copy-done.10, bf16[4,416,128]{2,1,0:T(8,128)(2,1)} %collective-permute-done.18.b_ref), custom_call_target="tpu_custom_call" | custom-call | tf_op jit(solution)/shard_map/merge_pair/pallas_call | solution.py:489
  115.7 1.1 collective-permute-start.23
  116.9 0.9 collective-permute-start.25
  117.8 1.6 copy-done.1
  119.3 1.2 copy-done.6
  120.6 3.5 %far_tiles.8.a_ref = bf16[4,416,128]{2,1,0:T(8,128)(2,1)S(1)} custom-call(bf16[512,1024]{1,0:T(8,128)(2,1)S(1)} %copy-done.6, bf16[2,2,512,384]{3,2,1,0:T(8,128)(2,1)S(1)} %collective-permute-done.20.k2_ref.v2_ref, bf16[2,2,512,384]{3,2,1,0:T(8,128)(2,1)S(1)} %collective-permute-done.20.k2_ref.v2_ref, ...), custom_call_target="tpu_custom_call" | custom-call | flops 805306368 | bytes 3145728 | tf_op jit(solution)/shard_map/far_tiles/pallas_call | solution.py:460
  124.1 0.7 copy-done.11
  124.8 2.1 %merge_pair.4 = (bf16[416,128]{1,0:T(8,128)(2,1)}, bf16[416,128]{1,0:T(8,128)(2,1)}, bf16[416,128]{1,0:T(8,128)(2,1)}, bf16[416,128]{1,0:T(8,128)(2,1)}) custom-call(bf16[4,416,128]{2,1,0:T(8,128)(2,1)} %copy-done.11, bf16[4,416,128]{2,1,0:T(8,128)(2,1)} %collective-permute-done.22.b_ref), custom_call_target="tpu_custom_call" | custom-call | tf_op jit(solution)/shard_map/merge_pair/pallas_call | solution.py:489
  127.0 1.9 %collective-permute-done.26.k3_ref.v3_ref = bf16[2,512,256]{2,1,0:T(8,128)(2,1)S(1)} collective-permute-done((bf16[2,512,256]{2,1,0:T(8,128)(2,1)S(1)}, bf16[2,512,256]{2,1,0:T(8,128)(2,1)S(1)}, u32[]{:S(2)}, u32[]{:S(2)}) %collective-permute-start.26) | collective-permute-done | bytes 524320 | tf_op jit(solution)/shard_map/ppermute | solution.py:28
  128.9 1.6 copy-done.4
  130.5 1.2 copy-done.9
  131.8 0.9 copy-done.13
  132.7 2.5 %far_tiles.10 = bf16[4,272,128]{2,1,0:T(8,128)(2,1)S(1)} custom-call(bf16[512,1024]{1,0:T(8,128)(2,1)S(1)} %copy-done.9, bf16[2,2,512,256]{3,2,1,0:T(8,128)(2,1)S(1)} %collective-permute-done.19.k2_ref.v2_ref, bf16[2,2,512,256]{3,2,1,0:T(8,128)(2,1)S(1)} %collective-permute-done.19.k2_ref.v2_ref, ...), custom_call_target="tpu_custom_call" | custom-call | flops 536870912 | bytes 3145728 | tf_op jit(solution)/shard_map/far_tiles/pallas_call | solution.py:460
  135.2 1.4 collective-permute-start.30
  136.6 3.3 %collective-permute-start.27 = (bf16[416,128]{1,0:T(8,128)(2,1)}, bf16[416,128]{1,0:T(8,128)(2,1)S(1)}, u32[]{:S(2)}, u32[]{:S(2)}) collective-permute-start(bf16[416,128]{1,0:T(8,128)(2,1)} %get-tuple-element.75), channel_id=1, source_target_pairs={{0,24},{4,28},{8,0},{12,4},{16,8},{20,12},{24,16},{28,20},{1,25},{... | collective-permute-start | bytes 319496 | tf_op jit(solution)/shard_map/ppermute | solution.py:33
  139.8 1.1 collective-permute-start.28
  141.0 2.5 %far_tiles.11.a_ref = bf16[4,272,128]{2,1,0:T(8,128)(2,1)S(1)} custom-call(bf16[512,1024]{1,0:T(8,128)(2,1)S(1)} %copy-done.7, bf16[2,2,512,256]{3,2,1,0:T(8,128)(2,1)S(1)} %collective-permute-done.19.k2_ref.v2_ref, bf16[2,2,512,256]{3,2,1,0:T(8,128)(2,1)S(1)} %collective-permute-done.19.k2_ref.v2_ref, ...), custom_call_target="tpu_custom_call" | custom-call | flops 536870912 | bytes 3145728 | tf_op jit(solution)/shard_map/far_tiles/pallas_call | solution.py:460
  143.5 0.7 copy-done.14
  144.2 0.7 copy-done.21
  144.9 1.8 %merge_pair.5 = (bf16[272,128]{1,0:T(8,128)(2,1)}, bf16[272,128]{1,0:T(8,128)(2,1)}, bf16[272,128]{1,0:T(8,128)(2,1)}, bf16[272,128]{1,0:T(8,128)(2,1)}) custom-call(bf16[4,272,128]{2,1,0:T(8,128)(2,1)} %copy-done.14, bf16[4,272,128]{2,1,0:T(8,128)(2,1)} %copy-done.21), custom_call_target="tpu_custom_call" | custom-call | tf_op jit(solution)/shard_map/merge_pair/pallas_call | solution.py:489
  146.7 3.8 %collective-permute-start.31 = (bf16[272,128]{1,0:T(8,128)(2,1)}, bf16[272,128]{1,0:T(8,128)(2,1)S(1)}, u32[]{:S(2)}, u32[]{:S(2)}) collective-permute-start(bf16[272,128]{1,0:T(8,128)(2,1)} %get-tuple-element.79), channel_id=1, source_target_pairs={{0,24},{4,28},{8,0},{12,4},{16,8},{20,12},{24,16},{28,20},{1,25},{... | collective-permute-start | bytes 208904 | tf_op jit(solution)/shard_map/ppermute | solution.py:33
  150.6 0.9 collective-permute-start.33
  151.4 0.7 broadcast_in_dim.20.refs_5_
  152.1 2.0 %merge_all.3 = bf16[384,128]{1,0:T(8,128)(2,1)} custom-call(bf16[416,128]{1,0:T(8,128)(2,1)} %get-tuple-element.73.refs_0_, bf16[416,128]{1,0:T(8,128)(2,1)} %collective-permute-done.23.refs_1_, bf16[416,128]{1,0:T(8,128)(2,1)} %collective-permute-done.24.refs_2_, bf16[416,128]{1,0:T(8,128)(2,1)} %collective-permute-done.25.refs_3_, ...), custom_call_target="tpu_custom_call" | custom-call | tf_op jit(solution)/shard_map/merge_all/pallas_call | solution.py:504
  154.2 0.6 copy-done.27
  154.8 0.6 copy-done.28
  155.4 2.0 %merge_all.4 = bf16[384,128]{1,0:T(8,128)(2,1)} custom-call(bf16[416,128]{1,0:T(8,128)(2,1)} %get-tuple-element.74.refs_0_, bf16[416,128]{1,0:T(8,128)(2,1)} %copy-done.26, bf16[416,128]{1,0:T(8,128)(2,1)} %copy-done.27, bf16[416,128]{1,0:T(8,128)(2,1)} %copy-done.28, f32[1024,128]{1,0:T(8,128)} %local_window.1.refs_4_, f32[16,128]{1,0:T(8,128)} %broadcast_in_dim.20.refs_5_), custom_call_target="tpu_custom_call" | custom-call | tf_op jit(solution)/shard_map/merge_all/pallas_call | solution.py:504
  158.1 1.9 %merge_all.5 = bf16[256,128]{1,0:T(8,128)(2,1)} custom-call(bf16[272,128]{1,0:T(8,128)(2,1)} %get-tuple-element.78.refs_0_, bf16[272,128]{1,0:T(8,128)(2,1)} %copy-done.29, bf16[272,128]{1,0:T(8,128)(2,1)} %copy-done.30, bf16[272,128]{1,0:T(8,128)(2,1)} %copy-done.31, f32[1024,128]{1,0:T(8,128)} %local_window.1.refs_4_, f32[16,128]{1,0:T(8,128)} %broadcast_in_dim.20.refs_5_), custom_call_target="tpu_custom_call" | custom-call | tf_op jit(solution)/shard_map/merge_all/pallas_call | solution.py:504
  160.0 2.2 %fusion.14 = bf16[128,1024]{1,0:T(8,128)(2,1)S(1)} fusion(bf16[1024,4096]{1,0:T(8,128)(2,1)} %param.19, s32[]{:T(128)S(6)} %select_n.46, bf16[256,128]{1,0:T(8,128)(2,1)} %merge_all.5, bf16[384,128]{1,0:T(8,128)(2,1)} %merge_all.4, bf16[384,128]{1,0:T(8,128)(2,1)} %merge_all.3), kind=kOutput, calls=%fused_computation.10 | convolution fusion | flops 269352960 | bytes 2621444 | tf_op jit(solution)/shard_map/dot_general | solution.py:514
  162.4 1.5 collective-permute-done.34
  163.9 2.1 %fusion.11 = bf16[128,1024]{1,0:T(8,128)(2,1)S(1)} fusion(bf16[1024,4096]{1,0:T(8,128)(2,1)} %param.19, s32[]{:T(128)S(6)} %select_n.45, bf16[128,1024]{1,0:T(8,128)(2,1)S(1)} %collective-permute-done.34, bf16[256,128]{1,0:T(8,128)(2,1)S(1)} %copy-done.20, bf16[384,128]{1,0:T(8,128)(2,1)S(1)} %copy-done.17, bf16[384,128]{1,0:T(8,128)(2,1)S(1)} %copy-done.16), kind=kOutput, calls=%fused_computation.9 | convolution fusion | flops 269615104 | bytes 2883588 | tf_op jit(solution)/shard_map/dot_general | solution.py:514
  166.0 2.1 %fusion.17 = bf16[128,1024]{1,0:T(8,128)(2,1)S(1)} fusion(bf16[1024,128]{1,0:T(8,128)(2,1)S(1)} %pad_maximum_fusion.2, bf16[1024,4096]{1,0:T(8,128)(2,1)} %param.19, s32[]{:T(128)S(6)} %select_n.44), kind=kOutput, calls=%fused_computation.11 | convolution fusion | flops 268566528 | bytes 2621444 | tf_op jit(solution)/shard_map/dot_general | solution.py:514
  168.8 2.1 %fusion.2 = f32[128,1024]{1,0:T(8,128)S(1)} fusion(bf16[1024,128]{1,0:T(8,128)(2,1)S(1)} %pad_maximum_fusion.2, bf16[1024,4096]{1,0:T(8,128)(2,1)} %param.19, s32[]{:T(128)S(6)} %select_n.43), kind=kOutput, calls=%fused_computation.2 | convolution fusion | flops 268435456 | bytes 2883588 | tf_op jit(solution)/shard_map/dot_general | solution.py:514
  170.9 5.9 %collective-permute-done.36 = bf16[128,1024]{1,0:T(8,128)(2,1)S(1)} collective-permute-done((bf16[128,1024]{1,0:T(8,128)(2,1)S(1)}, bf16[128,1024]{1,0:T(8,128)(2,1)S(1)}, u32[]{:S(2)}, u32[]{:S(2)}) %collective-permute-start.36) | collective-permute-done | bytes 262176 | tf_op jit(solution)/shard_map/ppermute | solution.py:28
  176.8 0.8 add_convert_fusion
  (125 shorter events, 4.6 us)
Async XLA Ops:
  0.0 6.9 %copy-start.32 = (s32[128,16]{0,1:T(8,128)S(1)}, s32[128,16]{0,1:T(8,128)}, u32[]{:S(2)}) copy-start(s32[128,16]{0,1:T(8,128)} %param.16) | copy-start | bytes 24580
  0.0 6.9 %copy-start.33 = (s32[128]{0:T(128)S(1)}, s32[128]{0:T(128)}, u32[]{:S(2)}) copy-start(s32[128]{0:T(128)} %param.17) | copy-start | bytes 1540
  0.0 9.5 %copy-start.22 = (bf16[128,1024]{1,0:T(8,128)(2,1)S(1)}, bf16[128,1024]{1,0:T(8,128)(2,1)}, u32[]{:S(2)}) copy-start(bf16[128,1024]{1,0:T(8,128)(2,1)} %param.10) | copy-start | bytes 786436
  0.0 14.3 %copy-start.18 = (bf16[128,1024]{1,0:T(8,128)(2,1)S(1)}, bf16[128,1024]{1,0:T(8,128)(2,1)}, u32[]{:S(2)}) copy-start(bf16[128,1024]{1,0:T(8,128)(2,1)} %v1_ref.1) | copy-start | bytes 786436
  0.0 14.3 %copy-start.19 = (bf16[128,1024]{1,0:T(8,128)(2,1)S(1)}, bf16[128,1024]{1,0:T(8,128)(2,1)}, u32[]{:S(2)}) copy-start(bf16[128,1024]{1,0:T(8,128)(2,1)} %k1_ref.1) | copy-start | bytes 786436
  6.5 21.4 %collective-permute-start.7 = (bf16[2,512,1024]{2,1,0:T(8,128)(2,1)}, bf16[2,512,1024]{2,1,0:T(8,128)(2,1)}, u32[]{:S(2)}, u32[]{:S(2)}) collective-permute-start(bf16[2,512,1024]{2,1,0:T(8,128)(2,1)} %get-tuple-element.45), channel_id=1, source_target_pairs={{0,1},{1,0},{2,3},{3,2},{4,5},{5,4},{6,7},{7,6},{8,9},{9,8},{10,11... | collective-permute-start | bytes 6291464 | tf_op jit(solution)/shard_map/ppermute | solution.py:28
  6.9 4.2 %collective-permute-start.3 = (s32[16,128]{1,0:T(8,128)S(1)}, s32[16,128]{1,0:T(8,128)S(1)}, u32[]{:S(2)}, u32[]{:S(2)}) collective-permute-start(s32[16,128]{1,0:T(8,128)S(1)} %get-tuple-element.86), channel_id=1, source_target_pairs={{0,4},{4,0},{8,12},{12,8},{16,20},{20,16},{24,28},{28,24},{1,5},{5... | collective-permute-start | bytes 24584 | tf_op jit(solution)/shard_map/ppermute | solution.py:28
  9.5 15.0 %collective-permute-start.1 = (bf16[128,1024]{1,0:T(8,128)(2,1)S(1)}, bf16[128,1024]{1,0:T(8,128)(2,1)S(1)}, u32[]{:S(2)}, u32[]{:S(2)}) collective-permute-start(bf16[128,1024]{1,0:T(8,128)(2,1)S(1)} %copy-done.22), channel_id=1, source_target_pairs={{0,2},{1,3},{2,0},{3,1},{4,6},{5,7},{6,4},{7,5},{8,10},{9,11},{10,... | collective-permute-start | bytes 786440 | tf_op jit(solution)/shard_map/ppermute | solution.py:28
  11.0 13.6 %collective-permute-start = (bf16[128,1024]{1,0:T(8,128)(2,1)S(1)}, bf16[128,1024]{1,0:T(8,128)(2,1)S(1)}, u32[]{:S(2)}, u32[]{:S(2)}) collective-permute-start(bf16[128,1024]{1,0:T(8,128)(2,1)S(1)} %copy-done.22), channel_id=1, source_target_pairs={{0,1},{1,0},{2,3},{3,2},{4,5},{5,4},{6,7},{7,6},{8,9},{9,8},{10,11... | collective-permute-start | bytes 786440 | tf_op jit(solution)/shard_map/ppermute | solution.py:28
  11.2 4.8 %collective-permute-start.5 = (s32[2,16,128]{2,1,0:T(8,128)S(1)}, s32[2,16,128]{2,1,0:T(8,128)S(1)}, u32[]{:S(2)}, u32[]{:S(2)}) collective-permute-start(s32[2,16,128]{2,1,0:T(8,128)S(1)} %get-tuple-element.84), channel_id=1, source_target_pairs={{0,16},{4,20},{8,24},{12,28},{16,0},{20,4},{24,8},{28,12},{1,17},{... | collective-permute-start | bytes 49160 | tf_op jit(solution)/shard_map/ppermute | solution.py:33
  14.3 5.8 %collective-permute-start.4 = (s32[2,16,128]{2,1,0:T(8,128)S(1)}, s32[2,16,128]{2,1,0:T(8,128)S(1)}, u32[]{:S(2)}, u32[]{:S(2)}) collective-permute-start(s32[2,16,128]{2,1,0:T(8,128)S(1)} %get-tuple-element.84), channel_id=1, source_target_pairs={{0,8},{4,12},{8,16},{12,20},{16,24},{20,28},{24,0},{28,4},{1,9},{5... | collective-permute-start | bytes 49160 | tf_op jit(solution)/shard_map/ppermute | solution.py:33
  16.0 8.4 %collective-permute-start.6 = (s32[2,16,128]{2,1,0:T(8,128)S(1)}, s32[2,16,128]{2,1,0:T(8,128)S(1)}, u32[]{:S(2)}, u32[]{:S(2)}) collective-permute-start(s32[2,16,128]{2,1,0:T(8,128)S(1)} %get-tuple-element.84), channel_id=1, source_target_pairs={{0,24},{4,28},{8,0},{12,4},{16,8},{20,12},{24,16},{28,20},{1,25},{... | collective-permute-start | bytes 49160 | tf_op jit(solution)/shard_map/ppermute | solution.py:33
  20.2 21.6 %collective-permute-start.13 = (bf16[2,128,1024]{2,1,0:T(8,128)(2,1)S(1)}, bf16[2,128,1024]{2,1,0:T(8,128)(2,1)}, u32[]{:S(2)}, u32[]{:S(2)}) collective-permute-start(bf16[2,128,1024]{2,1,0:T(8,128)(2,1)S(1)} %pad_maximum_fusion.1), channel_id=1, source_target_pairs={{0,4},{4,8},{8,12},{12,16},{16,20},{20,24},{24,28},{1,5},{5,9},{9,... | collective-permute-start | bytes 1572872 | tf_op jit(solution)/shard_map/ppermute | solution.py:39
  24.5 3.3 %collective-permute-start.2 = (bf16[128,1024]{1,0:T(8,128)(2,1)S(1)}, bf16[128,1024]{1,0:T(8,128)(2,1)S(1)}, u32[]{:S(2)}, u32[]{:S(2)}) collective-permute-start(bf16[128,1024]{1,0:T(8,128)(2,1)S(1)} %collective-permute-done.1), channel_id=1, source_target_pairs={{0,1},{1,0},{2,3},{3,2},{4,5},{5,4},{6,7},{7,6},{8,9},{9,8},{10,11... | collective-permute-start | bytes 786440 | tf_op jit(solution)/shard_map/ppermute | solution.py:28
  25.3 37.4 %collective-permute-start.12 = (bf16[2,2,512,384]{3,2,1,0:T(8,128)(2,1)}, bf16[2,2,512,384]{3,2,1,0:T(8,128)(2,1)S(1)}, u32[]{:S(2)}, u32[]{:S(2)}) collective-permute-start(bf16[2,2,512,384]{3,2,1,0:T(8,128)(2,1)} %get-tuple-element.48), channel_id=1, source_target_pairs={{0,2},{1,3},{2,0},{3,1},{4,6},{5,7},{6,4},{7,5},{8,10},{9,11},{10,... | collective-permute-start | bytes 4718600 | tf_op jit(solution)/shard_map/ppermute | solution.py:28
  32.6 9.7 %copy-start.15 = (bf16[128,1024]{1,0:T(8,128)(2,1)}, bf16[128,1024]{1,0:T(8,128)(2,1)S(1)}, u32[]{:S(2)}) copy-start(bf16[128,1024]{1,0:T(8,128)(2,1)S(1)} %convolution_convert_fusion.q_ref) | copy-start | bytes 786436
  32.6 8.5 %collective-permute-start.9 = (bf16[128,1024]{1,0:T(8,128)(2,1)S(1)}, bf16[128,1024]{1,0:T(8,128)(2,1)S(1)}, u32[]{:S(2)}, u32[]{:S(2)}) collective-permute-start(bf16[128,1024]{1,0:T(8,128)(2,1)S(1)} %convolution_convert_fusion.q_ref), channel_id=1, source_target_pairs={{0,4},{4,0},{8,12},{12,8},{16,20},{20,16},{24,28},{28,24},{1,5},{5... | collective-permute-start | bytes 786440 | tf_op jit(solution)/shard_map/ppermute | solution.py:28
  32.7 15.9 %collective-permute-start.11 = (bf16[128,1024]{1,0:T(8,128)(2,1)S(1)}, bf16[128,1024]{1,0:T(8,128)(2,1)}, u32[]{:S(2)}, u32[]{:S(2)}) collective-permute-start(bf16[128,1024]{1,0:T(8,128)(2,1)S(1)} %convolution_convert_fusion.q_ref), channel_id=1, source_target_pairs={{0,24},{4,28},{8,0},{12,4},{16,8},{20,12},{24,16},{28,20},{1,25},{... | collective-permute-start | bytes 786440 | tf_op jit(solution)/shard_map/ppermute | solution.py:33
  35.5 14.0 %collective-permute-start.8 = (bf16[128,1024]{1,0:T(8,128)(2,1)S(1)}, bf16[128,1024]{1,0:T(8,128)(2,1)}, u32[]{:S(2)}, u32[]{:S(2)}) collective-permute-start(bf16[128,1024]{1,0:T(8,128)(2,1)S(1)} %convolution_convert_fusion.q_ref), channel_id=1, source_target_pairs={{0,8},{4,12},{8,16},{12,20},{16,24},{20,28},{24,0},{28,4},{1,9},{5... | collective-permute-start | bytes 786440 | tf_op jit(solution)/shard_map/ppermute | solution.py:33
  41.1 17.7 %collective-permute-start.10 = (bf16[128,1024]{1,0:T(8,128)(2,1)S(1)}, bf16[128,1024]{1,0:T(8,128)(2,1)}, u32[]{:S(2)}, u32[]{:S(2)}) collective-permute-start(bf16[128,1024]{1,0:T(8,128)(2,1)S(1)} %convolution_convert_fusion.q_ref), channel_id=1, source_target_pairs={{0,16},{4,20},{8,24},{12,28},{16,0},{20,4},{24,8},{28,12},{1,17},{... | collective-permute-start | bytes 786440 | tf_op jit(solution)/shard_map/ppermute | solution.py:33
  41.8 57.4 %collective-permute-start.20 = (bf16[2,2,512,384]{3,2,1,0:T(8,128)(2,1)}, bf16[2,2,512,384]{3,2,1,0:T(8,128)(2,1)S(1)}, u32[]{:S(2)}, u32[]{:S(2)}) collective-permute-start(bf16[2,2,512,384]{3,2,1,0:T(8,128)(2,1)} %get-tuple-element.65), channel_id=1, source_target_pairs={{0,2},{1,3},{2,0},{3,1},{4,6},{5,7},{6,4},{7,5},{8,10},{9,11},{10,... | collective-permute-start | bytes 4718600 | tf_op jit(solution)/shard_map/ppermute | solution.py:28
  48.6 24.9 %collective-permute-start.16 = (bf16[128,1024]{1,0:T(8,128)(2,1)}, bf16[128,1024]{1,0:T(8,128)(2,1)S(1)}, u32[]{:S(2)}, u32[]{:S(2)}) collective-permute-start(bf16[128,1024]{1,0:T(8,128)(2,1)} %collective-permute-done.11), channel_id=1, source_target_pairs={{0,4},{4,0},{8,12},{12,8},{16,20},{20,16},{24,28},{28,24},{1,5},{5... | collective-permute-start | bytes 786440 | tf_op jit(solution)/shard_map/ppermute | solution.py:28
  49.4 24.1 %collective-permute-start.14 = (bf16[128,1024]{1,0:T(8,128)(2,1)}, bf16[128,1024]{1,0:T(8,128)(2,1)S(1)}, u32[]{:S(2)}, u32[]{:S(2)}) collective-permute-start(bf16[128,1024]{1,0:T(8,128)(2,1)} %collective-permute-done.8), channel_id=1, source_target_pairs={{0,4},{4,0},{8,12},{12,8},{16,20},{20,16},{24,28},{28,24},{1,5},{5... | collective-permute-start | bytes 786440 | tf_op jit(solution)/shard_map/ppermute | solution.py:28
  60.1 35.7 %copy-start.5 = (bf16[512,1024]{1,0:T(8,128)(2,1)}, bf16[512,1024]{1,0:T(8,128)(2,1)S(1)}, u32[]{:S(2)}) copy-start(bf16[512,1024]{1,0:T(8,128)(2,1)S(1)} %pad_maximum_fusion.q_ref) | copy-start | bytes 3145732
  60.1 21.0 %copy-start.25 = (bf16[128,1024]{1,0:T(8,128)(2,1)S(1)}, bf16[128,1024]{1,0:T(8,128)(2,1)}, u32[]{:S(2)}) copy-start(bf16[128,1024]{1,0:T(8,128)(2,1)} %copy-done.24) | copy-start | bytes 786436
  73.3 22.5 %copy-start = (f32[1024,512]{1,0:T(8,128)}, f32[1024,512]{1,0:T(8,128)S(1)}, u32[]{:S(2)}) copy-start(f32[1024,512]{1,0:T(8,128)S(1)} %get-tuple-element.58.acc_ref) | copy-start | bytes 6291460
  73.3 7.8 %collective-permute-start.15 = (bf16[128,1024]{1,0:T(8,128)(2,1)}, bf16[128,1024]{1,0:T(8,128)(2,1)S(1)}, u32[]{:S(2)}, u32[]{:S(2)}) collective-permute-start(bf16[128,1024]{1,0:T(8,128)(2,1)} %collective-permute-done.10), channel_id=1, source_target_pairs={{0,4},{4,0},{8,12},{12,8},{16,20},{20,16},{24,28},{28,24},{1,5},{5... | collective-permute-start | bytes 786440 | tf_op jit(solution)/shard_map/ppermute | solution.py:28
  73.5 18.8 %collective-permute-start.17 = (bf16[2,512,384]{2,1,0:T(8,128)(2,1)S(1)}, bf16[2,512,384]{2,1,0:T(8,128)(2,1)S(1)}, u32[]{:S(2)}, u32[]{:S(2)}) collective-permute-start(bf16[2,512,384]{2,1,0:T(8,128)(2,1)S(1)} %slice_bitcast_fusion.1), channel_id=1, source_target_pairs={{0,1},{1,0},{2,3},{3,2},{4,5},{5,4},{6,7},{7,6},{8,9},{9,8},{10,11... | collective-permute-start | bytes 2359304 | tf_op jit(solution)/shard_map/ppermute | solution.py:28
  81.2 20.5 %copy-start.8 = (bf16[512,1024]{1,0:T(8,128)(2,1)}, bf16[512,1024]{1,0:T(8,128)(2,1)S(1)}, u32[]{:S(2)}) copy-start(bf16[512,1024]{1,0:T(8,128)(2,1)S(1)} %constant_dynamic-update-slice_fusion.q_ref) | copy-start | bytes 3145732
  92.3 9.4 %copy-start.3 = (f32[1024,512]{1,0:T(8,128)}, f32[1024,512]{1,0:T(8,128)S(1)}, u32[]{:S(2)}) copy-start(f32[1024,512]{1,0:T(8,128)S(1)} %get-tuple-element.60.acc_ref) | copy-start | bytes 6291460
  92.3 9.4 %copy-start.12 = (f32[8,8,512]{2,1,0:T(8,128)}, f32[8,8,512]{2,1,0:T(8,128)S(1)}, u32[]{:S(2)}) copy-start(f32[8,8,512]{2,1,0:T(8,128)S(1)} %get-tuple-element.55.stat_ref) | copy-start | bytes 393220
  99.2 6.8 %copy-start.10 = (bf16[4,416,128]{2,1,0:T(8,128)(2,1)}, bf16[4,416,128]{2,1,0:T(8,128)(2,1)S(1)}, u32[]{:S(2)}) copy-start(bf16[4,416,128]{2,1,0:T(8,128)(2,1)S(1)} %far_tiles.6.a_ref) | copy-start | bytes 1277956
  99.3 2.4 %collective-permute-start.21 = (bf16[2,512,384]{2,1,0:T(8,128)(2,1)S(1)}, bf16[2,512,384]{2,1,0:T(8,128)(2,1)S(1)}, u32[]{:S(2)}, u32[]{:S(2)}) collective-permute-start(bf16[2,512,384]{2,1,0:T(8,128)(2,1)S(1)} %slice_bitcast_fusion), channel_id=1, source_target_pairs={{0,1},{1,0},{2,3},{3,2},{4,5},{5,4},{6,7},{7,6},{8,9},{9,8},{10,11... | collective-permute-start | bytes 2359304 | tf_op jit(solution)/shard_map/ppermute | solution.py:28
  99.4 27.5 %collective-permute-start.19 = (bf16[2,2,512,256]{3,2,1,0:T(8,128)(2,1)}, bf16[2,2,512,256]{3,2,1,0:T(8,128)(2,1)S(1)}, u32[]{:S(2)}, u32[]{:S(2)}) collective-permute-start(bf16[2,2,512,256]{3,2,1,0:T(8,128)(2,1)} %get-tuple-element.63), channel_id=1, source_target_pairs={{0,2},{1,3},{2,0},{3,1},{4,6},{5,7},{6,4},{7,5},{8,10},{9,11},{10,... | collective-permute-start | bytes 3145736 | tf_op jit(solution)/shard_map/ppermute | solution.py:28
  100.9 12.8 %collective-permute-start.18 = (bf16[4,416,128]{2,1,0:T(8,128)(2,1)S(1)}, bf16[4,416,128]{2,1,0:T(8,128)(2,1)}, u32[]{:S(2)}, u32[]{:S(2)}) collective-permute-start(bf16[4,416,128]{2,1,0:T(8,128)(2,1)S(1)} %far_tiles.7), channel_id=1, source_target_pairs={{0,4},{4,0},{8,12},{12,8},{16,20},{20,16},{24,28},{28,24},{1,5},{5... | collective-permute-start | bytes 1277960 | tf_op jit(solution)/shard_map/ppermute | solution.py:28
  106.0 18.9 %collective-permute-start.22 = (bf16[4,416,128]{2,1,0:T(8,128)(2,1)}, bf16[4,416,128]{2,1,0:T(8,128)(2,1)}, u32[]{:S(2)}, u32[]{:S(2)}) collective-permute-start(bf16[4,416,128]{2,1,0:T(8,128)(2,1)} %far_tiles.9), channel_id=1, source_target_pairs={{0,4},{4,0},{8,12},{12,8},{16,20},{20,16},{24,28},{28,24},{1,5},{5... | collective-permute-start | bytes 1277960 | tf_op jit(solution)/shard_map/ppermute | solution.py:28
  115.7 11.2 %collective-permute-start.23 = (bf16[416,128]{1,0:T(8,128)(2,1)}, bf16[416,128]{1,0:T(8,128)(2,1)}, u32[]{:S(2)}, u32[]{:S(2)}) collective-permute-start(bf16[416,128]{1,0:T(8,128)(2,1)} %get-tuple-element.68), channel_id=1, source_target_pairs={{0,24},{4,28},{8,0},{12,4},{16,8},{20,12},{24,16},{28,20},{1,25},{... | collective-permute-start | bytes 319496 | tf_op jit(solution)/shard_map/ppermute | solution.py:33
  116.9 10.0 %collective-permute-start.24 = (bf16[416,128]{1,0:T(8,128)(2,1)}, bf16[416,128]{1,0:T(8,128)(2,1)}, u32[]{:S(2)}, u32[]{:S(2)}) collective-permute-start(bf16[416,128]{1,0:T(8,128)(2,1)} %get-tuple-element.69), channel_id=1, source_target_pairs={{0,16},{4,20},{8,24},{12,28},{16,0},{20,4},{24,8},{28,12},{1,17},{... | collective-permute-start | bytes 319496 | tf_op jit(solution)/shard_map/ppermute | solution.py:33
  116.9 10.0 %collective-permute-start.25 = (bf16[416,128]{1,0:T(8,128)(2,1)}, bf16[416,128]{1,0:T(8,128)(2,1)}, u32[]{:S(2)}, u32[]{:S(2)}) collective-permute-start(bf16[416,128]{1,0:T(8,128)(2,1)} %get-tuple-element.70), channel_id=1, source_target_pairs={{0,8},{4,12},{8,16},{12,20},{16,24},{20,28},{24,0},{28,4},{1,9},{5... | collective-permute-start | bytes 319496 | tf_op jit(solution)/shard_map/ppermute | solution.py:33
  117.7 1.6 copy-start.1
  119.3 1.2 copy-start.6
  124.0 0.8 copy-start.11
  126.9 14.0 %copy-start.7 = (bf16[512,1024]{1,0:T(8,128)(2,1)S(1)}, bf16[512,1024]{1,0:T(8,128)(2,1)}, u32[]{:S(2)}) copy-start(bf16[512,1024]{1,0:T(8,128)(2,1)} %copy-done.5) | copy-start | bytes 3145732
  127.0 14.0 %copy-start.2 = (f32[1024,512]{1,0:T(8,128)S(1)}, f32[1024,512]{1,0:T(8,128)}, u32[]{:S(2)}) copy-start(f32[1024,512]{1,0:T(8,128)} %copy-done) | copy-start | bytes 6291460
  127.0 2.0 %collective-permute-start.26 = (bf16[2,512,256]{2,1,0:T(8,128)(2,1)S(1)}, bf16[2,512,256]{2,1,0:T(8,128)(2,1)S(1)}, u32[]{:S(2)}, u32[]{:S(2)}) collective-permute-start(bf16[2,512,256]{2,1,0:T(8,128)(2,1)S(1)} %slice_bitcast_fusion.2), channel_id=1, source_target_pairs={{0,1},{1,0},{2,3},{3,2},{4,5},{5,4},{6,7},{7,6},{8,9},{9,8},{10,11... | collective-permute-start | bytes 1572872 | tf_op jit(solution)/shard_map/ppermute | solution.py:28
  128.9 1.6 copy-start.4
  130.5 1.2 copy-start.9
  131.8 0.9 copy-start.13
  132.7 8.3 %copy-start.34 = (bf16[416,128]{1,0:T(8,128)(2,1)S(1)}, bf16[416,128]{1,0:T(8,128)(2,1)}, u32[]{:S(2)}) copy-start(bf16[416,128]{1,0:T(8,128)(2,1)} %get-tuple-element.77) | copy-start | bytes 319492
  135.2 9.0 %collective-permute-start.30 = (bf16[4,272,128]{2,1,0:T(8,128)(2,1)S(1)}, bf16[4,272,128]{2,1,0:T(8,128)(2,1)S(1)}, u32[]{:S(2)}, u32[]{:S(2)}) collective-permute-start(bf16[4,272,128]{2,1,0:T(8,128)(2,1)S(1)} %far_tiles.10), channel_id=1, source_target_pairs={{0,4},{4,0},{8,12},{12,8},{16,20},{20,16},{24,28},{28,24},{1,5},{5... | collective-permute-start | bytes 835592 | tf_op jit(solution)/shard_map/ppermute | solution.py:28
  136.6 14.0 %collective-permute-start.27 = (bf16[416,128]{1,0:T(8,128)(2,1)}, bf16[416,128]{1,0:T(8,128)(2,1)S(1)}, u32[]{:S(2)}, u32[]{:S(2)}) collective-permute-start(bf16[416,128]{1,0:T(8,128)(2,1)} %get-tuple-element.75), channel_id=1, source_target_pairs={{0,24},{4,28},{8,0},{12,4},{16,8},{20,12},{24,16},{28,20},{1,25},{... | collective-permute-start | bytes 319496 | tf_op jit(solution)/shard_map/ppermute | solution.py:33
  139.8 14.3 %collective-permute-start.28 = (bf16[416,128]{1,0:T(8,128)(2,1)}, bf16[416,128]{1,0:T(8,128)(2,1)S(1)}, u32[]{:S(2)}, u32[]{:S(2)}) collective-permute-start(bf16[416,128]{1,0:T(8,128)(2,1)} %get-tuple-element.76), channel_id=1, source_target_pairs={{0,16},{4,20},{8,24},{12,28},{16,0},{20,4},{24,8},{28,12},{1,17},{... | collective-permute-start | bytes 319496 | tf_op jit(solution)/shard_map/ppermute | solution.py:33
  140.9 10.5 %copy-start.35 = (f32[16]{0:T(128)S(1)}, f32[16]{0:T(128)}, u32[]{:S(2)}) copy-start(f32[16]{0:T(128)} %param.18) | copy-start | bytes 196
  140.9 13.2 %collective-permute-start.29 = (bf16[416,128]{1,0:T(8,128)(2,1)S(1)}, bf16[416,128]{1,0:T(8,128)(2,1)S(1)}, u32[]{:S(2)}, u32[]{:S(2)}) collective-permute-start(bf16[416,128]{1,0:T(8,128)(2,1)S(1)} %copy-done.34), channel_id=1, source_target_pairs={{0,8},{4,12},{8,16},{12,20},{16,24},{20,28},{24,0},{28,4},{1,9},{5... | collective-permute-start | bytes 319496 | tf_op jit(solution)/shard_map/ppermute | solution.py:33
  146.7 10.7 %collective-permute-start.31 = (bf16[272,128]{1,0:T(8,128)(2,1)}, bf16[272,128]{1,0:T(8,128)(2,1)S(1)}, u32[]{:S(2)}, u32[]{:S(2)}) collective-permute-start(bf16[272,128]{1,0:T(8,128)(2,1)} %get-tuple-element.79), channel_id=1, source_target_pairs={{0,24},{4,28},{8,0},{12,4},{16,8},{20,12},{24,16},{28,20},{1,25},{... | collective-permute-start | bytes 208904 | tf_op jit(solution)/shard_map/ppermute | solution.py:33
  150.6 6.9 %collective-permute-start.32 = (bf16[272,128]{1,0:T(8,128)(2,1)}, bf16[272,128]{1,0:T(8,128)(2,1)S(1)}, u32[]{:S(2)}, u32[]{:S(2)}) collective-permute-start(bf16[272,128]{1,0:T(8,128)(2,1)} %get-tuple-element.80), channel_id=1, source_target_pairs={{0,16},{4,20},{8,24},{12,28},{16,0},{20,4},{24,8},{28,12},{1,17},{... | collective-permute-start | bytes 208904 | tf_op jit(solution)/shard_map/ppermute | solution.py:33
  150.6 3.6 %copy-start.26 = (bf16[416,128]{1,0:T(8,128)(2,1)}, bf16[416,128]{1,0:T(8,128)(2,1)S(1)}, u32[]{:S(2)}) copy-start(bf16[416,128]{1,0:T(8,128)(2,1)S(1)} %collective-permute-done.27.refs_1_) | copy-start | bytes 319492
  150.6 6.9 %collective-permute-start.33 = (bf16[272,128]{1,0:T(8,128)(2,1)}, bf16[272,128]{1,0:T(8,128)(2,1)S(1)}, u32[]{:S(2)}, u32[]{:S(2)}) collective-permute-start(bf16[272,128]{1,0:T(8,128)(2,1)} %get-tuple-element.81), channel_id=1, source_target_pairs={{0,8},{4,12},{8,16},{12,20},{16,24},{20,28},{24,0},{28,4},{1,9},{5... | collective-permute-start | bytes 208904 | tf_op jit(solution)/shard_map/ppermute | solution.py:33
  154.1 8.2 %copy-start.16 = (bf16[384,128]{1,0:T(8,128)(2,1)S(1)}, bf16[384,128]{1,0:T(8,128)(2,1)}, u32[]{:S(2)}) copy-start(bf16[384,128]{1,0:T(8,128)(2,1)} %merge_all.3) | copy-start | bytes 294916
  157.5 4.9 %copy-start.17 = (bf16[384,128]{1,0:T(8,128)(2,1)S(1)}, bf16[384,128]{1,0:T(8,128)(2,1)}, u32[]{:S(2)}) copy-start(bf16[384,128]{1,0:T(8,128)(2,1)} %merge_all.4) | copy-start | bytes 294916
  160.0 2.3 %copy-start.20 = (bf16[256,128]{1,0:T(8,128)(2,1)S(1)}, bf16[256,128]{1,0:T(8,128)(2,1)}, u32[]{:S(2)}) copy-start(bf16[256,128]{1,0:T(8,128)(2,1)} %merge_all.5) | copy-start | bytes 196612
  162.3 1.6 collective-permute-start.34
  168.0 2.8 %collective-permute-start.35 = (bf16[128,1024]{1,0:T(8,128)(2,1)S(1)}, bf16[128,1024]{1,0:T(8,128)(2,1)S(1)}, u32[]{:S(2)}, u32[]{:S(2)}) collective-permute-start(bf16[128,1024]{1,0:T(8,128)(2,1)S(1)} %fusion.17), channel_id=1, source_target_pairs={{0,1},{1,0},{2,3},{3,2},{4,5},{5,4},{6,7},{7,6},{8,9},{9,8},{10,11... | collective-permute-start | bytes 786440 | tf_op jit(solution)/shard_map/ppermute | solution.py:28
  168.2 8.6 %collective-permute-start.36 = (bf16[128,1024]{1,0:T(8,128)(2,1)S(1)}, bf16[128,1024]{1,0:T(8,128)(2,1)S(1)}, u32[]{:S(2)}, u32[]{:S(2)}) collective-permute-start(bf16[128,1024]{1,0:T(8,128)(2,1)S(1)} %fusion.11), channel_id=1, source_target_pairs={{0,2},{1,3},{2,0},{3,1},{4,6},{5,7},{6,4},{7,5},{8,10},{9,11},{10,... | collective-permute-start | bytes 786440 | tf_op jit(solution)/shard_map/ppermute | solution.py:28
  (9 other events, 6.0 us)

commit v8 on v7

--- a/solution.py
+++ b/solution.py
@@ -308,23 +308,20 @@
         return lax.optimization_barrier((value, earlier))[0]
 
     live = jnp.arange(pick_count, dtype=jnp.int32)[None, :] < tile_counts[:, None]
-    ids = jnp.transpose(jnp.where(live, tile_ids, -1))
-    ids = jnp.stack([ids, swap(ids, "ctx", 1)])
-    ids = [ids] + [turn(ids, "ctx", 2 * k) for k in range(1, turns)]
-    ids = jnp.stack(ids, axis=1)
-    here = (ids >= my_ctx * group_tiles) & (ids < (my_ctx + 1) * group_tiles)
-    place = (((ids // tiles_here) % mem_size) ^ me) * tiles_here + ids % tiles_here
-    bits = jnp.sum(jnp.where(here, 1 << jnp.where(here, place, 0), 0), axis=2)
-    bits = [bits[part].reshape(1, half) for part in range(2)]
-
-
-    h1 = swap(hidden_states, "mem", 1)
-    h2 = swap(hidden_states, "mem", 2)
-    h3 = swap(h2, "mem", 1)
-    have = [hidden_states, h1, h2, h3]
-    hidden = jnp.zeros((row_count, mem_size * hidden_states.shape[1]), jnp.bfloat16)
-    for k in range(mem_size):
-        hidden = lax.dynamic_update_slice(hidden, have[k], (0, (me ^ k) * hidden_states.shape[1]))
+    picks = jnp.concatenate(
+        [jnp.where(live, tile_ids // group_tiles, -1), tile_ids % group_tiles], axis=1
+    )
+    picks = jnp.transpose(picks).astype(jnp.bfloat16).reshape(-1, features)
+    pick_rows = picks.shape[0]
+    picks = jnp.concatenate([picks, jnp.zeros((-pick_rows % 8, features), jnp.bfloat16)], axis=0)
+
+    def bits_of(blocks):
+        got = jnp.stack([x[row_count : row_count + pick_rows] for x in blocks]).astype(jnp.int32)
+        got = got.reshape(len(blocks), 2, pick_count, row_count)
+        place = ((got[:, 1] // tiles_here) ^ me) * tiles_here + got[:, 1] % tiles_here
+        bits = jnp.where(got[:, 0] == my_ctx, 1 << place, 0)
+        return jnp.sum(bits, axis=1).reshape(1, len(blocks) * row_count)
+
     share_rows = mem_rows // 4
     near_block, *far_blocks = pl.pallas_call(
         functools.partial(share_kernel, sizes),
@@ -343,20 +340,32 @@
         cost_estimate=pl.CostEstimate(flops=0, transcendentals=0, bytes_accessed=14 << 20),
         name="share_tiles",
     )(me.reshape(1), memory_keys, memory_values)
+    h2 = swap(hidden_states, "mem", 2)
+    h13 = swap(jnp.stack([hidden_states, after(h2, far_blocks[0])]), "mem", 1)
+    have = [hidden_states, h13[0], h2, h13[1]]
+    hidden = jnp.zeros((row_count, mem_size * hidden_states.shape[1]), jnp.bfloat16)
+    for k in range(mem_size):
+        hidden = lax.dynamic_update_slice(hidden, have[k], (0, (me ^ k) * hidden_states.shape[1]))
     near = swap(near_block, "mem", 1)
     queries = jnp.dot(
-        after(hidden, far_blocks[0], bits[0], near), w_query, preferred_element_type=f32
+        after(hidden, near), w_query, preferred_element_type=f32
     ).astype(jnp.bfloat16)
-    crossed = [swap(after(far_blocks[0], h1), "mem", 2)]
-
-    own_swapped = swap(queries, "ctx", 1)
-    q_blocks = [queries]
+    crossed = [swap(after(far_blocks[0], h2), "mem", 2)]
+
+    message = jnp.concatenate([queries, picks], axis=0)
+    own_swapped = swap(message, "ctx", 1)
+    q_blocks = [message]
     for k in range(1, turns):
-        near_by = k in (1, turns - 1)
-        q_blocks.append(turn(queries if near_by else after(queries, own_swapped), "ctx", 2 * k))
-    q_blocks += [own_swapped] + [swap(q, "ctx", 1) for q in q_blocks[1:]]
+        q_blocks.append(turn(message if k in (1, turns - 1) else after(message, own_swapped), "ctx", 2 * k))
+    near_by = sorted({1, turns - 1})
+    both = swap(jnp.stack([q_blocks[k] for k in near_by]), "ctx", 1)
+    q_blocks += [own_swapped] + [
+        both[near_by.index(k)] if k in near_by else swap(q_blocks[k], "ctx", 1)
+        for k in range(1, turns)
+    ]
     crossed.append(swap(after(far_blocks[1], queries), "mem", 2))
-    q_halves = [jnp.concatenate(q_blocks[:turns], 0), None]
+    q_halves = [jnp.concatenate([x[:row_count] for x in q_blocks[:turns]], 0), None]
+    bits = [bits_of(q_blocks[:turns]), None]
 
     window = from_behind(jnp.stack([local_keys, local_values]), "ctx", 1)
     pair_spec = pl.BlockSpec((row_count, PAIR), lambda p, c: (0, p))
@@ -396,7 +405,9 @@
     q_halves[0] = after(q_halves[0], crossed[0], local_out)
     for part in range(2):
         if part == 1:
-            q_halves[1] = jnp.concatenate(after(q_blocks[turns:], near_state[0][1]), 0)
+            late_blocks = after(q_blocks[turns:], near_state[0][1])
+            q_halves[1] = jnp.concatenate([x[:row_count] for x in late_blocks], 0)
+            bits[1] = bits_of(late_blocks)
             crossed.append(
                 swap(after(far_blocks[2], near_state[0][1]), "mem", 2)
             )
@@ -440,15 +451,29 @@
     over_rows = (((0,), (0,)), ((), ()))
 
     messages = []
+    others = []
     merges = []
     answers = []
+
+    def merge(j, *tokens):
+        msg_shape = jax.ShapeDtypeStruct(messages[j][0].shape[1:], jnp.bfloat16)
+        merged = pl.pallas_call(
+            functools.partial(merge_kernel, sizes[j]),
+            out_shape=[msg_shape] * turns,
+            name="merge_pair",
+        )(messages[j][0], after(others[j], *tokens))
+        merges.append(merged[0])
+        answers.append([merged[0]] + [turn(merged[k], "ctx", -2 * k) for k in range(1, turns)])
+
     for j in range(chunks):
         heads, first = sizes[j], firsts[j]
         wide = heads * DH
         msg_rows = wide + stat_rows(heads)
         tokens = messages[j - 1] if j >= 1 else [near_state[0][1]]
         if j == chunks - 1:
-            tokens = tokens + merges + answers[0]
+            for i in range(j):
+                merge(i, messages[j - 1][0])
+            tokens = tokens + merges
         far2 = after(crossed[j], *tokens)
         far3 = swap(far2[1], "mem", 1)
         message = [None, None]
@@ -485,14 +510,8 @@
                 name="far_tiles",
             )(asked, far2, far2, far3, far3, bits[part], acc, stat)
         messages.append(message)
-        other = swap(message[1], "ctx", 1)
-        merged = pl.pallas_call(
-            functools.partial(merge_kernel, heads),
-            out_shape=[jax.ShapeDtypeStruct((msg_rows, row_count), jnp.bfloat16)] * turns,
-            name="merge_pair",
-        )(message[0], other)
-        merges.append(merged[0])
-        answers.append([merged[0]] + [turn(merged[k], "ctx", -2 * k) for k in range(1, turns)])
+        others.append(swap(message[1], "ctx", 1))
+    merge(chunks - 1)
 
     combined = []
     for j in range(chunks):
@@ -513,11 +532,11 @@
         w = lax.dynamic_slice(w_output, (0, (me ^ k) * cols), (features, cols))
         return lax.dot_general(rows, w, over_rows, preferred_element_type=f32)
 
-    away = swap(piece(3, combined).astype(jnp.bfloat16), "mem", 1)
-    away = (piece(2, combined) + away.astype(f32)).astype(jnp.bfloat16)
-    rest = after(combined, away)
-    away = swap(away, "mem", 2)
-    result = piece(0, rest) + swap(piece(1, rest).astype(jnp.bfloat16), "mem", 1).astype(f32)
+    given = jnp.stack([piece(3, combined), piece(1, combined)]).astype(jnp.bfloat16)
+    taken = swap(given, "mem", 1)
+    away = piece(2, after(combined, given)) + taken[0].astype(f32)
+    away = swap(away.astype(jnp.bfloat16), "mem", 2)
+    result = piece(0, after(combined, taken)) + taken[1].astype(f32)
     return (result + away.astype(f32)).astype(jnp.bfloat16)
 
 

time: 179 us -> 191 us (1.067)
  waiting for transfers between devices: 40.4 us -> 47.7 us
  starting transfers between devices: 41.2 us -> 34.6 us
  local copies, waits for them, and re-layouts: 14.2 us -> 18.6 us
  other arithmetic: 2.26 us -> 5.44 us
  Pallas kernels: 65.9 us -> 68.6 us
    ppermute x21 -> x17, waiting for transfers between devices: 32.2 us -> 42.7 us  [swap(): lax.ppermute(block, axis, [(i, i ^ distance) for i in range(lax.axis_size...]
    slice x0 -> x15, local copies, waits for them, and re-layouts: none -> 9.45 us  [the longest x3 4.31 us: on_device(): x[:row_count]]
    unnamed x75 -> x80, local copies, waits for them, and re-layouts: 12.1 us -> 5.9 us
    ppermute x15 -> x12, starting transfers between devices: 22.6 us -> 18.8 us  [turn(): lax.ppermute(block, axis, [(i, (i + distance) % size) for i in range(size)])]
    ppermute x15 -> x12, waiting for transfers between devices: 8.22 us -> 4.95 us  [turn(): lax.ppermute(block, axis, [(i, (i + distance) % size) for i in range(size)])]
    ppermute x21 -> x17, starting transfers between devices: 14.4 us -> 11.3 us  [swap(): lax.ppermute(block, axis, [(i, i ^ distance) for i in range(lax.axis_size...]
    pallas_call x6, Pallas kernels: 19.6 us -> 22.6 us  [on_device(): pl.pallas_call(far_kernel, grid=(1,), in_specs=[pl.BlockSpec((pl.Element(...]
    another operation x2 -> x4, other arithmetic: 0.01 us -> 2.01 us  [the longest x1 1.89 us: on_device(): both = swap(jnp.stack([q_blocks[k] for k in near_by]), 'ctx', 1)]
  transfers between devices with their start and end apart: 37 -> 30, of which waited for: 10 -> 13; matrix products, arithmetic and copies ran while one was open for 6% -> 12% of each run, Pallas kernels for 31% -> 31%
where the time goes in v8:
time: 191 us; the launch traced here: 189 us
  Pallas kernels  68.6 us (36%)
  waiting for transfers between devices  47.7 us (25%)
  starting transfers between devices  34.6 us (18%)
  local copies, waits for them, and re-layouts  18.6 us (10%)
  matrix products  13.9 us (7%)
  other arithmetic  5.44 us (3%)
    ppermute x17, waiting for transfers between devices, swap(): lax.ppermute(block, axis, [(i, i ^ distance) for i in range(lax.axis_size...  42.7 us
    pallas_call x6, Pallas kernels, on_device(): pl.pallas_call(far_kernel, grid=(1,), in_specs=[pl.BlockSpec((pl.Element(...  22.6 us
    pallas_call x2, Pallas kernels, on_device(): pl.pallas_call(near_kernel, grid_spec=pltpu.PrefetchScalarGridSpec(num_sc...  21.8 us
    ppermute x12, starting transfers between devices, turn(): lax.ppermute(block, axis, [(i, (i + distance) % size) for i in range(size)])  18.8 us
    ppermute x17, starting transfers between devices, swap(): lax.ppermute(block, axis, [(i, i ^ distance) for i in range(lax.axis_size...  11.3 us
    dot_general x4, matrix products, piece(): return lax.dot_general(rows, w, over_rows, preferred_element_type=f32)  9.14 us
    pallas_call x1, Pallas kernels, on_device(): pl.pallas_call(local_kernel, grid_spec=pltpu.PrefetchScalarGridSpec(num_s...  6.27 us
    pallas_call x1, Pallas kernels, on_device(): pl.pallas_call(functools.partial(share_kernel, sizes), grid_spec=pltpu.Pr...  6.02 us
  transfers between devices with their start and end apart: 30, of which 13 were waited for; matrix products, arithmetic and copies ran while one was open for 12% of the time, Pallas kernels for 31%

profile of v8, /device:TPU:0, one launch (start us, length us, event | category | flops | bytes accessed | tf_op | source)
XLA Modules:
  0.0 189.3 jit_solution(2335711029863874788)
XLA Ops:
  0.0 6.0 %share_tiles.1 = (bf16[2,512,1024]{2,1,0:T(8,128)(2,1)}, bf16[2,2,512,384]{3,2,1,0:T(8,128)(2,1)}, bf16[2,2,512,384]{3,2,1,0:T(8,128)(2,1)S(1)}, bf16[2,2,512,256]{3,2,1,0:T(8,128)(2,1)}) custom-call(s32[1]{0:T(128)} %bitcast.1.me_ref.m_ref, bf16[512,4096]{1,0:T(8,128)(2,1)} %k0_ref.3, bf16[512,4096]{1,0:T(8,128)(2,1)} %v0_ref.3), custom_call_target="tpu_custom_call" | custom-call | bytes 14680064 | tf_op jit(solution)/shard_map/share_tiles/pallas_call | solution.py:326
  6.0 1.1 copy-done.13
  7.6 2.6 %collective-permute-start = (bf16[128,1024]{1,0:T(8,128)(2,1)S(1)}, bf16[128,1024]{1,0:T(8,128)(2,1)S(1)}, u32[]{:S(2)}, u32[]{:S(2)}) collective-permute-start(bf16[128,1024]{1,0:T(8,128)(2,1)S(1)} %copy-done.20), channel_id=1, source_target_pairs={{0,2},{1,3},{2,0},{3,1},{4,6},{5,7},{6,4},{7,5},{8,10},{9,11},{10,... | collective-permute-start | bytes 786440 | tf_op jit(solution)/shard_map/ppermute | solution.py:28
  10.2 6.9 %collective-permute-done = bf16[128,1024]{1,0:T(8,128)(2,1)S(1)} collective-permute-done((bf16[128,1024]{1,0:T(8,128)(2,1)S(1)}, bf16[128,1024]{1,0:T(8,128)(2,1)S(1)}, u32[]{:S(2)}, u32[]{:S(2)}) %collective-permute-start) | collective-permute-done | bytes 262176 | tf_op jit(solution)/shard_map/ppermute | solution.py:28
  17.3 4.5 %collective-permute-start.8 = (bf16[2,128,1024]{2,1,0:T(8,128)(2,1)S(1)}, bf16[2,128,1024]{2,1,0:T(8,128)(2,1)}, u32[]{:S(2)}, u32[]{:S(2)}) collective-permute-start(bf16[2,128,1024]{2,1,0:T(8,128)(2,1)S(1)} %pad_maximum_fusion.4), channel_id=1, source_target_pairs={{0,4},{4,8},{8,12},{12,16},{16,20},{20,24},{24,28},{1,5},{5,9},{9,... | collective-permute-start | bytes 1572872 | tf_op jit(solution)/shard_map/ppermute | solution.py:39
  22.1 1.6 collective-permute-start.7
  23.8 4.7 %convolution_convert_fusion.q_ref = bf16[128,1024]{1,0:T(8,128)(2,1)S(1)} fusion(bf16[128,4096]{1,0:T(8,128)(2,1)S(1)} %fusion.30, bf16[4096,1024]{1,0:T(8,128)(2,1)} %param.11), kind=kOutput, calls=%fused_computation.13 | convolution fusion | flops 1073872896 | bytes 9699328 | tf_op jit(solution)/shard_map/dot_general | solution.py:350
  28.5 0.8 maximum_maximum_fusion
  29.3 0.8 collective-permute-start.4
  30.1 2.1 %collective-permute-start.6 = (bf16[136,1024]{1,0:T(8,128)(2,1)}, bf16[136,1024]{1,0:T(8,128)(2,1)}, u32[]{:S(2)}, u32[]{:S(2)}) collective-permute-start(bf16[136,1024]{1,0:T(8,128)(2,1)} %maximum_maximum_fusion), channel_id=1, source_target_pairs={{0,24},{4,28},{8,0},{12,4},{16,8},{20,12},{24,16},{28,20},{1,25},{... | collective-permute-start | bytes 835592 | tf_op jit(solution)/shard_map/ppermute | solution.py:33
  32.2 6.7 %collective-permute-done.4 = bf16[136,1024]{1,0:T(8,128)(2,1)S(1)} collective-permute-done((bf16[136,1024]{1,0:T(8,128)(2,1)}, bf16[136,1024]{1,0:T(8,128)(2,1)S(1)}, u32[]{:S(2)}, u32[]{:S(2)}) %collective-permute-start.4) | collective-permute-done | bytes 278560 | tf_op jit(solution)/shard_map/ppermute | solution.py:28
  38.9 4.3 %collective-permute-start.5 = (bf16[136,1024]{1,0:T(8,128)(2,1)}, bf16[136,1024]{1,0:T(8,128)(2,1)}, u32[]{:S(2)}, u32[]{:S(2)}) collective-permute-start(bf16[136,1024]{1,0:T(8,128)(2,1)} %maximum_maximum_fusion), channel_id=1, source_target_pairs={{0,16},{4,20},{8,24},{12,28},{16,0},{20,4},{24,8},{28,12},{1,17},{... | collective-permute-start | bytes 835592 | tf_op jit(solution)/shard_map/ppermute | solution.py:33
  43.2 1.3 collective-permute-start.13
  44.6 6.3 %local_window.1.refs_4_ = f32[1024,128]{1,0:T(8,128)} custom-call(s32[1]{0:T(128)} %bitcast.6.ctx_ref, bf16[128,1024]{1,0:T(8,128)(2,1)} %copy-done.14, bf16[2,128,1024]{2,1,0:T(8,128)(2,1)} %collective-permute-done.8.k0_ref.v0_ref, bf16[128,1024]{1,0:T(8,128)(2,1)} %k1_ref.1, bf16[2,128,1024]{2,1,0:T(8,128)(2,1)} %collective-permute-done.8.k0_ref.v0_ref, ...), custom_call_target="tpu_custom_call" | custom-call | flops 134217728 | bytes 2097152 | tf_op jit(solution)/shard_map/local_window/pallas_call | solution.py:372
  50.8 0.8 slice.119
  51.6 0.7 slice.117
  52.4 1.9 %pad_maximum_fusion.2 = bf16[2,136,1024]{2,1,0:T(8,128)(2,1)} fusion(bf16[1,136,1024]{2,1,0:T(8,128)(2,1)} %bitcast.10, bf16[1,136,1024]{2,1,0:T(8,128)(2,1)} %bitcast.9), kind=kLoop, calls=%fused_computation.20 | loop fusion | flops 278528 | bytes 1114112 | tf_op jit(solution)/shard_map/stack | solution.py:361
  54.3 0.8 collective-permute-start.9
  55.0 1.7 slice.114
  56.7 1.7 slice.112
  58.5 0.7 slice.118
  59.3 1.0 slice.113
  60.3 1.1 pad_maximum_fusion.q_ref
  61.5 10.8 %near_tiles.2 = (f32[1024,512]{1,0:T(8,128)S(1)}, f32[8,8,512]{2,1,0:T(8,128)S(1)}) custom-call(s32[1]{0:T(128)} %bitcast.1.me_ref.m_ref, bf16[512,1024]{1,0:T(8,128)(2,1)S(1)} %pad_maximum_fusion.q_ref, bf16[512,4096]{1,0:T(8,128)(2,1)} %k0_ref.3, bf16[512,4096]{1,0:T(8,128)(2,1)} %v0_ref.3, bf16[2,512,1024]{2,1,0:T(8,128)(2,1)} %collective-permute-done.2.k1_ref.v1_ref, ...), custom_call_target="tpu_custom_call" | custom-call | flops 2147483648 | bytes 8388608 | tf_op jit(solution)/shard_map/near_tiles/pallas_call | solution.py:415
  72.3 1.2 collective-permute-start.10
  73.4 1.0 slice_bitcast_fusion.1
  74.4 1.1 slice_bitcast_fusion.3
  75.5 5.7 %collective-permute-done.10 = bf16[136,1024]{1,0:T(8,128)(2,1)S(1)} collective-permute-done((bf16[136,1024]{1,0:T(8,128)(2,1)}, bf16[136,1024]{1,0:T(8,128)(2,1)S(1)}, u32[]{:S(2)}, u32[]{:S(2)}) %collective-permute-start.10) | collective-permute-done | bytes 278560 | tf_op jit(solution)/shard_map/ppermute | solution.py:28
  81.2 0.7 slice.95
  81.9 0.7 slice.96
  83.4 0.7 slice.98
  84.2 1.3 pad_maximum_fusion.1.q_ref
  85.5 11.1 %near_tiles.3 = (f32[1024,512]{1,0:T(8,128)S(1)}, f32[8,8,512]{2,1,0:T(8,128)S(1)}) custom-call(s32[1]{0:T(128)} %bitcast.1.me_ref.m_ref, bf16[512,1024]{1,0:T(8,128)(2,1)S(1)} %pad_maximum_fusion.1.q_ref, bf16[512,4096]{1,0:T(8,128)(2,1)} %k0_ref.3, bf16[512,4096]{1,0:T(8,128)(2,1)} %v0_ref.3, bf16[2,512,1024]{2,1,0:T(8,128)(2,1)} %collective-permute-done.2.k1_ref.v1_ref, ...), custom_call_target="tpu_custom_call" | custom-call | flops 2147483648 | bytes 8388608 | tf_op jit(solution)/shard_map/near_tiles/pallas_call | solution.py:415
  96.6 5.3 %far_tiles.7 = bf16[4,416,128]{2,1,0:T(8,128)(2,1)S(1)} custom-call(bf16[512,1024]{1,0:T(8,128)(2,1)S(1)} %pad_maximum_fusion.1.q_ref, bf16[2,2,512,384]{3,2,1,0:T(8,128)(2,1)S(1)} %collective-permute-done.7.k2_ref.v2_ref, bf16[2,2,512,384]{3,2,1,0:T(8,128)(2,1)S(1)} %collective-permute-done.7.k2_ref.v2_ref, ...), custom_call_target="tpu_custom_call" | custom-call | flops 805306368 | bytes 3145728 | tf_op jit(solution)/shard_map/far_tiles/pallas_call | solution.py:485
  102.0 4.5 %far_tiles.6.a_ref = bf16[4,416,128]{2,1,0:T(8,128)(2,1)S(1)} custom-call(bf16[512,1024]{1,0:T(8,128)(2,1)S(1)} %copy-done.6, bf16[2,2,512,384]{3,2,1,0:T(8,128)(2,1)S(1)} %collective-permute-done.7.k2_ref.v2_ref, bf16[2,2,512,384]{3,2,1,0:T(8,128)(2,1)S(1)} %collective-permute-done.7.k2_ref.v2_ref, ...), custom_call_target="tpu_custom_call" | custom-call | flops 805306368 | bytes 3145728 | tf_op jit(solution)/shard_map/far_tiles/pallas_call | solution.py:485
  107.8 1.2 collective-permute-done.14.k3_ref.v3_ref
  109.0 4.2 %far_tiles.9 = bf16[4,416,128]{2,1,0:T(8,128)(2,1)} custom-call(bf16[512,1024]{1,0:T(8,128)(2,1)S(1)} %pad_maximum_fusion.1.q_ref, bf16[2,2,512,384]{3,2,1,0:T(8,128)(2,1)S(1)} %collective-permute-done.13.k2_ref.v2_ref, bf16[2,2,512,384]{3,2,1,0:T(8,128)(2,1)S(1)} %collective-permute-done.13.k2_ref.v2_ref, ...), custom_call_target="tpu_custom_call" | custom-call | flops 805306368 | bytes 3145728 | tf_op jit(solution)/shard_map/far_tiles/pallas_call | solution.py:485
  113.7 3.6 %far_tiles.8.a_ref = bf16[4,416,128]{2,1,0:T(8,128)(2,1)S(1)} custom-call(bf16[512,1024]{1,0:T(8,128)(2,1)S(1)} %copy-done.6, bf16[2,2,512,384]{3,2,1,0:T(8,128)(2,1)S(1)} %collective-permute-done.13.k2_ref.v2_ref, bf16[2,2,512,384]{3,2,1,0:T(8,128)(2,1)S(1)} %collective-permute-done.13.k2_ref.v2_ref, ...), custom_call_target="tpu_custom_call" | custom-call | flops 805306368 | bytes 3145728 | tf_op jit(solution)/shard_map/far_tiles/pallas_call | solution.py:485
  117.3 0.8 copy-done.11
  118.1 2.0 %collective-permute-done.12.b_ref = bf16[4,416,128]{2,1,0:T(8,128)(2,1)} collective-permute-done((bf16[4,416,128]{2,1,0:T(8,128)(2,1)S(1)}, bf16[4,416,128]{2,1,0:T(8,128)(2,1)}, u32[]{:S(2)}, u32[]{:S(2)}) %collective-permute-start.12) | collective-permute-done | bytes 426016 | tf_op jit(solution)/shard_map/ppermute | solution.py:28
  120.1 2.0 %merge_pair.3 = (bf16[416,128]{1,0:T(8,128)(2,1)}, bf16[416,128]{1,0:T(8,128)(2,1)}, bf16[416,128]{1,0:T(8,128)(2,1)}, bf16[416,128]{1,0:T(8,128)(2,1)}) custom-call(bf16[4,416,128]{2,1,0:T(8,128)(2,1)} %copy-done.10, bf16[4,416,128]{2,1,0:T(8,128)(2,1)} %collective-permute-done.12.b_ref), custom_call_target="tpu_custom_call" | custom-call | tf_op jit(solution)/shard_map/merge_pair/pallas_call | solution.py:460
  122.1 6.3 %collective-permute-done.16.b_ref = bf16[4,416,128]{2,1,0:T(8,128)(2,1)} collective-permute-done((bf16[4,416,128]{2,1,0:T(8,128)(2,1)}, bf16[4,416,128]{2,1,0:T(8,128)(2,1)}, u32[]{:S(2)}, u32[]{:S(2)}) %collective-permute-start.16) | collective-permute-done | bytes 426016 | tf_op jit(solution)/shard_map/ppermute | solution.py:28
  128.4 2.0 %merge_pair.4 = (bf16[416,128]{1,0:T(8,128)(2,1)}, bf16[416,128]{1,0:T(8,128)(2,1)}, bf16[416,128]{1,0:T(8,128)(2,1)}, bf16[416,128]{1,0:T(8,128)(2,1)}) custom-call(bf16[4,416,128]{2,1,0:T(8,128)(2,1)} %copy-done.11, bf16[4,416,128]{2,1,0:T(8,128)(2,1)} %collective-permute-done.16.b_ref), custom_call_target="tpu_custom_call" | custom-call | tf_op jit(solution)/shard_map/merge_pair/pallas_call | solution.py:460
  130.5 2.0 %collective-permute-done.15.k2_ref.v2_ref = bf16[2,2,512,256]{3,2,1,0:T(8,128)(2,1)S(1)} collective-permute-done((bf16[2,2,512,256]{3,2,1,0:T(8,128)(2,1)}, bf16[2,2,512,256]{3,2,1,0:T(8,128)(2,1)S(1)}, u32[]{:S(2)}, u32[]{:S(2)}) %collective-permute-start.15) | collective-permute-done | bytes 1048608 | tf_op jit(solution)/shard_map/ppermute | solution.py:28
  132.6 1.9 %collective-permute-done.17.k3_ref.v3_ref = bf16[2,512,256]{2,1,0:T(8,128)(2,1)S(1)} collective-permute-done((bf16[2,512,256]{2,1,0:T(8,128)(2,1)S(1)}, bf16[2,512,256]{2,1,0:T(8,128)(2,1)S(1)}, u32[]{:S(2)}, u32[]{:S(2)}) %collective-permute-start.17) | collective-permute-done | bytes 524320 | tf_op jit(solution)/shard_map/ppermute | solution.py:28
  134.5 1.2 copy-done.9
  135.8 2.4 %far_tiles.10 = bf16[4,272,128]{2,1,0:T(8,128)(2,1)S(1)} custom-call(bf16[512,1024]{1,0:T(8,128)(2,1)S(1)} %copy-done.9, bf16[2,2,512,256]{3,2,1,0:T(8,128)(2,1)S(1)} %collective-permute-done.15.k2_ref.v2_ref, bf16[2,2,512,256]{3,2,1,0:T(8,128)(2,1)S(1)} %collective-permute-done.15.k2_ref.v2_ref, ...), custom_call_target="tpu_custom_call" | custom-call | flops 536870912 | bytes 3145728 | tf_op jit(solution)/shard_map/far_tiles/pallas_call | solution.py:485
  138.7 3.4 %collective-permute-start.18 = (bf16[416,128]{1,0:T(8,128)(2,1)}, bf16[416,128]{1,0:T(8,128)(2,1)S(1)}, u32[]{:S(2)}, u32[]{:S(2)}) collective-permute-start(bf16[416,128]{1,0:T(8,128)(2,1)} %get-tuple-element.78), channel_id=1, source_target_pairs={{0,24},{4,28},{8,0},{12,4},{16,8},{20,12},{24,16},{28,20},{1,25},{... | collective-permute-start | bytes 319496 | tf_op jit(solution)/shard_map/ppermute | solution.py:33
  142.2 2.0 %collective-permute-start.23 = (bf16[416,128]{1,0:T(8,128)(2,1)S(1)}, bf16[416,128]{1,0:T(8,128)(2,1)S(1)}, u32[]{:S(2)}, u32[]{:S(2)}) collective-permute-start(bf16[416,128]{1,0:T(8,128)(2,1)S(1)} %copy-done.38), channel_id=1, source_target_pairs={{0,8},{4,12},{8,16},{12,20},{16,24},{20,28},{24,0},{28,4},{1,9},{5... | collective-permute-start | bytes 319496 | tf_op jit(solution)/shard_map/ppermute | solution.py:33
  144.2 2.5 %far_tiles.11.a_ref = bf16[4,272,128]{2,1,0:T(8,128)(2,1)S(1)} custom-call(bf16[512,1024]{1,0:T(8,128)(2,1)S(1)} %copy-done.7, bf16[2,2,512,256]{3,2,1,0:T(8,128)(2,1)S(1)} %collective-permute-done.15.k2_ref.v2_ref, bf16[2,2,512,256]{3,2,1,0:T(8,128)(2,1)S(1)} %collective-permute-done.15.k2_ref.v2_ref, ...), custom_call_target="tpu_custom_call" | custom-call | flops 536870912 | bytes 3145728 | tf_op jit(solution)/shard_map/far_tiles/pallas_call | solution.py:485
  146.7 0.7 copy-done.12
  147.4 3.0 %collective-permute-start.19 = (bf16[416,128]{1,0:T(8,128)(2,1)S(1)}, bf16[416,128]{1,0:T(8,128)(2,1)S(1)}, u32[]{:S(2)}, u32[]{:S(2)}) collective-permute-start(bf16[416,128]{1,0:T(8,128)(2,1)S(1)} %copy-done.37), channel_id=1, source_target_pairs={{0,16},{4,20},{8,24},{12,28},{16,0},{20,4},{24,8},{28,12},{1,17},{... | collective-permute-start | bytes 319496 | tf_op jit(solution)/shard_map/ppermute | solution.py:33
  150.4 1.9 merge_pair.5
  152.4 3.8 %collective-permute-start.25 = (bf16[272,128]{1,0:T(8,128)(2,1)}, bf16[272,128]{1,0:T(8,128)(2,1)S(1)}, u32[]{:S(2)}, u32[]{:S(2)}) collective-permute-start(bf16[272,128]{1,0:T(8,128)(2,1)} %get-tuple-element.86), channel_id=1, source_target_pairs={{0,24},{4,28},{8,0},{12,4},{16,8},{20,12},{24,16},{28,20},{1,25},{... | collective-permute-start | bytes 208904 | tf_op jit(solution)/shard_map/ppermute | solution.py:33
  156.2 4.3 %collective-permute-done.22.refs_2_ = bf16[416,128]{1,0:T(8,128)(2,1)S(1)} collective-permute-done((bf16[416,128]{1,0:T(8,128)(2,1)}, bf16[416,128]{1,0:T(8,128)(2,1)S(1)}, u32[]{:S(2)}, u32[]{:S(2)}) %collective-permute-start.22) | collective-permute-done | bytes 106528 | tf_op jit(solution)/shard_map/ppermute | solution.py:33
  161.2 2.0 %merge_all.4 = bf16[384,128]{1,0:T(8,128)(2,1)} custom-call(bf16[416,128]{1,0:T(8,128)(2,1)} %get-tuple-element.81.refs_0_, bf16[416,128]{1,0:T(8,128)(2,1)} %copy-done.26, bf16[416,128]{1,0:T(8,128)(2,1)} %copy-done.27, bf16[416,128]{1,0:T(8,128)(2,1)} %copy-done.28, f32[1024,128]{1,0:T(8,128)} %local_window.1.refs_4_, f32[16,128]{1,0:T(8,128)} %broadcast_in_dim.21.refs_5_), custom_call_target="tpu_custom_call" | custom-call | tf_op jit(solution)/shard_map/merge_all/pallas_call | solution.py:523
  165.1 2.0 %merge_all.3 = bf16[384,128]{1,0:T(8,128)(2,1)} custom-call(bf16[416,128]{1,0:T(8,128)(2,1)} %get-tuple-element.77.refs_0_, bf16[416,128]{1,0:T(8,128)(2,1)} %copy-done.25, bf16[416,128]{1,0:T(8,128)(2,1)} %copy-done.29, bf16[416,128]{1,0:T(8,128)(2,1)} %copy-done.30, f32[1024,128]{1,0:T(8,128)} %local_window.1.refs_4_, f32[16,128]{1,0:T(8,128)} %broadcast_in_dim.21.refs_5_), custom_call_target="tpu_custom_call" | custom-call | tf_op jit(solution)/shard_map/merge_all/pallas_call | solution.py:523
  167.8 1.9 %merge_all.5 = bf16[256,128]{1,0:T(8,128)(2,1)} custom-call(bf16[272,128]{1,0:T(8,128)(2,1)} %get-tuple-element.85.refs_0_, bf16[272,128]{1,0:T(8,128)(2,1)} %copy-done.31, bf16[272,128]{1,0:T(8,128)(2,1)} %copy-done.32, bf16[272,128]{1,0:T(8,128)(2,1)} %copy-done.33, f32[1024,128]{1,0:T(8,128)} %local_window.1.refs_4_, f32[16,128]{1,0:T(8,128)} %broadcast_in_dim.21.refs_5_), custom_call_target="tpu_custom_call" | custom-call | tf_op jit(solution)/shard_map/merge_all/pallas_call | solution.py:523
  169.7 2.2 %fusion.26 = bf16[1,128,1024]{2,1,0:T(8,128)(2,1)S(1)} fusion(bf16[1024,4096]{1,0:T(8,128)(2,1)} %param.19, s32[]{:T(128)S(6)} %select_n.60, bf16[256,128]{1,0:T(8,128)(2,1)} %merge_all.5, bf16[384,128]{1,0:T(8,128)(2,1)} %merge_all.4, bf16[384,128]{1,0:T(8,128)(2,1)} %merge_all.3), kind=kOutput, calls=%fused_computation.15 | convolution fusion | flops 269352960 | bytes 2621444 | tf_op jit(solution)/shard_map/dot_general | solution.py:533
  172.0 2.1 %fusion.23 = bf16[1,128,1024]{2,1,0:T(8,128)(2,1)S(1)} fusion(bf16[1024,4096]{1,0:T(8,128)(2,1)} %param.19, s32[]{:T(128)S(6)} %select_n.58, bf16[256,128]{1,0:T(8,128)(2,1)S(1)} %copy-done.21, bf16[384,128]{1,0:T(8,128)(2,1)S(1)} %copy-done.16, bf16[384,128]{1,0:T(8,128)(2,1)S(1)} %copy-done.17), kind=kOutput, calls=%fused_computation.14 | convolution fusion | flops 269352960 | bytes 2621444 | tf_op jit(solution)/shard_map/dot_general | solution.py:533
  174.2 1.9 collective-permute-done.28
  176.1 2.1 %fusion.29 = bf16[128,1024]{1,0:T(8,128)(2,1)S(1)} fusion(bf16[2,128,1024]{2,1,0:T(8,128)(2,1)S(1)} %collective-permute-done.28, bf16[1024,128]{1,0:T(8,128)(2,1)S(1)} %pad_maximum_fusion.6, bf16[1024,4096]{1,0:T(8,128)(2,1)} %param.19, s32[]{:T(128)S(6)} %select_n.59), kind=kOutput, calls=%fused_computation.25 | convolution fusion | flops 268828672 | bytes 2883588 | tf_op jit(solution)/shard_map/dot_general | solution.py:533
  178.4 8.1 %collective-permute-done.29 = bf16[128,1024]{1,0:T(8,128)(2,1)S(1)} collective-permute-done((bf16[128,1024]{1,0:T(8,128)(2,1)S(1)}, bf16[128,1024]{1,0:T(8,128)(2,1)S(1)}, u32[]{:S(2)}, u32[]{:S(2)}) %collective-permute-start.29) | collective-permute-done | bytes 262176 | tf_op jit(solution)/shard_map/ppermute | solution.py:28
  186.5 2.8 %fusion.14 = bf16[128,1024]{1,0:T(8,128)(2,1)} fusion(bf16[1024,128]{1,0:T(8,128)(2,1)S(1)} %pad_maximum_fusion.6, bf16[1024,4096]{1,0:T(8,128)(2,1)} %param.19, s32[]{:T(128)S(6)} %select_n.57, bf16[128,1024]{1,0:T(8,128)(2,1)S(1)} %collective-permute-done.29, bf16[2,128,1024]{2,1,0:T(8,128)(2,1)S(1)} %collective-permute-done.28), kind=kOutput, calls=%fused_computation.10 | convolution fusion | flops 269090816 | bytes 3145732 | tf_op jit(solution)/shard_map/dot_general | solution.py:533
  (147 shorter events, 8.4 us)
Async XLA Ops:
  0.0 7.6 %copy-start.20 = (bf16[128,1024]{1,0:T(8,128)(2,1)S(1)}, bf16[128,1024]{1,0:T(8,128)(2,1)}, u32[]{:S(2)}) copy-start(bf16[128,1024]{1,0:T(8,128)(2,1)} %param.10) | copy-start | bytes 786436
  0.0 17.2 %copy-start.18 = (bf16[128,1024]{1,0:T(8,128)(2,1)S(1)}, bf16[128,1024]{1,0:T(8,128)(2,1)}, u32[]{:S(2)}) copy-start(bf16[128,1024]{1,0:T(8,128)(2,1)} %v1_ref.1) | copy-start | bytes 786436
  0.0 17.2 %copy-start.19 = (bf16[128,1024]{1,0:T(8,128)(2,1)S(1)}, bf16[128,1024]{1,0:T(8,128)(2,1)}, u32[]{:S(2)}) copy-start(bf16[128,1024]{1,0:T(8,128)(2,1)} %k1_ref.1) | copy-start | bytes 786436
  6.0 1.1 copy-start.13
  7.2 14.6 %copy-start.34 = (s32[128,16]{0,1:T(8,128)S(1)}, s32[128,16]{0,1:T(8,128)}, u32[]{:S(2)}) copy-start(s32[128,16]{0,1:T(8,128)} %param.16) | copy-start | bytes 24580
  7.2 14.6 %copy-start.35 = (s32[128]{0:T(128)S(1)}, s32[128]{0:T(128)}, u32[]{:S(2)}) copy-start(s32[128]{0:T(128)} %param.17) | copy-start | bytes 1540
  7.2 16.6 %collective-permute-start.2 = (bf16[2,512,1024]{2,1,0:T(8,128)(2,1)}, bf16[2,512,1024]{2,1,0:T(8,128)(2,1)}, u32[]{:S(2)}, u32[]{:S(2)}) collective-permute-start(bf16[2,512,1024]{2,1,0:T(8,128)(2,1)} %get-tuple-element.50), channel_id=1, source_target_pairs={{0,1},{1,0},{2,3},{3,2},{4,5},{5,4},{6,7},{7,6},{8,9},{9,8},{10,11... | collective-permute-start | bytes 6291464 | tf_op jit(solution)/shard_map/ppermute | solution.py:28
  7.6 9.5 %collective-permute-start = (bf16[128,1024]{1,0:T(8,128)(2,1)S(1)}, bf16[128,1024]{1,0:T(8,128)(2,1)S(1)}, u32[]{:S(2)}, u32[]{:S(2)}) collective-permute-start(bf16[128,1024]{1,0:T(8,128)(2,1)S(1)} %copy-done.20), channel_id=1, source_target_pairs={{0,2},{1,3},{2,0},{3,1},{4,6},{5,7},{6,4},{7,5},{8,10},{9,11},{10,... | collective-permute-start | bytes 786440 | tf_op jit(solution)/shard_map/ppermute | solution.py:28
  17.2 6.5 %collective-permute-start.1 = (bf16[2,128,1024]{2,1,0:T(8,128)(2,1)S(1)}, bf16[2,128,1024]{2,1,0:T(8,128)(2,1)S(1)}, u32[]{:S(2)}, u32[]{:S(2)}) collective-permute-start(bf16[2,128,1024]{2,1,0:T(8,128)(2,1)S(1)} %pad_maximum_fusion.3), channel_id=1, source_target_pairs={{0,1},{1,0},{2,3},{3,2},{4,5},{5,4},{6,7},{7,6},{8,9},{9,8},{10,11... | collective-permute-start | bytes 1572872 | tf_op jit(solution)/shard_map/ppermute | solution.py:28
  17.3 25.9 %collective-permute-start.8 = (bf16[2,128,1024]{2,1,0:T(8,128)(2,1)S(1)}, bf16[2,128,1024]{2,1,0:T(8,128)(2,1)}, u32[]{:S(2)}, u32[]{:S(2)}) collective-permute-start(bf16[2,128,1024]{2,1,0:T(8,128)(2,1)S(1)} %pad_maximum_fusion.4), channel_id=1, source_target_pairs={{0,4},{4,8},{8,12},{12,16},{16,20},{20,24},{24,28},{1,5},{5,9},{9,... | collective-permute-start | bytes 1572872 | tf_op jit(solution)/shard_map/ppermute | solution.py:39
  22.1 39.3 %collective-permute-start.7 = (bf16[2,2,512,384]{3,2,1,0:T(8,128)(2,1)}, bf16[2,2,512,384]{3,2,1,0:T(8,128)(2,1)S(1)}, u32[]{:S(2)}, u32[]{:S(2)}) collective-permute-start(bf16[2,2,512,384]{3,2,1,0:T(8,128)(2,1)} %get-tuple-element.53), channel_id=1, source_target_pairs={{0,2},{1,3},{2,0},{3,1},{4,6},{5,7},{6,4},{7,5},{8,10},{9,11},{10,... | collective-permute-start | bytes 4718600 | tf_op jit(solution)/shard_map/ppermute | solution.py:28
  28.5 16.1 %copy-start.14 = (bf16[128,1024]{1,0:T(8,128)(2,1)}, bf16[128,1024]{1,0:T(8,128)(2,1)S(1)}, u32[]{:S(2)}) copy-start(bf16[128,1024]{1,0:T(8,128)(2,1)S(1)} %convolution_convert_fusion.q_ref) | copy-start | bytes 786436
  29.3 9.5 %collective-permute-start.4 = (bf16[136,1024]{1,0:T(8,128)(2,1)}, bf16[136,1024]{1,0:T(8,128)(2,1)S(1)}, u32[]{:S(2)}, u32[]{:S(2)}) collective-permute-start(bf16[136,1024]{1,0:T(8,128)(2,1)} %maximum_maximum_fusion), channel_id=1, source_target_pairs={{0,4},{4,0},{8,12},{12,8},{16,20},{20,16},{24,28},{28,24},{1,5},{5... | collective-permute-start | bytes 835592 | tf_op jit(solution)/shard_map/ppermute | solution.py:28
  30.1 20.7 %collective-permute-start.6 = (bf16[136,1024]{1,0:T(8,128)(2,1)}, bf16[136,1024]{1,0:T(8,128)(2,1)}, u32[]{:S(2)}, u32[]{:S(2)}) collective-permute-start(bf16[136,1024]{1,0:T(8,128)(2,1)} %maximum_maximum_fusion), channel_id=1, source_target_pairs={{0,24},{4,28},{8,0},{12,4},{16,8},{20,12},{24,16},{28,20},{1,25},{... | collective-permute-start | bytes 835592 | tf_op jit(solution)/shard_map/ppermute | solution.py:33
  32.2 19.4 %collective-permute-start.3 = (bf16[136,1024]{1,0:T(8,128)(2,1)}, bf16[136,1024]{1,0:T(8,128)(2,1)}, u32[]{:S(2)}, u32[]{:S(2)}) collective-permute-start(bf16[136,1024]{1,0:T(8,128)(2,1)} %maximum_maximum_fusion), channel_id=1, source_target_pairs={{0,8},{4,12},{8,16},{12,20},{16,24},{20,28},{24,0},{28,4},{1,9},{5... | collective-permute-start | bytes 835592 | tf_op jit(solution)/shard_map/ppermute | solution.py:33
  38.9 4.3 %copy-start.23 = (bf16[136,1024]{1,0:T(8,128)(2,1)}, bf16[136,1024]{1,0:T(8,128)(2,1)S(1)}, u32[]{:S(2)}) copy-start(bf16[136,1024]{1,0:T(8,128)(2,1)S(1)} %collective-permute-done.4) | copy-start | bytes 835588
  38.9 19.7 %collective-permute-start.5 = (bf16[136,1024]{1,0:T(8,128)(2,1)}, bf16[136,1024]{1,0:T(8,128)(2,1)}, u32[]{:S(2)}, u32[]{:S(2)}) collective-permute-start(bf16[136,1024]{1,0:T(8,128)(2,1)} %maximum_maximum_fusion), channel_id=1, source_target_pairs={{0,16},{4,20},{8,24},{12,28},{16,0},{20,4},{24,8},{28,12},{1,17},{... | collective-permute-start | bytes 835592 | tf_op jit(solution)/shard_map/ppermute | solution.py:33
  43.2 63.3 %collective-permute-start.13 = (bf16[2,2,512,384]{3,2,1,0:T(8,128)(2,1)}, bf16[2,2,512,384]{3,2,1,0:T(8,128)(2,1)S(1)}, u32[]{:S(2)}, u32[]{:S(2)}) collective-permute-start(bf16[2,2,512,384]{3,2,1,0:T(8,128)(2,1)} %copy-done.13), channel_id=1, source_target_pairs={{0,2},{1,3},{2,0},{3,1},{4,6},{5,7},{6,4},{7,5},{8,10},{9,11},{10,... | collective-permute-start | bytes 4718600 | tf_op jit(solution)/shard_map/ppermute | solution.py:28
  50.8 9.4 %copy-start.15 = (bf16[128,1024]{1,0:T(8,128)(2,1)S(1)}, bf16[128,1024]{1,0:T(8,128)(2,1)}, u32[]{:S(2)}) copy-start(bf16[128,1024]{1,0:T(8,128)(2,1)} %copy-done.14) | copy-start | bytes 786436
  54.3 20.2 %collective-permute-start.9 = (bf16[2,136,1024]{2,1,0:T(8,128)(2,1)}, bf16[2,136,1024]{2,1,0:T(8,128)(2,1)}, u32[]{:S(2)}, u32[]{:S(2)}) collective-permute-start(bf16[2,136,1024]{2,1,0:T(8,128)(2,1)} %pad_maximum_fusion.2), channel_id=1, source_target_pairs={{0,4},{4,0},{8,12},{12,8},{16,20},{20,16},{24,28},{28,24},{1,5},{5... | collective-permute-start | bytes 1671176 | tf_op jit(solution)/shard_map/ppermute | solution.py:28
  61.4 10.9 %copy-start.5 = (bf16[512,1024]{1,0:T(8,128)(2,1)}, bf16[512,1024]{1,0:T(8,128)(2,1)S(1)}, u32[]{:S(2)}) copy-start(bf16[512,1024]{1,0:T(8,128)(2,1)S(1)} %pad_maximum_fusion.q_ref) | copy-start | bytes 3145732
  72.3 11.1 %copy-start = (f32[1024,512]{1,0:T(8,128)}, f32[1024,512]{1,0:T(8,128)S(1)}, u32[]{:S(2)}) copy-start(f32[1024,512]{1,0:T(8,128)S(1)} %get-tuple-element.63.acc_ref) | copy-start | bytes 6291460
  72.3 8.9 %copy-start.24 = (bf16[136,1024]{1,0:T(8,128)(2,1)S(1)}, bf16[136,1024]{1,0:T(8,128)(2,1)}, u32[]{:S(2)}) copy-start(bf16[136,1024]{1,0:T(8,128)(2,1)} %copy-done.23) | copy-start | bytes 835588
  72.3 11.8 %slice-start = ((bf16[136,1024]{1,0:T(8,128)(2,1)}), bf16[4,1024]{1,0:T(4,128)(2,1)S(1)}, s32[]{:S(2)}) async-start(bf16[136,1024]{1,0:T(8,128)(2,1)} %copy-done.23), calls=%async_computation | async-start | bytes 16384 | tf_op jit(solution)/shard_map/slice | solution.py:319
  72.3 8.9 %collective-permute-start.10 = (bf16[136,1024]{1,0:T(8,128)(2,1)}, bf16[136,1024]{1,0:T(8,128)(2,1)S(1)}, u32[]{:S(2)}, u32[]{:S(2)}) collective-permute-start(bf16[136,1024]{1,0:T(8,128)(2,1)} %collective-permute-done.5), channel_id=1, source_target_pairs={{0,4},{4,0},{8,12},{12,8},{16,20},{20,16},{24,28},{28,24},{1,5},{5... | collective-permute-start | bytes 835592 | tf_op jit(solution)/shard_map/ppermute | solution.py:28
  74.4 22.2 %collective-permute-start.11 = (bf16[2,512,384]{2,1,0:T(8,128)(2,1)}, bf16[2,512,384]{2,1,0:T(8,128)(2,1)}, u32[]{:S(2)}, u32[]{:S(2)}) collective-permute-start(bf16[2,512,384]{2,1,0:T(8,128)(2,1)} %slice_bitcast_fusion.1), channel_id=1, source_target_pairs={{0,1},{1,0},{2,3},{3,2},{4,5},{5,4},{6,7},{7,6},{8,9},{9,8},{10,11... | collective-permute-start | bytes 2359304 | tf_op jit(solution)/shard_map/ppermute | solution.py:28
  85.5 23.5 %copy-start.8 = (bf16[512,1024]{1,0:T(8,128)(2,1)}, bf16[512,1024]{1,0:T(8,128)(2,1)S(1)}, u32[]{:S(2)}) copy-start(bf16[512,1024]{1,0:T(8,128)(2,1)S(1)} %pad_maximum_fusion.1.q_ref) | copy-start | bytes 3145732
  96.6 12.4 %copy-start.3 = (f32[1024,512]{1,0:T(8,128)}, f32[1024,512]{1,0:T(8,128)S(1)}, u32[]{:S(2)}) copy-start(f32[1024,512]{1,0:T(8,128)S(1)} %get-tuple-element.65.acc_ref) | copy-start | bytes 6291460
  96.6 5.3 %copy-start.1 = (f32[1024,512]{1,0:T(8,128)S(1)}, f32[1024,512]{1,0:T(8,128)}, u32[]{:S(2)}) copy-start(f32[1024,512]{1,0:T(8,128)} %copy-done) | copy-start | bytes 6291460
  96.6 5.3 %copy-start.6 = (bf16[512,1024]{1,0:T(8,128)(2,1)S(1)}, bf16[512,1024]{1,0:T(8,128)(2,1)}, u32[]{:S(2)}) copy-start(bf16[512,1024]{1,0:T(8,128)(2,1)} %copy-done.5) | copy-start | bytes 3145732
  106.5 0.8 copy-start.10
  106.6 2.4 %collective-permute-start.14 = (bf16[2,512,384]{2,1,0:T(8,128)(2,1)S(1)}, bf16[2,512,384]{2,1,0:T(8,128)(2,1)S(1)}, u32[]{:S(2)}, u32[]{:S(2)}) collective-permute-start(bf16[2,512,384]{2,1,0:T(8,128)(2,1)S(1)} %slice_bitcast_fusion), channel_id=1, source_target_pairs={{0,1},{1,0},{2,3},{3,2},{4,5},{5,4},{6,7},{7,6},{8,9},{9,8},{10,11... | collective-permute-start | bytes 2359304 | tf_op jit(solution)/shard_map/ppermute | solution.py:28
  106.7 25.8 %collective-permute-start.15 = (bf16[2,2,512,256]{3,2,1,0:T(8,128)(2,1)}, bf16[2,2,512,256]{3,2,1,0:T(8,128)(2,1)S(1)}, u32[]{:S(2)}, u32[]{:S(2)}) collective-permute-start(bf16[2,2,512,256]{3,2,1,0:T(8,128)(2,1)} %get-tuple-element.72), channel_id=1, source_target_pairs={{0,2},{1,3},{2,0},{3,1},{4,6},{5,7},{6,4},{7,5},{8,10},{9,11},{10,... | collective-permute-start | bytes 3145736 | tf_op jit(solution)/shard_map/ppermute | solution.py:28
  107.3 12.8 %collective-permute-start.12 = (bf16[4,416,128]{2,1,0:T(8,128)(2,1)S(1)}, bf16[4,416,128]{2,1,0:T(8,128)(2,1)}, u32[]{:S(2)}, u32[]{:S(2)}) collective-permute-start(bf16[4,416,128]{2,1,0:T(8,128)(2,1)S(1)} %far_tiles.7), channel_id=1, source_target_pairs={{0,4},{4,0},{8,12},{12,8},{16,20},{20,16},{24,28},{28,24},{1,5},{5... | collective-permute-start | bytes 1277960 | tf_op jit(solution)/shard_map/ppermute | solution.py:28
  113.2 15.2 %collective-permute-start.16 = (bf16[4,416,128]{2,1,0:T(8,128)(2,1)}, bf16[4,416,128]{2,1,0:T(8,128)(2,1)}, u32[]{:S(2)}, u32[]{:S(2)}) collective-permute-start(bf16[4,416,128]{2,1,0:T(8,128)(2,1)} %far_tiles.9), channel_id=1, source_target_pairs={{0,4},{4,0},{8,12},{12,8},{16,20},{20,16},{24,28},{28,24},{1,5},{5... | collective-permute-start | bytes 1277960 | tf_op jit(solution)/shard_map/ppermute | solution.py:28
  118.1 16.5 %copy-start.4 = (f32[1024,512]{1,0:T(8,128)S(1)}, f32[1024,512]{1,0:T(8,128)}, u32[]{:S(2)}) copy-start(f32[1024,512]{1,0:T(8,128)} %copy-done.3) | copy-start | bytes 6291460
  132.5 9.7 %copy-start.38 = (bf16[416,128]{1,0:T(8,128)(2,1)S(1)}, bf16[416,128]{1,0:T(8,128)(2,1)}, u32[]{:S(2)}) copy-start(bf16[416,128]{1,0:T(8,128)(2,1)} %get-tuple-element.84) | copy-start | bytes 319492
  132.5 11.7 %copy-start.2 = (f32[1024,512]{1,0:T(8,128)S(1)}, f32[1024,512]{1,0:T(8,128)}, u32[]{:S(2)}) copy-start(f32[1024,512]{1,0:T(8,128)} %copy-done) | copy-start | bytes 6291460
  132.5 11.7 %copy-start.7 = (bf16[512,1024]{1,0:T(8,128)(2,1)S(1)}, bf16[512,1024]{1,0:T(8,128)(2,1)}, u32[]{:S(2)}) copy-start(bf16[512,1024]{1,0:T(8,128)(2,1)} %copy-done.5) | copy-start | bytes 3145732
  132.5 2.0 %collective-permute-start.17 = (bf16[2,512,256]{2,1,0:T(8,128)(2,1)S(1)}, bf16[2,512,256]{2,1,0:T(8,128)(2,1)S(1)}, u32[]{:S(2)}, u32[]{:S(2)}) collective-permute-start(bf16[2,512,256]{2,1,0:T(8,128)(2,1)S(1)} %slice_bitcast_fusion.2), channel_id=1, source_target_pairs={{0,1},{1,0},{2,3},{3,2},{4,5},{5,4},{6,7},{7,6},{8,9},{9,8},{10,11... | collective-permute-start | bytes 1572872 | tf_op jit(solution)/shard_map/ppermute | solution.py:28
  134.5 1.2 copy-start.9
  138.2 9.3 %collective-permute-start.24 = (bf16[4,272,128]{2,1,0:T(8,128)(2,1)S(1)}, bf16[4,272,128]{2,1,0:T(8,128)(2,1)S(1)}, u32[]{:S(2)}, u32[]{:S(2)}) collective-permute-start(bf16[4,272,128]{2,1,0:T(8,128)(2,1)S(1)} %far_tiles.10), channel_id=1, source_target_pairs={{0,4},{4,0},{8,12},{12,8},{16,20},{20,16},{24,28},{28,24},{1,5},{5... | collective-permute-start | bytes 835592 | tf_op jit(solution)/shard_map/ppermute | solution.py:28
  138.7 13.6 %collective-permute-start.18 = (bf16[416,128]{1,0:T(8,128)(2,1)}, bf16[416,128]{1,0:T(8,128)(2,1)S(1)}, u32[]{:S(2)}, u32[]{:S(2)}) collective-permute-start(bf16[416,128]{1,0:T(8,128)(2,1)} %get-tuple-element.78), channel_id=1, source_target_pairs={{0,24},{4,28},{8,0},{12,4},{16,8},{20,12},{24,16},{28,20},{1,25},{... | collective-permute-start | bytes 319496 | tf_op jit(solution)/shard_map/ppermute | solution.py:33
  142.1 10.2 %collective-permute-start.21 = (bf16[416,128]{1,0:T(8,128)(2,1)}, bf16[416,128]{1,0:T(8,128)(2,1)S(1)}, u32[]{:S(2)}, u32[]{:S(2)}) collective-permute-start(bf16[416,128]{1,0:T(8,128)(2,1)} %get-tuple-element.82), channel_id=1, source_target_pairs={{0,24},{4,28},{8,0},{12,4},{16,8},{20,12},{24,16},{28,20},{1,25},{... | collective-permute-start | bytes 319496 | tf_op jit(solution)/shard_map/ppermute | solution.py:33
  142.2 18.3 %collective-permute-start.22 = (bf16[416,128]{1,0:T(8,128)(2,1)}, bf16[416,128]{1,0:T(8,128)(2,1)S(1)}, u32[]{:S(2)}, u32[]{:S(2)}) collective-permute-start(bf16[416,128]{1,0:T(8,128)(2,1)} %get-tuple-element.83), channel_id=1, source_target_pairs={{0,16},{4,20},{8,24},{12,28},{16,0},{20,4},{24,8},{28,12},{1,17},{... | collective-permute-start | bytes 319496 | tf_op jit(solution)/shard_map/ppermute | solution.py:33
  142.2 5.2 %copy-start.37 = (bf16[416,128]{1,0:T(8,128)(2,1)S(1)}, bf16[416,128]{1,0:T(8,128)(2,1)}, u32[]{:S(2)}) copy-start(bf16[416,128]{1,0:T(8,128)(2,1)} %get-tuple-element.79) | copy-start | bytes 319492
  142.2 10.1 %copy-start.36 = (bf16[416,128]{1,0:T(8,128)(2,1)S(1)}, bf16[416,128]{1,0:T(8,128)(2,1)}, u32[]{:S(2)}) copy-start(bf16[416,128]{1,0:T(8,128)(2,1)} %get-tuple-element.80) | copy-start | bytes 319492
  142.2 18.3 %copy-start.39 = (f32[16]{0:T(128)S(1)}, f32[16]{0:T(128)}, u32[]{:S(2)}) copy-start(f32[16]{0:T(128)} %param.18) | copy-start | bytes 196
  142.2 18.2 %collective-permute-start.23 = (bf16[416,128]{1,0:T(8,128)(2,1)S(1)}, bf16[416,128]{1,0:T(8,128)(2,1)S(1)}, u32[]{:S(2)}, u32[]{:S(2)}) collective-permute-start(bf16[416,128]{1,0:T(8,128)(2,1)S(1)} %copy-done.38), channel_id=1, source_target_pairs={{0,8},{4,12},{8,16},{12,20},{16,24},{20,28},{24,0},{28,4},{1,9},{5... | collective-permute-start | bytes 319496 | tf_op jit(solution)/shard_map/ppermute | solution.py:33
  147.4 3.0 %copy-start.22 = (bf16[4,272,128]{2,1,0:T(8,128)(2,1)}, bf16[4,272,128]{2,1,0:T(8,128)(2,1)S(1)}, u32[]{:S(2)}) copy-start(bf16[4,272,128]{2,1,0:T(8,128)(2,1)S(1)} %collective-permute-done.24.b_ref) | copy-start | bytes 835588
  147.4 16.3 %collective-permute-start.19 = (bf16[416,128]{1,0:T(8,128)(2,1)S(1)}, bf16[416,128]{1,0:T(8,128)(2,1)S(1)}, u32[]{:S(2)}, u32[]{:S(2)}) collective-permute-start(bf16[416,128]{1,0:T(8,128)(2,1)S(1)} %copy-done.37), channel_id=1, source_target_pairs={{0,16},{4,20},{8,24},{12,28},{16,0},{20,4},{24,8},{28,12},{1,17},{... | collective-permute-start | bytes 319496 | tf_op jit(solution)/shard_map/ppermute | solution.py:33
  152.3 11.5 %copy-start.25 = (bf16[416,128]{1,0:T(8,128)(2,1)}, bf16[416,128]{1,0:T(8,128)(2,1)S(1)}, u32[]{:S(2)}) copy-start(bf16[416,128]{1,0:T(8,128)(2,1)S(1)} %collective-permute-done.18.refs_1_) | copy-start | bytes 319492
  152.3 11.5 %collective-permute-start.20 = (bf16[416,128]{1,0:T(8,128)(2,1)S(1)}, bf16[416,128]{1,0:T(8,128)(2,1)S(1)}, u32[]{:S(2)}, u32[]{:S(2)}) collective-permute-start(bf16[416,128]{1,0:T(8,128)(2,1)S(1)} %copy-done.36), channel_id=1, source_target_pairs={{0,8},{4,12},{8,16},{12,20},{16,24},{20,28},{24,0},{28,4},{1,9},{5... | collective-permute-start | bytes 319496 | tf_op jit(solution)/shard_map/ppermute | solution.py:33
  152.4 8.8 %copy-start.26 = (bf16[416,128]{1,0:T(8,128)(2,1)}, bf16[416,128]{1,0:T(8,128)(2,1)S(1)}, u32[]{:S(2)}) copy-start(bf16[416,128]{1,0:T(8,128)(2,1)S(1)} %collective-permute-done.21.refs_1_) | copy-start | bytes 319492
  152.4 14.7 %collective-permute-start.25 = (bf16[272,128]{1,0:T(8,128)(2,1)}, bf16[272,128]{1,0:T(8,128)(2,1)S(1)}, u32[]{:S(2)}, u32[]{:S(2)}) collective-permute-start(bf16[272,128]{1,0:T(8,128)(2,1)} %get-tuple-element.86), channel_id=1, source_target_pairs={{0,24},{4,28},{8,0},{12,4},{16,8},{20,12},{24,16},{28,20},{1,25},{... | collective-permute-start | bytes 208904 | tf_op jit(solution)/shard_map/ppermute | solution.py:33
  160.4 0.8 copy-start.27
  160.4 6.7 %collective-permute-start.26 = (bf16[272,128]{1,0:T(8,128)(2,1)}, bf16[272,128]{1,0:T(8,128)(2,1)S(1)}, u32[]{:S(2)}, u32[]{:S(2)}) collective-permute-start(bf16[272,128]{1,0:T(8,128)(2,1)} %get-tuple-element.87), channel_id=1, source_target_pairs={{0,16},{4,20},{8,24},{12,28},{16,0},{20,4},{24,8},{28,12},{1,17},{... | collective-permute-start | bytes 208904 | tf_op jit(solution)/shard_map/ppermute | solution.py:33
  160.4 0.8 copy-start.28
  160.4 6.7 %collective-permute-start.27 = (bf16[272,128]{1,0:T(8,128)(2,1)}, bf16[272,128]{1,0:T(8,128)(2,1)S(1)}, u32[]{:S(2)}, u32[]{:S(2)}) collective-permute-start(bf16[272,128]{1,0:T(8,128)(2,1)} %get-tuple-element.88), channel_id=1, source_target_pairs={{0,8},{4,12},{8,16},{12,20},{16,24},{20,28},{24,0},{28,4},{1,9},{5... | collective-permute-start | bytes 208904 | tf_op jit(solution)/shard_map/ppermute | solution.py:33
  163.2 8.7 %copy-start.16 = (bf16[384,128]{1,0:T(8,128)(2,1)S(1)}, bf16[384,128]{1,0:T(8,128)(2,1)}, u32[]{:S(2)}) copy-start(bf16[384,128]{1,0:T(8,128)(2,1)} %merge_all.4) | copy-start | bytes 294916
  167.1 4.8 %copy-start.17 = (bf16[384,128]{1,0:T(8,128)(2,1)S(1)}, bf16[384,128]{1,0:T(8,128)(2,1)}, u32[]{:S(2)}) copy-start(bf16[384,128]{1,0:T(8,128)(2,1)} %merge_all.3) | copy-start | bytes 294916
  169.7 2.3 %copy-start.21 = (bf16[256,128]{1,0:T(8,128)(2,1)S(1)}, bf16[256,128]{1,0:T(8,128)(2,1)}, u32[]{:S(2)}) copy-start(bf16[256,128]{1,0:T(8,128)(2,1)} %merge_all.5) | copy-start | bytes 196612
  174.1 2.0 %collective-permute-start.28 = (bf16[2,128,1024]{2,1,0:T(8,128)(2,1)S(1)}, bf16[2,128,1024]{2,1,0:T(8,128)(2,1)S(1)}, u32[]{:S(2)}, u32[]{:S(2)}) collective-permute-start(bf16[2,128,1024]{2,1,0:T(8,128)(2,1)S(1)} %pad_maximum_fusion.5), channel_id=1, source_target_pairs={{0,1},{1,0},{2,3},{3,2},{4,5},{5,4},{6,7},{7,6},{8,9},{9,8},{10,11... | collective-permute-start | bytes 1572872 | tf_op jit(solution)/shard_map/ppermute | solution.py:28
  178.1 8.4 %collective-permute-start.29 = (bf16[128,1024]{1,0:T(8,128)(2,1)S(1)}, bf16[128,1024]{1,0:T(8,128)(2,1)S(1)}, u32[]{:S(2)}, u32[]{:S(2)}) collective-permute-start(bf16[128,1024]{1,0:T(8,128)(2,1)S(1)} %fusion.29), channel_id=1, source_target_pairs={{0,2},{1,3},{2,0},{3,1},{4,6},{5,7},{6,4},{7,5},{8,10},{9,11},{10,... | collective-permute-start | bytes 786440 | tf_op jit(solution)/shard_map/ppermute | solution.py:28
  (7 other events, 4.7 us)

commit v9 on v7

--- a/solution.py
+++ b/solution.py
@@ -358,30 +358,32 @@
     crossed.append(swap(after(far_blocks[1], queries), "mem", 2))
     q_halves = [jnp.concatenate(q_blocks[:turns], 0), None]
 
-    window = from_behind(jnp.stack([local_keys, local_values]), "ctx", 1)
-    pair_spec = pl.BlockSpec((row_count, PAIR), lambda p, c: (0, p))
-    local_out = pl.pallas_call(
-        local_kernel,
-        grid_spec=pltpu.PrefetchScalarGridSpec(
-            num_scalar_prefetch=1,
-            grid=(pairs,),
-            in_specs=[
-                pair_spec,
-                pl.BlockSpec((None, row_count, PAIR), lambda p, c: (0, 0, p)),
-                pair_spec,
-                pl.BlockSpec((None, row_count, PAIR), lambda p, c: (1, 0, p)),
-                pair_spec,
-            ],
-            out_specs=pl.BlockSpec((PAIR, row_count), lambda p, c: (p, 0)),
-        ),
-        out_shape=jax.ShapeDtypeStruct((features, row_count), f32),
-        cost_estimate=pl.CostEstimate(
-            flops=8 * row_count * row_count * features,
-            transcendentals=2 * row_count * row_count * heads_here,
-            bytes_accessed=2 << 20,
-        ),
-        name="local_window",
-    )(my_ctx.reshape(1), queries, window, local_keys, window, local_values)
+    window = from_behind(jnp.stack([local_keys, after(local_values, q_blocks[1], q_blocks[turns - 1])]), "ctx", 1)
+
+    def attend_window(token):
+        pair_spec = pl.BlockSpec((row_count, PAIR), lambda p, c: (0, p))
+        return pl.pallas_call(
+            local_kernel,
+            grid_spec=pltpu.PrefetchScalarGridSpec(
+                num_scalar_prefetch=1,
+                grid=(pairs,),
+                in_specs=[
+                    pair_spec,
+                    pl.BlockSpec((None, row_count, PAIR), lambda p, c: (0, 0, p)),
+                    pair_spec,
+                    pl.BlockSpec((None, row_count, PAIR), lambda p, c: (1, 0, p)),
+                    pair_spec,
+                ],
+                out_specs=pl.BlockSpec((PAIR, row_count), lambda p, c: (p, 0)),
+            ),
+            out_shape=jax.ShapeDtypeStruct((features, row_count), f32),
+            cost_estimate=pl.CostEstimate(
+                flops=8 * row_count * row_count * features,
+                transcendentals=2 * row_count * row_count * heads_here,
+                bytes_accessed=2 << 20,
+            ),
+            name="local_window",
+        )(my_ctx.reshape(1), after(queries, token), window, local_keys, window, local_values)
 
     near_flops = 2 * 2 * half * 2 * mem_rows * features
 
@@ -393,10 +395,11 @@
 
     chunk_pairs = NEAR_HEADS // 2
     near_state = []
-    q_halves[0] = after(q_halves[0], crossed[0], local_out)
+    q_halves[0] = after(q_halves[0], crossed[0])
     for part in range(2):
         if part == 1:
-            q_halves[1] = jnp.concatenate(after(q_blocks[turns:], near_state[0][1]), 0)
+            local_out = attend_window(near_state[0][1])
+            q_halves[1] = jnp.concatenate(after(q_blocks[turns:], local_out), 0)
             crossed.append(
                 swap(after(far_blocks[2], near_state[0][1]), "mem", 2)
             )
@@ -446,7 +449,7 @@
         heads, first = sizes[j], firsts[j]
         wide = heads * DH
         msg_rows = wide + stat_rows(heads)
-        tokens = messages[j - 1] if j >= 1 else [near_state[0][1]]
+        tokens = messages[j - 1] if j >= 1 else [near_state[1][1]]
         if j == chunks - 1:
             tokens = tokens + merges + answers[0]
         far2 = after(crossed[j], *tokens)
@@ -514,10 +517,11 @@
         return lax.dot_general(rows, w, over_rows, preferred_element_type=f32)
 
     away = swap(piece(3, combined).astype(jnp.bfloat16), "mem", 1)
-    away = (piece(2, combined) + away.astype(f32)).astype(jnp.bfloat16)
+    own = piece(1, combined).astype(jnp.bfloat16)
+    away = (piece(2, after(combined, own)) + away.astype(f32)).astype(jnp.bfloat16)
     rest = after(combined, away)
     away = swap(away, "mem", 2)
-    result = piece(0, rest) + swap(piece(1, rest).astype(jnp.bfloat16), "mem", 1).astype(f32)
+    result = piece(0, rest) + swap(own, "mem", 1).astype(f32)
     return (result + away.astype(f32)).astype(jnp.bfloat16)
 
 

time: 179 us -> 187 us (1.045)
  local copies, waits for them, and re-layouts: 14.2 us -> 23.8 us
  waiting for transfers between devices: 40.4 us -> 34.7 us
  starting transfers between devices: 41.2 us -> 46.1 us
    ppermute x21, waiting for transfers between devices: 32.2 us -> 20.7 us  [swap(): lax.ppermute(block, axis, [(i, i ^ distance) for i in range(lax.axis_size...]
    ppermute x15, waiting for transfers between devices: 8.22 us -> 13.9 us  [turn(): lax.ppermute(block, axis, [(i, (i + distance) % size) for i in range(size)])]
    dynamic_update_slice x4, local copies, waits for them, and re-layouts: 1.04 us -> 4.92 us  [on_device(): lax.dynamic_update_slice(hidden, have[k], (0, (me ^ k) * hidden_states.sh...]
    unnamed x75 -> x83, local copies, waits for them, and re-layouts: 12.1 us -> 15.9 us
    ppermute x21, starting transfers between devices: 14.4 us -> 17.9 us  [swap(): lax.ppermute(block, axis, [(i, i ^ distance) for i in range(lax.axis_size...]
    ppermute x15, starting transfers between devices: 22.6 us -> 25 us  [turn(): lax.ppermute(block, axis, [(i, (i + distance) % size) for i in range(size)])]
  transfers between devices with their start and end apart: 37 -> 37, of which waited for: 10 -> 12; matrix products, arithmetic and copies ran while one was open for 6% -> 11% of each run, Pallas kernels for 31% -> 30%
where the time goes in v9:
time: 187 us; the launch traced here: 186 us
  Pallas kernels  65.3 us (35%)
  starting transfers between devices  46.1 us (25%)
  waiting for transfers between devices  34.7 us (19%)
  local copies, waits for them, and re-layouts  23.8 us (13%)
  matrix products  13.4 us (7%)
  other arithmetic  2.24 us (1%)
    ppermute x15, starting transfers between devices, turn(): lax.ppermute(block, axis, [(i, (i + distance) % size) for i in range(size)])  25 us
    pallas_call x2, Pallas kernels, on_device(): pl.pallas_call(near_kernel, grid_spec=pltpu.PrefetchScalarGridSpec(num_sc...  21.6 us
    ppermute x21, waiting for transfers between devices, swap(): lax.ppermute(block, axis, [(i, i ^ distance) for i in range(lax.axis_size...  20.7 us
    pallas_call x6, Pallas kernels, on_device(): pl.pallas_call(far_kernel, grid=(1,), in_specs=[pl.BlockSpec((pl.Element(...  19.5 us
    ppermute x21, starting transfers between devices, swap(): lax.ppermute(block, axis, [(i, i ^ distance) for i in range(lax.axis_size...  17.9 us
    unnamed x83, local copies, waits for them, and re-layouts  15.9 us
    ppermute x15, waiting for transfers between devices, turn(): lax.ppermute(block, axis, [(i, (i + distance) % size) for i in range(size)])  13.9 us
    dot_general x4, matrix products, piece(): return lax.dot_general(rows, w, over_rows, preferred_element_type=f32)  8.42 us
  transfers between devices with their start and end apart: 37, of which 12 were waited for; matrix products, arithmetic and copies ran while one was open for 11% of the time, Pallas kernels for 30%

profile of v9, /device:TPU:0, one launch (start us, length us, event | category | flops | bytes accessed | tf_op | source)
XLA Modules:
  0.0 186.0 jit_solution(12655177162790248135)
XLA Ops:
  0.0 6.0 %share_tiles.1 = (bf16[2,512,1024]{2,1,0:T(8,128)(2,1)}, bf16[2,2,512,384]{3,2,1,0:T(8,128)(2,1)S(1)}, bf16[2,2,512,384]{3,2,1,0:T(8,128)(2,1)}, bf16[2,2,512,256]{3,2,1,0:T(8,128)(2,1)}) custom-call(s32[1]{0:T(128)} %bitcast.me_ref.m_ref, bf16[512,4096]{1,0:T(8,128)(2,1)} %k0_ref.3, bf16[512,4096]{1,0:T(8,128)(2,1)} %v0_ref.3), custom_call_target="tpu_custom_call" | custom-call | bytes 14680064 | tf_op jit(solution)/shard_map/share_tiles/pallas_call | solution.py:329
  6.5 2.6 %collective-permute-start.3 = (s32[16,128]{1,0:T(8,128)S(1)}, s32[16,128]{1,0:T(8,128)S(1)}, u32[]{:S(2)}, u32[]{:S(2)}) collective-permute-start(s32[16,128]{1,0:T(8,128)S(1)} %get-tuple-element.92), channel_id=1, source_target_pairs={{0,4},{4,0},{8,12},{12,8},{16,20},{20,16},{24,28},{28,24},{1,5},{5... | collective-permute-start | bytes 24584 | tf_op jit(solution)/shard_map/ppermute | solution.py:28
  9.1 1.5 collective-permute-start.1
  10.7 3.1 %collective-permute-start.5 = (s32[2,16,128]{2,1,0:T(8,128)S(1)}, s32[2,16,128]{2,1,0:T(8,128)S(1)}, u32[]{:S(2)}, u32[]{:S(2)}) collective-permute-start(s32[2,16,128]{2,1,0:T(8,128)S(1)} %get-tuple-element.90), channel_id=1, source_target_pairs={{0,16},{4,20},{8,24},{12,28},{16,0},{20,4},{24,8},{28,12},{1,17},{... | collective-permute-start | bytes 49160 | tf_op jit(solution)/shard_map/ppermute | solution.py:33
  13.8 1.6 collective-permute-start.4
  15.5 4.1 %collective-permute-start.6 = (s32[2,16,128]{2,1,0:T(8,128)S(1)}, s32[2,16,128]{2,1,0:T(8,128)S(1)}, u32[]{:S(2)}, u32[]{:S(2)}) collective-permute-start(s32[2,16,128]{2,1,0:T(8,128)S(1)} %get-tuple-element.90), channel_id=1, source_target_pairs={{0,24},{4,28},{8,0},{12,4},{16,8},{20,12},{24,16},{28,20},{1,25},{... | collective-permute-start | bytes 49160 | tf_op jit(solution)/shard_map/ppermute | solution.py:33
  19.6 1.1 broadcast_in_dim.18
  21.8 1.5 collective-permute-start.12
  23.3 1.7 constant_dynamic-update-slice_fusion.6
  25.0 1.7 constant_dynamic-update-slice_fusion.5
  27.5 5.0 %convolution_convert_fusion.q_ref = bf16[128,1024]{1,0:T(8,128)(2,1)S(1)} fusion(bf16[128,4096]{1,0:T(8,128)(2,1)} %constant_dynamic-update-slice_fusion.4, bf16[4096,1024]{1,0:T(8,128)(2,1)} %param.11), kind=kOutput, calls=%fused_computation.10 | convolution fusion | flops 1073872896 | bytes 9699328 | tf_op jit(solution)/shard_map/dot_general | solution.py:347
  32.5 1.6 collective-permute-start.9
  34.1 3.7 %collective-permute-start.11 = (bf16[128,1024]{1,0:T(8,128)(2,1)S(1)}, bf16[128,1024]{1,0:T(8,128)(2,1)}, u32[]{:S(2)}, u32[]{:S(2)}) collective-permute-start(bf16[128,1024]{1,0:T(8,128)(2,1)S(1)} %convolution_convert_fusion.q_ref), channel_id=1, source_target_pairs={{0,24},{4,28},{8,0},{12,4},{16,8},{20,12},{24,16},{28,20},{1,25},{... | collective-permute-start | bytes 786440 | tf_op jit(solution)/shard_map/ppermute | solution.py:33
  37.8 3.3 %collective-permute-done.9 = bf16[128,1024]{1,0:T(8,128)(2,1)S(1)} collective-permute-done((bf16[128,1024]{1,0:T(8,128)(2,1)S(1)}, bf16[128,1024]{1,0:T(8,128)(2,1)S(1)}, u32[]{:S(2)}, u32[]{:S(2)}) %collective-permute-start.9) | collective-permute-done | bytes 262176 | tf_op jit(solution)/shard_map/ppermute | solution.py:28
  41.8 2.7 %collective-permute-done.11 = bf16[128,1024]{1,0:T(8,128)(2,1)} collective-permute-done((bf16[128,1024]{1,0:T(8,128)(2,1)S(1)}, bf16[128,1024]{1,0:T(8,128)(2,1)}, u32[]{:S(2)}, u32[]{:S(2)}) %collective-permute-start.11) | collective-permute-done | bytes 262176 | tf_op jit(solution)/shard_map/ppermute | solution.py:33
  44.5 6.2 %collective-permute-done.8 = bf16[128,1024]{1,0:T(8,128)(2,1)} collective-permute-done((bf16[128,1024]{1,0:T(8,128)(2,1)S(1)}, bf16[128,1024]{1,0:T(8,128)(2,1)}, u32[]{:S(2)}, u32[]{:S(2)}) %collective-permute-start.8) | collective-permute-done | bytes 262176 | tf_op jit(solution)/shard_map/ppermute | solution.py:33
  50.8 3.2 %collective-permute-start.16 = (bf16[2,128,1024]{2,1,0:T(8,128)(2,1)S(1)}, bf16[2,128,1024]{2,1,0:T(8,128)(2,1)}, u32[]{:S(2)}, u32[]{:S(2)}) collective-permute-start(bf16[2,128,1024]{2,1,0:T(8,128)(2,1)S(1)} %pad_maximum_fusion.1), channel_id=1, source_target_pairs={{0,4},{4,8},{8,12},{12,16},{16,20},{20,24},{24,28},{1,5},{5,9},{9,... | collective-permute-start | bytes 1572872 | tf_op jit(solution)/shard_map/ppermute | solution.py:39
  54.0 2.2 %collective-permute-start.15 = (bf16[128,1024]{1,0:T(8,128)(2,1)}, bf16[128,1024]{1,0:T(8,128)(2,1)}, u32[]{:S(2)}, u32[]{:S(2)}) collective-permute-start(bf16[128,1024]{1,0:T(8,128)(2,1)} %collective-permute-done.11), channel_id=1, source_target_pairs={{0,4},{4,0},{8,12},{12,8},{16,20},{20,16},{24,28},{28,24},{1,5},{5... | collective-permute-start | bytes 786440 | tf_op jit(solution)/shard_map/ppermute | solution.py:28
  56.3 4.4 %collective-permute-done.10 = bf16[128,1024]{1,0:T(8,128)(2,1)} collective-permute-done((bf16[128,1024]{1,0:T(8,128)(2,1)S(1)}, bf16[128,1024]{1,0:T(8,128)(2,1)}, u32[]{:S(2)}, u32[]{:S(2)}) %collective-permute-start.10) | collective-permute-done | bytes 262176 | tf_op jit(solution)/shard_map/ppermute | solution.py:33
  60.7 0.9 collective-permute-start.14
  61.6 1.2 pad_maximum_fusion.q_ref
  63.4 10.5 %near_tiles.2 = (f32[1024,512]{1,0:T(8,128)S(1)}, f32[8,8,512]{2,1,0:T(8,128)S(1)}) custom-call(s32[1]{0:T(128)} %bitcast.me_ref.m_ref, bf16[512,1024]{1,0:T(8,128)(2,1)S(1)} %pad_maximum_fusion.q_ref, bf16[512,4096]{1,0:T(8,128)(2,1)} %k0_ref.3, bf16[512,4096]{1,0:T(8,128)(2,1)} %v0_ref.3, bf16[2,512,1024]{2,1,0:T(8,128)(2,1)} %collective-permute-done.7.k1_ref.v1_ref, ...), custom_call_target="tpu_custom_call" | custom-call | flops 2147483648 | bytes 8388608 | tf_op jit(solution)/shard_map/near_tiles/pallas_call | solution.py:407
  74.0 1.3 copy-done
  75.3 6.3 %local_window.1.refs_4_ = f32[1024,128]{1,0:T(8,128)} custom-call(s32[1]{0:T(128)} %bitcast.9.ctx_ref, bf16[128,1024]{1,0:T(8,128)(2,1)} %copy-done.17, bf16[2,128,1024]{2,1,0:T(8,128)(2,1)} %collective-permute-done.16.k0_ref.v0_ref, bf16[128,1024]{1,0:T(8,128)(2,1)} %k1_ref.1, bf16[2,128,1024]{2,1,0:T(8,128)(2,1)} %collective-permute-done.16.k0_ref.v0_ref, ...), custom_call_target="tpu_custom_call" | custom-call | flops 134217728 | bytes 2097152 | tf_op jit(solution)/shard_map/local_window/pallas_call | solution.py:365
  81.5 1.0 constant_dynamic-update-slice_fusion.3
  82.5 1.0 constant_dynamic-update-slice_fusion.2
  83.5 1.0 constant_dynamic-update-slice_fusion.1
  84.5 1.0 constant_dynamic-update-slice_fusion.q_ref
  85.4 11.1 %near_tiles.3 = (f32[1024,512]{1,0:T(8,128)S(1)}, f32[8,8,512]{2,1,0:T(8,128)S(1)}) custom-call(s32[1]{0:T(128)} %bitcast.me_ref.m_ref, bf16[512,1024]{1,0:T(8,128)(2,1)S(1)} %constant_dynamic-update-slice_fusion.q_ref, bf16[512,4096]{1,0:T(8,128)(2,1)} %k0_ref.3, bf16[512,4096]{1,0:T(8,128)(2,1)} %v0_ref.3, ...), custom_call_target="tpu_custom_call" | custom-call | flops 2147483648 | bytes 8388608 | tf_op jit(solution)/shard_map/near_tiles/pallas_call | solution.py:407
  96.7 2.3 %collective-permute-done.17.k3_ref.v3_ref = bf16[2,512,384]{2,1,0:T(8,128)(2,1)S(1)} collective-permute-done((bf16[2,512,384]{2,1,0:T(8,128)(2,1)S(1)}, bf16[2,512,384]{2,1,0:T(8,128)(2,1)S(1)}, u32[]{:S(2)}, u32[]{:S(2)}) %collective-permute-start.17) | collective-permute-done | bytes 786464 | tf_op jit(solution)/shard_map/ppermute | solution.py:28
  99.0 3.5 %far_tiles.7 = bf16[4,416,128]{2,1,0:T(8,128)(2,1)S(1)} custom-call(bf16[512,1024]{1,0:T(8,128)(2,1)S(1)} %constant_dynamic-update-slice_fusion.q_ref, bf16[2,2,512,384]{3,2,1,0:T(8,128)(2,1)S(1)} %collective-permute-done.12.k2_ref.v2_ref, bf16[2,2,512,384]{3,2,1,0:T(8,128)(2,1)S(1)} %collective-permute-done.12.k2_ref.v2_ref, ...), custom_call_target="tpu_custom_call" | custom-call | flops 805306368 | bytes 3145728 | tf_op jit(solution)/shard_map/far_tiles/pallas_call | solution.py:463
  102.4 3.5 %far_tiles.6.a_ref = bf16[4,416,128]{2,1,0:T(8,128)(2,1)S(1)} custom-call(bf16[512,1024]{1,0:T(8,128)(2,1)S(1)} %copy-done.7, bf16[2,2,512,384]{3,2,1,0:T(8,128)(2,1)S(1)} %collective-permute-done.12.k2_ref.v2_ref, bf16[2,2,512,384]{3,2,1,0:T(8,128)(2,1)S(1)} %collective-permute-done.12.k2_ref.v2_ref, ...), custom_call_target="tpu_custom_call" | custom-call | flops 805306368 | bytes 3145728 | tf_op jit(solution)/shard_map/far_tiles/pallas_call | solution.py:463
  106.2 1.6 collective-permute-start.19
  107.8 1.1 collective-permute-start.18
  108.9 4.2 %far_tiles.9 = bf16[4,416,128]{2,1,0:T(8,128)(2,1)} custom-call(bf16[512,1024]{1,0:T(8,128)(2,1)S(1)} %constant_dynamic-update-slice_fusion.q_ref, bf16[2,2,512,384]{3,2,1,0:T(8,128)(2,1)S(1)} %collective-permute-done.20.k2_ref.v2_ref, bf16[2,2,512,384]{3,2,1,0:T(8,128)(2,1)S(1)} %collective-permute-done.20.k2_ref.v2_ref, ...), custom_call_target="tpu_custom_call" | custom-call | flops 805306368 | bytes 3145728 | tf_op jit(solution)/shard_map/far_tiles/pallas_call | solution.py:463
  114.1 6.4 %collective-permute-done.18.b_ref = bf16[4,416,128]{2,1,0:T(8,128)(2,1)S(1)} collective-permute-done((bf16[4,416,128]{2,1,0:T(8,128)(2,1)S(1)}, bf16[4,416,128]{2,1,0:T(8,128)(2,1)S(1)}, u32[]{:S(2)}, u32[]{:S(2)}) %collective-permute-start.18) | collective-permute-done | bytes 426016 | tf_op jit(solution)/shard_map/ppermute | solution.py:28
  121.2 2.0 %merge_pair.3 = (bf16[416,128]{1,0:T(8,128)(2,1)}, bf16[416,128]{1,0:T(8,128)(2,1)}, bf16[416,128]{1,0:T(8,128)(2,1)}, bf16[416,128]{1,0:T(8,128)(2,1)}) custom-call(bf16[4,416,128]{2,1,0:T(8,128)(2,1)} %copy-done.14, bf16[4,416,128]{2,1,0:T(8,128)(2,1)} %copy-done.23), custom_call_target="tpu_custom_call" | custom-call | tf_op jit(solution)/shard_map/merge_pair/pallas_call | solution.py:492
  123.3 3.6 %collective-permute-start.23 = (bf16[416,128]{1,0:T(8,128)(2,1)}, bf16[416,128]{1,0:T(8,128)(2,1)S(1)}, u32[]{:S(2)}, u32[]{:S(2)}) collective-permute-start(bf16[416,128]{1,0:T(8,128)(2,1)} %get-tuple-element.73), channel_id=1, source_target_pairs={{0,24},{4,28},{8,0},{12,4},{16,8},{20,12},{24,16},{28,20},{1,25},{... | collective-permute-start | bytes 319496 | tf_op jit(solution)/shard_map/ppermute | solution.py:33
  126.9 1.8 collective-permute-start.25
  128.7 1.6 copy-done.2
  130.3 1.2 copy-done.8
  131.5 1.1 copy-done.11
  132.6 3.5 %far_tiles.8.a_ref = bf16[4,416,128]{2,1,0:T(8,128)(2,1)S(1)} custom-call(bf16[512,1024]{1,0:T(8,128)(2,1)S(1)} %copy-done.8, bf16[2,2,512,384]{3,2,1,0:T(8,128)(2,1)S(1)} %collective-permute-done.20.k2_ref.v2_ref, bf16[2,2,512,384]{3,2,1,0:T(8,128)(2,1)S(1)} %collective-permute-done.20.k2_ref.v2_ref, bf16[2,512,384]{2,1,0:T(8,128)(2,1)S(1)} %copy-done.11, ...), custom_call_target="tpu_custom_call" | custom-call | flops 805306368 | bytes 3145728 | tf_op jit(solution)/shard_map/far_tiles/pallas_call | solution.py:463
  136.9 2.0 %merge_pair.4 = (bf16[416,128]{1,0:T(8,128)(2,1)}, bf16[416,128]{1,0:T(8,128)(2,1)}, bf16[416,128]{1,0:T(8,128)(2,1)}, bf16[416,128]{1,0:T(8,128)(2,1)}) custom-call(bf16[4,416,128]{2,1,0:T(8,128)(2,1)} %copy-done.15, bf16[4,416,128]{2,1,0:T(8,128)(2,1)} %collective-permute-done.22.b_ref), custom_call_target="tpu_custom_call" | custom-call | tf_op jit(solution)/shard_map/merge_pair/pallas_call | solution.py:492
  139.1 1.9 %collective-permute-done.26.k3_ref.v3_ref = bf16[2,512,256]{2,1,0:T(8,128)(2,1)S(1)} collective-permute-done((bf16[2,512,256]{2,1,0:T(8,128)(2,1)S(1)}, bf16[2,512,256]{2,1,0:T(8,128)(2,1)S(1)}, u32[]{:S(2)}, u32[]{:S(2)}) %collective-permute-start.26) | collective-permute-done | bytes 524320 | tf_op jit(solution)/shard_map/ppermute | solution.py:28
  141.0 1.6 copy-done.5
  142.6 1.2 copy-done.13
  143.8 2.4 %far_tiles.10 = bf16[4,272,128]{2,1,0:T(8,128)(2,1)S(1)} custom-call(bf16[512,1024]{1,0:T(8,128)(2,1)S(1)} %copy-done.13, bf16[2,2,512,256]{3,2,1,0:T(8,128)(2,1)S(1)} %collective-permute-done.19.k2_ref.v2_ref, bf16[2,2,512,256]{3,2,1,0:T(8,128)(2,1)S(1)} %collective-permute-done.19.k2_ref.v2_ref, ...), custom_call_target="tpu_custom_call" | custom-call | flops 536870912 | bytes 3145728 | tf_op jit(solution)/shard_map/far_tiles/pallas_call | solution.py:463
  146.3 2.1 %collective-permute-start.27 = (bf16[416,128]{1,0:T(8,128)(2,1)S(1)}, bf16[416,128]{1,0:T(8,128)(2,1)S(1)}, u32[]{:S(2)}, u32[]{:S(2)}) collective-permute-start(bf16[416,128]{1,0:T(8,128)(2,1)S(1)} %copy-done.38), channel_id=1, source_target_pairs={{0,24},{4,28},{8,0},{12,4},{16,8},{20,12},{24,16},{28,20},{1,25},{... | collective-permute-start | bytes 319496 | tf_op jit(solution)/shard_map/ppermute | solution.py:33
  148.4 1.1 collective-permute-start.28
  149.6 2.5 %far_tiles.11.a_ref = bf16[4,272,128]{2,1,0:T(8,128)(2,1)S(1)} custom-call(bf16[512,1024]{1,0:T(8,128)(2,1)S(1)} %copy-done.9, bf16[2,2,512,256]{3,2,1,0:T(8,128)(2,1)S(1)} %collective-permute-done.19.k2_ref.v2_ref, bf16[2,2,512,256]{3,2,1,0:T(8,128)(2,1)S(1)} %collective-permute-done.19.k2_ref.v2_ref, ...), custom_call_target="tpu_custom_call" | custom-call | flops 536870912 | bytes 3145728 | tf_op jit(solution)/shard_map/far_tiles/pallas_call | solution.py:463
  152.7 2.3 %collective-permute-done.30.b_ref = bf16[4,272,128]{2,1,0:T(8,128)(2,1)S(1)} collective-permute-done((bf16[4,272,128]{2,1,0:T(8,128)(2,1)S(1)}, bf16[4,272,128]{2,1,0:T(8,128)(2,1)S(1)}, u32[]{:S(2)}, u32[]{:S(2)}) %collective-permute-start.30) | collective-permute-done | bytes 278560 | tf_op jit(solution)/shard_map/ppermute | solution.py:28
  155.7 1.8 merge_pair.5
  157.6 2.0 %collective-permute-start.31 = (bf16[272,128]{1,0:T(8,128)(2,1)}, bf16[272,128]{1,0:T(8,128)(2,1)S(1)}, u32[]{:S(2)}, u32[]{:S(2)}) collective-permute-start(bf16[272,128]{1,0:T(8,128)(2,1)} %get-tuple-element.84), channel_id=1, source_target_pairs={{0,24},{4,28},{8,0},{12,4},{16,8},{20,12},{24,16},{28,20},{1,25},{... | collective-permute-start | bytes 208904 | tf_op jit(solution)/shard_map/ppermute | solution.py:33
  159.6 1.1 collective-permute-start.32
  161.4 2.0 %merge_all.3 = bf16[384,128]{1,0:T(8,128)(2,1)} custom-call(bf16[416,128]{1,0:T(8,128)(2,1)} %get-tuple-element.78.refs_0_, bf16[416,128]{1,0:T(8,128)(2,1)} %copy-done.27, bf16[416,128]{1,0:T(8,128)(2,1)} %collective-permute-done.24.refs_2_, bf16[416,128]{1,0:T(8,128)(2,1)} %collective-permute-done.25.refs_3_, f32[1024,128]{1,0:T(8,128)} %local_window.1.refs_4_, ...), custom_call_target="tpu_custom_call" | custom-call | tf_op jit(solution)/shard_map/merge_all/pallas_call | solution.py:507
  164.7 2.0 %merge_all.4 = bf16[384,128]{1,0:T(8,128)(2,1)} custom-call(bf16[416,128]{1,0:T(8,128)(2,1)} %get-tuple-element.79.refs_0_, bf16[416,128]{1,0:T(8,128)(2,1)} %copy-done.28, bf16[416,128]{1,0:T(8,128)(2,1)} %copy-done.29, bf16[416,128]{1,0:T(8,128)(2,1)} %copy-done.30, f32[1024,128]{1,0:T(8,128)} %local_window.1.refs_4_, f32[16,128]{1,0:T(8,128)} %broadcast_in_dim.20.refs_5_), custom_call_target="tpu_custom_call" | custom-call | tf_op jit(solution)/shard_map/merge_all/pallas_call | solution.py:507
  167.8 1.9 %merge_all.5 = bf16[256,128]{1,0:T(8,128)(2,1)} custom-call(bf16[272,128]{1,0:T(8,128)(2,1)} %get-tuple-element.83.refs_0_, bf16[272,128]{1,0:T(8,128)(2,1)} %copy-done.31, bf16[272,128]{1,0:T(8,128)(2,1)} %copy-done.32, bf16[272,128]{1,0:T(8,128)(2,1)} %copy-done.33, f32[1024,128]{1,0:T(8,128)} %local_window.1.refs_4_, f32[16,128]{1,0:T(8,128)} %broadcast_in_dim.20.refs_5_), custom_call_target="tpu_custom_call" | custom-call | tf_op jit(solution)/shard_map/merge_all/pallas_call | solution.py:507
  169.7 2.2 %fusion.8 = bf16[128,1024]{1,0:T(8,128)(2,1)S(1)} fusion(bf16[1024,4096]{1,0:T(8,128)(2,1)} %param.19, s32[]{:T(128)S(6)} %select_n.44, bf16[256,128]{1,0:T(8,128)(2,1)} %merge_all.5, bf16[384,128]{1,0:T(8,128)(2,1)} %merge_all.4, bf16[384,128]{1,0:T(8,128)(2,1)} %merge_all.3), kind=kOutput, calls=%fused_computation.8 | convolution fusion | flops 269352960 | bytes 2621444 | tf_op jit(solution)/shard_map/dot_general | solution.py:517
  172.0 2.1 %fusion.11 = bf16[128,1024]{1,0:T(8,128)(2,1)S(1)} fusion(bf16[1024,4096]{1,0:T(8,128)(2,1)} %param.19, s32[]{:T(128)S(6)} %select_n.46, bf16[256,128]{1,0:T(8,128)(2,1)S(1)} %copy-done.22, bf16[384,128]{1,0:T(8,128)(2,1)S(1)} %copy-done.19, bf16[384,128]{1,0:T(8,128)(2,1)S(1)} %copy-done.18), kind=kOutput, calls=%fused_computation.9 | convolution fusion | flops 269352960 | bytes 2621444 | tf_op jit(solution)/shard_map/dot_general | solution.py:517
  174.7 2.1 %fusion.4 = f32[128,1024]{1,0:T(8,128)S(1)} fusion(bf16[1024,128]{1,0:T(8,128)(2,1)S(1)} %pad_maximum_fusion.2, bf16[1024,4096]{1,0:T(8,128)(2,1)} %param.19, s32[]{:T(128)S(6)} %select_n.45), kind=kOutput, calls=%fused_computation.4 | convolution fusion | flops 268435456 | bytes 2883588 | tf_op jit(solution)/shard_map/dot_general | solution.py:517
  176.9 1.7 collective-permute-start.36
  178.6 2.1 %fusion = f32[128,1024]{1,0:T(8,128)S(1)} fusion(bf16[1024,128]{1,0:T(8,128)(2,1)S(1)} %pad_maximum_fusion.2, bf16[1024,4096]{1,0:T(8,128)(2,1)} %param.19, s32[]{:T(128)S(6)} %select_n.43), kind=kOutput, calls=%fused_computation | convolution fusion | flops 268435456 | bytes 2883588 | tf_op jit(solution)/shard_map/dot_general | solution.py:517
  180.7 4.5 %collective-permute-done.36 = bf16[128,1024]{1,0:T(8,128)(2,1)S(1)} collective-permute-done((bf16[128,1024]{1,0:T(8,128)(2,1)S(1)}, bf16[128,1024]{1,0:T(8,128)(2,1)S(1)}, u32[]{:S(2)}, u32[]{:S(2)}) %collective-permute-start.36) | collective-permute-done | bytes 262176 | tf_op jit(solution)/shard_map/ppermute | solution.py:28
  (134 shorter events, 13.1 us)
Async XLA Ops:
  0.0 6.5 %copy-start.34 = (s32[128,16]{0,1:T(8,128)S(1)}, s32[128,16]{0,1:T(8,128)}, u32[]{:S(2)}) copy-start(s32[128,16]{0,1:T(8,128)} %param.16) | copy-start | bytes 24580
  0.0 6.5 %copy-start.35 = (s32[128]{0:T(128)S(1)}, s32[128]{0:T(128)}, u32[]{:S(2)}) copy-start(s32[128]{0:T(128)} %param.17) | copy-start | bytes 1540
  0.0 9.1 %copy-start.25 = (bf16[128,1024]{1,0:T(8,128)(2,1)S(1)}, bf16[128,1024]{1,0:T(8,128)(2,1)}, u32[]{:S(2)}) copy-start(bf16[128,1024]{1,0:T(8,128)(2,1)} %param.10) | copy-start | bytes 786436
  6.0 21.5 %collective-permute-start.7 = (bf16[2,512,1024]{2,1,0:T(8,128)(2,1)}, bf16[2,512,1024]{2,1,0:T(8,128)(2,1)}, u32[]{:S(2)}, u32[]{:S(2)}) collective-permute-start(bf16[2,512,1024]{2,1,0:T(8,128)(2,1)} %get-tuple-element.48), channel_id=1, source_target_pairs={{0,1},{1,0},{2,3},{3,2},{4,5},{5,4},{6,7},{7,6},{8,9},{9,8},{10,11... | collective-permute-start | bytes 6291464 | tf_op jit(solution)/shard_map/ppermute | solution.py:28
  6.5 4.2 %collective-permute-start.3 = (s32[16,128]{1,0:T(8,128)S(1)}, s32[16,128]{1,0:T(8,128)S(1)}, u32[]{:S(2)}, u32[]{:S(2)}) collective-permute-start(s32[16,128]{1,0:T(8,128)S(1)} %get-tuple-element.92), channel_id=1, source_target_pairs={{0,4},{4,0},{8,12},{12,8},{16,20},{20,16},{24,28},{28,24},{1,5},{5... | collective-permute-start | bytes 24584 | tf_op jit(solution)/shard_map/ppermute | solution.py:28
  9.1 12.6 %collective-permute-start.1 = (bf16[128,1024]{1,0:T(8,128)(2,1)S(1)}, bf16[128,1024]{1,0:T(8,128)(2,1)}, u32[]{:S(2)}, u32[]{:S(2)}) collective-permute-start(bf16[128,1024]{1,0:T(8,128)(2,1)S(1)} %copy-done.25), channel_id=1, source_target_pairs={{0,2},{1,3},{2,0},{3,1},{4,6},{5,7},{6,4},{7,5},{8,10},{9,11},{10,... | collective-permute-start | bytes 786440 | tf_op jit(solution)/shard_map/ppermute | solution.py:28
  10.7 4.8 %collective-permute-start.5 = (s32[2,16,128]{2,1,0:T(8,128)S(1)}, s32[2,16,128]{2,1,0:T(8,128)S(1)}, u32[]{:S(2)}, u32[]{:S(2)}) collective-permute-start(s32[2,16,128]{2,1,0:T(8,128)S(1)} %get-tuple-element.90), channel_id=1, source_target_pairs={{0,16},{4,20},{8,24},{12,28},{16,0},{20,4},{24,8},{28,12},{1,17},{... | collective-permute-start | bytes 49160 | tf_op jit(solution)/shard_map/ppermute | solution.py:33
  13.8 7.9 %collective-permute-start = (bf16[128,1024]{1,0:T(8,128)(2,1)S(1)}, bf16[128,1024]{1,0:T(8,128)(2,1)}, u32[]{:S(2)}, u32[]{:S(2)}) collective-permute-start(bf16[128,1024]{1,0:T(8,128)(2,1)S(1)} %copy-done.25), channel_id=1, source_target_pairs={{0,1},{1,0},{2,3},{3,2},{4,5},{5,4},{6,7},{7,6},{8,9},{9,8},{10,11... | collective-permute-start | bytes 786440 | tf_op jit(solution)/shard_map/ppermute | solution.py:28
  13.8 7.7 %collective-permute-start.4 = (s32[2,16,128]{2,1,0:T(8,128)S(1)}, s32[2,16,128]{2,1,0:T(8,128)S(1)}, u32[]{:S(2)}, u32[]{:S(2)}) collective-permute-start(s32[2,16,128]{2,1,0:T(8,128)S(1)} %get-tuple-element.90), channel_id=1, source_target_pairs={{0,8},{4,12},{8,16},{12,20},{16,24},{20,28},{24,0},{28,4},{1,9},{5... | collective-permute-start | bytes 49160 | tf_op jit(solution)/shard_map/ppermute | solution.py:33
  15.5 6.0 %collective-permute-start.6 = (s32[2,16,128]{2,1,0:T(8,128)S(1)}, s32[2,16,128]{2,1,0:T(8,128)S(1)}, u32[]{:S(2)}, u32[]{:S(2)}) collective-permute-start(s32[2,16,128]{2,1,0:T(8,128)S(1)} %get-tuple-element.90), channel_id=1, source_target_pairs={{0,24},{4,28},{8,0},{12,4},{16,8},{20,12},{24,16},{28,20},{1,25},{... | collective-permute-start | bytes 49160 | tf_op jit(solution)/shard_map/ppermute | solution.py:33
  21.7 5.0 %collective-permute-start.2 = (bf16[128,1024]{1,0:T(8,128)(2,1)}, bf16[128,1024]{1,0:T(8,128)(2,1)S(1)}, u32[]{:S(2)}, u32[]{:S(2)}) collective-permute-start(bf16[128,1024]{1,0:T(8,128)(2,1)} %collective-permute-done.1), channel_id=1, source_target_pairs={{0,1},{1,0},{2,3},{3,2},{4,5},{5,4},{6,7},{7,6},{8,9},{9,8},{10,11... | collective-permute-start | bytes 786440 | tf_op jit(solution)/shard_map/ppermute | solution.py:28
  21.8 41.1 %collective-permute-start.12 = (bf16[2,2,512,384]{3,2,1,0:T(8,128)(2,1)S(1)}, bf16[2,2,512,384]{3,2,1,0:T(8,128)(2,1)S(1)}, u32[]{:S(2)}, u32[]{:S(2)}) collective-permute-start(bf16[2,2,512,384]{3,2,1,0:T(8,128)(2,1)S(1)} %get-tuple-element.51), channel_id=1, source_target_pairs={{0,2},{1,3},{2,0},{3,1},{4,6},{5,7},{6,4},{7,5},{8,10},{9,11},{10,... | collective-permute-start | bytes 4718600 | tf_op jit(solution)/shard_map/ppermute | solution.py:28
  27.5 23.2 %copy-start.20 = (bf16[128,1024]{1,0:T(8,128)(2,1)S(1)}, bf16[128,1024]{1,0:T(8,128)(2,1)}, u32[]{:S(2)}) copy-start(bf16[128,1024]{1,0:T(8,128)(2,1)} %v1_ref.1) | copy-start | bytes 786436
  27.5 23.2 %copy-start.21 = (bf16[128,1024]{1,0:T(8,128)(2,1)S(1)}, bf16[128,1024]{1,0:T(8,128)(2,1)}, u32[]{:S(2)}) copy-start(bf16[128,1024]{1,0:T(8,128)(2,1)} %k1_ref.1) | copy-start | bytes 786436
  32.5 30.3 %copy-start.17 = (bf16[128,1024]{1,0:T(8,128)(2,1)}, bf16[128,1024]{1,0:T(8,128)(2,1)S(1)}, u32[]{:S(2)}) copy-start(bf16[128,1024]{1,0:T(8,128)(2,1)S(1)} %convolution_convert_fusion.q_ref) | copy-start | bytes 786436
  32.5 8.5 %collective-permute-start.9 = (bf16[128,1024]{1,0:T(8,128)(2,1)S(1)}, bf16[128,1024]{1,0:T(8,128)(2,1)S(1)}, u32[]{:S(2)}, u32[]{:S(2)}) collective-permute-start(bf16[128,1024]{1,0:T(8,128)(2,1)S(1)} %convolution_convert_fusion.q_ref), channel_id=1, source_target_pairs={{0,4},{4,0},{8,12},{12,8},{16,20},{20,16},{24,28},{28,24},{1,5},{5... | collective-permute-start | bytes 786440 | tf_op jit(solution)/shard_map/ppermute | solution.py:28
  34.1 10.4 %collective-permute-start.11 = (bf16[128,1024]{1,0:T(8,128)(2,1)S(1)}, bf16[128,1024]{1,0:T(8,128)(2,1)}, u32[]{:S(2)}, u32[]{:S(2)}) collective-permute-start(bf16[128,1024]{1,0:T(8,128)(2,1)S(1)} %convolution_convert_fusion.q_ref), channel_id=1, source_target_pairs={{0,24},{4,28},{8,0},{12,4},{16,8},{20,12},{24,16},{28,20},{1,25},{... | collective-permute-start | bytes 786440 | tf_op jit(solution)/shard_map/ppermute | solution.py:33
  37.8 12.9 %collective-permute-start.8 = (bf16[128,1024]{1,0:T(8,128)(2,1)S(1)}, bf16[128,1024]{1,0:T(8,128)(2,1)}, u32[]{:S(2)}, u32[]{:S(2)}) collective-permute-start(bf16[128,1024]{1,0:T(8,128)(2,1)S(1)} %convolution_convert_fusion.q_ref), channel_id=1, source_target_pairs={{0,8},{4,12},{8,16},{12,20},{16,24},{20,28},{24,0},{28,4},{1,9},{5... | collective-permute-start | bytes 786440 | tf_op jit(solution)/shard_map/ppermute | solution.py:33
  41.0 9.7 %copy-start.26 = (bf16[128,1024]{1,0:T(8,128)(2,1)}, bf16[128,1024]{1,0:T(8,128)(2,1)S(1)}, u32[]{:S(2)}) copy-start(bf16[128,1024]{1,0:T(8,128)(2,1)S(1)} %collective-permute-done.9) | copy-start | bytes 786436
  41.0 19.7 %collective-permute-start.10 = (bf16[128,1024]{1,0:T(8,128)(2,1)S(1)}, bf16[128,1024]{1,0:T(8,128)(2,1)}, u32[]{:S(2)}, u32[]{:S(2)}) collective-permute-start(bf16[128,1024]{1,0:T(8,128)(2,1)S(1)} %convolution_convert_fusion.q_ref), channel_id=1, source_target_pairs={{0,16},{4,20},{8,24},{12,28},{16,0},{20,4},{24,8},{28,12},{1,17},{... | collective-permute-start | bytes 786440 | tf_op jit(solution)/shard_map/ppermute | solution.py:33
  50.8 24.5 %collective-permute-start.16 = (bf16[2,128,1024]{2,1,0:T(8,128)(2,1)S(1)}, bf16[2,128,1024]{2,1,0:T(8,128)(2,1)}, u32[]{:S(2)}, u32[]{:S(2)}) collective-permute-start(bf16[2,128,1024]{2,1,0:T(8,128)(2,1)S(1)} %pad_maximum_fusion.1), channel_id=1, source_target_pairs={{0,4},{4,8},{8,12},{12,16},{16,20},{20,24},{24,28},{1,5},{5,9},{9,... | collective-permute-start | bytes 1572872 | tf_op jit(solution)/shard_map/ppermute | solution.py:39
  54.0 27.5 %collective-permute-start.15 = (bf16[128,1024]{1,0:T(8,128)(2,1)}, bf16[128,1024]{1,0:T(8,128)(2,1)}, u32[]{:S(2)}, u32[]{:S(2)}) collective-permute-start(bf16[128,1024]{1,0:T(8,128)(2,1)} %collective-permute-done.11), channel_id=1, source_target_pairs={{0,4},{4,0},{8,12},{12,8},{16,20},{20,16},{24,28},{28,24},{1,5},{5... | collective-permute-start | bytes 786440 | tf_op jit(solution)/shard_map/ppermute | solution.py:28
  56.2 25.3 %collective-permute-start.13 = (bf16[128,1024]{1,0:T(8,128)(2,1)}, bf16[128,1024]{1,0:T(8,128)(2,1)}, u32[]{:S(2)}, u32[]{:S(2)}) collective-permute-start(bf16[128,1024]{1,0:T(8,128)(2,1)} %collective-permute-done.8), channel_id=1, source_target_pairs={{0,4},{4,0},{8,12},{12,8},{16,20},{20,16},{24,28},{28,24},{1,5},{5... | collective-permute-start | bytes 786440 | tf_op jit(solution)/shard_map/ppermute | solution.py:28
  60.7 20.8 %collective-permute-start.14 = (bf16[128,1024]{1,0:T(8,128)(2,1)}, bf16[128,1024]{1,0:T(8,128)(2,1)}, u32[]{:S(2)}, u32[]{:S(2)}) collective-permute-start(bf16[128,1024]{1,0:T(8,128)(2,1)} %collective-permute-done.10), channel_id=1, source_target_pairs={{0,4},{4,0},{8,12},{12,8},{16,20},{20,16},{24,28},{28,24},{1,5},{5... | collective-permute-start | bytes 786440 | tf_op jit(solution)/shard_map/ppermute | solution.py:28
  62.8 11.1 %copy-start.6 = (bf16[512,1024]{1,0:T(8,128)(2,1)}, bf16[512,1024]{1,0:T(8,128)(2,1)S(1)}, u32[]{:S(2)}) copy-start(bf16[512,1024]{1,0:T(8,128)(2,1)S(1)} %pad_maximum_fusion.q_ref) | copy-start | bytes 3145732
  62.9 43.1 %collective-permute-start.20 = (bf16[2,2,512,384]{3,2,1,0:T(8,128)(2,1)}, bf16[2,2,512,384]{3,2,1,0:T(8,128)(2,1)S(1)}, u32[]{:S(2)}, u32[]{:S(2)}) collective-permute-start(bf16[2,2,512,384]{3,2,1,0:T(8,128)(2,1)} %get-tuple-element.70), channel_id=1, source_target_pairs={{0,2},{1,3},{2,0},{3,1},{4,6},{5,7},{6,4},{7,5},{8,10},{9,11},{10,... | collective-permute-start | bytes 4718600 | tf_op jit(solution)/shard_map/ppermute | solution.py:28
  85.4 23.5 %copy-start.12 = (bf16[512,1024]{1,0:T(8,128)(2,1)}, bf16[512,1024]{1,0:T(8,128)(2,1)S(1)}, u32[]{:S(2)}) copy-start(bf16[512,1024]{1,0:T(8,128)(2,1)S(1)} %constant_dynamic-update-slice_fusion.q_ref) | copy-start | bytes 3145732
  96.5 12.4 %copy-start.4 = (f32[1024,512]{1,0:T(8,128)}, f32[1024,512]{1,0:T(8,128)S(1)}, u32[]{:S(2)}) copy-start(f32[1024,512]{1,0:T(8,128)S(1)} %get-tuple-element.65.acc_ref) | copy-start | bytes 6291460
  96.6 2.4 %collective-permute-start.17 = (bf16[2,512,384]{2,1,0:T(8,128)(2,1)S(1)}, bf16[2,512,384]{2,1,0:T(8,128)(2,1)S(1)}, u32[]{:S(2)}, u32[]{:S(2)}) collective-permute-start(bf16[2,512,384]{2,1,0:T(8,128)(2,1)S(1)} %slice_bitcast_fusion.1), channel_id=1, source_target_pairs={{0,1},{1,0},{2,3},{3,2},{4,5},{5,4},{6,7},{7,6},{8,9},{9,8},{10,11... | collective-permute-start | bytes 2359304 | tf_op jit(solution)/shard_map/ppermute | solution.py:28
  99.0 3.5 %copy-start.1 = (f32[1024,512]{1,0:T(8,128)S(1)}, f32[1024,512]{1,0:T(8,128)}, u32[]{:S(2)}) copy-start(f32[1024,512]{1,0:T(8,128)} %copy-done) | copy-start | bytes 6291460
  99.0 3.5 %copy-start.7 = (bf16[512,1024]{1,0:T(8,128)(2,1)S(1)}, bf16[512,1024]{1,0:T(8,128)(2,1)}, u32[]{:S(2)}) copy-start(bf16[512,1024]{1,0:T(8,128)(2,1)} %copy-done.6) | copy-start | bytes 3145732
  105.9 7.3 %copy-start.14 = (bf16[4,416,128]{2,1,0:T(8,128)(2,1)}, bf16[4,416,128]{2,1,0:T(8,128)(2,1)S(1)}, u32[]{:S(2)}) copy-start(bf16[4,416,128]{2,1,0:T(8,128)(2,1)S(1)} %far_tiles.6.a_ref) | copy-start | bytes 1277956
  106.0 2.9 %collective-permute-start.21 = (bf16[2,512,384]{2,1,0:T(8,128)(2,1)S(1)}, bf16[2,512,384]{2,1,0:T(8,128)(2,1)S(1)}, u32[]{:S(2)}, u32[]{:S(2)}) collective-permute-start(bf16[2,512,384]{2,1,0:T(8,128)(2,1)S(1)} %slice_bitcast_fusion), channel_id=1, source_target_pairs={{0,1},{1,0},{2,3},{3,2},{4,5},{5,4},{6,7},{7,6},{8,9},{9,8},{10,11... | collective-permute-start | bytes 2359304 | tf_op jit(solution)/shard_map/ppermute | solution.py:28
  106.2 32.7 %collective-permute-start.19 = (bf16[2,2,512,256]{3,2,1,0:T(8,128)(2,1)}, bf16[2,2,512,256]{3,2,1,0:T(8,128)(2,1)S(1)}, u32[]{:S(2)}, u32[]{:S(2)}) collective-permute-start(bf16[2,2,512,256]{3,2,1,0:T(8,128)(2,1)} %get-tuple-element.68), channel_id=1, source_target_pairs={{0,2},{1,3},{2,0},{3,1},{4,6},{5,7},{6,4},{7,5},{8,10},{9,11},{10,... | collective-permute-start | bytes 3145736 | tf_op jit(solution)/shard_map/ppermute | solution.py:28
  107.8 12.7 %collective-permute-start.18 = (bf16[4,416,128]{2,1,0:T(8,128)(2,1)S(1)}, bf16[4,416,128]{2,1,0:T(8,128)(2,1)S(1)}, u32[]{:S(2)}, u32[]{:S(2)}) collective-permute-start(bf16[4,416,128]{2,1,0:T(8,128)(2,1)S(1)} %far_tiles.7), channel_id=1, source_target_pairs={{0,4},{4,0},{8,12},{12,8},{16,20},{20,16},{24,28},{28,24},{1,5},{5... | collective-permute-start | bytes 1277960 | tf_op jit(solution)/shard_map/ppermute | solution.py:28
  108.9 4.3 %copy-start.10 = (bf16[2,512,384]{2,1,0:T(8,128)(2,1)}, bf16[2,512,384]{2,1,0:T(8,128)(2,1)S(1)}, u32[]{:S(2)}) copy-start(bf16[2,512,384]{2,1,0:T(8,128)(2,1)S(1)} %collective-permute-done.21.k3_ref.v3_ref) | copy-start | bytes 2359300
  113.2 23.7 %collective-permute-start.22 = (bf16[4,416,128]{2,1,0:T(8,128)(2,1)}, bf16[4,416,128]{2,1,0:T(8,128)(2,1)}, u32[]{:S(2)}, u32[]{:S(2)}) collective-permute-start(bf16[4,416,128]{2,1,0:T(8,128)(2,1)} %far_tiles.9), channel_id=1, source_target_pairs={{0,4},{4,0},{8,12},{12,8},{16,20},{20,16},{24,28},{28,24},{1,5},{5... | collective-permute-start | bytes 1277960 | tf_op jit(solution)/shard_map/ppermute | solution.py:28
  123.3 15.7 %collective-permute-start.23 = (bf16[416,128]{1,0:T(8,128)(2,1)}, bf16[416,128]{1,0:T(8,128)(2,1)S(1)}, u32[]{:S(2)}, u32[]{:S(2)}) collective-permute-start(bf16[416,128]{1,0:T(8,128)(2,1)} %get-tuple-element.73), channel_id=1, source_target_pairs={{0,24},{4,28},{8,0},{12,4},{16,8},{20,12},{24,16},{28,20},{1,25},{... | collective-permute-start | bytes 319496 | tf_op jit(solution)/shard_map/ppermute | solution.py:33
  126.9 12.1 %collective-permute-start.24 = (bf16[416,128]{1,0:T(8,128)(2,1)}, bf16[416,128]{1,0:T(8,128)(2,1)}, u32[]{:S(2)}, u32[]{:S(2)}) collective-permute-start(bf16[416,128]{1,0:T(8,128)(2,1)} %get-tuple-element.74), channel_id=1, source_target_pairs={{0,16},{4,20},{8,24},{12,28},{16,0},{20,4},{24,8},{28,12},{1,17},{... | collective-permute-start | bytes 319496 | tf_op jit(solution)/shard_map/ppermute | solution.py:33
  126.9 12.1 %collective-permute-start.25 = (bf16[416,128]{1,0:T(8,128)(2,1)}, bf16[416,128]{1,0:T(8,128)(2,1)}, u32[]{:S(2)}, u32[]{:S(2)}) collective-permute-start(bf16[416,128]{1,0:T(8,128)(2,1)} %get-tuple-element.75), channel_id=1, source_target_pairs={{0,8},{4,12},{8,16},{12,20},{16,24},{20,28},{24,0},{28,4},{1,9},{5... | collective-permute-start | bytes 319496 | tf_op jit(solution)/shard_map/ppermute | solution.py:33
  128.7 1.6 copy-start.2
  138.9 7.3 %copy-start.27 = (bf16[416,128]{1,0:T(8,128)(2,1)}, bf16[416,128]{1,0:T(8,128)(2,1)S(1)}, u32[]{:S(2)}) copy-start(bf16[416,128]{1,0:T(8,128)(2,1)S(1)} %collective-permute-done.23.refs_1_) | copy-start | bytes 319492
  138.9 10.6 %copy-start.9 = (bf16[512,1024]{1,0:T(8,128)(2,1)S(1)}, bf16[512,1024]{1,0:T(8,128)(2,1)}, u32[]{:S(2)}) copy-start(bf16[512,1024]{1,0:T(8,128)(2,1)} %copy-done.6) | copy-start | bytes 3145732
  139.0 10.6 %copy-start.3 = (f32[1024,512]{1,0:T(8,128)S(1)}, f32[1024,512]{1,0:T(8,128)}, u32[]{:S(2)}) copy-start(f32[1024,512]{1,0:T(8,128)} %copy-done) | copy-start | bytes 6291460
  139.0 2.0 %collective-permute-start.26 = (bf16[2,512,256]{2,1,0:T(8,128)(2,1)S(1)}, bf16[2,512,256]{2,1,0:T(8,128)(2,1)S(1)}, u32[]{:S(2)}, u32[]{:S(2)}) collective-permute-start(bf16[2,512,256]{2,1,0:T(8,128)(2,1)S(1)} %slice_bitcast_fusion.2), channel_id=1, source_target_pairs={{0,1},{1,0},{2,3},{3,2},{4,5},{5,4},{6,7},{7,6},{8,9},{9,8},{10,11... | collective-permute-start | bytes 1572872 | tf_op jit(solution)/shard_map/ppermute | solution.py:28
  141.0 1.6 copy-start.5
  143.8 2.5 %copy-start.38 = (bf16[416,128]{1,0:T(8,128)(2,1)S(1)}, bf16[416,128]{1,0:T(8,128)(2,1)}, u32[]{:S(2)}) copy-start(bf16[416,128]{1,0:T(8,128)(2,1)} %get-tuple-element.80) | copy-start | bytes 319492
  143.8 4.6 %copy-start.37 = (bf16[416,128]{1,0:T(8,128)(2,1)S(1)}, bf16[416,128]{1,0:T(8,128)(2,1)}, u32[]{:S(2)}) copy-start(bf16[416,128]{1,0:T(8,128)(2,1)} %get-tuple-element.81) | copy-start | bytes 319492
  143.8 5.7 %copy-start.36 = (bf16[416,128]{1,0:T(8,128)(2,1)S(1)}, bf16[416,128]{1,0:T(8,128)(2,1)}, u32[]{:S(2)}) copy-start(bf16[416,128]{1,0:T(8,128)(2,1)} %get-tuple-element.82) | copy-start | bytes 319492
  146.3 8.8 %collective-permute-start.30 = (bf16[4,272,128]{2,1,0:T(8,128)(2,1)S(1)}, bf16[4,272,128]{2,1,0:T(8,128)(2,1)S(1)}, u32[]{:S(2)}, u32[]{:S(2)}) collective-permute-start(bf16[4,272,128]{2,1,0:T(8,128)(2,1)S(1)} %far_tiles.10), channel_id=1, source_target_pairs={{0,4},{4,0},{8,12},{12,8},{16,20},{20,16},{24,28},{28,24},{1,5},{5... | collective-permute-start | bytes 835592 | tf_op jit(solution)/shard_map/ppermute | solution.py:28
  146.3 14.4 %collective-permute-start.27 = (bf16[416,128]{1,0:T(8,128)(2,1)S(1)}, bf16[416,128]{1,0:T(8,128)(2,1)S(1)}, u32[]{:S(2)}, u32[]{:S(2)}) collective-permute-start(bf16[416,128]{1,0:T(8,128)(2,1)S(1)} %copy-done.38), channel_id=1, source_target_pairs={{0,24},{4,28},{8,0},{12,4},{16,8},{20,12},{24,16},{28,20},{1,25},{... | collective-permute-start | bytes 319496 | tf_op jit(solution)/shard_map/ppermute | solution.py:33
  148.4 15.0 %collective-permute-start.28 = (bf16[416,128]{1,0:T(8,128)(2,1)S(1)}, bf16[416,128]{1,0:T(8,128)(2,1)S(1)}, u32[]{:S(2)}, u32[]{:S(2)}) collective-permute-start(bf16[416,128]{1,0:T(8,128)(2,1)S(1)} %copy-done.37), channel_id=1, source_target_pairs={{0,16},{4,20},{8,24},{12,28},{16,0},{20,4},{24,8},{28,12},{1,17},{... | collective-permute-start | bytes 319496 | tf_op jit(solution)/shard_map/ppermute | solution.py:33
  149.5 11.2 %copy-start.39 = (f32[16]{0:T(128)S(1)}, f32[16]{0:T(128)}, u32[]{:S(2)}) copy-start(f32[16]{0:T(128)} %param.18) | copy-start | bytes 196
  149.6 13.9 %collective-permute-start.29 = (bf16[416,128]{1,0:T(8,128)(2,1)S(1)}, bf16[416,128]{1,0:T(8,128)(2,1)S(1)}, u32[]{:S(2)}, u32[]{:S(2)}) collective-permute-start(bf16[416,128]{1,0:T(8,128)(2,1)S(1)} %copy-done.36), channel_id=1, source_target_pairs={{0,8},{4,12},{8,16},{12,20},{16,24},{20,28},{24,0},{28,4},{1,9},{5... | collective-permute-start | bytes 319496 | tf_op jit(solution)/shard_map/ppermute | solution.py:33
  157.6 9.2 %collective-permute-start.31 = (bf16[272,128]{1,0:T(8,128)(2,1)}, bf16[272,128]{1,0:T(8,128)(2,1)S(1)}, u32[]{:S(2)}, u32[]{:S(2)}) collective-permute-start(bf16[272,128]{1,0:T(8,128)(2,1)} %get-tuple-element.84), channel_id=1, source_target_pairs={{0,24},{4,28},{8,0},{12,4},{16,8},{20,12},{24,16},{28,20},{1,25},{... | collective-permute-start | bytes 208904 | tf_op jit(solution)/shard_map/ppermute | solution.py:33
  159.6 7.6 %collective-permute-start.32 = (bf16[272,128]{1,0:T(8,128)(2,1)}, bf16[272,128]{1,0:T(8,128)(2,1)S(1)}, u32[]{:S(2)}, u32[]{:S(2)}) collective-permute-start(bf16[272,128]{1,0:T(8,128)(2,1)} %get-tuple-element.85), channel_id=1, source_target_pairs={{0,16},{4,20},{8,24},{12,28},{16,0},{20,4},{24,8},{28,12},{1,17},{... | collective-permute-start | bytes 208904 | tf_op jit(solution)/shard_map/ppermute | solution.py:33
  160.7 2.8 %copy-start.28 = (bf16[416,128]{1,0:T(8,128)(2,1)}, bf16[416,128]{1,0:T(8,128)(2,1)S(1)}, u32[]{:S(2)}) copy-start(bf16[416,128]{1,0:T(8,128)(2,1)S(1)} %collective-permute-done.27.refs_1_) | copy-start | bytes 319492
  160.7 6.5 %collective-permute-start.33 = (bf16[272,128]{1,0:T(8,128)(2,1)}, bf16[272,128]{1,0:T(8,128)(2,1)S(1)}, u32[]{:S(2)}, u32[]{:S(2)}) collective-permute-start(bf16[272,128]{1,0:T(8,128)(2,1)} %get-tuple-element.86), channel_id=1, source_target_pairs={{0,8},{4,12},{8,16},{12,20},{16,24},{20,28},{24,0},{28,4},{1,9},{5... | collective-permute-start | bytes 208904 | tf_op jit(solution)/shard_map/ppermute | solution.py:33
  163.4 8.5 %copy-start.18 = (bf16[384,128]{1,0:T(8,128)(2,1)S(1)}, bf16[384,128]{1,0:T(8,128)(2,1)}, u32[]{:S(2)}) copy-start(bf16[384,128]{1,0:T(8,128)(2,1)} %merge_all.3) | copy-start | bytes 294916
  166.8 5.2 %copy-start.19 = (bf16[384,128]{1,0:T(8,128)(2,1)S(1)}, bf16[384,128]{1,0:T(8,128)(2,1)}, u32[]{:S(2)}) copy-start(bf16[384,128]{1,0:T(8,128)(2,1)} %merge_all.4) | copy-start | bytes 294916
  169.7 2.3 %copy-start.22 = (bf16[256,128]{1,0:T(8,128)(2,1)S(1)}, bf16[256,128]{1,0:T(8,128)(2,1)}, u32[]{:S(2)}) copy-start(bf16[256,128]{1,0:T(8,128)(2,1)} %merge_all.5) | copy-start | bytes 196612
  174.1 2.7 %collective-permute-start.34 = (bf16[128,1024]{1,0:T(8,128)(2,1)S(1)}, bf16[128,1024]{1,0:T(8,128)(2,1)S(1)}, u32[]{:S(2)}, u32[]{:S(2)}) collective-permute-start(bf16[128,1024]{1,0:T(8,128)(2,1)S(1)} %fusion.11), channel_id=1, source_target_pairs={{0,1},{1,0},{2,3},{3,2},{4,5},{5,4},{6,7},{7,6},{8,9},{9,8},{10,11... | collective-permute-start | bytes 786440 | tf_op jit(solution)/shard_map/ppermute | solution.py:28
  174.2 6.5 %collective-permute-start.35 = (bf16[128,1024]{1,0:T(8,128)(2,1)S(1)}, bf16[128,1024]{1,0:T(8,128)(2,1)S(1)}, u32[]{:S(2)}, u32[]{:S(2)}) collective-permute-start(bf16[128,1024]{1,0:T(8,128)(2,1)S(1)} %fusion.8), channel_id=1, source_target_pairs={{0,1},{1,0},{2,3},{3,2},{4,5},{5,4},{6,7},{7,6},{8,9},{9,8},{10,11... | collective-permute-start | bytes 786440 | tf_op jit(solution)/shard_map/ppermute | solution.py:28
  176.9 8.3 %collective-permute-start.36 = (bf16[128,1024]{1,0:T(8,128)(2,1)S(1)}, bf16[128,1024]{1,0:T(8,128)(2,1)S(1)}, u32[]{:S(2)}, u32[]{:S(2)}) collective-permute-start(bf16[128,1024]{1,0:T(8,128)(2,1)S(1)} %add_convert_fusion.1), channel_id=1, source_target_pairs={{0,2},{1,3},{2,0},{3,1},{4,6},{5,7},{6,4},{7,5},{8,10},{9,11},{10,... | collective-permute-start | bytes 786440 | tf_op jit(solution)/shard_map/ppermute | solution.py:28
  (13 other events, 11.0 us)

commit v10 on v7

--- a/solution.py
+++ b/solution.py
@@ -446,7 +446,7 @@
         heads, first = sizes[j], firsts[j]
         wide = heads * DH
         msg_rows = wide + stat_rows(heads)
-        tokens = messages[j - 1] if j >= 1 else [near_state[0][1]]
+        tokens = messages[j - 1] if j >= 1 else [near_state[1][1]]
         if j == chunks - 1:
             tokens = tokens + merges + answers[0]
         far2 = after(crossed[j], *tokens)
@@ -514,10 +514,11 @@
         return lax.dot_general(rows, w, over_rows, preferred_element_type=f32)
 
     away = swap(piece(3, combined).astype(jnp.bfloat16), "mem", 1)
-    away = (piece(2, combined) + away.astype(f32)).astype(jnp.bfloat16)
+    own = piece(1, combined).astype(jnp.bfloat16)
+    away = (piece(2, after(combined, own)) + away.astype(f32)).astype(jnp.bfloat16)
     rest = after(combined, away)
     away = swap(away, "mem", 2)
-    result = piece(0, rest) + swap(piece(1, rest).astype(jnp.bfloat16), "mem", 1).astype(f32)
+    result = piece(0, rest) + swap(own, "mem", 1).astype(f32)
     return (result + away.astype(f32)).astype(jnp.bfloat16)
 
 

time: 179 us -> 174 us (0.972)
  waiting for transfers between devices: 40.4 us -> 34.8 us
    ppermute x21, waiting for transfers between devices: 32.2 us -> 26.6 us  [swap(): lax.ppermute(block, axis, [(i, i ^ distance) for i in range(lax.axis_size...]
  transfers between devices with their start and end apart: 37 -> 37, of which waited for: 10 -> 10; matrix products, arithmetic and copies ran while one was open for 6% -> 7% of each run, Pallas kernels for 31% -> 32%
where the time goes in v10:
time: 174 us; the launch traced here: 173 us
  Pallas kernels  66.4 us (38%)
  starting transfers between devices  41.7 us (24%)
  waiting for transfers between devices  34.8 us (20%)
  local copies, waits for them, and re-layouts  14.2 us (8%)
  matrix products  13.1 us (8%)
  other arithmetic  2.32 us (1%)
    ppermute x21, waiting for transfers between devices, swap(): lax.ppermute(block, axis, [(i, i ^ distance) for i in range(lax.axis_size...  26.6 us
    ppermute x15, starting transfers between devices, turn(): lax.ppermute(block, axis, [(i, (i + distance) % size) for i in range(size)])  22.6 us
    pallas_call x2, Pallas kernels, on_device(): pl.pallas_call(near_kernel, grid_spec=pltpu.PrefetchScalarGridSpec(num_sc...  22.1 us
    pallas_call x6, Pallas kernels, on_device(): pl.pallas_call(far_kernel, grid=(1,), in_specs=[pl.BlockSpec((pl.Element(...  19.6 us
    ppermute x21, starting transfers between devices, swap(): lax.ppermute(block, axis, [(i, i ^ distance) for i in range(lax.axis_size...  14.9 us
    unnamed x75, local copies, waits for them, and re-layouts  12.1 us
    dot_general x4, matrix products, piece(): return lax.dot_general(rows, w, over_rows, preferred_element_type=f32)  8.41 us
    ppermute x15, waiting for transfers between devices, turn(): lax.ppermute(block, axis, [(i, (i + distance) % size) for i in range(size)])  8.22 us
  transfers between devices with their start and end apart: 37, of which 10 were waited for; matrix products, arithmetic and copies ran while one was open for 7% of the time, Pallas kernels for 32%

profile of v10, /device:TPU:0, one launch (start us, length us, event | category | flops | bytes accessed | tf_op | source)
XLA Modules:
  0.0 173.1 jit_solution(10637747472769127230)
XLA Ops:
  0.0 6.4 %share_tiles.1 = (bf16[2,512,1024]{2,1,0:T(8,128)(2,1)}, bf16[2,2,512,384]{3,2,1,0:T(8,128)(2,1)}, bf16[2,2,512,384]{3,2,1,0:T(8,128)(2,1)}, bf16[2,2,512,256]{3,2,1,0:T(8,128)(2,1)}) custom-call(s32[1]{0:T(128)} %bitcast.me_ref.m_ref, bf16[512,4096]{1,0:T(8,128)(2,1)} %k0_ref.3, bf16[512,4096]{1,0:T(8,128)(2,1)} %v0_ref.3), custom_call_target="tpu_custom_call" | custom-call | bytes 14680064 | tf_op jit(solution)/shard_map/share_tiles/pallas_call | solution.py:329
  6.9 2.6 %collective-permute-start.3 = (s32[16,128]{1,0:T(8,128)S(1)}, s32[16,128]{1,0:T(8,128)S(1)}, u32[]{:S(2)}, u32[]{:S(2)}) collective-permute-start(s32[16,128]{1,0:T(8,128)S(1)} %get-tuple-element.88), channel_id=1, source_target_pairs={{0,4},{4,0},{8,12},{12,8},{16,20},{20,16},{24,28},{28,24},{1,5},{5... | collective-permute-start | bytes 24584 | tf_op jit(solution)/shard_map/ppermute | solution.py:28
  9.5 1.5 collective-permute-start.1
  11.2 3.1 %collective-permute-start.5 = (s32[2,16,128]{2,1,0:T(8,128)S(1)}, s32[2,16,128]{2,1,0:T(8,128)S(1)}, u32[]{:S(2)}, u32[]{:S(2)}) collective-permute-start(s32[2,16,128]{2,1,0:T(8,128)S(1)} %get-tuple-element.86), channel_id=1, source_target_pairs={{0,16},{4,20},{8,24},{12,28},{16,0},{20,4},{24,8},{28,12},{1,17},{... | collective-permute-start | bytes 49160 | tf_op jit(solution)/shard_map/ppermute | solution.py:33
  14.3 1.6 collective-permute-start.4
  16.0 4.0 %collective-permute-start.6 = (s32[2,16,128]{2,1,0:T(8,128)S(1)}, s32[2,16,128]{2,1,0:T(8,128)S(1)}, u32[]{:S(2)}, u32[]{:S(2)}) collective-permute-start(s32[2,16,128]{2,1,0:T(8,128)S(1)} %get-tuple-element.86), channel_id=1, source_target_pairs={{0,24},{4,28},{8,0},{12,4},{16,8},{20,12},{24,16},{28,20},{1,25},{... | collective-permute-start | bytes 49160 | tf_op jit(solution)/shard_map/ppermute | solution.py:33
  20.2 4.2 %collective-permute-start.13 = (bf16[2,128,1024]{2,1,0:T(8,128)(2,1)S(1)}, bf16[2,128,1024]{2,1,0:T(8,128)(2,1)}, u32[]{:S(2)}, u32[]{:S(2)}) collective-permute-start(bf16[2,128,1024]{2,1,0:T(8,128)(2,1)S(1)} %pad_maximum_fusion.1), channel_id=1, source_target_pairs={{0,4},{4,8},{8,12},{12,16},{16,20},{20,24},{24,28},{1,5},{5,9},{9,... | collective-permute-start | bytes 1572872 | tf_op jit(solution)/shard_map/ppermute | solution.py:39
  24.6 0.7 copy-done.23
  25.3 1.5 collective-permute-start.12
  26.8 1.0 constant_dynamic-update-slice_fusion.6
  27.9 4.7 %convolution_convert_fusion.q_ref = bf16[128,1024]{1,0:T(8,128)(2,1)S(1)} fusion(bf16[128,4096]{1,0:T(8,128)(2,1)S(1)} %constant_dynamic-update-slice_fusion.4, bf16[4096,1024]{1,0:T(8,128)(2,1)} %param.11), kind=kOutput, calls=%fused_computation.10 | convolution fusion | flops 1073872896 | bytes 9699328 | tf_op jit(solution)/shard_map/dot_general | solution.py:347
  32.7 2.8 %collective-permute-start.11 = (bf16[128,1024]{1,0:T(8,128)(2,1)S(1)}, bf16[128,1024]{1,0:T(8,128)(2,1)}, u32[]{:S(2)}, u32[]{:S(2)}) collective-permute-start(bf16[128,1024]{1,0:T(8,128)(2,1)S(1)} %convolution_convert_fusion.q_ref), channel_id=1, source_target_pairs={{0,24},{4,28},{8,0},{12,4},{16,8},{20,12},{24,16},{28,20},{1,25},{... | collective-permute-start | bytes 786440 | tf_op jit(solution)/shard_map/ppermute | solution.py:33
  35.5 5.6 %collective-permute-done.9 = bf16[128,1024]{1,0:T(8,128)(2,1)S(1)} collective-permute-done((bf16[128,1024]{1,0:T(8,128)(2,1)S(1)}, bf16[128,1024]{1,0:T(8,128)(2,1)S(1)}, u32[]{:S(2)}, u32[]{:S(2)}) %collective-permute-start.9) | collective-permute-done | bytes 262176 | tf_op jit(solution)/shard_map/ppermute | solution.py:28
  41.1 0.7 copy-done.24
  42.3 6.3 %local_window.1.refs_4_ = f32[1024,128]{1,0:T(8,128)} custom-call(s32[1]{0:T(128)} %bitcast.9.ctx_ref, bf16[128,1024]{1,0:T(8,128)(2,1)} %copy-done.15, bf16[2,128,1024]{2,1,0:T(8,128)(2,1)} %collective-permute-done.13.k0_ref.v0_ref, bf16[128,1024]{1,0:T(8,128)(2,1)} %k1_ref.1, bf16[2,128,1024]{2,1,0:T(8,128)(2,1)} %collective-permute-done.13.k0_ref.v0_ref, ...), custom_call_target="tpu_custom_call" | custom-call | flops 134217728 | bytes 2097152 | tf_op jit(solution)/shard_map/local_window/pallas_call | solution.py:363
  48.6 0.8 collective-permute-start.16
  49.4 1.2 collective-permute-start.14
  50.6 8.2 %collective-permute-done.10 = bf16[128,1024]{1,0:T(8,128)(2,1)} collective-permute-done((bf16[128,1024]{1,0:T(8,128)(2,1)S(1)}, bf16[128,1024]{1,0:T(8,128)(2,1)}, u32[]{:S(2)}, u32[]{:S(2)}) %collective-permute-start.10) | collective-permute-done | bytes 262176 | tf_op jit(solution)/shard_map/ppermute | solution.py:33
  59.2 1.3 pad_maximum_fusion.q_ref
  60.5 2.2 %collective-permute-done.12.k2_ref.v2_ref = bf16[2,2,512,384]{3,2,1,0:T(8,128)(2,1)S(1)} collective-permute-done((bf16[2,2,512,384]{3,2,1,0:T(8,128)(2,1)}, bf16[2,2,512,384]{3,2,1,0:T(8,128)(2,1)S(1)}, u32[]{:S(2)}, u32[]{:S(2)}) %collective-permute-start.12) | collective-permute-done | bytes 1572896 | tf_op jit(solution)/shard_map/ppermute | solution.py:28
  62.7 10.5 %near_tiles.2 = (f32[1024,512]{1,0:T(8,128)S(1)}, f32[8,8,512]{2,1,0:T(8,128)S(1)}) custom-call(s32[1]{0:T(128)} %bitcast.me_ref.m_ref, bf16[512,1024]{1,0:T(8,128)(2,1)S(1)} %pad_maximum_fusion.q_ref, bf16[512,4096]{1,0:T(8,128)(2,1)} %k0_ref.3, bf16[512,4096]{1,0:T(8,128)(2,1)} %v0_ref.3, bf16[2,512,1024]{2,1,0:T(8,128)(2,1)} %collective-permute-done.7.k1_ref.v1_ref, ...), custom_call_target="tpu_custom_call" | custom-call | flops 2147483648 | bytes 8388608 | tf_op jit(solution)/shard_map/near_tiles/pallas_call | solution.py:404
  73.5 11.6 %near_tiles.3 = (f32[1024,512]{1,0:T(8,128)S(1)}, f32[8,8,512]{2,1,0:T(8,128)S(1)}) custom-call(s32[1]{0:T(128)} %bitcast.me_ref.m_ref, bf16[512,1024]{1,0:T(8,128)(2,1)S(1)} %constant_dynamic-update-slice_fusion.q_ref, bf16[512,4096]{1,0:T(8,128)(2,1)} %k0_ref.3, bf16[512,4096]{1,0:T(8,128)(2,1)} %v0_ref.3, ...), custom_call_target="tpu_custom_call" | custom-call | flops 2147483648 | bytes 8388608 | tf_op jit(solution)/shard_map/near_tiles/pallas_call | solution.py:404
  85.2 2.3 %collective-permute-done.17.k3_ref.v3_ref = bf16[2,512,384]{2,1,0:T(8,128)(2,1)S(1)} collective-permute-done((bf16[2,512,384]{2,1,0:T(8,128)(2,1)S(1)}, bf16[2,512,384]{2,1,0:T(8,128)(2,1)S(1)}, u32[]{:S(2)}, u32[]{:S(2)}) %collective-permute-start.17) | collective-permute-done | bytes 786464 | tf_op jit(solution)/shard_map/ppermute | solution.py:28
  87.5 3.4 %far_tiles.7 = bf16[4,416,128]{2,1,0:T(8,128)(2,1)S(1)} custom-call(bf16[512,1024]{1,0:T(8,128)(2,1)S(1)} %constant_dynamic-update-slice_fusion.q_ref, bf16[2,2,512,384]{3,2,1,0:T(8,128)(2,1)S(1)} %collective-permute-done.12.k2_ref.v2_ref, bf16[2,2,512,384]{3,2,1,0:T(8,128)(2,1)S(1)} %collective-permute-done.12.k2_ref.v2_ref, ...), custom_call_target="tpu_custom_call" | custom-call | flops 805306368 | bytes 3145728 | tf_op jit(solution)/shard_map/far_tiles/pallas_call | solution.py:460
  90.9 3.4 %far_tiles.6.a_ref = bf16[4,416,128]{2,1,0:T(8,128)(2,1)S(1)} custom-call(bf16[512,1024]{1,0:T(8,128)(2,1)S(1)} %pad_maximum_fusion.q_ref, bf16[2,2,512,384]{3,2,1,0:T(8,128)(2,1)S(1)} %collective-permute-done.12.k2_ref.v2_ref, bf16[2,2,512,384]{3,2,1,0:T(8,128)(2,1)S(1)} %collective-permute-done.12.k2_ref.v2_ref, ...), custom_call_target="tpu_custom_call" | custom-call | flops 805306368 | bytes 3145728 | tf_op jit(solution)/shard_map/far_tiles/pallas_call | solution.py:460
  94.4 1.6 collective-permute-done.20.k2_ref.v2_ref
  96.2 1.6 collective-permute-start.19
  97.8 0.7 collective-permute-done.21.k3_ref.v3_ref
  98.5 4.3 %far_tiles.9 = bf16[4,416,128]{2,1,0:T(8,128)(2,1)} custom-call(bf16[512,1024]{1,0:T(8,128)(2,1)S(1)} %constant_dynamic-update-slice_fusion.q_ref, bf16[2,2,512,384]{3,2,1,0:T(8,128)(2,1)S(1)} %collective-permute-done.20.k2_ref.v2_ref, bf16[2,2,512,384]{3,2,1,0:T(8,128)(2,1)S(1)} %collective-permute-done.20.k2_ref.v2_ref, ...), custom_call_target="tpu_custom_call" | custom-call | flops 805306368 | bytes 3145728 | tf_op jit(solution)/shard_map/far_tiles/pallas_call | solution.py:460
  102.8 1.3 collective-permute-start.22
  104.1 6.4 %collective-permute-done.18.b_ref = bf16[4,416,128]{2,1,0:T(8,128)(2,1)} collective-permute-done((bf16[4,416,128]{2,1,0:T(8,128)(2,1)S(1)}, bf16[4,416,128]{2,1,0:T(8,128)(2,1)}, u32[]{:S(2)}, u32[]{:S(2)}) %collective-permute-start.18) | collective-permute-done | bytes 426016 | tf_op jit(solution)/shard_map/ppermute | solution.py:28
  110.5 2.0 %merge_pair.3 = (bf16[416,128]{1,0:T(8,128)(2,1)}, bf16[416,128]{1,0:T(8,128)(2,1)}, bf16[416,128]{1,0:T(8,128)(2,1)}, bf16[416,128]{1,0:T(8,128)(2,1)}) custom-call(bf16[4,416,128]{2,1,0:T(8,128)(2,1)} %copy-done.10, bf16[4,416,128]{2,1,0:T(8,128)(2,1)} %collective-permute-done.18.b_ref), custom_call_target="tpu_custom_call" | custom-call | tf_op jit(solution)/shard_map/merge_pair/pallas_call | solution.py:489
  112.6 1.1 collective-permute-start.23
  113.7 0.9 collective-permute-start.25
  114.6 1.6 copy-done.1
  116.2 1.2 copy-done.6
  117.4 3.5 %far_tiles.8.a_ref = bf16[4,416,128]{2,1,0:T(8,128)(2,1)S(1)} custom-call(bf16[512,1024]{1,0:T(8,128)(2,1)S(1)} %copy-done.6, bf16[2,2,512,384]{3,2,1,0:T(8,128)(2,1)S(1)} %collective-permute-done.20.k2_ref.v2_ref, bf16[2,2,512,384]{3,2,1,0:T(8,128)(2,1)S(1)} %collective-permute-done.20.k2_ref.v2_ref, ...), custom_call_target="tpu_custom_call" | custom-call | flops 805306368 | bytes 3145728 | tf_op jit(solution)/shard_map/far_tiles/pallas_call | solution.py:460
  120.9 0.7 copy-done.11
  121.7 2.1 %merge_pair.4 = (bf16[416,128]{1,0:T(8,128)(2,1)}, bf16[416,128]{1,0:T(8,128)(2,1)}, bf16[416,128]{1,0:T(8,128)(2,1)}, bf16[416,128]{1,0:T(8,128)(2,1)}) custom-call(bf16[4,416,128]{2,1,0:T(8,128)(2,1)} %copy-done.11, bf16[4,416,128]{2,1,0:T(8,128)(2,1)} %collective-permute-done.22.b_ref), custom_call_target="tpu_custom_call" | custom-call | tf_op jit(solution)/shard_map/merge_pair/pallas_call | solution.py:489
  123.9 1.9 %collective-permute-done.26.k3_ref.v3_ref = bf16[2,512,256]{2,1,0:T(8,128)(2,1)S(1)} collective-permute-done((bf16[2,512,256]{2,1,0:T(8,128)(2,1)S(1)}, bf16[2,512,256]{2,1,0:T(8,128)(2,1)S(1)}, u32[]{:S(2)}, u32[]{:S(2)}) %collective-permute-start.26) | collective-permute-done | bytes 524320 | tf_op jit(solution)/shard_map/ppermute | solution.py:28
  125.8 1.6 copy-done.4
  127.4 1.2 copy-done.9
  128.6 0.9 copy-done.13
  129.5 2.5 %far_tiles.10 = bf16[4,272,128]{2,1,0:T(8,128)(2,1)S(1)} custom-call(bf16[512,1024]{1,0:T(8,128)(2,1)S(1)} %copy-done.9, bf16[2,2,512,256]{3,2,1,0:T(8,128)(2,1)S(1)} %collective-permute-done.19.k2_ref.v2_ref, bf16[2,2,512,256]{3,2,1,0:T(8,128)(2,1)S(1)} %collective-permute-done.19.k2_ref.v2_ref, ...), custom_call_target="tpu_custom_call" | custom-call | flops 536870912 | bytes 3145728 | tf_op jit(solution)/shard_map/far_tiles/pallas_call | solution.py:460
  132.0 1.4 collective-permute-start.30
  133.4 3.3 %collective-permute-start.27 = (bf16[416,128]{1,0:T(8,128)(2,1)}, bf16[416,128]{1,0:T(8,128)(2,1)S(1)}, u32[]{:S(2)}, u32[]{:S(2)}) collective-permute-start(bf16[416,128]{1,0:T(8,128)(2,1)} %get-tuple-element.76), channel_id=1, source_target_pairs={{0,24},{4,28},{8,0},{12,4},{16,8},{20,12},{24,16},{28,20},{1,25},{... | collective-permute-start | bytes 319496 | tf_op jit(solution)/shard_map/ppermute | solution.py:33
  136.6 1.1 collective-permute-start.28
  137.8 2.5 %far_tiles.11.a_ref = bf16[4,272,128]{2,1,0:T(8,128)(2,1)S(1)} custom-call(bf16[512,1024]{1,0:T(8,128)(2,1)S(1)} %copy-done.7, bf16[2,2,512,256]{3,2,1,0:T(8,128)(2,1)S(1)} %collective-permute-done.19.k2_ref.v2_ref, bf16[2,2,512,256]{3,2,1,0:T(8,128)(2,1)S(1)} %collective-permute-done.19.k2_ref.v2_ref, ...), custom_call_target="tpu_custom_call" | custom-call | flops 536870912 | bytes 3145728 | tf_op jit(solution)/shard_map/far_tiles/pallas_call | solution.py:460
  140.3 0.7 copy-done.14
  141.0 0.7 copy-done.21
  141.7 1.8 %merge_pair.5 = (bf16[272,128]{1,0:T(8,128)(2,1)}, bf16[272,128]{1,0:T(8,128)(2,1)}, bf16[272,128]{1,0:T(8,128)(2,1)}, bf16[272,128]{1,0:T(8,128)(2,1)}) custom-call(bf16[4,272,128]{2,1,0:T(8,128)(2,1)} %copy-done.14, bf16[4,272,128]{2,1,0:T(8,128)(2,1)} %copy-done.21), custom_call_target="tpu_custom_call" | custom-call | tf_op jit(solution)/shard_map/merge_pair/pallas_call | solution.py:489
  143.6 3.8 %collective-permute-start.31 = (bf16[272,128]{1,0:T(8,128)(2,1)}, bf16[272,128]{1,0:T(8,128)(2,1)S(1)}, u32[]{:S(2)}, u32[]{:S(2)}) collective-permute-start(bf16[272,128]{1,0:T(8,128)(2,1)} %get-tuple-element.80), channel_id=1, source_target_pairs={{0,24},{4,28},{8,0},{12,4},{16,8},{20,12},{24,16},{28,20},{1,25},{... | collective-permute-start | bytes 208904 | tf_op jit(solution)/shard_map/ppermute | solution.py:33
  147.4 0.9 collective-permute-start.33
  148.3 0.7 broadcast_in_dim.20.refs_5_
  149.0 2.0 %merge_all.3 = bf16[384,128]{1,0:T(8,128)(2,1)} custom-call(bf16[416,128]{1,0:T(8,128)(2,1)} %get-tuple-element.74.refs_0_, bf16[416,128]{1,0:T(8,128)(2,1)} %collective-permute-done.23.refs_1_, bf16[416,128]{1,0:T(8,128)(2,1)} %collective-permute-done.24.refs_2_, bf16[416,128]{1,0:T(8,128)(2,1)} %collective-permute-done.25.refs_3_, ...), custom_call_target="tpu_custom_call" | custom-call | tf_op jit(solution)/shard_map/merge_all/pallas_call | solution.py:504
  151.6 0.6 copy-done.28
  152.3 2.0 %merge_all.4 = bf16[384,128]{1,0:T(8,128)(2,1)} custom-call(bf16[416,128]{1,0:T(8,128)(2,1)} %get-tuple-element.75.refs_0_, bf16[416,128]{1,0:T(8,128)(2,1)} %copy-done.26, bf16[416,128]{1,0:T(8,128)(2,1)} %copy-done.27, bf16[416,128]{1,0:T(8,128)(2,1)} %copy-done.28, f32[1024,128]{1,0:T(8,128)} %local_window.1.refs_4_, f32[16,128]{1,0:T(8,128)} %broadcast_in_dim.20.refs_5_), custom_call_target="tpu_custom_call" | custom-call | tf_op jit(solution)/shard_map/merge_all/pallas_call | solution.py:504
  155.0 1.9 %merge_all.5 = bf16[256,128]{1,0:T(8,128)(2,1)} custom-call(bf16[272,128]{1,0:T(8,128)(2,1)} %get-tuple-element.79.refs_0_, bf16[272,128]{1,0:T(8,128)(2,1)} %copy-done.29, bf16[272,128]{1,0:T(8,128)(2,1)} %copy-done.30, bf16[272,128]{1,0:T(8,128)(2,1)} %copy-done.31, f32[1024,128]{1,0:T(8,128)} %local_window.1.refs_4_, f32[16,128]{1,0:T(8,128)} %broadcast_in_dim.20.refs_5_), custom_call_target="tpu_custom_call" | custom-call | tf_op jit(solution)/shard_map/merge_all/pallas_call | solution.py:504
  156.9 2.2 %fusion.8 = bf16[128,1024]{1,0:T(8,128)(2,1)S(1)} fusion(bf16[1024,4096]{1,0:T(8,128)(2,1)} %param.19, s32[]{:T(128)S(6)} %select_n.44, bf16[256,128]{1,0:T(8,128)(2,1)} %merge_all.5, bf16[384,128]{1,0:T(8,128)(2,1)} %merge_all.4, bf16[384,128]{1,0:T(8,128)(2,1)} %merge_all.3), kind=kOutput, calls=%fused_computation.8 | convolution fusion | flops 269352960 | bytes 2621444 | tf_op jit(solution)/shard_map/dot_general | solution.py:514
  159.2 2.1 %fusion.11 = bf16[128,1024]{1,0:T(8,128)(2,1)S(1)} fusion(bf16[1024,4096]{1,0:T(8,128)(2,1)} %param.19, s32[]{:T(128)S(6)} %select_n.46, bf16[256,128]{1,0:T(8,128)(2,1)S(1)} %copy-done.20, bf16[384,128]{1,0:T(8,128)(2,1)S(1)} %copy-done.17, bf16[384,128]{1,0:T(8,128)(2,1)S(1)} %copy-done.16), kind=kOutput, calls=%fused_computation.9 | convolution fusion | flops 269352960 | bytes 2621444 | tf_op jit(solution)/shard_map/dot_general | solution.py:514
  161.9 2.1 %fusion.4 = f32[128,1024]{1,0:T(8,128)S(1)} fusion(bf16[1024,128]{1,0:T(8,128)(2,1)S(1)} %pad_maximum_fusion.2, bf16[1024,4096]{1,0:T(8,128)(2,1)} %param.19, s32[]{:T(128)S(6)} %select_n.45), kind=kOutput, calls=%fused_computation.4 | convolution fusion | flops 268435456 | bytes 2883588 | tf_op jit(solution)/shard_map/dot_general | solution.py:514
  164.6 2.1 %fusion = f32[128,1024]{1,0:T(8,128)S(1)} fusion(bf16[1024,128]{1,0:T(8,128)(2,1)S(1)} %pad_maximum_fusion.2, bf16[1024,4096]{1,0:T(8,128)(2,1)} %param.19, s32[]{:T(128)S(6)} %select_n.43), kind=kOutput, calls=%fused_computation | convolution fusion | flops 268435456 | bytes 2883588 | tf_op jit(solution)/shard_map/dot_general | solution.py:514
  166.7 5.6 %collective-permute-done.36 = bf16[128,1024]{1,0:T(8,128)(2,1)S(1)} collective-permute-done((bf16[128,1024]{1,0:T(8,128)(2,1)S(1)}, bf16[128,1024]{1,0:T(8,128)(2,1)S(1)}, u32[]{:S(2)}, u32[]{:S(2)}) %collective-permute-start.36) | collective-permute-done | bytes 262176 | tf_op jit(solution)/shard_map/ppermute | solution.py:28
  172.3 0.8 add_convert_fusion
  (126 shorter events, 5.3 us)
Async XLA Ops:
  0.0 6.9 %copy-start.32 = (s32[128,16]{0,1:T(8,128)S(1)}, s32[128,16]{0,1:T(8,128)}, u32[]{:S(2)}) copy-start(s32[128,16]{0,1:T(8,128)} %param.16) | copy-start | bytes 24580
  0.0 6.9 %copy-start.33 = (s32[128]{0:T(128)S(1)}, s32[128]{0:T(128)}, u32[]{:S(2)}) copy-start(s32[128]{0:T(128)} %param.17) | copy-start | bytes 1540
  0.0 9.5 %copy-start.22 = (bf16[128,1024]{1,0:T(8,128)(2,1)S(1)}, bf16[128,1024]{1,0:T(8,128)(2,1)}, u32[]{:S(2)}) copy-start(bf16[128,1024]{1,0:T(8,128)(2,1)} %param.10) | copy-start | bytes 786436
  0.0 14.3 %copy-start.18 = (bf16[128,1024]{1,0:T(8,128)(2,1)S(1)}, bf16[128,1024]{1,0:T(8,128)(2,1)}, u32[]{:S(2)}) copy-start(bf16[128,1024]{1,0:T(8,128)(2,1)} %v1_ref.1) | copy-start | bytes 786436
  0.0 14.3 %copy-start.19 = (bf16[128,1024]{1,0:T(8,128)(2,1)S(1)}, bf16[128,1024]{1,0:T(8,128)(2,1)}, u32[]{:S(2)}) copy-start(bf16[128,1024]{1,0:T(8,128)(2,1)} %k1_ref.1) | copy-start | bytes 786436
  6.5 21.4 %collective-permute-start.7 = (bf16[2,512,1024]{2,1,0:T(8,128)(2,1)}, bf16[2,512,1024]{2,1,0:T(8,128)(2,1)}, u32[]{:S(2)}, u32[]{:S(2)}) collective-permute-start(bf16[2,512,1024]{2,1,0:T(8,128)(2,1)} %get-tuple-element.46), channel_id=1, source_target_pairs={{0,1},{1,0},{2,3},{3,2},{4,5},{5,4},{6,7},{7,6},{8,9},{9,8},{10,11... | collective-permute-start | bytes 6291464 | tf_op jit(solution)/shard_map/ppermute | solution.py:28
  6.9 4.2 %collective-permute-start.3 = (s32[16,128]{1,0:T(8,128)S(1)}, s32[16,128]{1,0:T(8,128)S(1)}, u32[]{:S(2)}, u32[]{:S(2)}) collective-permute-start(s32[16,128]{1,0:T(8,128)S(1)} %get-tuple-element.88), channel_id=1, source_target_pairs={{0,4},{4,0},{8,12},{12,8},{16,20},{20,16},{24,28},{28,24},{1,5},{5... | collective-permute-start | bytes 24584 | tf_op jit(solution)/shard_map/ppermute | solution.py:28
  9.5 15.0 %collective-permute-start.1 = (bf16[128,1024]{1,0:T(8,128)(2,1)S(1)}, bf16[128,1024]{1,0:T(8,128)(2,1)S(1)}, u32[]{:S(2)}, u32[]{:S(2)}) collective-permute-start(bf16[128,1024]{1,0:T(8,128)(2,1)S(1)} %copy-done.22), channel_id=1, source_target_pairs={{0,2},{1,3},{2,0},{3,1},{4,6},{5,7},{6,4},{7,5},{8,10},{9,11},{10,... | collective-permute-start | bytes 786440 | tf_op jit(solution)/shard_map/ppermute | solution.py:28
  11.0 13.6 %collective-permute-start = (bf16[128,1024]{1,0:T(8,128)(2,1)S(1)}, bf16[128,1024]{1,0:T(8,128)(2,1)S(1)}, u32[]{:S(2)}, u32[]{:S(2)}) collective-permute-start(bf16[128,1024]{1,0:T(8,128)(2,1)S(1)} %copy-done.22), channel_id=1, source_target_pairs={{0,1},{1,0},{2,3},{3,2},{4,5},{5,4},{6,7},{7,6},{8,9},{9,8},{10,11... | collective-permute-start | bytes 786440 | tf_op jit(solution)/shard_map/ppermute | solution.py:28
  11.2 4.8 %collective-permute-start.5 = (s32[2,16,128]{2,1,0:T(8,128)S(1)}, s32[2,16,128]{2,1,0:T(8,128)S(1)}, u32[]{:S(2)}, u32[]{:S(2)}) collective-permute-start(s32[2,16,128]{2,1,0:T(8,128)S(1)} %get-tuple-element.86), channel_id=1, source_target_pairs={{0,16},{4,20},{8,24},{12,28},{16,0},{20,4},{24,8},{28,12},{1,17},{... | collective-permute-start | bytes 49160 | tf_op jit(solution)/shard_map/ppermute | solution.py:33
  14.3 5.8 %collective-permute-start.4 = (s32[2,16,128]{2,1,0:T(8,128)S(1)}, s32[2,16,128]{2,1,0:T(8,128)S(1)}, u32[]{:S(2)}, u32[]{:S(2)}) collective-permute-start(s32[2,16,128]{2,1,0:T(8,128)S(1)} %get-tuple-element.86), channel_id=1, source_target_pairs={{0,8},{4,12},{8,16},{12,20},{16,24},{20,28},{24,0},{28,4},{1,9},{5... | collective-permute-start | bytes 49160 | tf_op jit(solution)/shard_map/ppermute | solution.py:33
  16.0 8.4 %collective-permute-start.6 = (s32[2,16,128]{2,1,0:T(8,128)S(1)}, s32[2,16,128]{2,1,0:T(8,128)S(1)}, u32[]{:S(2)}, u32[]{:S(2)}) collective-permute-start(s32[2,16,128]{2,1,0:T(8,128)S(1)} %get-tuple-element.86), channel_id=1, source_target_pairs={{0,24},{4,28},{8,0},{12,4},{16,8},{20,12},{24,16},{28,20},{1,25},{... | collective-permute-start | bytes 49160 | tf_op jit(solution)/shard_map/ppermute | solution.py:33
  20.2 21.6 %collective-permute-start.13 = (bf16[2,128,1024]{2,1,0:T(8,128)(2,1)S(1)}, bf16[2,128,1024]{2,1,0:T(8,128)(2,1)}, u32[]{:S(2)}, u32[]{:S(2)}) collective-permute-start(bf16[2,128,1024]{2,1,0:T(8,128)(2,1)S(1)} %pad_maximum_fusion.1), channel_id=1, source_target_pairs={{0,4},{4,8},{8,12},{12,16},{16,20},{20,24},{24,28},{1,5},{5,9},{9,... | collective-permute-start | bytes 1572872 | tf_op jit(solution)/shard_map/ppermute | solution.py:39
  24.5 3.3 %collective-permute-start.2 = (bf16[128,1024]{1,0:T(8,128)(2,1)S(1)}, bf16[128,1024]{1,0:T(8,128)(2,1)S(1)}, u32[]{:S(2)}, u32[]{:S(2)}) collective-permute-start(bf16[128,1024]{1,0:T(8,128)(2,1)S(1)} %collective-permute-done.1), channel_id=1, source_target_pairs={{0,1},{1,0},{2,3},{3,2},{4,5},{5,4},{6,7},{7,6},{8,9},{9,8},{10,11... | collective-permute-start | bytes 786440 | tf_op jit(solution)/shard_map/ppermute | solution.py:28
  25.3 37.4 %collective-permute-start.12 = (bf16[2,2,512,384]{3,2,1,0:T(8,128)(2,1)}, bf16[2,2,512,384]{3,2,1,0:T(8,128)(2,1)S(1)}, u32[]{:S(2)}, u32[]{:S(2)}) collective-permute-start(bf16[2,2,512,384]{3,2,1,0:T(8,128)(2,1)} %get-tuple-element.49), channel_id=1, source_target_pairs={{0,2},{1,3},{2,0},{3,1},{4,6},{5,7},{6,4},{7,5},{8,10},{9,11},{10,... | collective-permute-start | bytes 4718600 | tf_op jit(solution)/shard_map/ppermute | solution.py:28
  32.6 9.7 %copy-start.15 = (bf16[128,1024]{1,0:T(8,128)(2,1)}, bf16[128,1024]{1,0:T(8,128)(2,1)S(1)}, u32[]{:S(2)}) copy-start(bf16[128,1024]{1,0:T(8,128)(2,1)S(1)} %convolution_convert_fusion.q_ref) | copy-start | bytes 786436
  32.6 8.5 %collective-permute-start.9 = (bf16[128,1024]{1,0:T(8,128)(2,1)S(1)}, bf16[128,1024]{1,0:T(8,128)(2,1)S(1)}, u32[]{:S(2)}, u32[]{:S(2)}) collective-permute-start(bf16[128,1024]{1,0:T(8,128)(2,1)S(1)} %convolution_convert_fusion.q_ref), channel_id=1, source_target_pairs={{0,4},{4,0},{8,12},{12,8},{16,20},{20,16},{24,28},{28,24},{1,5},{5... | collective-permute-start | bytes 786440 | tf_op jit(solution)/shard_map/ppermute | solution.py:28
  32.7 15.9 %collective-permute-start.11 = (bf16[128,1024]{1,0:T(8,128)(2,1)S(1)}, bf16[128,1024]{1,0:T(8,128)(2,1)}, u32[]{:S(2)}, u32[]{:S(2)}) collective-permute-start(bf16[128,1024]{1,0:T(8,128)(2,1)S(1)} %convolution_convert_fusion.q_ref), channel_id=1, source_target_pairs={{0,24},{4,28},{8,0},{12,4},{16,8},{20,12},{24,16},{28,20},{1,25},{... | collective-permute-start | bytes 786440 | tf_op jit(solution)/shard_map/ppermute | solution.py:33
  35.5 14.0 %collective-permute-start.8 = (bf16[128,1024]{1,0:T(8,128)(2,1)S(1)}, bf16[128,1024]{1,0:T(8,128)(2,1)}, u32[]{:S(2)}, u32[]{:S(2)}) collective-permute-start(bf16[128,1024]{1,0:T(8,128)(2,1)S(1)} %convolution_convert_fusion.q_ref), channel_id=1, source_target_pairs={{0,8},{4,12},{8,16},{12,20},{16,24},{20,28},{24,0},{28,4},{1,9},{5... | collective-permute-start | bytes 786440 | tf_op jit(solution)/shard_map/ppermute | solution.py:33
  41.1 17.7 %collective-permute-start.10 = (bf16[128,1024]{1,0:T(8,128)(2,1)S(1)}, bf16[128,1024]{1,0:T(8,128)(2,1)}, u32[]{:S(2)}, u32[]{:S(2)}) collective-permute-start(bf16[128,1024]{1,0:T(8,128)(2,1)S(1)} %convolution_convert_fusion.q_ref), channel_id=1, source_target_pairs={{0,16},{4,20},{8,24},{12,28},{16,0},{20,4},{24,8},{28,12},{1,17},{... | collective-permute-start | bytes 786440 | tf_op jit(solution)/shard_map/ppermute | solution.py:33
  41.8 54.2 %collective-permute-start.20 = (bf16[2,2,512,384]{3,2,1,0:T(8,128)(2,1)}, bf16[2,2,512,384]{3,2,1,0:T(8,128)(2,1)S(1)}, u32[]{:S(2)}, u32[]{:S(2)}) collective-permute-start(bf16[2,2,512,384]{3,2,1,0:T(8,128)(2,1)} %get-tuple-element.66), channel_id=1, source_target_pairs={{0,2},{1,3},{2,0},{3,1},{4,6},{5,7},{6,4},{7,5},{8,10},{9,11},{10,... | collective-permute-start | bytes 4718600 | tf_op jit(solution)/shard_map/ppermute | solution.py:28
  48.6 24.7 %collective-permute-start.16 = (bf16[128,1024]{1,0:T(8,128)(2,1)}, bf16[128,1024]{1,0:T(8,128)(2,1)S(1)}, u32[]{:S(2)}, u32[]{:S(2)}) collective-permute-start(bf16[128,1024]{1,0:T(8,128)(2,1)} %collective-permute-done.11), channel_id=1, source_target_pairs={{0,4},{4,0},{8,12},{12,8},{16,20},{20,16},{24,28},{28,24},{1,5},{5... | collective-permute-start | bytes 786440 | tf_op jit(solution)/shard_map/ppermute | solution.py:28
  49.4 23.9 %collective-permute-start.14 = (bf16[128,1024]{1,0:T(8,128)(2,1)}, bf16[128,1024]{1,0:T(8,128)(2,1)S(1)}, u32[]{:S(2)}, u32[]{:S(2)}) collective-permute-start(bf16[128,1024]{1,0:T(8,128)(2,1)} %collective-permute-done.8), channel_id=1, source_target_pairs={{0,4},{4,0},{8,12},{12,8},{16,20},{20,16},{24,28},{28,24},{1,5},{5... | collective-permute-start | bytes 786440 | tf_op jit(solution)/shard_map/ppermute | solution.py:28
  58.8 14.5 %collective-permute-start.15 = (bf16[128,1024]{1,0:T(8,128)(2,1)}, bf16[128,1024]{1,0:T(8,128)(2,1)S(1)}, u32[]{:S(2)}, u32[]{:S(2)}) collective-permute-start(bf16[128,1024]{1,0:T(8,128)(2,1)} %collective-permute-done.10), channel_id=1, source_target_pairs={{0,4},{4,0},{8,12},{12,8},{16,20},{20,16},{24,28},{28,24},{1,5},{5... | collective-permute-start | bytes 786440 | tf_op jit(solution)/shard_map/ppermute | solution.py:28
  60.5 30.4 %copy-start.5 = (bf16[512,1024]{1,0:T(8,128)(2,1)}, bf16[512,1024]{1,0:T(8,128)(2,1)S(1)}, u32[]{:S(2)}) copy-start(bf16[512,1024]{1,0:T(8,128)(2,1)S(1)} %pad_maximum_fusion.q_ref) | copy-start | bytes 3145732
  60.5 12.8 %copy-start.25 = (bf16[128,1024]{1,0:T(8,128)(2,1)S(1)}, bf16[128,1024]{1,0:T(8,128)(2,1)}, u32[]{:S(2)}) copy-start(bf16[128,1024]{1,0:T(8,128)(2,1)} %copy-done.24) | copy-start | bytes 786436
  73.3 17.7 %copy-start = (f32[1024,512]{1,0:T(8,128)}, f32[1024,512]{1,0:T(8,128)S(1)}, u32[]{:S(2)}) copy-start(f32[1024,512]{1,0:T(8,128)S(1)} %get-tuple-element.59.acc_ref) | copy-start | bytes 6291460
  73.4 25.0 %copy-start.8 = (bf16[512,1024]{1,0:T(8,128)(2,1)}, bf16[512,1024]{1,0:T(8,128)(2,1)S(1)}, u32[]{:S(2)}) copy-start(bf16[512,1024]{1,0:T(8,128)(2,1)S(1)} %constant_dynamic-update-slice_fusion.q_ref) | copy-start | bytes 3145732
  85.0 13.4 %copy-start.3 = (f32[1024,512]{1,0:T(8,128)}, f32[1024,512]{1,0:T(8,128)S(1)}, u32[]{:S(2)}) copy-start(f32[1024,512]{1,0:T(8,128)S(1)} %get-tuple-element.61.acc_ref) | copy-start | bytes 6291460
  85.0 13.4 %copy-start.12 = (f32[8,8,512]{2,1,0:T(8,128)}, f32[8,8,512]{2,1,0:T(8,128)S(1)}, u32[]{:S(2)}) copy-start(f32[8,8,512]{2,1,0:T(8,128)S(1)} %get-tuple-element.56.stat_ref) | copy-start | bytes 393220
  85.2 2.4 %collective-permute-start.17 = (bf16[2,512,384]{2,1,0:T(8,128)(2,1)S(1)}, bf16[2,512,384]{2,1,0:T(8,128)(2,1)S(1)}, u32[]{:S(2)}, u32[]{:S(2)}) collective-permute-start(bf16[2,512,384]{2,1,0:T(8,128)(2,1)S(1)} %slice_bitcast_fusion.1), channel_id=1, source_target_pairs={{0,1},{1,0},{2,3},{3,2},{4,5},{5,4},{6,7},{7,6},{8,9},{9,8},{10,11... | collective-permute-start | bytes 2359304 | tf_op jit(solution)/shard_map/ppermute | solution.py:28
  94.4 8.4 %copy-start.10 = (bf16[4,416,128]{2,1,0:T(8,128)(2,1)}, bf16[4,416,128]{2,1,0:T(8,128)(2,1)S(1)}, u32[]{:S(2)}) copy-start(bf16[4,416,128]{2,1,0:T(8,128)(2,1)S(1)} %far_tiles.6.a_ref) | copy-start | bytes 1277956
  96.1 2.4 %collective-permute-start.21 = (bf16[2,512,384]{2,1,0:T(8,128)(2,1)S(1)}, bf16[2,512,384]{2,1,0:T(8,128)(2,1)S(1)}, u32[]{:S(2)}, u32[]{:S(2)}) collective-permute-start(bf16[2,512,384]{2,1,0:T(8,128)(2,1)S(1)} %slice_bitcast_fusion), channel_id=1, source_target_pairs={{0,1},{1,0},{2,3},{3,2},{4,5},{5,4},{6,7},{7,6},{8,9},{9,8},{10,11... | collective-permute-start | bytes 2359304 | tf_op jit(solution)/shard_map/ppermute | solution.py:28
  96.2 27.5 %collective-permute-start.19 = (bf16[2,2,512,256]{3,2,1,0:T(8,128)(2,1)}, bf16[2,2,512,256]{3,2,1,0:T(8,128)(2,1)S(1)}, u32[]{:S(2)}, u32[]{:S(2)}) collective-permute-start(bf16[2,2,512,256]{3,2,1,0:T(8,128)(2,1)} %get-tuple-element.64), channel_id=1, source_target_pairs={{0,2},{1,3},{2,0},{3,1},{4,6},{5,7},{6,4},{7,5},{8,10},{9,11},{10,... | collective-permute-start | bytes 3145736 | tf_op jit(solution)/shard_map/ppermute | solution.py:28
  97.8 12.8 %collective-permute-start.18 = (bf16[4,416,128]{2,1,0:T(8,128)(2,1)S(1)}, bf16[4,416,128]{2,1,0:T(8,128)(2,1)}, u32[]{:S(2)}, u32[]{:S(2)}) collective-permute-start(bf16[4,416,128]{2,1,0:T(8,128)(2,1)S(1)} %far_tiles.7), channel_id=1, source_target_pairs={{0,4},{4,0},{8,12},{12,8},{16,20},{20,16},{24,28},{28,24},{1,5},{5... | collective-permute-start | bytes 1277960 | tf_op jit(solution)/shard_map/ppermute | solution.py:28
  102.8 18.9 %collective-permute-start.22 = (bf16[4,416,128]{2,1,0:T(8,128)(2,1)}, bf16[4,416,128]{2,1,0:T(8,128)(2,1)}, u32[]{:S(2)}, u32[]{:S(2)}) collective-permute-start(bf16[4,416,128]{2,1,0:T(8,128)(2,1)} %far_tiles.9), channel_id=1, source_target_pairs={{0,4},{4,0},{8,12},{12,8},{16,20},{20,16},{24,28},{28,24},{1,5},{5... | collective-permute-start | bytes 1277960 | tf_op jit(solution)/shard_map/ppermute | solution.py:28
  112.6 11.2 %collective-permute-start.23 = (bf16[416,128]{1,0:T(8,128)(2,1)}, bf16[416,128]{1,0:T(8,128)(2,1)}, u32[]{:S(2)}, u32[]{:S(2)}) collective-permute-start(bf16[416,128]{1,0:T(8,128)(2,1)} %get-tuple-element.69), channel_id=1, source_target_pairs={{0,24},{4,28},{8,0},{12,4},{16,8},{20,12},{24,16},{28,20},{1,25},{... | collective-permute-start | bytes 319496 | tf_op jit(solution)/shard_map/ppermute | solution.py:33
  113.7 10.0 %collective-permute-start.24 = (bf16[416,128]{1,0:T(8,128)(2,1)}, bf16[416,128]{1,0:T(8,128)(2,1)}, u32[]{:S(2)}, u32[]{:S(2)}) collective-permute-start(bf16[416,128]{1,0:T(8,128)(2,1)} %get-tuple-element.70), channel_id=1, source_target_pairs={{0,16},{4,20},{8,24},{12,28},{16,0},{20,4},{24,8},{28,12},{1,17},{... | collective-permute-start | bytes 319496 | tf_op jit(solution)/shard_map/ppermute | solution.py:33
  113.7 10.0 %collective-permute-start.25 = (bf16[416,128]{1,0:T(8,128)(2,1)}, bf16[416,128]{1,0:T(8,128)(2,1)}, u32[]{:S(2)}, u32[]{:S(2)}) collective-permute-start(bf16[416,128]{1,0:T(8,128)(2,1)} %get-tuple-element.71), channel_id=1, source_target_pairs={{0,8},{4,12},{8,16},{12,20},{16,24},{20,28},{24,0},{28,4},{1,9},{5... | collective-permute-start | bytes 319496 | tf_op jit(solution)/shard_map/ppermute | solution.py:33
  114.6 1.6 copy-start.1
  116.2 1.2 copy-start.6
  120.9 0.8 copy-start.11
  123.7 14.0 %copy-start.7 = (bf16[512,1024]{1,0:T(8,128)(2,1)S(1)}, bf16[512,1024]{1,0:T(8,128)(2,1)}, u32[]{:S(2)}) copy-start(bf16[512,1024]{1,0:T(8,128)(2,1)} %copy-done.5) | copy-start | bytes 3145732
  123.8 14.0 %copy-start.2 = (f32[1024,512]{1,0:T(8,128)S(1)}, f32[1024,512]{1,0:T(8,128)}, u32[]{:S(2)}) copy-start(f32[1024,512]{1,0:T(8,128)} %copy-done) | copy-start | bytes 6291460
  123.8 2.0 %collective-permute-start.26 = (bf16[2,512,256]{2,1,0:T(8,128)(2,1)S(1)}, bf16[2,512,256]{2,1,0:T(8,128)(2,1)S(1)}, u32[]{:S(2)}, u32[]{:S(2)}) collective-permute-start(bf16[2,512,256]{2,1,0:T(8,128)(2,1)S(1)} %slice_bitcast_fusion.2), channel_id=1, source_target_pairs={{0,1},{1,0},{2,3},{3,2},{4,5},{5,4},{6,7},{7,6},{8,9},{9,8},{10,11... | collective-permute-start | bytes 1572872 | tf_op jit(solution)/shard_map/ppermute | solution.py:28
  125.8 1.6 copy-start.4
  127.4 1.2 copy-start.9
  128.6 0.9 copy-start.13
  129.5 8.3 %copy-start.34 = (bf16[416,128]{1,0:T(8,128)(2,1)S(1)}, bf16[416,128]{1,0:T(8,128)(2,1)}, u32[]{:S(2)}) copy-start(bf16[416,128]{1,0:T(8,128)(2,1)} %get-tuple-element.78) | copy-start | bytes 319492
  132.0 9.0 %collective-permute-start.30 = (bf16[4,272,128]{2,1,0:T(8,128)(2,1)S(1)}, bf16[4,272,128]{2,1,0:T(8,128)(2,1)S(1)}, u32[]{:S(2)}, u32[]{:S(2)}) collective-permute-start(bf16[4,272,128]{2,1,0:T(8,128)(2,1)S(1)} %far_tiles.10), channel_id=1, source_target_pairs={{0,4},{4,0},{8,12},{12,8},{16,20},{20,16},{24,28},{28,24},{1,5},{5... | collective-permute-start | bytes 835592 | tf_op jit(solution)/shard_map/ppermute | solution.py:28
  133.4 14.0 %collective-permute-start.27 = (bf16[416,128]{1,0:T(8,128)(2,1)}, bf16[416,128]{1,0:T(8,128)(2,1)S(1)}, u32[]{:S(2)}, u32[]{:S(2)}) collective-permute-start(bf16[416,128]{1,0:T(8,128)(2,1)} %get-tuple-element.76), channel_id=1, source_target_pairs={{0,24},{4,28},{8,0},{12,4},{16,8},{20,12},{24,16},{28,20},{1,25},{... | collective-permute-start | bytes 319496 | tf_op jit(solution)/shard_map/ppermute | solution.py:33
  136.6 14.4 %collective-permute-start.28 = (bf16[416,128]{1,0:T(8,128)(2,1)}, bf16[416,128]{1,0:T(8,128)(2,1)S(1)}, u32[]{:S(2)}, u32[]{:S(2)}) collective-permute-start(bf16[416,128]{1,0:T(8,128)(2,1)} %get-tuple-element.77), channel_id=1, source_target_pairs={{0,16},{4,20},{8,24},{12,28},{16,0},{20,4},{24,8},{28,12},{1,17},{... | collective-permute-start | bytes 319496 | tf_op jit(solution)/shard_map/ppermute | solution.py:33
  137.8 10.5 %copy-start.35 = (f32[16]{0:T(128)S(1)}, f32[16]{0:T(128)}, u32[]{:S(2)}) copy-start(f32[16]{0:T(128)} %param.18) | copy-start | bytes 196
  137.8 13.2 %collective-permute-start.29 = (bf16[416,128]{1,0:T(8,128)(2,1)S(1)}, bf16[416,128]{1,0:T(8,128)(2,1)S(1)}, u32[]{:S(2)}, u32[]{:S(2)}) collective-permute-start(bf16[416,128]{1,0:T(8,128)(2,1)S(1)} %copy-done.34), channel_id=1, source_target_pairs={{0,8},{4,12},{8,16},{12,20},{16,24},{20,28},{24,0},{28,4},{1,9},{5... | collective-permute-start | bytes 319496 | tf_op jit(solution)/shard_map/ppermute | solution.py:33
  143.6 10.7 %collective-permute-start.31 = (bf16[272,128]{1,0:T(8,128)(2,1)}, bf16[272,128]{1,0:T(8,128)(2,1)S(1)}, u32[]{:S(2)}, u32[]{:S(2)}) collective-permute-start(bf16[272,128]{1,0:T(8,128)(2,1)} %get-tuple-element.80), channel_id=1, source_target_pairs={{0,24},{4,28},{8,0},{12,4},{16,8},{20,12},{24,16},{28,20},{1,25},{... | collective-permute-start | bytes 208904 | tf_op jit(solution)/shard_map/ppermute | solution.py:33
  147.4 6.9 %collective-permute-start.32 = (bf16[272,128]{1,0:T(8,128)(2,1)}, bf16[272,128]{1,0:T(8,128)(2,1)S(1)}, u32[]{:S(2)}, u32[]{:S(2)}) collective-permute-start(bf16[272,128]{1,0:T(8,128)(2,1)} %get-tuple-element.81), channel_id=1, source_target_pairs={{0,16},{4,20},{8,24},{12,28},{16,0},{20,4},{24,8},{28,12},{1,17},{... | collective-permute-start | bytes 208904 | tf_op jit(solution)/shard_map/ppermute | solution.py:33
  147.4 3.6 %copy-start.26 = (bf16[416,128]{1,0:T(8,128)(2,1)}, bf16[416,128]{1,0:T(8,128)(2,1)S(1)}, u32[]{:S(2)}) copy-start(bf16[416,128]{1,0:T(8,128)(2,1)S(1)} %collective-permute-done.27.refs_1_) | copy-start | bytes 319492
  147.4 7.0 %collective-permute-start.33 = (bf16[272,128]{1,0:T(8,128)(2,1)}, bf16[272,128]{1,0:T(8,128)(2,1)S(1)}, u32[]{:S(2)}, u32[]{:S(2)}) collective-permute-start(bf16[272,128]{1,0:T(8,128)(2,1)} %get-tuple-element.82), channel_id=1, source_target_pairs={{0,8},{4,12},{8,16},{12,20},{16,24},{20,28},{24,0},{28,4},{1,9},{5... | collective-permute-start | bytes 208904 | tf_op jit(solution)/shard_map/ppermute | solution.py:33
  151.0 8.1 %copy-start.16 = (bf16[384,128]{1,0:T(8,128)(2,1)S(1)}, bf16[384,128]{1,0:T(8,128)(2,1)}, u32[]{:S(2)}) copy-start(bf16[384,128]{1,0:T(8,128)(2,1)} %merge_all.3) | copy-start | bytes 294916
  154.3 4.8 %copy-start.17 = (bf16[384,128]{1,0:T(8,128)(2,1)S(1)}, bf16[384,128]{1,0:T(8,128)(2,1)}, u32[]{:S(2)}) copy-start(bf16[384,128]{1,0:T(8,128)(2,1)} %merge_all.4) | copy-start | bytes 294916
  156.9 2.3 %copy-start.20 = (bf16[256,128]{1,0:T(8,128)(2,1)S(1)}, bf16[256,128]{1,0:T(8,128)(2,1)}, u32[]{:S(2)}) copy-start(bf16[256,128]{1,0:T(8,128)(2,1)} %merge_all.5) | copy-start | bytes 196612
  161.2 2.7 %collective-permute-start.34 = (bf16[128,1024]{1,0:T(8,128)(2,1)S(1)}, bf16[128,1024]{1,0:T(8,128)(2,1)S(1)}, u32[]{:S(2)}, u32[]{:S(2)}) collective-permute-start(bf16[128,1024]{1,0:T(8,128)(2,1)S(1)} %fusion.11), channel_id=1, source_target_pairs={{0,1},{1,0},{2,3},{3,2},{4,5},{5,4},{6,7},{7,6},{8,9},{9,8},{10,11... | collective-permute-start | bytes 786440 | tf_op jit(solution)/shard_map/ppermute | solution.py:28
  161.3 5.3 %collective-permute-start.35 = (bf16[128,1024]{1,0:T(8,128)(2,1)S(1)}, bf16[128,1024]{1,0:T(8,128)(2,1)S(1)}, u32[]{:S(2)}, u32[]{:S(2)}) collective-permute-start(bf16[128,1024]{1,0:T(8,128)(2,1)S(1)} %fusion.8), channel_id=1, source_target_pairs={{0,1},{1,0},{2,3},{3,2},{4,5},{5,4},{6,7},{7,6},{8,9},{9,8},{10,11... | collective-permute-start | bytes 786440 | tf_op jit(solution)/shard_map/ppermute | solution.py:28
  164.0 8.3 %collective-permute-start.36 = (bf16[128,1024]{1,0:T(8,128)(2,1)S(1)}, bf16[128,1024]{1,0:T(8,128)(2,1)S(1)}, u32[]{:S(2)}, u32[]{:S(2)}) collective-permute-start(bf16[128,1024]{1,0:T(8,128)(2,1)S(1)} %add_convert_fusion.1), channel_id=1, source_target_pairs={{0,2},{1,3},{2,0},{3,1},{4,6},{5,7},{6,4},{7,5},{8,10},{9,11},{10,... | collective-permute-start | bytes 786440 | tf_op jit(solution)/shard_map/ppermute | solution.py:28
  (9 other events, 6.0 us)

commit v11 on v10

--- a/solution.py
+++ b/solution.py
@@ -393,7 +393,7 @@
 
     chunk_pairs = NEAR_HEADS // 2
     near_state = []
-    q_halves[0] = after(q_halves[0], crossed[0], local_out)
+    q_halves[0] = after(q_halves[0], local_out)
     for part in range(2):
         if part == 1:
             q_halves[1] = jnp.concatenate(after(q_blocks[turns:], near_state[0][1]), 0)

time: 174 us -> 174 us (level)
  transfers between devices with their start and end apart: 37 -> 37, of which waited for: 10 -> 9; matrix products, arithmetic and copies ran while one was open for 7% -> 7% of each run, Pallas kernels for 32% -> 32%
where the time goes in v11:
time: 174 us; the launch traced here: 173 us
  Pallas kernels  66.8 us (38%)
  starting transfers between devices  41.7 us (24%)
  waiting for transfers between devices  34.4 us (20%)
  local copies, waits for them, and re-layouts  14.2 us (8%)
  matrix products  13.1 us (8%)
  other arithmetic  2.32 us (1%)
    ppermute x21, waiting for transfers between devices, swap(): lax.ppermute(block, axis, [(i, i ^ distance) for i in range(lax.axis_size...  26.2 us
    pallas_call x2, Pallas kernels, on_device(): pl.pallas_call(near_kernel, grid_spec=pltpu.PrefetchScalarGridSpec(num_sc...  22.6 us
    ppermute x15, starting transfers between devices, turn(): lax.ppermute(block, axis, [(i, (i + distance) % size) for i in range(size)])  22.6 us
    pallas_call x6, Pallas kernels, on_device(): pl.pallas_call(far_kernel, grid=(1,), in_specs=[pl.BlockSpec((pl.Element(...  19.6 us
    ppermute x21, starting transfers between devices, swap(): lax.ppermute(block, axis, [(i, i ^ distance) for i in range(lax.axis_size...  14.9 us
    unnamed x75, local copies, waits for them, and re-layouts  12.2 us
    dot_general x4, matrix products, piece(): return lax.dot_general(rows, w, over_rows, preferred_element_type=f32)  8.41 us
    ppermute x15, waiting for transfers between devices, turn(): lax.ppermute(block, axis, [(i, (i + distance) % size) for i in range(size)])  8.21 us
  transfers between devices with their start and end apart: 37, of which 9 were waited for; matrix products, arithmetic and copies ran while one was open for 7% of the time, Pallas kernels for 32%

profile of v11, /device:TPU:0, one launch (start us, length us, event | category | flops | bytes accessed | tf_op | source)
XLA Modules:
  0.0 173.1 jit_solution(13692961411598168809)
XLA Ops:
  0.0 6.4 %share_tiles.1 = (bf16[2,512,1024]{2,1,0:T(8,128)(2,1)}, bf16[2,2,512,384]{3,2,1,0:T(8,128)(2,1)}, bf16[2,2,512,384]{3,2,1,0:T(8,128)(2,1)}, bf16[2,2,512,256]{3,2,1,0:T(8,128)(2,1)}) custom-call(s32[1]{0:T(128)} %bitcast.me_ref.m_ref, bf16[512,4096]{1,0:T(8,128)(2,1)} %k0_ref.3, bf16[512,4096]{1,0:T(8,128)(2,1)} %v0_ref.3), custom_call_target="tpu_custom_call" | custom-call | bytes 14680064 | tf_op jit(solution)/shard_map/share_tiles/pallas_call | solution.py:329
  6.9 2.6 %collective-permute-start.3 = (s32[16,128]{1,0:T(8,128)S(1)}, s32[16,128]{1,0:T(8,128)S(1)}, u32[]{:S(2)}, u32[]{:S(2)}) collective-permute-start(s32[16,128]{1,0:T(8,128)S(1)} %get-tuple-element.88), channel_id=1, source_target_pairs={{0,4},{4,0},{8,12},{12,8},{16,20},{20,16},{24,28},{28,24},{1,5},{5... | collective-permute-start | bytes 24584 | tf_op jit(solution)/shard_map/ppermute | solution.py:28
  9.5 1.5 collective-permute-start.1
  11.2 3.1 %collective-permute-start.5 = (s32[2,16,128]{2,1,0:T(8,128)S(1)}, s32[2,16,128]{2,1,0:T(8,128)S(1)}, u32[]{:S(2)}, u32[]{:S(2)}) collective-permute-start(s32[2,16,128]{2,1,0:T(8,128)S(1)} %get-tuple-element.86), channel_id=1, source_target_pairs={{0,16},{4,20},{8,24},{12,28},{16,0},{20,4},{24,8},{28,12},{1,17},{... | collective-permute-start | bytes 49160 | tf_op jit(solution)/shard_map/ppermute | solution.py:33
  14.3 1.6 collective-permute-start.4
  16.0 4.0 %collective-permute-start.6 = (s32[2,16,128]{2,1,0:T(8,128)S(1)}, s32[2,16,128]{2,1,0:T(8,128)S(1)}, u32[]{:S(2)}, u32[]{:S(2)}) collective-permute-start(s32[2,16,128]{2,1,0:T(8,128)S(1)} %get-tuple-element.86), channel_id=1, source_target_pairs={{0,24},{4,28},{8,0},{12,4},{16,8},{20,12},{24,16},{28,20},{1,25},{... | collective-permute-start | bytes 49160 | tf_op jit(solution)/shard_map/ppermute | solution.py:33
  20.2 4.2 %collective-permute-start.12 = (bf16[2,128,1024]{2,1,0:T(8,128)(2,1)S(1)}, bf16[2,128,1024]{2,1,0:T(8,128)(2,1)}, u32[]{:S(2)}, u32[]{:S(2)}) collective-permute-start(bf16[2,128,1024]{2,1,0:T(8,128)(2,1)S(1)} %pad_maximum_fusion.1), channel_id=1, source_target_pairs={{0,4},{4,8},{8,12},{12,16},{16,20},{20,24},{24,28},{1,5},{5,9},{9,... | collective-permute-start | bytes 1572872 | tf_op jit(solution)/shard_map/ppermute | solution.py:39
  24.6 0.7 copy-done.23
  25.3 1.5 collective-permute-start.16
  26.8 1.0 constant_dynamic-update-slice_fusion.6
  27.9 4.7 %convolution_convert_fusion.q_ref = bf16[128,1024]{1,0:T(8,128)(2,1)S(1)} fusion(bf16[128,4096]{1,0:T(8,128)(2,1)S(1)} %constant_dynamic-update-slice_fusion.4, bf16[4096,1024]{1,0:T(8,128)(2,1)} %param.11), kind=kOutput, calls=%fused_computation.10 | convolution fusion | flops 1073872896 | bytes 9699328 | tf_op jit(solution)/shard_map/dot_general | solution.py:347
  32.7 2.8 %collective-permute-start.11 = (bf16[128,1024]{1,0:T(8,128)(2,1)S(1)}, bf16[128,1024]{1,0:T(8,128)(2,1)}, u32[]{:S(2)}, u32[]{:S(2)}) collective-permute-start(bf16[128,1024]{1,0:T(8,128)(2,1)S(1)} %convolution_convert_fusion.q_ref), channel_id=1, source_target_pairs={{0,24},{4,28},{8,0},{12,4},{16,8},{20,12},{24,16},{28,20},{1,25},{... | collective-permute-start | bytes 786440 | tf_op jit(solution)/shard_map/ppermute | solution.py:33
  35.5 5.6 %collective-permute-done.9 = bf16[128,1024]{1,0:T(8,128)(2,1)S(1)} collective-permute-done((bf16[128,1024]{1,0:T(8,128)(2,1)S(1)}, bf16[128,1024]{1,0:T(8,128)(2,1)S(1)}, u32[]{:S(2)}, u32[]{:S(2)}) %collective-permute-start.9) | collective-permute-done | bytes 262176 | tf_op jit(solution)/shard_map/ppermute | solution.py:28
  41.1 0.7 copy-done.24
  42.4 6.3 %local_window.1.refs_4_ = f32[1024,128]{1,0:T(8,128)} custom-call(s32[1]{0:T(128)} %bitcast.9.ctx_ref, bf16[128,1024]{1,0:T(8,128)(2,1)} %copy-done.15, bf16[2,128,1024]{2,1,0:T(8,128)(2,1)} %collective-permute-done.12.k0_ref.v0_ref, bf16[128,1024]{1,0:T(8,128)(2,1)} %k1_ref.1, bf16[2,128,1024]{2,1,0:T(8,128)(2,1)} %collective-permute-done.12.k0_ref.v0_ref, ...), custom_call_target="tpu_custom_call" | custom-call | flops 134217728 | bytes 2097152 | tf_op jit(solution)/shard_map/local_window/pallas_call | solution.py:363
  48.6 0.8 collective-permute-start.15
  49.4 1.2 collective-permute-start.13
  50.7 8.1 %collective-permute-done.10 = bf16[128,1024]{1,0:T(8,128)(2,1)} collective-permute-done((bf16[128,1024]{1,0:T(8,128)(2,1)S(1)}, bf16[128,1024]{1,0:T(8,128)(2,1)}, u32[]{:S(2)}, u32[]{:S(2)}) %collective-permute-start.10) | collective-permute-done | bytes 262176 | tf_op jit(solution)/shard_map/ppermute | solution.py:33
  59.2 1.3 pad_maximum_fusion.q_ref
  60.5 11.0 %near_tiles.2 = (f32[1024,512]{1,0:T(8,128)S(1)}, f32[8,8,512]{2,1,0:T(8,128)S(1)}) custom-call(s32[1]{0:T(128)} %bitcast.me_ref.m_ref, bf16[512,1024]{1,0:T(8,128)(2,1)S(1)} %pad_maximum_fusion.q_ref, bf16[512,4096]{1,0:T(8,128)(2,1)} %k0_ref.3, bf16[512,4096]{1,0:T(8,128)(2,1)} %v0_ref.3, bf16[2,512,1024]{2,1,0:T(8,128)(2,1)} %collective-permute-done.7.k1_ref.v1_ref, ...), custom_call_target="tpu_custom_call" | custom-call | flops 2147483648 | bytes 8388608 | tf_op jit(solution)/shard_map/near_tiles/pallas_call | solution.py:404
  71.7 11.6 %near_tiles.3 = (f32[1024,512]{1,0:T(8,128)S(1)}, f32[8,8,512]{2,1,0:T(8,128)S(1)}) custom-call(s32[1]{0:T(128)} %bitcast.me_ref.m_ref, bf16[512,1024]{1,0:T(8,128)(2,1)S(1)} %constant_dynamic-update-slice_fusion.q_ref, bf16[512,4096]{1,0:T(8,128)(2,1)} %k0_ref.3, bf16[512,4096]{1,0:T(8,128)(2,1)} %v0_ref.3, ...), custom_call_target="tpu_custom_call" | custom-call | flops 2147483648 | bytes 8388608 | tf_op jit(solution)/shard_map/near_tiles/pallas_call | solution.py:404
  83.5 2.3 %collective-permute-done.17.k3_ref.v3_ref = bf16[2,512,384]{2,1,0:T(8,128)(2,1)S(1)} collective-permute-done((bf16[2,512,384]{2,1,0:T(8,128)(2,1)S(1)}, bf16[2,512,384]{2,1,0:T(8,128)(2,1)S(1)}, u32[]{:S(2)}, u32[]{:S(2)}) %collective-permute-start.17) | collective-permute-done | bytes 786464 | tf_op jit(solution)/shard_map/ppermute | solution.py:28
  85.8 3.4 %far_tiles.7 = bf16[4,416,128]{2,1,0:T(8,128)(2,1)S(1)} custom-call(bf16[512,1024]{1,0:T(8,128)(2,1)S(1)} %constant_dynamic-update-slice_fusion.q_ref, bf16[2,2,512,384]{3,2,1,0:T(8,128)(2,1)S(1)} %collective-permute-done.16.k2_ref.v2_ref, bf16[2,2,512,384]{3,2,1,0:T(8,128)(2,1)S(1)} %collective-permute-done.16.k2_ref.v2_ref, ...), custom_call_target="tpu_custom_call" | custom-call | flops 805306368 | bytes 3145728 | tf_op jit(solution)/shard_map/far_tiles/pallas_call | solution.py:460
  89.2 3.4 %far_tiles.6.a_ref = bf16[4,416,128]{2,1,0:T(8,128)(2,1)S(1)} custom-call(bf16[512,1024]{1,0:T(8,128)(2,1)S(1)} %pad_maximum_fusion.q_ref, bf16[2,2,512,384]{3,2,1,0:T(8,128)(2,1)S(1)} %collective-permute-done.16.k2_ref.v2_ref, bf16[2,2,512,384]{3,2,1,0:T(8,128)(2,1)S(1)} %collective-permute-done.16.k2_ref.v2_ref, ...), custom_call_target="tpu_custom_call" | custom-call | flops 805306368 | bytes 3145728 | tf_op jit(solution)/shard_map/far_tiles/pallas_call | solution.py:460
  92.6 3.4 %collective-permute-done.20.k2_ref.v2_ref = bf16[2,2,512,384]{3,2,1,0:T(8,128)(2,1)S(1)} collective-permute-done((bf16[2,2,512,384]{3,2,1,0:T(8,128)(2,1)}, bf16[2,2,512,384]{3,2,1,0:T(8,128)(2,1)S(1)}, u32[]{:S(2)}, u32[]{:S(2)}) %collective-permute-start.20) | collective-permute-done | bytes 1572896 | tf_op jit(solution)/shard_map/ppermute | solution.py:28
  96.2 1.6 collective-permute-start.19
  97.8 0.7 collective-permute-done.21.k3_ref.v3_ref
  98.5 4.2 %far_tiles.9 = bf16[4,416,128]{2,1,0:T(8,128)(2,1)} custom-call(bf16[512,1024]{1,0:T(8,128)(2,1)S(1)} %constant_dynamic-update-slice_fusion.q_ref, bf16[2,2,512,384]{3,2,1,0:T(8,128)(2,1)S(1)} %collective-permute-done.20.k2_ref.v2_ref, bf16[2,2,512,384]{3,2,1,0:T(8,128)(2,1)S(1)} %collective-permute-done.20.k2_ref.v2_ref, ...), custom_call_target="tpu_custom_call" | custom-call | flops 805306368 | bytes 3145728 | tf_op jit(solution)/shard_map/far_tiles/pallas_call | solution.py:460
  102.7 1.3 collective-permute-start.22
  104.1 6.5 %collective-permute-done.18.b_ref = bf16[4,416,128]{2,1,0:T(8,128)(2,1)} collective-permute-done((bf16[4,416,128]{2,1,0:T(8,128)(2,1)S(1)}, bf16[4,416,128]{2,1,0:T(8,128)(2,1)}, u32[]{:S(2)}, u32[]{:S(2)}) %collective-permute-start.18) | collective-permute-done | bytes 426016 | tf_op jit(solution)/shard_map/ppermute | solution.py:28
  110.5 2.0 %merge_pair.3 = (bf16[416,128]{1,0:T(8,128)(2,1)}, bf16[416,128]{1,0:T(8,128)(2,1)}, bf16[416,128]{1,0:T(8,128)(2,1)}, bf16[416,128]{1,0:T(8,128)(2,1)}) custom-call(bf16[4,416,128]{2,1,0:T(8,128)(2,1)} %copy-done.10, bf16[4,416,128]{2,1,0:T(8,128)(2,1)} %collective-permute-done.18.b_ref), custom_call_target="tpu_custom_call" | custom-call | tf_op jit(solution)/shard_map/merge_pair/pallas_call | solution.py:489
  112.6 1.1 collective-permute-start.23
  113.7 0.9 collective-permute-start.25
  114.6 1.6 copy-done.1
  116.2 1.2 copy-done.6
  117.4 3.5 %far_tiles.8.a_ref = bf16[4,416,128]{2,1,0:T(8,128)(2,1)S(1)} custom-call(bf16[512,1024]{1,0:T(8,128)(2,1)S(1)} %copy-done.6, bf16[2,2,512,384]{3,2,1,0:T(8,128)(2,1)S(1)} %collective-permute-done.20.k2_ref.v2_ref, bf16[2,2,512,384]{3,2,1,0:T(8,128)(2,1)S(1)} %collective-permute-done.20.k2_ref.v2_ref, ...), custom_call_target="tpu_custom_call" | custom-call | flops 805306368 | bytes 3145728 | tf_op jit(solution)/shard_map/far_tiles/pallas_call | solution.py:460
  120.9 0.8 copy-done.11
  121.7 2.1 %merge_pair.4 = (bf16[416,128]{1,0:T(8,128)(2,1)}, bf16[416,128]{1,0:T(8,128)(2,1)}, bf16[416,128]{1,0:T(8,128)(2,1)}, bf16[416,128]{1,0:T(8,128)(2,1)}) custom-call(bf16[4,416,128]{2,1,0:T(8,128)(2,1)} %copy-done.11, bf16[4,416,128]{2,1,0:T(8,128)(2,1)} %collective-permute-done.22.b_ref), custom_call_target="tpu_custom_call" | custom-call | tf_op jit(solution)/shard_map/merge_pair/pallas_call | solution.py:489
  123.9 1.9 %collective-permute-done.26.k3_ref.v3_ref = bf16[2,512,256]{2,1,0:T(8,128)(2,1)S(1)} collective-permute-done((bf16[2,512,256]{2,1,0:T(8,128)(2,1)S(1)}, bf16[2,512,256]{2,1,0:T(8,128)(2,1)S(1)}, u32[]{:S(2)}, u32[]{:S(2)}) %collective-permute-start.26) | collective-permute-done | bytes 524320 | tf_op jit(solution)/shard_map/ppermute | solution.py:28
  125.8 1.6 copy-done.4
  127.4 1.2 copy-done.9
  128.6 0.9 copy-done.13
  129.5 2.5 %far_tiles.10 = bf16[4,272,128]{2,1,0:T(8,128)(2,1)S(1)} custom-call(bf16[512,1024]{1,0:T(8,128)(2,1)S(1)} %copy-done.9, bf16[2,2,512,256]{3,2,1,0:T(8,128)(2,1)S(1)} %collective-permute-done.19.k2_ref.v2_ref, bf16[2,2,512,256]{3,2,1,0:T(8,128)(2,1)S(1)} %collective-permute-done.19.k2_ref.v2_ref, ...), custom_call_target="tpu_custom_call" | custom-call | flops 536870912 | bytes 3145728 | tf_op jit(solution)/shard_map/far_tiles/pallas_call | solution.py:460
  132.0 1.4 collective-permute-start.30
  133.4 3.3 %collective-permute-start.27 = (bf16[416,128]{1,0:T(8,128)(2,1)}, bf16[416,128]{1,0:T(8,128)(2,1)S(1)}, u32[]{:S(2)}, u32[]{:S(2)}) collective-permute-start(bf16[416,128]{1,0:T(8,128)(2,1)} %get-tuple-element.76), channel_id=1, source_target_pairs={{0,24},{4,28},{8,0},{12,4},{16,8},{20,12},{24,16},{28,20},{1,25},{... | collective-permute-start | bytes 319496 | tf_op jit(solution)/shard_map/ppermute | solution.py:33
  136.6 1.1 collective-permute-start.28
  137.8 2.5 %far_tiles.11.a_ref = bf16[4,272,128]{2,1,0:T(8,128)(2,1)S(1)} custom-call(bf16[512,1024]{1,0:T(8,128)(2,1)S(1)} %copy-done.7, bf16[2,2,512,256]{3,2,1,0:T(8,128)(2,1)S(1)} %collective-permute-done.19.k2_ref.v2_ref, bf16[2,2,512,256]{3,2,1,0:T(8,128)(2,1)S(1)} %collective-permute-done.19.k2_ref.v2_ref, ...), custom_call_target="tpu_custom_call" | custom-call | flops 536870912 | bytes 3145728 | tf_op jit(solution)/shard_map/far_tiles/pallas_call | solution.py:460
  140.3 0.7 copy-done.14
  141.0 0.7 copy-done.21
  141.7 1.8 %merge_pair.5 = (bf16[272,128]{1,0:T(8,128)(2,1)}, bf16[272,128]{1,0:T(8,128)(2,1)}, bf16[272,128]{1,0:T(8,128)(2,1)}, bf16[272,128]{1,0:T(8,128)(2,1)}) custom-call(bf16[4,272,128]{2,1,0:T(8,128)(2,1)} %copy-done.14, bf16[4,272,128]{2,1,0:T(8,128)(2,1)} %copy-done.21), custom_call_target="tpu_custom_call" | custom-call | tf_op jit(solution)/shard_map/merge_pair/pallas_call | solution.py:489
  143.6 3.8 %collective-permute-start.31 = (bf16[272,128]{1,0:T(8,128)(2,1)}, bf16[272,128]{1,0:T(8,128)(2,1)S(1)}, u32[]{:S(2)}, u32[]{:S(2)}) collective-permute-start(bf16[272,128]{1,0:T(8,128)(2,1)} %get-tuple-element.80), channel_id=1, source_target_pairs={{0,24},{4,28},{8,0},{12,4},{16,8},{20,12},{24,16},{28,20},{1,25},{... | collective-permute-start | bytes 208904 | tf_op jit(solution)/shard_map/ppermute | solution.py:33
  147.4 0.9 collective-permute-start.33
  148.3 0.7 broadcast_in_dim.20.refs_5_
  148.9 2.0 %merge_all.3 = bf16[384,128]{1,0:T(8,128)(2,1)} custom-call(bf16[416,128]{1,0:T(8,128)(2,1)} %get-tuple-element.74.refs_0_, bf16[416,128]{1,0:T(8,128)(2,1)} %collective-permute-done.23.refs_1_, bf16[416,128]{1,0:T(8,128)(2,1)} %collective-permute-done.24.refs_2_, bf16[416,128]{1,0:T(8,128)(2,1)} %collective-permute-done.25.refs_3_, ...), custom_call_target="tpu_custom_call" | custom-call | tf_op jit(solution)/shard_map/merge_all/pallas_call | solution.py:504
  151.0 0.6 copy-done.27
  151.6 0.6 copy-done.28
  152.3 2.0 %merge_all.4 = bf16[384,128]{1,0:T(8,128)(2,1)} custom-call(bf16[416,128]{1,0:T(8,128)(2,1)} %get-tuple-element.75.refs_0_, bf16[416,128]{1,0:T(8,128)(2,1)} %copy-done.26, bf16[416,128]{1,0:T(8,128)(2,1)} %copy-done.27, bf16[416,128]{1,0:T(8,128)(2,1)} %copy-done.28, f32[1024,128]{1,0:T(8,128)} %local_window.1.refs_4_, f32[16,128]{1,0:T(8,128)} %broadcast_in_dim.20.refs_5_), custom_call_target="tpu_custom_call" | custom-call | tf_op jit(solution)/shard_map/merge_all/pallas_call | solution.py:504
  155.0 1.9 %merge_all.5 = bf16[256,128]{1,0:T(8,128)(2,1)} custom-call(bf16[272,128]{1,0:T(8,128)(2,1)} %get-tuple-element.79.refs_0_, bf16[272,128]{1,0:T(8,128)(2,1)} %copy-done.29, bf16[272,128]{1,0:T(8,128)(2,1)} %copy-done.30, bf16[272,128]{1,0:T(8,128)(2,1)} %copy-done.31, f32[1024,128]{1,0:T(8,128)} %local_window.1.refs_4_, f32[16,128]{1,0:T(8,128)} %broadcast_in_dim.20.refs_5_), custom_call_target="tpu_custom_call" | custom-call | tf_op jit(solution)/shard_map/merge_all/pallas_call | solution.py:504
  156.9 2.2 %fusion.8 = bf16[128,1024]{1,0:T(8,128)(2,1)S(1)} fusion(bf16[1024,4096]{1,0:T(8,128)(2,1)} %param.19, s32[]{:T(128)S(6)} %select_n.44, bf16[256,128]{1,0:T(8,128)(2,1)} %merge_all.5, bf16[384,128]{1,0:T(8,128)(2,1)} %merge_all.4, bf16[384,128]{1,0:T(8,128)(2,1)} %merge_all.3), kind=kOutput, calls=%fused_computation.8 | convolution fusion | flops 269352960 | bytes 2621444 | tf_op jit(solution)/shard_map/dot_general | solution.py:514
  159.2 2.1 %fusion.11 = bf16[128,1024]{1,0:T(8,128)(2,1)S(1)} fusion(bf16[1024,4096]{1,0:T(8,128)(2,1)} %param.19, s32[]{:T(128)S(6)} %select_n.46, bf16[256,128]{1,0:T(8,128)(2,1)S(1)} %copy-done.20, bf16[384,128]{1,0:T(8,128)(2,1)S(1)} %copy-done.17, bf16[384,128]{1,0:T(8,128)(2,1)S(1)} %copy-done.16), kind=kOutput, calls=%fused_computation.9 | convolution fusion | flops 269352960 | bytes 2621444 | tf_op jit(solution)/shard_map/dot_general | solution.py:514
  161.9 2.1 %fusion.4 = f32[128,1024]{1,0:T(8,128)S(1)} fusion(bf16[1024,128]{1,0:T(8,128)(2,1)S(1)} %pad_maximum_fusion.2, bf16[1024,4096]{1,0:T(8,128)(2,1)} %param.19, s32[]{:T(128)S(6)} %select_n.45), kind=kOutput, calls=%fused_computation.4 | convolution fusion | flops 268435456 | bytes 2883588 | tf_op jit(solution)/shard_map/dot_general | solution.py:514
  164.7 2.1 %fusion = f32[128,1024]{1,0:T(8,128)S(1)} fusion(bf16[1024,128]{1,0:T(8,128)(2,1)S(1)} %pad_maximum_fusion.2, bf16[1024,4096]{1,0:T(8,128)(2,1)} %param.19, s32[]{:T(128)S(6)} %select_n.43), kind=kOutput, calls=%fused_computation | convolution fusion | flops 268435456 | bytes 2883588 | tf_op jit(solution)/shard_map/dot_general | solution.py:514
  166.7 5.6 %collective-permute-done.36 = bf16[128,1024]{1,0:T(8,128)(2,1)S(1)} collective-permute-done((bf16[128,1024]{1,0:T(8,128)(2,1)S(1)}, bf16[128,1024]{1,0:T(8,128)(2,1)S(1)}, u32[]{:S(2)}, u32[]{:S(2)}) %collective-permute-start.36) | collective-permute-done | bytes 262176 | tf_op jit(solution)/shard_map/ppermute | solution.py:28
  172.3 0.8 add_convert_fusion
  (126 shorter events, 4.7 us)
Async XLA Ops:
  0.0 6.9 %copy-start.32 = (s32[128,16]{0,1:T(8,128)S(1)}, s32[128,16]{0,1:T(8,128)}, u32[]{:S(2)}) copy-start(s32[128,16]{0,1:T(8,128)} %param.16) | copy-start | bytes 24580
  0.0 6.9 %copy-start.33 = (s32[128]{0:T(128)S(1)}, s32[128]{0:T(128)}, u32[]{:S(2)}) copy-start(s32[128]{0:T(128)} %param.17) | copy-start | bytes 1540
  0.0 9.5 %copy-start.22 = (bf16[128,1024]{1,0:T(8,128)(2,1)S(1)}, bf16[128,1024]{1,0:T(8,128)(2,1)}, u32[]{:S(2)}) copy-start(bf16[128,1024]{1,0:T(8,128)(2,1)} %param.10) | copy-start | bytes 786436
  0.0 14.3 %copy-start.18 = (bf16[128,1024]{1,0:T(8,128)(2,1)S(1)}, bf16[128,1024]{1,0:T(8,128)(2,1)}, u32[]{:S(2)}) copy-start(bf16[128,1024]{1,0:T(8,128)(2,1)} %v1_ref.1) | copy-start | bytes 786436
  0.0 14.3 %copy-start.19 = (bf16[128,1024]{1,0:T(8,128)(2,1)S(1)}, bf16[128,1024]{1,0:T(8,128)(2,1)}, u32[]{:S(2)}) copy-start(bf16[128,1024]{1,0:T(8,128)(2,1)} %k1_ref.1) | copy-start | bytes 786436
  6.5 21.4 %collective-permute-start.7 = (bf16[2,512,1024]{2,1,0:T(8,128)(2,1)}, bf16[2,512,1024]{2,1,0:T(8,128)(2,1)}, u32[]{:S(2)}, u32[]{:S(2)}) collective-permute-start(bf16[2,512,1024]{2,1,0:T(8,128)(2,1)} %get-tuple-element.46), channel_id=1, source_target_pairs={{0,1},{1,0},{2,3},{3,2},{4,5},{5,4},{6,7},{7,6},{8,9},{9,8},{10,11... | collective-permute-start | bytes 6291464 | tf_op jit(solution)/shard_map/ppermute | solution.py:28
  6.9 4.2 %collective-permute-start.3 = (s32[16,128]{1,0:T(8,128)S(1)}, s32[16,128]{1,0:T(8,128)S(1)}, u32[]{:S(2)}, u32[]{:S(2)}) collective-permute-start(s32[16,128]{1,0:T(8,128)S(1)} %get-tuple-element.88), channel_id=1, source_target_pairs={{0,4},{4,0},{8,12},{12,8},{16,20},{20,16},{24,28},{28,24},{1,5},{5... | collective-permute-start | bytes 24584 | tf_op jit(solution)/shard_map/ppermute | solution.py:28
  9.5 15.0 %collective-permute-start.1 = (bf16[128,1024]{1,0:T(8,128)(2,1)S(1)}, bf16[128,1024]{1,0:T(8,128)(2,1)S(1)}, u32[]{:S(2)}, u32[]{:S(2)}) collective-permute-start(bf16[128,1024]{1,0:T(8,128)(2,1)S(1)} %copy-done.22), channel_id=1, source_target_pairs={{0,2},{1,3},{2,0},{3,1},{4,6},{5,7},{6,4},{7,5},{8,10},{9,11},{10,... | collective-permute-start | bytes 786440 | tf_op jit(solution)/shard_map/ppermute | solution.py:28
  11.0 13.6 %collective-permute-start = (bf16[128,1024]{1,0:T(8,128)(2,1)S(1)}, bf16[128,1024]{1,0:T(8,128)(2,1)S(1)}, u32[]{:S(2)}, u32[]{:S(2)}) collective-permute-start(bf16[128,1024]{1,0:T(8,128)(2,1)S(1)} %copy-done.22), channel_id=1, source_target_pairs={{0,1},{1,0},{2,3},{3,2},{4,5},{5,4},{6,7},{7,6},{8,9},{9,8},{10,11... | collective-permute-start | bytes 786440 | tf_op jit(solution)/shard_map/ppermute | solution.py:28
  11.2 4.8 %collective-permute-start.5 = (s32[2,16,128]{2,1,0:T(8,128)S(1)}, s32[2,16,128]{2,1,0:T(8,128)S(1)}, u32[]{:S(2)}, u32[]{:S(2)}) collective-permute-start(s32[2,16,128]{2,1,0:T(8,128)S(1)} %get-tuple-element.86), channel_id=1, source_target_pairs={{0,16},{4,20},{8,24},{12,28},{16,0},{20,4},{24,8},{28,12},{1,17},{... | collective-permute-start | bytes 49160 | tf_op jit(solution)/shard_map/ppermute | solution.py:33
  14.3 5.8 %collective-permute-start.4 = (s32[2,16,128]{2,1,0:T(8,128)S(1)}, s32[2,16,128]{2,1,0:T(8,128)S(1)}, u32[]{:S(2)}, u32[]{:S(2)}) collective-permute-start(s32[2,16,128]{2,1,0:T(8,128)S(1)} %get-tuple-element.86), channel_id=1, source_target_pairs={{0,8},{4,12},{8,16},{12,20},{16,24},{20,28},{24,0},{28,4},{1,9},{5... | collective-permute-start | bytes 49160 | tf_op jit(solution)/shard_map/ppermute | solution.py:33
  16.0 8.4 %collective-permute-start.6 = (s32[2,16,128]{2,1,0:T(8,128)S(1)}, s32[2,16,128]{2,1,0:T(8,128)S(1)}, u32[]{:S(2)}, u32[]{:S(2)}) collective-permute-start(s32[2,16,128]{2,1,0:T(8,128)S(1)} %get-tuple-element.86), channel_id=1, source_target_pairs={{0,24},{4,28},{8,0},{12,4},{16,8},{20,12},{24,16},{28,20},{1,25},{... | collective-permute-start | bytes 49160 | tf_op jit(solution)/shard_map/ppermute | solution.py:33
  20.2 21.7 %collective-permute-start.12 = (bf16[2,128,1024]{2,1,0:T(8,128)(2,1)S(1)}, bf16[2,128,1024]{2,1,0:T(8,128)(2,1)}, u32[]{:S(2)}, u32[]{:S(2)}) collective-permute-start(bf16[2,128,1024]{2,1,0:T(8,128)(2,1)S(1)} %pad_maximum_fusion.1), channel_id=1, source_target_pairs={{0,4},{4,8},{8,12},{12,16},{16,20},{20,24},{24,28},{1,5},{5,9},{9,... | collective-permute-start | bytes 1572872 | tf_op jit(solution)/shard_map/ppermute | solution.py:39
  24.5 3.3 %collective-permute-start.2 = (bf16[128,1024]{1,0:T(8,128)(2,1)S(1)}, bf16[128,1024]{1,0:T(8,128)(2,1)S(1)}, u32[]{:S(2)}, u32[]{:S(2)}) collective-permute-start(bf16[128,1024]{1,0:T(8,128)(2,1)S(1)} %collective-permute-done.1), channel_id=1, source_target_pairs={{0,1},{1,0},{2,3},{3,2},{4,5},{5,4},{6,7},{7,6},{8,9},{9,8},{10,11... | collective-permute-start | bytes 786440 | tf_op jit(solution)/shard_map/ppermute | solution.py:28
  25.3 58.0 %collective-permute-start.16 = (bf16[2,2,512,384]{3,2,1,0:T(8,128)(2,1)}, bf16[2,2,512,384]{3,2,1,0:T(8,128)(2,1)S(1)}, u32[]{:S(2)}, u32[]{:S(2)}) collective-permute-start(bf16[2,2,512,384]{3,2,1,0:T(8,128)(2,1)} %get-tuple-element.57), channel_id=1, source_target_pairs={{0,2},{1,3},{2,0},{3,1},{4,6},{5,7},{6,4},{7,5},{8,10},{9,11},{10,... | collective-permute-start | bytes 4718600 | tf_op jit(solution)/shard_map/ppermute | solution.py:28
  32.6 9.8 %copy-start.15 = (bf16[128,1024]{1,0:T(8,128)(2,1)}, bf16[128,1024]{1,0:T(8,128)(2,1)S(1)}, u32[]{:S(2)}) copy-start(bf16[128,1024]{1,0:T(8,128)(2,1)S(1)} %convolution_convert_fusion.q_ref) | copy-start | bytes 786436
  32.6 8.5 %collective-permute-start.9 = (bf16[128,1024]{1,0:T(8,128)(2,1)S(1)}, bf16[128,1024]{1,0:T(8,128)(2,1)S(1)}, u32[]{:S(2)}, u32[]{:S(2)}) collective-permute-start(bf16[128,1024]{1,0:T(8,128)(2,1)S(1)} %convolution_convert_fusion.q_ref), channel_id=1, source_target_pairs={{0,4},{4,0},{8,12},{12,8},{16,20},{20,16},{24,28},{28,24},{1,5},{5... | collective-permute-start | bytes 786440 | tf_op jit(solution)/shard_map/ppermute | solution.py:28
  32.7 15.9 %collective-permute-start.11 = (bf16[128,1024]{1,0:T(8,128)(2,1)S(1)}, bf16[128,1024]{1,0:T(8,128)(2,1)}, u32[]{:S(2)}, u32[]{:S(2)}) collective-permute-start(bf16[128,1024]{1,0:T(8,128)(2,1)S(1)} %convolution_convert_fusion.q_ref), channel_id=1, source_target_pairs={{0,24},{4,28},{8,0},{12,4},{16,8},{20,12},{24,16},{28,20},{1,25},{... | collective-permute-start | bytes 786440 | tf_op jit(solution)/shard_map/ppermute | solution.py:33
  35.5 14.0 %collective-permute-start.8 = (bf16[128,1024]{1,0:T(8,128)(2,1)S(1)}, bf16[128,1024]{1,0:T(8,128)(2,1)}, u32[]{:S(2)}, u32[]{:S(2)}) collective-permute-start(bf16[128,1024]{1,0:T(8,128)(2,1)S(1)} %convolution_convert_fusion.q_ref), channel_id=1, source_target_pairs={{0,8},{4,12},{8,16},{12,20},{16,24},{20,28},{24,0},{28,4},{1,9},{5... | collective-permute-start | bytes 786440 | tf_op jit(solution)/shard_map/ppermute | solution.py:33
  41.1 17.7 %collective-permute-start.10 = (bf16[128,1024]{1,0:T(8,128)(2,1)S(1)}, bf16[128,1024]{1,0:T(8,128)(2,1)}, u32[]{:S(2)}, u32[]{:S(2)}) collective-permute-start(bf16[128,1024]{1,0:T(8,128)(2,1)S(1)} %convolution_convert_fusion.q_ref), channel_id=1, source_target_pairs={{0,16},{4,20},{8,24},{12,28},{16,0},{20,4},{24,8},{28,12},{1,17},{... | collective-permute-start | bytes 786440 | tf_op jit(solution)/shard_map/ppermute | solution.py:33
  41.8 54.2 %collective-permute-start.20 = (bf16[2,2,512,384]{3,2,1,0:T(8,128)(2,1)}, bf16[2,2,512,384]{3,2,1,0:T(8,128)(2,1)S(1)}, u32[]{:S(2)}, u32[]{:S(2)}) collective-permute-start(bf16[2,2,512,384]{3,2,1,0:T(8,128)(2,1)} %get-tuple-element.66), channel_id=1, source_target_pairs={{0,2},{1,3},{2,0},{3,1},{4,6},{5,7},{6,4},{7,5},{8,10},{9,11},{10,... | collective-permute-start | bytes 4718600 | tf_op jit(solution)/shard_map/ppermute | solution.py:28
  48.6 22.9 %collective-permute-start.15 = (bf16[128,1024]{1,0:T(8,128)(2,1)}, bf16[128,1024]{1,0:T(8,128)(2,1)S(1)}, u32[]{:S(2)}, u32[]{:S(2)}) collective-permute-start(bf16[128,1024]{1,0:T(8,128)(2,1)} %collective-permute-done.11), channel_id=1, source_target_pairs={{0,4},{4,0},{8,12},{12,8},{16,20},{20,16},{24,28},{28,24},{1,5},{5... | collective-permute-start | bytes 786440 | tf_op jit(solution)/shard_map/ppermute | solution.py:28
  49.4 22.1 %collective-permute-start.13 = (bf16[128,1024]{1,0:T(8,128)(2,1)}, bf16[128,1024]{1,0:T(8,128)(2,1)S(1)}, u32[]{:S(2)}, u32[]{:S(2)}) collective-permute-start(bf16[128,1024]{1,0:T(8,128)(2,1)} %collective-permute-done.8), channel_id=1, source_target_pairs={{0,4},{4,0},{8,12},{12,8},{16,20},{20,16},{24,28},{28,24},{1,5},{5... | collective-permute-start | bytes 786440 | tf_op jit(solution)/shard_map/ppermute | solution.py:28
  58.8 12.7 %collective-permute-start.14 = (bf16[128,1024]{1,0:T(8,128)(2,1)}, bf16[128,1024]{1,0:T(8,128)(2,1)S(1)}, u32[]{:S(2)}, u32[]{:S(2)}) collective-permute-start(bf16[128,1024]{1,0:T(8,128)(2,1)} %collective-permute-done.10), channel_id=1, source_target_pairs={{0,4},{4,0},{8,12},{12,8},{16,20},{20,16},{24,28},{28,24},{1,5},{5... | collective-permute-start | bytes 786440 | tf_op jit(solution)/shard_map/ppermute | solution.py:28
  60.5 28.7 %copy-start.5 = (bf16[512,1024]{1,0:T(8,128)(2,1)}, bf16[512,1024]{1,0:T(8,128)(2,1)S(1)}, u32[]{:S(2)}) copy-start(bf16[512,1024]{1,0:T(8,128)(2,1)S(1)} %pad_maximum_fusion.q_ref) | copy-start | bytes 3145732
  60.5 11.0 %copy-start.25 = (bf16[128,1024]{1,0:T(8,128)(2,1)S(1)}, bf16[128,1024]{1,0:T(8,128)(2,1)}, u32[]{:S(2)}) copy-start(bf16[128,1024]{1,0:T(8,128)(2,1)} %copy-done.24) | copy-start | bytes 786436
  71.5 17.7 %copy-start = (f32[1024,512]{1,0:T(8,128)}, f32[1024,512]{1,0:T(8,128)S(1)}, u32[]{:S(2)}) copy-start(f32[1024,512]{1,0:T(8,128)S(1)} %get-tuple-element.59.acc_ref) | copy-start | bytes 6291460
  71.7 26.8 %copy-start.8 = (bf16[512,1024]{1,0:T(8,128)(2,1)}, bf16[512,1024]{1,0:T(8,128)(2,1)S(1)}, u32[]{:S(2)}) copy-start(bf16[512,1024]{1,0:T(8,128)(2,1)S(1)} %constant_dynamic-update-slice_fusion.q_ref) | copy-start | bytes 3145732
  83.3 15.2 %copy-start.3 = (f32[1024,512]{1,0:T(8,128)}, f32[1024,512]{1,0:T(8,128)S(1)}, u32[]{:S(2)}) copy-start(f32[1024,512]{1,0:T(8,128)S(1)} %get-tuple-element.61.acc_ref) | copy-start | bytes 6291460
  83.3 15.2 %copy-start.12 = (f32[8,8,512]{2,1,0:T(8,128)}, f32[8,8,512]{2,1,0:T(8,128)S(1)}, u32[]{:S(2)}) copy-start(f32[8,8,512]{2,1,0:T(8,128)S(1)} %get-tuple-element.55.stat_ref) | copy-start | bytes 393220
  83.4 2.4 %collective-permute-start.17 = (bf16[2,512,384]{2,1,0:T(8,128)(2,1)S(1)}, bf16[2,512,384]{2,1,0:T(8,128)(2,1)S(1)}, u32[]{:S(2)}, u32[]{:S(2)}) collective-permute-start(bf16[2,512,384]{2,1,0:T(8,128)(2,1)S(1)} %slice_bitcast_fusion.1), channel_id=1, source_target_pairs={{0,1},{1,0},{2,3},{3,2},{4,5},{5,4},{6,7},{7,6},{8,9},{9,8},{10,11... | collective-permute-start | bytes 2359304 | tf_op jit(solution)/shard_map/ppermute | solution.py:28
  92.6 10.1 %copy-start.10 = (bf16[4,416,128]{2,1,0:T(8,128)(2,1)}, bf16[4,416,128]{2,1,0:T(8,128)(2,1)S(1)}, u32[]{:S(2)}) copy-start(bf16[4,416,128]{2,1,0:T(8,128)(2,1)S(1)} %far_tiles.6.a_ref) | copy-start | bytes 1277956
  96.1 2.4 %collective-permute-start.21 = (bf16[2,512,384]{2,1,0:T(8,128)(2,1)S(1)}, bf16[2,512,384]{2,1,0:T(8,128)(2,1)S(1)}, u32[]{:S(2)}, u32[]{:S(2)}) collective-permute-start(bf16[2,512,384]{2,1,0:T(8,128)(2,1)S(1)} %slice_bitcast_fusion), channel_id=1, source_target_pairs={{0,1},{1,0},{2,3},{3,2},{4,5},{5,4},{6,7},{7,6},{8,9},{9,8},{10,11... | collective-permute-start | bytes 2359304 | tf_op jit(solution)/shard_map/ppermute | solution.py:28
  96.2 27.5 %collective-permute-start.19 = (bf16[2,2,512,256]{3,2,1,0:T(8,128)(2,1)}, bf16[2,2,512,256]{3,2,1,0:T(8,128)(2,1)S(1)}, u32[]{:S(2)}, u32[]{:S(2)}) collective-permute-start(bf16[2,2,512,256]{3,2,1,0:T(8,128)(2,1)} %get-tuple-element.64), channel_id=1, source_target_pairs={{0,2},{1,3},{2,0},{3,1},{4,6},{5,7},{6,4},{7,5},{8,10},{9,11},{10,... | collective-permute-start | bytes 3145736 | tf_op jit(solution)/shard_map/ppermute | solution.py:28
  97.8 12.8 %collective-permute-start.18 = (bf16[4,416,128]{2,1,0:T(8,128)(2,1)S(1)}, bf16[4,416,128]{2,1,0:T(8,128)(2,1)}, u32[]{:S(2)}, u32[]{:S(2)}) collective-permute-start(bf16[4,416,128]{2,1,0:T(8,128)(2,1)S(1)} %far_tiles.7), channel_id=1, source_target_pairs={{0,4},{4,0},{8,12},{12,8},{16,20},{20,16},{24,28},{28,24},{1,5},{5... | collective-permute-start | bytes 1277960 | tf_op jit(solution)/shard_map/ppermute | solution.py:28
  102.7 18.9 %collective-permute-start.22 = (bf16[4,416,128]{2,1,0:T(8,128)(2,1)}, bf16[4,416,128]{2,1,0:T(8,128)(2,1)}, u32[]{:S(2)}, u32[]{:S(2)}) collective-permute-start(bf16[4,416,128]{2,1,0:T(8,128)(2,1)} %far_tiles.9), channel_id=1, source_target_pairs={{0,4},{4,0},{8,12},{12,8},{16,20},{20,16},{24,28},{28,24},{1,5},{5... | collective-permute-start | bytes 1277960 | tf_op jit(solution)/shard_map/ppermute | solution.py:28
  112.6 11.2 %collective-permute-start.23 = (bf16[416,128]{1,0:T(8,128)(2,1)}, bf16[416,128]{1,0:T(8,128)(2,1)}, u32[]{:S(2)}, u32[]{:S(2)}) collective-permute-start(bf16[416,128]{1,0:T(8,128)(2,1)} %get-tuple-element.69), channel_id=1, source_target_pairs={{0,24},{4,28},{8,0},{12,4},{16,8},{20,12},{24,16},{28,20},{1,25},{... | collective-permute-start | bytes 319496 | tf_op jit(solution)/shard_map/ppermute | solution.py:33
  113.7 10.0 %collective-permute-start.24 = (bf16[416,128]{1,0:T(8,128)(2,1)}, bf16[416,128]{1,0:T(8,128)(2,1)}, u32[]{:S(2)}, u32[]{:S(2)}) collective-permute-start(bf16[416,128]{1,0:T(8,128)(2,1)} %get-tuple-element.70), channel_id=1, source_target_pairs={{0,16},{4,20},{8,24},{12,28},{16,0},{20,4},{24,8},{28,12},{1,17},{... | collective-permute-start | bytes 319496 | tf_op jit(solution)/shard_map/ppermute | solution.py:33
  113.7 10.0 %collective-permute-start.25 = (bf16[416,128]{1,0:T(8,128)(2,1)}, bf16[416,128]{1,0:T(8,128)(2,1)}, u32[]{:S(2)}, u32[]{:S(2)}) collective-permute-start(bf16[416,128]{1,0:T(8,128)(2,1)} %get-tuple-element.71), channel_id=1, source_target_pairs={{0,8},{4,12},{8,16},{12,20},{16,24},{20,28},{24,0},{28,4},{1,9},{5... | collective-permute-start | bytes 319496 | tf_op jit(solution)/shard_map/ppermute | solution.py:33
  114.6 1.6 copy-start.1
  116.2 1.2 copy-start.6
  120.9 0.8 copy-start.11
  123.7 14.0 %copy-start.7 = (bf16[512,1024]{1,0:T(8,128)(2,1)S(1)}, bf16[512,1024]{1,0:T(8,128)(2,1)}, u32[]{:S(2)}) copy-start(bf16[512,1024]{1,0:T(8,128)(2,1)} %copy-done.5) | copy-start | bytes 3145732
  123.8 14.0 %copy-start.2 = (f32[1024,512]{1,0:T(8,128)S(1)}, f32[1024,512]{1,0:T(8,128)}, u32[]{:S(2)}) copy-start(f32[1024,512]{1,0:T(8,128)} %copy-done) | copy-start | bytes 6291460
  123.8 2.0 %collective-permute-start.26 = (bf16[2,512,256]{2,1,0:T(8,128)(2,1)S(1)}, bf16[2,512,256]{2,1,0:T(8,128)(2,1)S(1)}, u32[]{:S(2)}, u32[]{:S(2)}) collective-permute-start(bf16[2,512,256]{2,1,0:T(8,128)(2,1)S(1)} %slice_bitcast_fusion.2), channel_id=1, source_target_pairs={{0,1},{1,0},{2,3},{3,2},{4,5},{5,4},{6,7},{7,6},{8,9},{9,8},{10,11... | collective-permute-start | bytes 1572872 | tf_op jit(solution)/shard_map/ppermute | solution.py:28
  125.8 1.6 copy-start.4
  127.4 1.2 copy-start.9
  128.6 0.9 copy-start.13
  129.5 8.3 %copy-start.34 = (bf16[416,128]{1,0:T(8,128)(2,1)S(1)}, bf16[416,128]{1,0:T(8,128)(2,1)}, u32[]{:S(2)}) copy-start(bf16[416,128]{1,0:T(8,128)(2,1)} %get-tuple-element.78) | copy-start | bytes 319492
  132.0 9.0 %collective-permute-start.30 = (bf16[4,272,128]{2,1,0:T(8,128)(2,1)S(1)}, bf16[4,272,128]{2,1,0:T(8,128)(2,1)S(1)}, u32[]{:S(2)}, u32[]{:S(2)}) collective-permute-start(bf16[4,272,128]{2,1,0:T(8,128)(2,1)S(1)} %far_tiles.10), channel_id=1, source_target_pairs={{0,4},{4,0},{8,12},{12,8},{16,20},{20,16},{24,28},{28,24},{1,5},{5... | collective-permute-start | bytes 835592 | tf_op jit(solution)/shard_map/ppermute | solution.py:28
  133.4 14.0 %collective-permute-start.27 = (bf16[416,128]{1,0:T(8,128)(2,1)}, bf16[416,128]{1,0:T(8,128)(2,1)S(1)}, u32[]{:S(2)}, u32[]{:S(2)}) collective-permute-start(bf16[416,128]{1,0:T(8,128)(2,1)} %get-tuple-element.76), channel_id=1, source_target_pairs={{0,24},{4,28},{8,0},{12,4},{16,8},{20,12},{24,16},{28,20},{1,25},{... | collective-permute-start | bytes 319496 | tf_op jit(solution)/shard_map/ppermute | solution.py:33
  136.6 14.3 %collective-permute-start.28 = (bf16[416,128]{1,0:T(8,128)(2,1)}, bf16[416,128]{1,0:T(8,128)(2,1)S(1)}, u32[]{:S(2)}, u32[]{:S(2)}) collective-permute-start(bf16[416,128]{1,0:T(8,128)(2,1)} %get-tuple-element.77), channel_id=1, source_target_pairs={{0,16},{4,20},{8,24},{12,28},{16,0},{20,4},{24,8},{28,12},{1,17},{... | collective-permute-start | bytes 319496 | tf_op jit(solution)/shard_map/ppermute | solution.py:33
  137.8 10.5 %copy-start.35 = (f32[16]{0:T(128)S(1)}, f32[16]{0:T(128)}, u32[]{:S(2)}) copy-start(f32[16]{0:T(128)} %param.18) | copy-start | bytes 196
  137.8 13.2 %collective-permute-start.29 = (bf16[416,128]{1,0:T(8,128)(2,1)S(1)}, bf16[416,128]{1,0:T(8,128)(2,1)S(1)}, u32[]{:S(2)}, u32[]{:S(2)}) collective-permute-start(bf16[416,128]{1,0:T(8,128)(2,1)S(1)} %copy-done.34), channel_id=1, source_target_pairs={{0,8},{4,12},{8,16},{12,20},{16,24},{20,28},{24,0},{28,4},{1,9},{5... | collective-permute-start | bytes 319496 | tf_op jit(solution)/shard_map/ppermute | solution.py:33
  143.6 10.7 %collective-permute-start.31 = (bf16[272,128]{1,0:T(8,128)(2,1)}, bf16[272,128]{1,0:T(8,128)(2,1)S(1)}, u32[]{:S(2)}, u32[]{:S(2)}) collective-permute-start(bf16[272,128]{1,0:T(8,128)(2,1)} %get-tuple-element.80), channel_id=1, source_target_pairs={{0,24},{4,28},{8,0},{12,4},{16,8},{20,12},{24,16},{28,20},{1,25},{... | collective-permute-start | bytes 208904 | tf_op jit(solution)/shard_map/ppermute | solution.py:33
  147.4 6.9 %collective-permute-start.32 = (bf16[272,128]{1,0:T(8,128)(2,1)}, bf16[272,128]{1,0:T(8,128)(2,1)S(1)}, u32[]{:S(2)}, u32[]{:S(2)}) collective-permute-start(bf16[272,128]{1,0:T(8,128)(2,1)} %get-tuple-element.81), channel_id=1, source_target_pairs={{0,16},{4,20},{8,24},{12,28},{16,0},{20,4},{24,8},{28,12},{1,17},{... | collective-permute-start | bytes 208904 | tf_op jit(solution)/shard_map/ppermute | solution.py:33
  147.4 3.6 %copy-start.26 = (bf16[416,128]{1,0:T(8,128)(2,1)}, bf16[416,128]{1,0:T(8,128)(2,1)S(1)}, u32[]{:S(2)}) copy-start(bf16[416,128]{1,0:T(8,128)(2,1)S(1)} %collective-permute-done.27.refs_1_) | copy-start | bytes 319492
  147.4 7.0 %collective-permute-start.33 = (bf16[272,128]{1,0:T(8,128)(2,1)}, bf16[272,128]{1,0:T(8,128)(2,1)S(1)}, u32[]{:S(2)}, u32[]{:S(2)}) collective-permute-start(bf16[272,128]{1,0:T(8,128)(2,1)} %get-tuple-element.82), channel_id=1, source_target_pairs={{0,8},{4,12},{8,16},{12,20},{16,24},{20,28},{24,0},{28,4},{1,9},{5... | collective-permute-start | bytes 208904 | tf_op jit(solution)/shard_map/ppermute | solution.py:33
  151.0 8.2 %copy-start.16 = (bf16[384,128]{1,0:T(8,128)(2,1)S(1)}, bf16[384,128]{1,0:T(8,128)(2,1)}, u32[]{:S(2)}) copy-start(bf16[384,128]{1,0:T(8,128)(2,1)} %merge_all.3) | copy-start | bytes 294916
  154.3 4.8 %copy-start.17 = (bf16[384,128]{1,0:T(8,128)(2,1)S(1)}, bf16[384,128]{1,0:T(8,128)(2,1)}, u32[]{:S(2)}) copy-start(bf16[384,128]{1,0:T(8,128)(2,1)} %merge_all.4) | copy-start | bytes 294916
  156.9 2.3 %copy-start.20 = (bf16[256,128]{1,0:T(8,128)(2,1)S(1)}, bf16[256,128]{1,0:T(8,128)(2,1)}, u32[]{:S(2)}) copy-start(bf16[256,128]{1,0:T(8,128)(2,1)} %merge_all.5) | copy-start | bytes 196612
  161.2 2.7 %collective-permute-start.34 = (bf16[128,1024]{1,0:T(8,128)(2,1)S(1)}, bf16[128,1024]{1,0:T(8,128)(2,1)S(1)}, u32[]{:S(2)}, u32[]{:S(2)}) collective-permute-start(bf16[128,1024]{1,0:T(8,128)(2,1)S(1)} %fusion.11), channel_id=1, source_target_pairs={{0,1},{1,0},{2,3},{3,2},{4,5},{5,4},{6,7},{7,6},{8,9},{9,8},{10,11... | collective-permute-start | bytes 786440 | tf_op jit(solution)/shard_map/ppermute | solution.py:28
  161.4 5.4 %collective-permute-start.35 = (bf16[128,1024]{1,0:T(8,128)(2,1)S(1)}, bf16[128,1024]{1,0:T(8,128)(2,1)S(1)}, u32[]{:S(2)}, u32[]{:S(2)}) collective-permute-start(bf16[128,1024]{1,0:T(8,128)(2,1)S(1)} %fusion.8), channel_id=1, source_target_pairs={{0,1},{1,0},{2,3},{3,2},{4,5},{5,4},{6,7},{7,6},{8,9},{9,8},{10,11... | collective-permute-start | bytes 786440 | tf_op jit(solution)/shard_map/ppermute | solution.py:28
  164.0 8.3 %collective-permute-start.36 = (bf16[128,1024]{1,0:T(8,128)(2,1)S(1)}, bf16[128,1024]{1,0:T(8,128)(2,1)S(1)}, u32[]{:S(2)}, u32[]{:S(2)}) collective-permute-start(bf16[128,1024]{1,0:T(8,128)(2,1)S(1)} %add_convert_fusion.1), channel_id=1, source_target_pairs={{0,2},{1,3},{2,0},{3,1},{4,6},{5,7},{6,4},{7,5},{8,10},{9,11},{10,... | collective-permute-start | bytes 786440 | tf_op jit(solution)/shard_map/ppermute | solution.py:28
  (9 other events, 6.0 us)
